TPU v7x, 32 devices: a whole 2x2x4 slice. The times are simulated.
32 devices in a mesh: groups: 2 (over y), seq: 4 (over z), head: 2 (over x), sub: 2 (over core).
Axes of the slice: x: 2, y: 2, z: 4, core: 2. Of those that a mesh axis runs over, the one named last changes fastest.
Arguments:
- inputs: bfloat16 [16384, 1536], P(('groups', 'seq'), ('head', 'sub')), parts along dimension 0, may hold values from -6 to 6
- b_proj: bfloat16 [16384, 128], P(('groups', 'seq')), parts along dimension 0, may hold values from -0.109375 to 0.109375
- c_proj: bfloat16 [16384, 128], P(('groups', 'seq')), parts along dimension 0, may hold values from -6 to 6
- step_codes: int32 [24, 16384], P(('head', 'sub'), ('groups', 'seq')), parts along dimension 1, may hold values from 0 to 3
- gate_codes: int32 [16384], P(('groups', 'seq')), parts along dimension 0, may hold values from 0 to 2
- decay_rates: float32 [24], P(('head', 'sub')), may hold values from 1.8310547e-05 to 0.12
- skip_gain: float32 [24], P(('head', 'sub')), may hold values from 0.5 to 1.5
- conv_weight: float32 [4, 1536], P(None, ('head', 'sub')), may hold values from -3 to 3
- out_cotangent: bfloat16 [16384, 1536], P(('groups', 'seq'), ('head', 'sub')), parts along dimension 0, may hold values from -6 to 6
Outputs:
- layer_out: bfloat16 [16384, 1536], P(('groups', 'seq'), ('head', 'sub')), parts along dimension 0
- input_grad: bfloat16 [16384, 1536], P(('groups', 'seq'), ('head', 'sub')), parts along dimension 0
- conv_grad: float32 [8, 1536], P('groups', ('head', 'sub')), parts along dimension 0
There are 2 independent parts, one for each index of `groups`. A program takes and returns all parts, laid end to end along the dimension named above; an argument that names none is the same for every part. Nothing has to cross between parts.
All inputs are finite; a program needn't handle non-finite values.
Results may differ from a plain program's by a relative error of at most 0.0062.
Values may be sent and summed in bfloat16 or wider, within the bound.
No kernel may reach another device: no remote copies, remote signals or barrier semaphores. Data moves between devices by JAX's collectives and lax.ppermute only.
A program may use at most 64 MiB of HBM per device.

v0:
```python
import jax
import jax.numpy as jnp
from jax import lax
from jax.sharding import PartitionSpec as P

BLOCK = 512


def shifted(block, axis, distance):
    devices = range(lax.axis_size(axis))
    route = [(i - distance, i) for i in devices if i - distance in devices]
    return lax.ppermute(block, axis, route)


def shards(
    inputs,
    b_proj,
    c_proj,
    step_codes,
    gate_codes,
    decay_rates,
    skip_gain,
    conv_weight,
    out_cotangent,
):
    row_count, channels = inputs.shape
    conv_taps = conv_weight.shape[0]
    head_count = decay_rates.shape[0]
    head_width = channels // head_count
    state_width = b_proj.shape[1]
    block_count = row_count // BLOCK
    highest = lax.Precision.HIGHEST
    before_rows = shifted(inputs[row_count - (conv_taps - 1) :], "seq", 1)
    padded = jnp.concatenate([before_rows, inputs], axis=0)
    preact = jnp.zeros((row_count, channels), jnp.float32)
    for offset in range(conv_taps):
        preact = preact + conv_weight[offset] * padded[offset : offset + row_count].astype(
            jnp.float32
        )
    mixed_in = jax.nn.silu(preact).astype(jnp.bfloat16)
    step_size = jnp.exp2(-step_codes.astype(jnp.float32))
    log_decay = (
        -decay_rates[:, None] * step_size
        + jnp.log(1.0 - gate_codes.astype(jnp.float32) / 4.0)[None, :]
    )
    cum_decay = jnp.cumsum(log_decay.reshape(head_count, block_count, BLOCK), axis=-1).transpose(
        1, 0, 2
    )
    step_blocks = step_size.reshape(head_count, block_count, BLOCK).transpose(1, 0, 2)
    mixed_blocks = mixed_in.reshape(block_count, BLOCK, head_count, head_width)
    grad_blocks = out_cotangent.reshape(block_count, BLOCK, head_count, head_width)
    b_blocks = b_proj.reshape(block_count, BLOCK, state_width)
    c_blocks = c_proj.reshape(block_count, BLOCK, state_width)
    causal = jnp.arange(BLOCK)[:, None] >= jnp.arange(BLOCK)[None, :]

    def local_block(unused, block_data):
        mixed_b, grad_b, b_block, c_block, cum_block, step_block = block_data
        scores = jnp.dot(c_block, b_block.T, preferred_element_type=jnp.float32)
        spread = cum_block[:, :, None] - cum_block[:, None, :]
        decays = jnp.exp(jnp.where(causal[None], spread, -jnp.inf))
        weights = (scores[None] * decays * step_block[:, None, :]).astype(jnp.bfloat16)
        ahead_part = jnp.einsum(
            "hts,shp->thp", weights, mixed_b, preferred_element_type=jnp.float32
        )
        behind_part = jnp.einsum(
            "hst,shp->thp", weights, grad_b, preferred_element_type=jnp.float32
        )
        block_total = cum_block[:, -1]
        in_factor = (jnp.exp(block_total[:, None] - cum_block) * step_block).T
        scaled_in = (mixed_b.astype(jnp.float32) * in_factor[:, :, None]).astype(jnp.bfloat16)
        fresh_state = jnp.einsum(
            "thp,tn->hpn", scaled_in, b_block, preferred_element_type=jnp.float32
        )
        scaled_out = (grad_b.astype(jnp.float32) * jnp.exp(cum_block).T[:, :, None]).astype(
            jnp.bfloat16
        )
        fresh_adjoint = jnp.einsum(
            "thp,tn->hpn", scaled_out, c_block, preferred_element_type=jnp.float32
        )
        return (unused, (ahead_part, behind_part, fresh_state, fresh_adjoint))

    unused_carry, block_results = lax.scan(
        local_block,
        jnp.zeros((), jnp.float32),
        (mixed_blocks, grad_blocks, b_blocks, c_blocks, cum_decay, step_blocks),
    )
    ahead_parts, behind_parts, fresh_states, fresh_adjoints = block_results
    block_totals = cum_decay[:, :, -1]
    zero_state = jnp.zeros((head_count, head_width, state_width), jnp.float32)
    running = zero_state
    start_list = []
    for block_index in range(block_count):
        start_list.append(running)
        running = (
            jnp.exp(block_totals[block_index])[:, None, None] * running + fresh_states[block_index]
        )
    local_end = running
    running = zero_state
    later_list = []
    for block_index in range(block_count - 1, -1, -1):
        later_list.append(running)
        running = (
            jnp.exp(block_totals[block_index])[:, None, None] * running
            + fresh_adjoints[block_index]
        )
    end_list = later_list[::-1]
    device_total = jnp.sum(block_totals, axis=0)
    totals_all = lax.all_gather(device_total[None], "seq", axis=0, tiled=True)
    position = lax.axis_index("seq")
    prefix = jnp.cumsum(totals_all, axis=0) - totals_all
    own_prefix = lax.dynamic_slice_in_dim(prefix, position, 1, 0)[0]
    end_pieces = lax.all_gather(local_end[None], "seq", axis=0, tiled=True)
    start_pieces = lax.all_gather(running[None], "seq", axis=0, tiled=True)
    piece_count = end_pieces.shape[0]
    sources = jnp.arange(piece_count, dtype=jnp.int32)
    from_below = (sources < position)[:, None]
    from_above = (sources > position)[:, None]
    forward_weight = jnp.exp(
        jnp.where(from_below, own_prefix[None] - prefix - totals_all, -jnp.inf)
    )
    backward_weight = jnp.exp(
        jnp.where(from_above, prefix - own_prefix[None] - device_total[None], -jnp.inf)
    )
    forward_sum = jnp.einsum("jh,jhpn->hpn", forward_weight, end_pieces, precision=highest)
    backward_sum = jnp.einsum("jh,jhpn->hpn", backward_weight, start_pieces, precision=highest)
    before_blocks = jnp.cumsum(block_totals, axis=0) - block_totals
    after_blocks = device_total[None] - jnp.cumsum(block_totals, axis=0)
    start_states = jnp.exp(before_blocks)[:, :, None, None] * forward_sum[None] + jnp.stack(
        start_list
    )
    end_adjoints = jnp.exp(after_blocks)[:, :, None, None] * backward_sum[None] + jnp.stack(
        end_list
    )
    carried_out = jnp.einsum(
        "btn,bhpn->bthp",
        c_blocks,
        start_states.astype(jnp.bfloat16),
        preferred_element_type=jnp.float32,
    )
    carried_out = carried_out * jnp.exp(cum_decay).transpose(0, 2, 1)[..., None]
    skip_wide = skip_gain[None, None, :, None]
    layer_out = (skip_wide * mixed_blocks.astype(jnp.float32) + ahead_parts + carried_out).astype(
        jnp.bfloat16
    )
    layer_out = layer_out.reshape(row_count, channels)
    back_factor = (step_blocks * jnp.exp(block_totals[:, :, None] - cum_decay)).transpose(0, 2, 1)
    carried_back = jnp.einsum(
        "btn,bhpn->bthp",
        b_blocks,
        end_adjoints.astype(jnp.bfloat16),
        preferred_element_type=jnp.float32,
    )
    carried_back = carried_back * back_factor[..., None]
    grad_in = (skip_wide * grad_blocks.astype(jnp.float32) + behind_parts + carried_back).reshape(
        row_count, channels
    )
    gate_value = jax.nn.sigmoid(preact)
    grad_pre = grad_in * gate_value * (1.0 + preact * (1.0 - gate_value))
    after_rows = shifted(grad_pre[: conv_taps - 1], "seq", -1)
    extended = jnp.concatenate([grad_pre, after_rows], axis=0)
    input_grad = jnp.zeros((row_count, channels), jnp.float32)
    for offset in range(conv_taps):
        shift_from = conv_taps - 1 - offset
        input_grad = (
            input_grad + conv_weight[offset] * extended[shift_from : shift_from + row_count]
        )
    tap_sums = [
        jnp.sum(grad_pre * padded[offset : offset + row_count].astype(jnp.float32), axis=0)
        for offset in range(conv_taps)
    ]
    local_grad = jnp.stack(tap_sums)
    conv_grad = lax.psum(local_grad, "seq") * (row_count * lax.axis_size("seq")) ** (-0.5)
    return (layer_out, input_grad.astype(jnp.bfloat16), conv_grad)


def solution(mesh):
    in_specs = (
        P(("groups", "seq"), ("head", "sub")),
        P(("groups", "seq"), None),
        P(("groups", "seq"), None),
        P(("head", "sub"), ("groups", "seq")),
        P(("groups", "seq")),
        P(("head", "sub")),
        P(("head", "sub")),
        P(None, ("head", "sub")),
        P(("groups", "seq"), ("head", "sub")),
    )
    out_specs = (
        P(("groups", "seq"), ("head", "sub")),
        P(("groups", "seq"), ("head", "sub")),
        P("groups", ("head", "sub")),
    )
    return jax.shard_map(shards, mesh=mesh, in_specs=in_specs, out_specs=out_specs, check_vma=False)
```

profile of v0, /device:TPU:0, one launch (start us, length us, event | category | flops | bytes accessed | tf_op | source)
XLA Modules:
  0.0 186.4 jit_solution(6552634328493133739)
XLA Ops:
  2.2 4.9 %collective-permute-start = (bf16[3,384]{0,1:T(8,128)(2,1)}, bf16[3,384]{0,1:T(8,128)(2,1)S(1)}, u32[]{:S(2)}, u32[]{:S(2)}) collective-permute-start(bf16[3,384]{0,1:T(8,128)(2,1)} %copy.102), channel_id=1, source_target_pairs={{0,4},{4,8},{8,12},{1,5},{5,9},{9,13},{2,6},{6,10},{10,14},{3,7},{... | collective-permute-start | bytes 6920 | tf_op jit(solution)/shard_map/ppermute | solution.py:12
  9.5 7.2 %reduce-window.6 = f32[6,4,4,128]{3,2,1,0:T(4,128)S(1)} reduce-window(f32[6,4,4,128]{3,2,1,0:T(4,128)S(1)} %reshape.125, f32[]{:T(128)} %constant.51.clone.1), window={size=1x1x1x128 pad=0_0x0_0x0_0x127_0}, to_apply=%region_0.1 | reduce-window | flops 1560576 | bytes 98308 | tf_op jit(solution)/shard_map/reduce-window
  20.7 9.9 %all-reduce = f32[24]{0:T(128)S(1)} all-reduce(f32[24]{0:T(128)S(1)} %dynamic-update-slice), channel_id=2, replica_groups=mesh['groups'=2,'seq'=4,'head'=2,'sub'=2] {'seq'}, use_global_device_ids=true, to_apply=%add | all-reduce | flops 24 | bytes 192
  35.9 2.9 %reshape.128 = bf16[4,512,6,64]{1,0,3,2:T(4,128)(2,1)S(1)} reshape(bf16[2048,384]{0,1:T(8,128)(2,1)} %copy.108) | data formatting | bytes 3145728 | tf_op jit(solution)/shard_map/reshape | solution.py:51
  40.7 4.2 %multiply_convert_fusion.13 = (bf16[2048,384]{0,1:T(8,128)(2,1)}, f32[2048,384]{0,1:T(8,128)}) fusion(bf16[2048,384]{0,1:T(8,128)(2,1)S(1)} %copy.103, f32[384]{0:T(512)S(1)} %get-tuple-element.162, bf16[3,384]{0,1:T(8,128)(2,1)S(1)} %collective-permute-done, f32[384]{0:T(512)S(1)} %get-tuple-element.163, f32[384]{0:T(512)S(1)} %get-tuple-element.161, ...), kind=kLoop, calls=%fused_computation.84 | loop fusion | flops 19660800 | bytes 6299904 | tf_op jit(solution)/shard_map/convert_element_type | solution.py:40
  44.9 2.9 %reshape.122 = bf16[4,512,6,64]{1,0,3,2:T(4,128)(2,1)S(1)} reshape(bf16[2048,384]{0,1:T(8,128)(2,1)} %get-tuple-element.195) | data formatting | bytes 3145728 | tf_op jit(solution)/shard_map/reshape | solution.py:50
  49.4 55.1 %while.17 = (s32[]{:T(128)}, f32[4,512,6,64]{1,3,2,0:T(8,128)}, f32[4,512,6,64]{1,3,2,0:T(8,128)}, f32[4,6,64,128]{3,2,1,0:T(8,128)}, f32[4,6,64,128]{3,2,1,0:T(...) while((s32[]{:T(128)}, f32[4,512,6,64]{1,3,2,0:T(8,128)}, ...), condition=%wide.region_3.4_spmd.clone, body=%wide.region_2.3_spmd.clone.sunk | while | flops 587601920 | bytes 8374465 | solution.py:82
  50.8 3.9 %fusion.108 = f32[4,512,6,64]{1,3,2,0:T(8,128)} fusion(f32[4,512,6,64]{1,3,2,0:T(8,128)} %get-tuple-element.310, s32[]{:T(128)} %get-tuple-element.308, f32[6,512]{1,0:T(8,128)S(1)} %bitcast.175, f32[6,512]{1,0:T(8,128)S(1)} %bitcast.177, f32[512,512]{1,0:T(8,128)S(1)} %fusion.106, pred[512,512]{1,0:T(8,128)(4,1)S(1)} %iota_compare_fusion.4, ...), kind=kOutput, calls=%fused_computation.7.clone.1 | convolution fusion | flops 209190912 | bytes 2540544 | tf_op jit(solution)/shard_map/while/body/eval_jaxpr/hst,shp->thp/dot_general | solution.py:65
  54.7 3.9 %fusion.107 = f32[4,512,6,64]{1,3,2,0:T(8,128)} fusion(f32[4,512,6,64]{1,3,2,0:T(8,128)} %get-tuple-element.309, s32[]{:T(128)} %get-tuple-element.308, f32[6,512]{1,0:T(8,128)S(1)} %bitcast.176, f32[6,512]{1,0:T(8,128)S(1)} %bitcast.178, f32[512,512]{1,0:T(8,128)S(1)} %fusion.106, pred[512,512]{1,0:T(8,128)(4,1)S(1)} %iota_compare_fusion.4, ...), kind=kOutput, calls=%fused_computation.5.clone.1 | convolution fusion | flops 209190912 | bytes 2540544 | tf_op jit(solution)/shard_map/while/body/eval_jaxpr/hts,shp->thp/dot_general | solution.py:62
  59.1 2.0 %fusion.109 = f32[4,6,64,128]{3,2,1,0:T(8,128)} fusion(f32[4,6,64,128]{3,2,1,0:T(8,128)} %get-tuple-element.311, s32[]{:T(128)} %get-tuple-element.308, f32[512,6]{0,1:T(8,128)S(1)} %copy.156, bf16[4,512,6,64]{1,3,2,0:T(8,128)(2,1)} %get-tuple-element.325, bf16[4,512,128]{2,1,0:T(8,128)(2,1)} %get-tuple-element.327), kind=kOutput, calls=%fused_computation.11.clone.1 | convolution fusion | flops 50921472 | bytes 734720 | tf_op jit(solution)/shard_map/while/body/eval_jaxpr/thp,tn->hpn/dot_general | solution.py:71
  61.2 2.0 %fusion.110 = f32[4,6,64,128]{3,2,1,0:T(8,128)} fusion(f32[4,6,64,128]{3,2,1,0:T(8,128)} %get-tuple-element.312, s32[]{:T(128)} %get-tuple-element.308, f32[512,6]{0,1:T(8,128)S(1)} %copy.157, bf16[4,512,6,64]{1,3,2,0:T(8,128)(2,1)} %get-tuple-element.330, bf16[4,512,128]{2,1,0:T(8,128)(2,1)S(1)} %get-tuple-element.326), kind=kOutput, calls=%fused_computation.9.clone.1 | convolution fusion | flops 50921472 | bytes 738816 | tf_op jit(solution)/shard_map/while/body/eval_jaxpr/thp,tn->hpn/dot_general | solution.py:77
  64.5 3.9 %fusion.108 = f32[4,512,6,64]{1,3,2,0:T(8,128)} fusion(f32[4,512,6,64]{1,3,2,0:T(8,128)} %get-tuple-element.310, s32[]{:T(128)} %get-tuple-element.308, f32[6,512]{1,0:T(8,128)S(1)} %bitcast.175, f32[6,512]{1,0:T(8,128)S(1)} %bitcast.177, f32[512,512]{1,0:T(8,128)S(1)} %fusion.106, pred[512,512]{1,0:T(8,128)(4,1)S(1)} %iota_compare_fusion.4, ...), kind=kOutput, calls=%fused_computation.7.clone.1 | convolution fusion | flops 209190912 | bytes 2540544 | tf_op jit(solution)/shard_map/while/body/eval_jaxpr/hst,shp->thp/dot_general | solution.py:65
  68.4 3.9 %fusion.107 = f32[4,512,6,64]{1,3,2,0:T(8,128)} fusion(f32[4,512,6,64]{1,3,2,0:T(8,128)} %get-tuple-element.309, s32[]{:T(128)} %get-tuple-element.308, f32[6,512]{1,0:T(8,128)S(1)} %bitcast.176, f32[6,512]{1,0:T(8,128)S(1)} %bitcast.178, f32[512,512]{1,0:T(8,128)S(1)} %fusion.106, pred[512,512]{1,0:T(8,128)(4,1)S(1)} %iota_compare_fusion.4, ...), kind=kOutput, calls=%fused_computation.5.clone.1 | convolution fusion | flops 209190912 | bytes 2540544 | tf_op jit(solution)/shard_map/while/body/eval_jaxpr/hts,shp->thp/dot_general | solution.py:62
  72.8 2.0 %fusion.109 = f32[4,6,64,128]{3,2,1,0:T(8,128)} fusion(f32[4,6,64,128]{3,2,1,0:T(8,128)} %get-tuple-element.311, s32[]{:T(128)} %get-tuple-element.308, f32[512,6]{0,1:T(8,128)S(1)} %copy.156, bf16[4,512,6,64]{1,3,2,0:T(8,128)(2,1)} %get-tuple-element.325, bf16[4,512,128]{2,1,0:T(8,128)(2,1)} %get-tuple-element.327), kind=kOutput, calls=%fused_computation.11.clone.1 | convolution fusion | flops 50921472 | bytes 734720 | tf_op jit(solution)/shard_map/while/body/eval_jaxpr/thp,tn->hpn/dot_general | solution.py:71
  74.9 2.0 %fusion.110 = f32[4,6,64,128]{3,2,1,0:T(8,128)} fusion(f32[4,6,64,128]{3,2,1,0:T(8,128)} %get-tuple-element.312, s32[]{:T(128)} %get-tuple-element.308, f32[512,6]{0,1:T(8,128)S(1)} %copy.157, bf16[4,512,6,64]{1,3,2,0:T(8,128)(2,1)} %get-tuple-element.330, bf16[4,512,128]{2,1,0:T(8,128)(2,1)S(1)} %get-tuple-element.326), kind=kOutput, calls=%fused_computation.9.clone.1 | convolution fusion | flops 50921472 | bytes 738816 | tf_op jit(solution)/shard_map/while/body/eval_jaxpr/thp,tn->hpn/dot_general | solution.py:77
  78.2 4.0 %fusion.108 = f32[4,512,6,64]{1,3,2,0:T(8,128)} fusion(f32[4,512,6,64]{1,3,2,0:T(8,128)} %get-tuple-element.310, s32[]{:T(128)} %get-tuple-element.308, f32[6,512]{1,0:T(8,128)S(1)} %bitcast.175, f32[6,512]{1,0:T(8,128)S(1)} %bitcast.177, f32[512,512]{1,0:T(8,128)S(1)} %fusion.106, pred[512,512]{1,0:T(8,128)(4,1)S(1)} %iota_compare_fusion.4, ...), kind=kOutput, calls=%fused_computation.7.clone.1 | convolution fusion | flops 209190912 | bytes 2540544 | tf_op jit(solution)/shard_map/while/body/eval_jaxpr/hst,shp->thp/dot_general | solution.py:65
  82.1 3.9 %fusion.107 = f32[4,512,6,64]{1,3,2,0:T(8,128)} fusion(f32[4,512,6,64]{1,3,2,0:T(8,128)} %get-tuple-element.309, s32[]{:T(128)} %get-tuple-element.308, f32[6,512]{1,0:T(8,128)S(1)} %bitcast.176, f32[6,512]{1,0:T(8,128)S(1)} %bitcast.178, f32[512,512]{1,0:T(8,128)S(1)} %fusion.106, pred[512,512]{1,0:T(8,128)(4,1)S(1)} %iota_compare_fusion.4, ...), kind=kOutput, calls=%fused_computation.5.clone.1 | convolution fusion | flops 209190912 | bytes 2540544 | tf_op jit(solution)/shard_map/while/body/eval_jaxpr/hts,shp->thp/dot_general | solution.py:62
  86.6 2.0 %fusion.109 = f32[4,6,64,128]{3,2,1,0:T(8,128)} fusion(f32[4,6,64,128]{3,2,1,0:T(8,128)} %get-tuple-element.311, s32[]{:T(128)} %get-tuple-element.308, f32[512,6]{0,1:T(8,128)S(1)} %copy.156, bf16[4,512,6,64]{1,3,2,0:T(8,128)(2,1)} %get-tuple-element.325, bf16[4,512,128]{2,1,0:T(8,128)(2,1)} %get-tuple-element.327), kind=kOutput, calls=%fused_computation.11.clone.1 | convolution fusion | flops 50921472 | bytes 734720 | tf_op jit(solution)/shard_map/while/body/eval_jaxpr/thp,tn->hpn/dot_general | solution.py:71
  88.7 2.0 %fusion.110 = f32[4,6,64,128]{3,2,1,0:T(8,128)} fusion(f32[4,6,64,128]{3,2,1,0:T(8,128)} %get-tuple-element.312, s32[]{:T(128)} %get-tuple-element.308, f32[512,6]{0,1:T(8,128)S(1)} %copy.157, bf16[4,512,6,64]{1,3,2,0:T(8,128)(2,1)} %get-tuple-element.330, bf16[4,512,128]{2,1,0:T(8,128)(2,1)S(1)} %get-tuple-element.326), kind=kOutput, calls=%fused_computation.9.clone.1 | convolution fusion | flops 50921472 | bytes 738816 | tf_op jit(solution)/shard_map/while/body/eval_jaxpr/thp,tn->hpn/dot_general | solution.py:77
  92.0 4.0 %fusion.108 = f32[4,512,6,64]{1,3,2,0:T(8,128)} fusion(f32[4,512,6,64]{1,3,2,0:T(8,128)} %get-tuple-element.310, s32[]{:T(128)} %get-tuple-element.308, f32[6,512]{1,0:T(8,128)S(1)} %bitcast.175, f32[6,512]{1,0:T(8,128)S(1)} %bitcast.177, f32[512,512]{1,0:T(8,128)S(1)} %fusion.106, pred[512,512]{1,0:T(8,128)(4,1)S(1)} %iota_compare_fusion.4, ...), kind=kOutput, calls=%fused_computation.7.clone.1 | convolution fusion | flops 209190912 | bytes 2540544 | tf_op jit(solution)/shard_map/while/body/eval_jaxpr/hst,shp->thp/dot_general | solution.py:65
  96.0 3.9 %fusion.107 = f32[4,512,6,64]{1,3,2,0:T(8,128)} fusion(f32[4,512,6,64]{1,3,2,0:T(8,128)} %get-tuple-element.309, s32[]{:T(128)} %get-tuple-element.308, f32[6,512]{1,0:T(8,128)S(1)} %bitcast.176, f32[6,512]{1,0:T(8,128)S(1)} %bitcast.178, f32[512,512]{1,0:T(8,128)S(1)} %fusion.106, pred[512,512]{1,0:T(8,128)(4,1)S(1)} %iota_compare_fusion.4, ...), kind=kOutput, calls=%fused_computation.5.clone.1 | convolution fusion | flops 209190912 | bytes 2540544 | tf_op jit(solution)/shard_map/while/body/eval_jaxpr/hts,shp->thp/dot_general | solution.py:62
  100.4 2.0 %fusion.109 = f32[4,6,64,128]{3,2,1,0:T(8,128)} fusion(f32[4,6,64,128]{3,2,1,0:T(8,128)} %get-tuple-element.311, s32[]{:T(128)} %get-tuple-element.308, f32[512,6]{0,1:T(8,128)S(1)} %copy.156, bf16[4,512,6,64]{1,3,2,0:T(8,128)(2,1)} %get-tuple-element.325, bf16[4,512,128]{2,1,0:T(8,128)(2,1)} %get-tuple-element.327), kind=kOutput, calls=%fused_computation.11.clone.1 | convolution fusion | flops 50921472 | bytes 734720 | tf_op jit(solution)/shard_map/while/body/eval_jaxpr/thp,tn->hpn/dot_general | solution.py:71
  106.3 17.3 %all_gather.11 = f32[4,6,64,128]{3,2,1,0:T(8,128)S(1)} all-gather(f32[1,6,64,128]{3,2,1,0:T(8,128)S(1)} %get-tuple-element.187), channel_id=1, replica_groups=mesh['groups'=2,'seq'=4,'head'=2,'sub'=2] {'seq'}, dimensions={0}, use_global_device_ids=true | all-gather | bytes 983040 | tf_op jit(solution)/shard_map/all_gather | solution.py:113
  125.5 2.2 %fusion.55 = f32[4,512,6,64]{1,3,2,0:T(8,128)S(1)} fusion(f32[4,512,6,64]{1,3,2,0:T(8,128)S(1)} %copy-done.7, bf16[4,512,128,1]{2,1,3,0:T(8,128)(2,1)} %bitcast.19, f32[4,512,6]{1,2,0:T(8,128)S(1)} %copy.118, f32[6]{0:T(128)S(1)} %copy-done.17, f32[1,6,64,128]{3,2,1,0:T(8,128)S(1)} %broadcast.73, f32[1,6,64,128]{3,2,1,0:T(8,128)S(1)} %get-tuple-element.190, ...), kind=kOutput, calls=%fused_computation.79 | convolution fusion | flops 206438400 | bytes 9420920 | tf_op jit(solution)/shard_map/btn,bhpn->bthp/dot_general | solution.py:147
  127.7 2.0 %copy.119 = f32[4,512,6,64]{1,0,3,2:T(4,128)S(1)} copy(f32[4,512,6,64]{1,3,2,0:T(8,128)S(1)} %fusion.55) | data formatting | bytes 6291456 | tf_op jit(solution)/shard_map/add | solution.py:154
  132.1 4.2 %fusion.50 = (f32[384]{0:T(512)S(1)}, f32[384]{0:T(512)S(1)}, f32[384]{0:T(512)S(1)}, f32[384]{0:T(512)S(1)}, f32[2048,384]{0,1:T(8,128)}) fusion(bf16[2048,384]{0,1:T(8,128)(2,1)S(1)} %copy-done.1, bf16[3,384]{0,1:T(8,128)(2,1)S(1)} %collective-permute-done, f32[2048,384]{0,1:T(8,128)S(1)} %copy-done.5, f32[2048,384]{0,1:T(8,128)S(1)} %bitcast.164), kind=kLoop, calls=%fused_computation.72 | loop fusion | flops 22804992 | bytes 11018496 | tf_op jit(solution)/shard_map/reduce_sum | solution.py:168
  136.3 10.1 %psum.7 = f32[4,384]{1,0:T(4,128)S(1)} all-reduce(f32[4,384]{1,0:T(4,128)S(1)} %pad_maximum_fusion.2), channel_id=1, replica_groups=mesh['groups'=2,'seq'=4,'head'=2,'sub'=2] {'seq'}, use_global_device_ids=true, to_apply=%region_11.12 | all-reduce | flops 1536 | bytes 12288 | tf_op jit(solution)/shard_map/psum | solution.py:172
  149.4 18.7 %all_gather.10 = f32[4,6,64,128]{3,2,1,0:T(8,128)S(1)} all-gather(f32[1,6,64,128]{3,2,1,0:T(8,128)S(1)} %get-tuple-element.211), channel_id=1, replica_groups=mesh['groups'=2,'seq'=4,'head'=2,'sub'=2] {'seq'}, dimensions={0}, use_global_device_ids=true | all-gather | bytes 983040 | tf_op jit(solution)/shard_map/all_gather | solution.py:112
  169.9 3.0 %fusion.57 = bf16[4,512,6,64]{1,3,2,0:T(8,128)(2,1)S(1)} fusion(f32[4,512,6,64]{1,3,2,0:T(8,128)} %get-tuple-element.68, bf16[4,512,128,1]{2,1,3,0:T(8,128)(2,1)S(1)} %bitcast.166, f32[4,512,6]{1,2,0:T(8,128)S(1)} %copy.114, f32[6]{0:T(128)S(1)} %copy-done.17, f32[1,6,64,128]{3,2,1,0:T(8,128)S(1)} %get-tuple-element.212, ...), kind=kOutput, calls=%fused_computation.82 | convolution fusion | flops 207224832 | bytes 7848056 | tf_op jit(solution)/shard_map/btn,bhpn->bthp/dot_general | solution.py:134
  176.2 2.6 %copy.120 = bf16[2048,384]{1,0:T(8,128)(2,1)} copy(bf16[2048,384]{0,1:T(8,128)(2,1)} %bitcast.168) | data formatting | bytes 3145728
  178.8 5.0 %fusion.44 = bf16[2048,384]{0,1:T(8,128)(2,1)} fusion(f32[2048,384]{0,1:T(8,128)S(1)} %copy-done.4, f32[3,384]{0,1:T(8,128)S(1)} %collective-permute-done.1, f32[384]{0:T(512)S(1)} %get-tuple-element.162, f32[384]{0:T(512)S(1)} %get-tuple-element.163, f32[384]{0:T(512)S(1)} %get-tuple-element.161, f32[384]{0:T(512)S(1)} %get-tuple-element.160), kind=kLoop, calls=%fused_computation.66 | loop fusion | flops 8650752 | bytes 4729344 | tf_op jit(solution)/shard_map/convert_element_type | solution.py:173
  183.8 2.6 %copy.121 = bf16[2048,384]{1,0:T(8,128)(2,1)} copy(bf16[2048,384]{0,1:T(8,128)(2,1)} %fusion.44) | data formatting | bytes 3145728
  (141 shorter events, 39.4 us)
Async XLA Ops:
  0.6 33.6 %copy-start.8 = (bf16[2048,384]{1,0:T(8,128)(2,1)S(1)}, bf16[2048,384]{1,0:T(8,128)(2,1)}, u32[]{:S(2)}) copy-start(bf16[2048,384]{1,0:T(8,128)(2,1)} %param.19) | copy-start | bytes 4718596
  2.2 38.4 %collective-permute-start = (bf16[3,384]{0,1:T(8,128)(2,1)}, bf16[3,384]{0,1:T(8,128)(2,1)S(1)}, u32[]{:S(2)}, u32[]{:S(2)}) collective-permute-start(bf16[3,384]{0,1:T(8,128)(2,1)} %copy.102), channel_id=1, source_target_pairs={{0,4},{4,8},{8,12},{1,5},{5,9},{9,13},{2,6},{6,10},{10,14},{3,7},{... | collective-permute-start | bytes 6920 | tf_op jit(solution)/shard_map/ppermute | solution.py:12
  18.1 13.4 %copy-start.9 = (f32[6]{0:T(128)}, f32[6]{0:T(128)S(1)}, u32[]{:S(2)}) copy-start(f32[6]{0:T(128)S(1)} %get-tuple-element.156) | copy-start | bytes 76
  18.1 13.4 %copy-start.11 = (f32[6]{0:T(128)}, f32[6]{0:T(128)S(1)}, u32[]{:S(2)}) copy-start(f32[6]{0:T(128)S(1)} %get-tuple-element.157) | copy-start | bytes 76
  34.2 6.5 %copy-start = (bf16[2048,384]{0,1:T(8,128)(2,1)}, bf16[2048,384]{0,1:T(8,128)(2,1)S(1)}, u32[]{:S(2)}) copy-start(bf16[2048,384]{0,1:T(8,128)(2,1)S(1)} %copy.103) | copy-start | bytes 4718596
  38.8 6.1 %copy-start.2 = (bf16[4,512,6,64]{1,0,3,2:T(4,128)(2,1)}, bf16[4,512,6,64]{1,0,3,2:T(4,128)(2,1)S(1)}, u32[]{:S(2)}) copy-start(bf16[4,512,6,64]{1,0,3,2:T(4,128)(2,1)S(1)} %reshape.128) | copy-start | bytes 4718596
  44.9 4.4 %copy-start.6 = (bf16[2048,128]{1,0:T(8,128)(2,1)S(1)}, bf16[2048,128]{1,0:T(8,128)(2,1)}, u32[]{:S(2)}) copy-start(bf16[2048,128]{1,0:T(8,128)(2,1)} %param.13) | copy-start | bytes 1572868
  49.3 55.1 %copy-start.10 = (f32[6]{0:T(128)S(1)}, f32[6]{0:T(128)}, u32[]{:S(2)}) copy-start(f32[6]{0:T(128)} %copy-done.9) | copy-start | bytes 76
  49.4 55.1 %copy-start.12 = (f32[6]{0:T(128)S(1)}, f32[6]{0:T(128)}, u32[]{:S(2)}) copy-start(f32[6]{0:T(128)} %copy-done.11) | copy-start | bytes 76
  49.4 55.1 %copy-start.13 = (f32[6]{0:T(128)S(1)}, f32[6]{0:T(128)}, u32[]{:S(2)}) copy-start(f32[6]{0:T(128)} %get-tuple-element.158) | copy-start | bytes 76
  49.4 55.1 %copy-start.14 = (f32[6]{0:T(128)S(1)}, f32[6]{0:T(128)}, u32[]{:S(2)}) copy-start(f32[6]{0:T(128)} %get-tuple-element.159) | copy-start | bytes 76
  49.4 55.1 %copy-start.15 = (f32[6]{0:T(128)S(1)}, f32[6]{0:T(128)}, u32[]{:S(2)}) copy-start(f32[6]{0:T(128)} %get-tuple-element.217) | copy-start | bytes 76
  49.4 55.1 %copy-start.16 = (f32[6]{0:T(128)S(1)}, f32[6]{0:T(128)}, u32[]{:S(2)}) copy-start(f32[6]{0:T(128)} %get-tuple-element.218) | copy-start | bytes 76
  104.5 21.0 %copy-start.3 = (bf16[4,512,6,64]{1,0,3,2:T(4,128)(2,1)S(1)}, bf16[4,512,6,64]{1,0,3,2:T(4,128)(2,1)}, u32[]{:S(2)}) copy-start(bf16[4,512,6,64]{1,0,3,2:T(4,128)(2,1)} %copy-done.2) | copy-start | bytes 4718596
  104.5 21.0 %copy-start.7 = (f32[4,512,6,64]{1,3,2,0:T(8,128)S(1)}, f32[4,512,6,64]{1,3,2,0:T(8,128)}, u32[]{:S(2)}) copy-start(f32[4,512,6,64]{1,3,2,0:T(8,128)} %get-tuple-element.70) | copy-start | bytes 9437188
  104.5 21.0 %copy-start.17 = (f32[6]{0:T(128)S(1)}, f32[6]{0:T(128)}, u32[]{:S(2)}) copy-start(f32[6]{0:T(128)} %param.17) | copy-start | bytes 76
  129.7 1.5 copy-start.1
  129.7 2.4 %copy-start.5 = (f32[2048,384]{0,1:T(8,128)S(1)}, f32[2048,384]{0,1:T(8,128)}, u32[]{:S(2)}) copy-start(f32[2048,384]{0,1:T(8,128)} %get-tuple-element.196) | copy-start | bytes 9437188
  148.1 30.7 %collective-permute-start.1 = (f32[3,384]{0,1:T(8,128)}, f32[3,384]{0,1:T(8,128)S(1)}, u32[]{:S(2)}, u32[]{:S(2)}) collective-permute-start(f32[3,384]{0,1:T(8,128)} %slice.143), channel_id=1, source_target_pairs={{4,0},{8,4},{12,8},{5,1},{9,5},{13,9},{6,2},{10,6},{14,10},{7,3},{... | collective-permute-start | bytes 13832 | tf_op jit(solution)/shard_map/ppermute | solution.py:12
  174.6 4.2 %copy-start.4 = (f32[2048,384]{0,1:T(8,128)S(1)}, f32[2048,384]{0,1:T(8,128)}, u32[]{:S(2)}) copy-start(f32[2048,384]{0,1:T(8,128)} %get-tuple-element.186) | copy-start | bytes 9437188
where the time goes:
time: 188 us; the launch traced here: 186 us
  matrix products  60.7 us (32%)
  blocking collectives  56 us (30%)
  local copies, waits for them, and re-layouts  34.3 us (18%)
  other arithmetic  27.2 us (14%)
  starting transfers between devices  6.2 us (3%)
    all_gather x1, blocking collectives, shards(): end_pieces = lax.all_gather(local_end[None], 'seq', axis=0, tiled=True)  18.7 us
    all_gather x1, blocking collectives, shards(): start_pieces = lax.all_gather(running[None], 'seq', axis=0, tiled=True)  17.3 us
    dot_general x4, matrix products, local_block(): jnp.einsum('hst,shp->thp', weights, grad_b, preferred_element_type=jnp.fl...  15.7 us
    dot_general x4, matrix products, local_block(): jnp.einsum('hts,shp->thp', weights, mixed_b, preferred_element_type=jnp.f...  15.7 us
    unnamed x46, local copies, waits for them, and re-layouts  15.7 us
    psum x1, blocking collectives, shards(): lax.psum(local_grad, 'seq') * (row_count * lax.axis_size('seq')) ** (-0.5)  10.1 us
    unnamed x1, blocking collectives  9.92 us
    dot_general x4, matrix products, local_block(): jnp.einsum('thp,tn->hpn', scaled_in, b_block, preferred_element_type=jnp....  7.97 us
  transfers between devices with their start and end apart: 2, of which 0 were waited for; matrix products, arithmetic and copies ran while one was open for 18% of the time, Pallas kernels for 0%

commit v1 on v0

v1 whole, which is shorter than its diff:
```python
import functools

import jax
import jax.numpy as jnp
from jax import lax
from jax.experimental import pallas as pl
from jax.experimental.pallas import tpu as pltpu
from jax.sharding import PartitionSpec as P

CHUNK = 128
STEP_ROWS = 512
LOG_ONE = -0.2876820724517809
LOG_TWO = -0.6931471805599453
F32 = jnp.float32
BF16 = jnp.bfloat16
HIGHEST = lax.Precision.HIGHEST
VMEM_LIMIT = 48 * 1024 * 1024


def dot(a, b, dims, precision=None):
    return lax.dot_general(a, b, (dims, ((), ())), preferred_element_type=F32, precision=precision)


def per_lane(scalars, count, channels):
    width = channels // count
    lane = lax.broadcasted_iota(jnp.int32, (1, channels), 1)
    row = jnp.zeros((1, channels), F32)
    for head in range(count):
        inside = (lane >= head * width) & (lane < (head + 1) * width)
        row = jnp.where(inside, scalars[head], row)
    return row


def split_two(value):
    high = value.astype(BF16)
    low = (value - high.astype(F32)).astype(BF16)
    return jnp.concatenate([high.astype(F32), low.astype(F32)], axis=0).astype(BF16)


def spread_matrix(count, channels):
    width = channels // count
    row = lax.broadcasted_iota(jnp.int32, (16, channels), 0)
    lane = lax.broadcasted_iota(jnp.int32, (16, channels), 1)
    return jnp.where((row % 8) == lane // width, 1.0, 0.0).astype(BF16)


def spread(pair, onehot):
    return dot(pair, onehot, ((0,), (0,)))


def adjoint_kernel(
    heads, rates, codes, gates, grad, c_proj, near_out, far_out, logs_out, pay_out,
    steps, front, total,
):
    rows = codes.shape[1]
    channels = grad.shape[1]
    chunks = rows // CHUNK
    step = pl.program_id(0)

    @pl.when(step == 0)
    def prepare():
        steps[...] = jnp.zeros_like(steps)
        steps[0:heads, :] = jnp.exp2(-codes[...].astype(F32))
        gate = gates[...]
        steps[6:7, :] = jnp.where(gate == 1, 1.0, 0.0).astype(F32)
        steps[7:8, :] = jnp.where(gate == 2, 1.0, 0.0).astype(F32)
        stacked = jnp.concatenate(
            [steps[:, j * CHUNK : (j + 1) * CHUNK] for j in range(chunks)], axis=0
        ).astype(BF16)
        low = lax.broadcasted_iota(jnp.int32, (CHUNK, CHUNK), 0)
        high = lax.broadcasted_iota(jnp.int32, (CHUNK, CHUNK), 1)
        upper = jnp.where(low <= high, 1.0, 0.0).astype(BF16)
        sums = dot(stacked, upper, ((1,), (0,)))
        sub = lax.broadcasted_iota(jnp.int32, (8, CHUNK), 0)
        rate = jnp.zeros((8, CHUNK), F32)
        for head in range(heads):
            rate = jnp.where(sub == head, rates[head], rate)
        cums, mids, befores = [], [], []
        before = jnp.zeros((8, 1), F32)
        for j in range(chunks):
            part = sums[8 * j : 8 * j + 8, :]
            cum = LOG_ONE * part[6:7, :] + LOG_TWO * part[7:8, :] - rate * part
            cums.append(cum)
            mids.append(cum[:, CHUNK // 2 - 1 : CHUNK // 2])
            befores.append(before)
            before = before + cum[:, CHUNK - 1 : CHUNK]
        for j in range(chunks):
            at = slice(j * CHUNK, (j + 1) * CHUNK)
            size = steps[:, at]
            near_out[0:16, at] = split_two(jnp.exp(cums[j] - mids[j]))
            near_out[16:32, at] = split_two(jnp.exp(mids[j] - cums[j]) * size)
            front[:, at] = split_two(jnp.exp(befores[j] + cums[j]))
            far_out[:, at] = split_two(jnp.exp(before - befores[j] - cums[j]) * size)
        pick = lax.broadcasted_iota(jnp.int32, (8, CHUNK), 0)
        place = lax.broadcasted_iota(jnp.int32, (8, CHUNK), 1)
        chosen = jnp.where((pick == 0) | ((pick == 1) & (place < CHUNK // 2)), 1.0, 0.0)
        flat = dot(chosen.astype(BF16), stacked, ((1,), (1,)))
        owner = lax.broadcasted_iota(jnp.int32, (chunks, 8 * chunks), 1) // 8
        chunk_at = lax.broadcasted_iota(jnp.int32, (chunks, 8 * chunks), 0)
        lane_rate = per_lane(rates, heads, channels)
        kind = lax.broadcasted_iota(jnp.int32, (8 * chunks, channels), 0) % 8
        lane_head = lax.broadcasted_iota(jnp.int32, (8 * chunks, channels), 1) // (
            channels // heads
        )
        mixer = jnp.where(kind == lane_head, -lane_rate, 0.0)
        mixer = jnp.where(kind == 6, LOG_ONE, jnp.where(kind == 7, LOG_TWO, mixer))
        table = []
        for which in range(2):
            own = jnp.where(owner == chunk_at, flat[which : which + 1, :], 0.0)
            table.append(dot(own, mixer, ((1,), (0,)), HIGHEST))
        logs_out[0] = jnp.exp(table[0])
        logs_out[1] = jnp.exp(table[1])
        logs_out[2] = jnp.exp(table[0] - table[1])
        decay = jnp.exp(jnp.sum(table[0], axis=0, keepdims=True))
        first = decay.astype(BF16).astype(F32)
        second = (decay - first).astype(BF16).astype(F32)
        third = decay - first - second
        row = lax.broadcasted_iota(jnp.int32, (16, channels), 0)
        tail = jnp.where(
            row == 0, first, jnp.where(row == 1, second, jnp.where(row == 2, third, 0.0))
        )
        pay_out[128:144, :] = tail.astype(BF16)
        total[...] = jnp.zeros_like(total)

    onehot = spread_matrix(heads, channels)
    here = pl.multiple_of(step * STEP_ROWS, STEP_ROWS)
    scale = spread(front[:, pl.ds(here, STEP_ROWS)], onehot)
    scaled = (grad[...].astype(F32) * scale).astype(BF16)
    total[...] += dot(c_proj[...], scaled, ((0,), (0,)))

    @pl.when(step == pl.num_programs(0) - 1)
    def finish():
        pay_out[0:128, :] = total[...].astype(BF16)


def state_kernel(
    heads, parts, taps, far, inputs, halo, b_proj, adjoint_pay, mixed_out, slope_out, *rest
):
    pays, (window, total) = rest[: parts - 1], rest[parts - 1 :]
    channels = inputs.shape[1]
    step = pl.program_id(0)

    @pl.when(step == 0)
    def first():
        window[0:16, :] = halo[...].astype(F32)
        total[...] = jnp.zeros_like(total)

    @pl.when(step > 0)
    def later():
        window[0:16, :] = window[STEP_ROWS : STEP_ROWS + 16, :]

    window[16 : STEP_ROWS + 16, :] = inputs[...].astype(F32)
    onehot = spread_matrix(heads, channels)
    scaled = []
    for q in range(STEP_ROWS // CHUNK):
        at = q * CHUNK
        preact = taps[0:1, :] * window[13 + at : 13 + at + CHUNK, :]
        for k in range(1, 4):
            preact = preact + taps[k : k + 1, :] * window[13 + k + at : 13 + k + at + CHUNK, :]
        sigma = 1.0 / (1.0 + jnp.exp(-preact))
        mixed = preact * sigma
        slope_out[at : at + CHUNK, :] = sigma + mixed * (1.0 - sigma)
        mixed_out[at : at + CHUNK, :] = mixed.astype(BF16)
        scale = spread(far[:, at : at + CHUNK], onehot)
        scaled.append((mixed * scale).astype(BF16))
    total[...] += dot(b_proj[...], jnp.concatenate(scaled, axis=0), ((0,), (0,)))

    @pl.when(step == pl.num_programs(0) - 1)
    def finish():
        me = lax.axis_index("seq")
        state = total[...].astype(BF16)
        for distance in range(1, parts):
            forward = me + distance < parts

            @pl.when(forward)
            def send_state():
                pays[distance - 1][0:128, :] = state
                pays[distance - 1][128:144, :] = adjoint_pay[128:144, :]

            @pl.when(jnp.logical_not(forward))
            def send_adjoint():
                pays[distance - 1][...] = adjoint_pay[...]


def merged(parts, pays, forward):
    me = lax.axis_index("seq")
    running = jnp.zeros((128, pays[0].shape[1]), F32)
    for distance in range(parts - 1, 0, -1):
        held = pays[distance - 1] if forward else pays[parts - distance - 1]
        there = (me >= distance) if forward else (me + distance < parts)
        decay = (
            held[128:129, :].astype(F32) + held[129:130, :].astype(F32)
        ) + held[130:131, :].astype(F32)
        running = jnp.where(there, held[0:128, :].astype(F32) + decay * running, 0.0)
    return running


def gradient_kernel(
    heads, parts, gains, taps, near, logs, grad, slope, inputs, halo, b_proj, c_proj, *rest
):
    pays = rest[: parts - 1]
    grad_out, tail_out, edge_out, running, window, sums = rest[parts - 1 :]
    channels = inputs.shape[1]
    step = pl.program_id(0)
    last = pl.num_programs(0) - 1

    @pl.when(step == 0)
    def first():
        running[...] = merged(parts, pays, False)
        window[STEP_ROWS : STEP_ROWS + 8, :] = jnp.zeros((8, channels), F32)
        sums[...] = jnp.zeros_like(sums)

    @pl.when(step > 0)
    def later():
        window[STEP_ROWS : STEP_ROWS + 8, :] = window[0:8, :]

    onehot = spread_matrix(heads, channels)
    gain = per_lane(gains, heads, channels)
    row = lax.broadcasted_iota(jnp.int32, (CHUNK, CHUNK), 0)
    col = lax.broadcasted_iota(jnp.int32, (CHUNK, CHUNK), 1)
    keep = row <= col
    per_step = STEP_ROWS // CHUNK
    adjoint = running[...]
    partial = [jnp.zeros((8, channels), F32) for _ in range(4)]
    for q in range(per_step - 1, -1, -1):
        at = q * CHUNK
        chunk = (last - step) * per_step + q
        both = slice(at, at + CHUNK)
        behind = spread(near[0:16, both], onehot)
        ahead = spread(near[16:32, both], onehot)
        whole = logs[0, pl.ds(chunk, 1), :]
        middle = logs[1, pl.ds(chunk, 1), :]
        rest_of = logs[2, pl.ds(chunk, 1), :]
        grad_f = grad[both, :].astype(F32)
        scaled = (grad_f * behind).astype(BF16)
        low = (adjoint * rest_of).astype(BF16)
        b_block = b_proj[both, :]
        c_block = c_proj[both, :]
        scores = dot(b_block, c_block, ((1,), (1,)))
        scores = jnp.where(keep, scores, 0.0).astype(BF16)
        inner = dot(
            jnp.concatenate([scores, b_block], axis=1),
            jnp.concatenate([scaled, low], axis=0),
            ((1,), (0,)),
        )
        grad_pre = (gain * grad_f + ahead * inner) * slope[both, :]
        window[both, :] = grad_pre
        adjoint = whole * adjoint + middle * dot(c_block, scaled, ((0,), (0,)))
        x = inputs[both, :].astype(F32)
        result = taps[3:4, :] * grad_pre
        partial[3] = partial[3] + (grad_pre * x).reshape(CHUNK // 8, 8, channels).sum(axis=0)
        for k in range(3):
            moved = window[at + 3 - k : at + 3 - k + CHUNK, :]
            result = result + taps[k : k + 1, :] * moved
            partial[k] = partial[k] + (moved * x).reshape(CHUNK // 8, 8, channels).sum(axis=0)
        grad_out[both, :] = result.astype(BF16)
        if q == per_step - 1:

            @pl.when(step == 0)
            def keep_edge():
                edge_out[...] = result[CHUNK - 8 :, :]

    running[...] = adjoint
    for k in range(4):
        sums[8 * k : 8 * k + 8, :] += partial[k]

    @pl.when(step == last)
    def finish():
        tail_out[...] = jnp.zeros_like(tail_out)
        for k in range(4):
            tap = jnp.sum(sums[8 * k : 8 * k + 8, :], axis=0, keepdims=True)
            for j in range(k, 3):
                tap = tap + window[j - k : j - k + 1, :] * halo[13 + j : 14 + j, :].astype(F32)
            tail_out[k : k + 1, :] = tap
        tail_out[4:7, :] = window[0:3, :]


def output_kernel(heads, parts, gains, near, logs, mixed, b_proj, c_proj, *rest):
    pays = rest[: parts - 1]
    out, running = rest[parts - 1 :]
    channels = mixed.shape[1]
    step = pl.program_id(0)

    @pl.when(step == 0)
    def first():
        running[...] = merged(parts, pays, True)

    onehot = spread_matrix(heads, channels)
    gain = per_lane(gains, heads, channels)
    row = lax.broadcasted_iota(jnp.int32, (CHUNK, CHUNK), 0)
    col = lax.broadcasted_iota(jnp.int32, (CHUNK, CHUNK), 1)
    keep = row >= col
    per_step = STEP_ROWS // CHUNK
    state = running[...]
    for q in range(per_step):
        at = q * CHUNK
        chunk = step * per_step + q
        both = slice(at, at + CHUNK)
        behind = spread(near[0:16, both], onehot)
        ahead = spread(near[16:32, both], onehot)
        whole = logs[0, pl.ds(chunk, 1), :]
        middle = logs[1, pl.ds(chunk, 1), :]
        rest_of = logs[2, pl.ds(chunk, 1), :]
        mixed_f = mixed[both, :].astype(F32)
        scaled = (mixed_f * ahead).astype(BF16)
        low = (state * middle).astype(BF16)
        b_block = b_proj[both, :]
        c_block = c_proj[both, :]
        scores = dot(c_block, b_block, ((1,), (1,)))
        scores = jnp.where(keep, scores, 0.0).astype(BF16)
        inner = dot(
            jnp.concatenate([scores, c_block], axis=1),
            jnp.concatenate([scaled, low], axis=0),
            ((1,), (0,)),
        )
        out[both, :] = (gain * mixed_f + behind * inner).astype(BF16)
        state = whole * state + rest_of * dot(b_block, scaled, ((0,), (0,)))
    running[...] = state


def finish_kernel(parts, scale, taps, tail, edge, *rest):
    others = rest[: parts - 1]
    unused, grad_out, conv_out = rest[parts - 1 :]
    total = tail[0:4, :]
    for other in others:
        total = total + other[0:4, :]
    conv_out[...] = total * scale
    me = lax.axis_index("seq")
    after = jnp.where(me + 1 < parts, others[parts - 2][...], 0.0)
    channels = tail.shape[1]
    row = lax.broadcasted_iota(jnp.int32, (8, channels), 0)
    result = edge[...]
    for r in range(3):
        extra = jnp.zeros((1, channels), F32)
        for k in range(r + 1):
            extra = extra + taps[k : k + 1, :] * after[4 + r - k : 5 + r - k, :]
        result = jnp.where(row == 5 + r, result + extra, result)
    grad_out[0:8, :] = unused[0:8, :]
    grad_out[8:16, :] = result.astype(BF16)


def rotated(block, axis, distance):
    size = lax.axis_size(axis)
    return lax.ppermute(block, axis, [(i, (i + distance) % size) for i in range(size)])


def shards(
    inputs,
    b_proj,
    c_proj,
    step_codes,
    gate_codes,
    decay_rates,
    skip_gain,
    conv_weight,
    out_cotangent,
):
    rows, channels = inputs.shape
    heads = decay_rates.shape[0]
    parts = lax.axis_size("seq")
    grid = rows // STEP_ROWS
    chunks = rows // CHUNK

    def call(kernel, grid_size, in_specs, out_specs, out_shape, scratch, flops, nbytes, aliases=None):
        return pl.pallas_call(
            kernel,
            grid=(grid_size,),
            in_specs=in_specs,
            out_specs=out_specs,
            out_shape=out_shape,
            scratch_shapes=scratch,
            input_output_aliases=aliases or {},
            compiler_params=pltpu.CompilerParams(
                dimension_semantics=("arbitrary",), vmem_limit_bytes=VMEM_LIMIT
            ),
            cost_estimate=pl.CostEstimate(
                flops=flops, bytes_accessed=nbytes, transcendentals=rows * channels
            ),
        )

    def full(*shape):
        return pl.BlockSpec(shape, lambda i: (0,) * len(shape))

    def tall(width, back=False):
        return pl.BlockSpec(
            (STEP_ROWS, width), (lambda i: (grid - 1 - i, 0)) if back else (lambda i: (i, 0))
        )

    def wide(height, back=False):
        return pl.BlockSpec(
            (height, STEP_ROWS), (lambda i: (0, grid - 1 - i)) if back else (lambda i: (0, i))
        )

    scalars = pl.BlockSpec(memory_space=pltpu.SMEM)
    shape = jax.ShapeDtypeStruct
    big = rows * channels

    halo_from = [(i, i + 1) for i in range(parts - 1)]
    halo = lax.ppermute(inputs[rows - 16 :], "seq", halo_from)

    near, far, logs, adjoint_pay = call(
        functools.partial(adjoint_kernel, heads),
        grid,
        [scalars, full(heads, rows), full(1, rows), tall(channels), tall(128)],
        [full(32, rows), full(16, rows), full(3, chunks, channels), full(144, channels)],
        [
            shape((32, rows), BF16),
            shape((16, rows), BF16),
            shape((3, chunks, channels), F32),
            shape((144, channels), BF16),
        ],
        [
            pltpu.VMEM((8, rows), F32),
            pltpu.VMEM((16, rows), BF16),
            pltpu.VMEM((128, channels), F32),
        ],
        2 * big * 128,
        big * 3,
    )(decay_rates, step_codes, gate_codes.reshape(1, rows), out_cotangent, c_proj)

    outs = call(
        functools.partial(state_kernel, heads, parts),
        grid,
        [full(4, channels), wide(16), tall(channels), full(16, channels), tall(128), full(144, channels)],
        [tall(channels), tall(channels)] + [full(144, channels)] * (parts - 1),
        [shape((rows, channels), BF16), shape((rows, channels), F32)]
        + [shape((144, channels), BF16)] * (parts - 1),
        [pltpu.VMEM((STEP_ROWS + 16, channels), F32), pltpu.VMEM((128, channels), F32)],
        2 * big * 128,
        big * 9,
    )(conv_weight, far, inputs, halo, b_proj, adjoint_pay)
    mixed, slope, sends = outs[0], outs[1], outs[2:]
    pays = [rotated(send, "seq", distance + 1) for distance, send in enumerate(sends)]

    grad_rows, tail, edge = call(
        functools.partial(gradient_kernel, heads, parts),
        grid,
        [
            scalars,
            full(4, channels),
            wide(32, True),
            full(3, chunks, channels),
            tall(channels, True),
            tall(channels, True),
            tall(channels, True),
            full(16, channels),
            tall(128, True),
            tall(128, True),
        ]
        + [full(144, channels)] * (parts - 1),
        [tall(channels, True), full(8, channels), full(8, channels)],
        [shape((rows, channels), BF16), shape((8, channels), F32), shape((8, channels), F32)],
        [
            pltpu.VMEM((128, channels), F32),
            pltpu.VMEM((STEP_ROWS + 8, channels), F32),
            pltpu.VMEM((32, channels), F32),
        ],
        6 * big * 128,
        big * 10,
    )(
        skip_gain, conv_weight, near, logs, out_cotangent, slope, inputs, halo, b_proj, c_proj,
        *pays,
    )
    tails = [rotated(tail, "seq", distance) for distance in range(1, parts)]

    layer_out = call(
        functools.partial(output_kernel, heads, parts),
        grid,
        [scalars, wide(32), full(3, chunks, channels), tall(channels), tall(128), tall(128)]
        + [full(144, channels)] * (parts - 1),
        tall(channels),
        shape((rows, channels), BF16),
        [pltpu.VMEM((128, channels), F32)],
        6 * big * 128,
        big * 4,
    )(skip_gain, near, logs, mixed, b_proj, c_proj, *pays)

    scale = float((rows * parts) ** -0.5)
    last_rows = pl.BlockSpec((16, channels), lambda i: (rows // 16 - 1, 0))
    input_grad, conv_grad = call(
        functools.partial(finish_kernel, parts, scale),
        1,
        [full(4, channels), full(8, channels), full(8, channels)]
        + [full(8, channels)] * (parts - 1)
        + [last_rows],
        [last_rows, full(4, channels)],
        [shape((rows, channels), BF16), shape((4, channels), F32)],
        [],
        1000,
        1000,
        {parts + 2: 0},
    )(conv_weight, tail, edge, *tails, grad_rows)
    return layer_out, input_grad, conv_grad


def solution(mesh):
    in_specs = (
        P(("groups", "seq"), ("head", "sub")),
        P(("groups", "seq"), None),
        P(("groups", "seq"), None),
        P(("head", "sub"), ("groups", "seq")),
        P(("groups", "seq")),
        P(("head", "sub")),
        P(("head", "sub")),
        P(None, ("head", "sub")),
        P(("groups", "seq"), ("head", "sub")),
    )
    out_specs = (
        P(("groups", "seq"), ("head", "sub")),
        P(("groups", "seq"), ("head", "sub")),
        P("groups", ("head", "sub")),
    )
    return jax.shard_map(shards, mesh=mesh, in_specs=in_specs, out_specs=out_specs, check_vma=False)
```

time: 188 us -> 56.3 us (0.30)
  matrix products: 60.7 us -> 0 us
  blocking collectives: 56 us -> 0 us
  Pallas kernels: 0 us -> 29.1 us
  local copies, waits for them, and re-layouts: 34.3 us -> 5.49 us
  other arithmetic: 27.2 us -> 0 us
  starting transfers between devices: 6.2 us -> 14.8 us
  waiting for transfers between devices: 0.01 us -> 5.79 us
    dot_general x24 -> x0, matrix products: 60.7 us -> none  [the longest x4 15.7 us: local_block(): jnp.einsum('hst,shp->thp', weights, grad_b, preferred_element_type=jnp.fl...]
    all_gather x2 -> x0, blocking collectives: 35.9 us -> none  [the longest x1 18.7 us: shards(): end_pieces = lax.all_gather(local_end[None], 'seq', axis=0, tiled=True)]
    pallas_call x0 -> x5, Pallas kernels: none -> 29.1 us  [the longest x1 11.5 us: shards(): call(functools.partial(gradient_kernel, heads, parts), grid, [scalars, fu...]
    unnamed x46 -> x22, local copies, waits for them, and re-layouts: 15.7 us -> 4.66 us
    psum x1 -> x0, blocking collectives: 10.1 us -> none  [shards(): lax.psum(local_grad, 'seq') * (row_count * lax.axis_size('seq')) ** (-0.5)]
    unnamed x1 -> x0, blocking collectives: 9.92 us -> none
    convert_element_type x2 -> x0, other arithmetic: 9.26 us -> none  [the longest x1 5.04 us: shards(): return (layer_out, input_grad.astype(jnp.bfloat16), conv_grad)]
    ppermute x2 -> x7, starting transfers between devices: 6.2 us -> 14.8 us  [the longest x6 9.91 us: rotated(): lax.ppermute(block, axis, [(i, (i + distance) % size) for i in range(size)])]
  transfers between devices with their start and end apart: 2 -> 7, of which waited for: 0 -> 2; matrix products, arithmetic and copies ran while one was open for 18% -> 0% of each run, Pallas kernels for 0% -> 17%
where the time goes in v1:
time: 56.3 us; the launch traced here: 55.9 us
  Pallas kernels  29.1 us (52%)
  starting transfers between devices  14.8 us (26%)
  waiting for transfers between devices  5.79 us (10%)
  local copies, waits for them, and re-layouts  5.49 us (10%)
  between operations  0.74 us (1%)
    pallas_call x1, Pallas kernels, shards(): call(functools.partial(gradient_kernel, heads, parts), grid, [scalars, fu...  11.5 us
    ppermute x6, starting transfers between devices, rotated(): lax.ppermute(block, axis, [(i, (i + distance) % size) for i in range(size)])  9.91 us
    pallas_call x1, Pallas kernels, shards(): call(functools.partial(state_kernel, heads, parts), grid, [full(4, channe...  6.73 us
    pallas_call x1, Pallas kernels, shards(): call(functools.partial(output_kernel, heads, parts), grid, [scalars, wide...  6.39 us
    ppermute x6, waiting for transfers between devices, rotated(): lax.ppermute(block, axis, [(i, (i + distance) % size) for i in range(size)])  5.78 us
    ppermute x1, starting transfers between devices, shards(): halo = lax.ppermute(inputs[rows - 16:], 'seq', halo_from)  4.92 us
    unnamed x22, local copies, waits for them, and re-layouts  4.66 us
    pallas_call x1, Pallas kernels, shards(): call(functools.partial(adjoint_kernel, heads), grid, [scalars, full(heads...  3.18 us
  transfers between devices with their start and end apart: 7, of which 2 were waited for; matrix products, arithmetic and copies ran while one was open for 0% of the time, Pallas kernels for 17%

profile of v1, /device:TPU:0, one launch (start us, length us, event | category | flops | bytes accessed | tf_op | source)
XLA Modules:
  0.0 55.9 jit_solution(10692618616442636099)
XLA Ops:
  0.6 0.0 copy-start
  0.6 0.8 %slice.3 = bf16[16,384]{1,0:T(8,128)(2,1)S(1)} slice(bf16[2048,384]{1,0:T(8,128)(2,1)} %inputs.3), slice={[2032:2048], [0:384]} | slice | bytes 24576 | tf_op jit(solution)/shard_map/slice | solution.py:399
  1.5 4.9 %collective-permute-start = (bf16[16,384]{1,0:T(8,128)(2,1)S(1)}, bf16[16,384]{1,0:T(8,128)(2,1)S(1)}, u32[]{:S(2)}, u32[]{:S(2)}) collective-permute-start(bf16[16,384]{1,0:T(8,128)(2,1)S(1)} %slice.3), channel_id=1, source_target_pairs={{0,4},{4,8},{8,12},{1,5},{5,9},{9,13},{2,6},{6,10},{10,14},{3,7},{... | collective-permute-start | bytes 36872 | tf_op jit(solution)/shard_map/ppermute | solution.py:399
  6.4 0.0 copy-start.1
  6.4 1.4 %copy-done.1 = bf16[2048,384]{1,0:T(8,128)(2,1)S(1)} copy-done((bf16[2048,384]{1,0:T(8,128)(2,1)S(1)}, bf16[2048,384]{1,0:T(8,128)(2,1)}, u32[]{:S(2)}) %copy-start.1) | copy-done | bytes 1572888
  7.8 1.0 %copy-done.3 = bf16[2048,128]{1,0:T(8,128)(2,1)S(1)} copy-done((bf16[2048,128]{1,0:T(8,128)(2,1)S(1)}, bf16[2048,128]{1,0:T(8,128)(2,1)}, u32[]{:S(2)}) %copy-start.3) | copy-done | bytes 524312
  8.8 0.8 %copy-done.6 = s32[6,2048]{1,0:T(8,128)S(1)} copy-done((s32[6,2048]{1,0:T(8,128)S(1)}, s32[6,2048]{1,0:T(8,128)}, u32[]{:S(2)}) %copy-start.6) | copy-done | bytes 49176
  9.7 0.7 %copy-done.8 = s32[2048]{0:T(1024)S(1)} copy-done((s32[2048]{0:T(1024)S(1)}, s32[2048]{0:T(1024)}, u32[]{:S(2)}) %copy-start.8) | copy-done | bytes 8216
  10.4 0.7 %copy-done.10 = f32[6]{0:T(128)S(1)} copy-done((f32[6]{0:T(128)S(1)}, f32[6]{0:T(128)}, u32[]{:S(2)}) %copy-start.10) | copy-done | bytes 48
  11.0 3.2 %shard_map.112 = (bf16[32,2048]{1,0:T(8,128)(2,1)S(1)}, bf16[16,2048]{1,0:T(8,128)(2,1)S(1)}, f32[3,16,384]{2,1,0:T(8,128)S(1)}, bf16[144,384]{1,0:T(8,128)(2,1)S(1)}) custom-call(f32[6]{0:T(128)S(1)} %copy-done.10, s32[6,2048]{1,0:T(8,128)S(1)} %copy-done.6, s32[1,2048]{1,0:T(1,128)S(1)} %bitcast.1, bf16[2048,384]{1,0:T(8,128)(2,1)S(1)} %copy-done.1, ...), custom_call_target="tpu_custom_call" | custom-call | flops 201326592 | bytes 2359296 | tf_op jit(solution)/shard_map/pallas_call | solution.py:401
  14.2 0.0 copy-start.2
  14.2 0.0 copy-start.4
  14.3 0.0 copy-start.9
  14.3 0.0 collective-permute-done.halo
  14.3 0.0 copy-done
  14.3 6.7 %shard_map.113 = (bf16[2048,384]{1,0:T(8,128)(2,1)S(1)}, f32[2048,384]{1,0:T(8,128)}, bf16[144,384]{1,0:T(8,128)(2,1)S(1)}, bf16[144,384]{1,0:T(8,128)(2,1)S(1)}, bf16[144,384]{1,0:T(8,128)(2,1)S(1)}) custom-call(f32[4,384]{1,0:T(4,128)S(1)} %copy-done.7, bf16[16,2048]{1,0:T(8,128)(2,1)S(1)} %get-tuple-element.19.far, bf16[2048,384]{1,0:T(8,128)(2,1)S(1)} %copy-done, ...), custom_call_target="tpu_custom_call" | custom-call | flops 201326592 | bytes 7077888 | tf_op jit(solution)/shard_map/pallas_call | solution.py:421
  21.0 1.6 %collective-permute-start.1 = (bf16[144,384]{1,0:T(8,128)(2,1)S(1)}, bf16[144,384]{1,0:T(8,128)(2,1)S(1)}, u32[]{:S(2)}, u32[]{:S(2)}) collective-permute-start(bf16[144,384]{1,0:T(8,128)(2,1)S(1)} %get-tuple-element.22), channel_id=1, source_target_pairs={{0,4},{4,8},{8,12},{12,0},{1,5},{5,9},{9,13},{13,1},{2,6},{6,10},{... | collective-permute-start | bytes 331784 | tf_op jit(solution)/shard_map/ppermute | solution.py:344
  22.6 1.0 %collective-permute-start.2 = (bf16[144,384]{1,0:T(8,128)(2,1)S(1)}, bf16[144,384]{1,0:T(8,128)(2,1)S(1)}, u32[]{:S(2)}, u32[]{:S(2)}) collective-permute-start(bf16[144,384]{1,0:T(8,128)(2,1)S(1)} %get-tuple-element.23), channel_id=1, source_target_pairs={{0,8},{4,12},{8,0},{12,4},{1,9},{5,13},{9,1},{13,5},{2,10},{6,14},... | collective-permute-start | bytes 331784 | tf_op jit(solution)/shard_map/ppermute | solution.py:344
  23.6 2.9 %collective-permute-start.3 = (bf16[144,384]{1,0:T(8,128)(2,1)S(1)}, bf16[144,384]{1,0:T(8,128)(2,1)S(1)}, u32[]{:S(2)}, u32[]{:S(2)}) collective-permute-start(bf16[144,384]{1,0:T(8,128)(2,1)S(1)} %get-tuple-element.24), channel_id=1, source_target_pairs={{0,12},{4,0},{8,4},{12,8},{1,13},{5,1},{9,5},{13,9},{2,14},{6,2},{... | collective-permute-start | bytes 331784 | tf_op jit(solution)/shard_map/ppermute | solution.py:344
  26.5 2.2 %collective-permute-done.1.rest_0_ = bf16[144,384]{1,0:T(8,128)(2,1)S(1)} collective-permute-done((bf16[144,384]{1,0:T(8,128)(2,1)S(1)}, bf16[144,384]{1,0:T(8,128)(2,1)S(1)}, u32[]{:S(2)}, u32[]{:S(2)}) %collective-permute-start.1) | collective-permute-done | bytes 110624 | tf_op jit(solution)/shard_map/ppermute | solution.py:344
  28.8 3.6 %collective-permute-done.2.rest_1_ = bf16[144,384]{1,0:T(8,128)(2,1)S(1)} collective-permute-done((bf16[144,384]{1,0:T(8,128)(2,1)S(1)}, bf16[144,384]{1,0:T(8,128)(2,1)S(1)}, u32[]{:S(2)}, u32[]{:S(2)}) %collective-permute-start.2) | collective-permute-done | bytes 110624 | tf_op jit(solution)/shard_map/ppermute | solution.py:344
  32.3 0.0 collective-permute-done.3.rest_2_
  32.3 0.0 copy-done.4
  32.3 11.5 %shard_map.115 = (bf16[2048,384]{1,0:T(8,128)(2,1)}, f32[8,384]{1,0:T(8,128)S(1)}, f32[8,384]{1,0:T(8,128)S(1)}) custom-call(f32[6]{0:T(128)S(1)} %copy-done.9, f32[4,384]{1,0:T(4,128)S(1)} %copy-done.7, bf16[32,2048]{1,0:T(8,128)(2,1)S(1)} %get-tuple-element.17.near, f32[3,16,384]{2,1,0:T(8,128)S(1)} %get-tuple-element.18.logs, ...), custom_call_target="tpu_custom_call" | custom-call | flops 603979776 | bytes 7864320 | tf_op jit(solution)/shard_map/pallas_call | solution.py:435
  43.8 3.8 %collective-permute-start.6 = (f32[8,384]{1,0:T(8,128)S(1)}, f32[8,384]{1,0:T(8,128)S(1)}, u32[]{:S(2)}, u32[]{:S(2)}) collective-permute-start(f32[8,384]{1,0:T(8,128)S(1)} %get-tuple-element.26.tail), channel_id=1, source_target_pairs={{0,12},{4,0},{8,4},{12,8},{1,13},{5,1},{9,5},{13,9},{2,14},{6,2},{... | collective-permute-start | bytes 36872 | tf_op jit(solution)/shard_map/ppermute | solution.py:344
  47.6 0.3 collective-permute-start.5
  48.0 0.2 collective-permute-start.4
  48.2 6.4 %shard_map.114 = bf16[2048,384]{1,0:T(8,128)(2,1)} custom-call(f32[6]{0:T(128)S(1)} %copy-done.9, bf16[32,2048]{1,0:T(8,128)(2,1)S(1)} %get-tuple-element.17.near, f32[3,16,384]{2,1,0:T(8,128)S(1)} %get-tuple-element.18.logs, bf16[2048,384]{1,0:T(8,128)(2,1)S(1)} %get-tuple-element.21.mixed, bf16[2048,128]{1,0:T(8,128)(2,1)S(1)} %copy-done.5, ...), custom_call_target="tpu_custom_call" | custom-call | flops 603979776 | bytes 3145728 | tf_op jit(solution)/shard_map/pallas_call | solution.py:466
  54.6 0.0 collective-permute-done.6.rest_2_
  54.6 0.0 collective-permute-done.5.rest_1_
  54.6 0.0 collective-permute-done.4.rest_0_
  54.6 1.3 %shard_map.116 = (bf16[2048,384]{1,0:T(8,128)(2,1)}, f32[4,384]{1,0:T(4,128)}) custom-call(f32[4,384]{1,0:T(4,128)S(1)} %copy-done.7, f32[8,384]{1,0:T(8,128)S(1)} %get-tuple-element.26.tail, f32[8,384]{1,0:T(8,128)S(1)} %get-tuple-element.27.edge, f32[8,384]{1,0:T(8,128)S(1)} %collective-permute-done.4.rest_0_, ...), custom_call_target="tpu_custom_call", output_to_operand_aliasing={{0}: (6, {})} | custom-call | flops 1000 | bytes 1000 | tf_op jit(solution)/shard_map/pallas_call | solution.py:480
  (10 shorter events, 0.0 us)
Async XLA Ops:
  0.6 13.6 %copy-start = (bf16[2048,384]{1,0:T(8,128)(2,1)S(1)}, bf16[2048,384]{1,0:T(8,128)(2,1)}, u32[]{:S(2)}) copy-start(bf16[2048,384]{1,0:T(8,128)(2,1)} %inputs.3) | copy-start | bytes 4718596
  1.5 12.8 %collective-permute-start = (bf16[16,384]{1,0:T(8,128)(2,1)S(1)}, bf16[16,384]{1,0:T(8,128)(2,1)S(1)}, u32[]{:S(2)}, u32[]{:S(2)}) collective-permute-start(bf16[16,384]{1,0:T(8,128)(2,1)S(1)} %slice.3), channel_id=1, source_target_pairs={{0,4},{4,8},{8,12},{1,5},{5,9},{9,13},{2,6},{6,10},{10,14},{3,7},{... | collective-permute-start | bytes 36872 | tf_op jit(solution)/shard_map/ppermute | solution.py:399
  6.4 1.4 %copy-start.1 = (bf16[2048,384]{1,0:T(8,128)(2,1)S(1)}, bf16[2048,384]{1,0:T(8,128)(2,1)}, u32[]{:S(2)}) copy-start(bf16[2048,384]{1,0:T(8,128)(2,1)} %grad.3) | copy-start | bytes 4718596
  7.8 1.0 %copy-start.3 = (bf16[2048,128]{1,0:T(8,128)(2,1)S(1)}, bf16[2048,128]{1,0:T(8,128)(2,1)}, u32[]{:S(2)}) copy-start(bf16[2048,128]{1,0:T(8,128)(2,1)} %c_proj.5) | copy-start | bytes 1572868
  8.8 0.8 %copy-start.6 = (s32[6,2048]{1,0:T(8,128)S(1)}, s32[6,2048]{1,0:T(8,128)}, u32[]{:S(2)}) copy-start(s32[6,2048]{1,0:T(8,128)} %codes.1) | copy-start | bytes 147460
  9.7 0.7 %copy-start.8 = (s32[2048]{0:T(1024)S(1)}, s32[2048]{0:T(1024)}, u32[]{:S(2)}) copy-start(s32[2048]{0:T(1024)} %param.13) | copy-start | bytes 24580
  10.4 0.7 %copy-start.10 = (f32[6]{0:T(128)S(1)}, f32[6]{0:T(128)}, u32[]{:S(2)}) copy-start(f32[6]{0:T(128)} %rates.1) | copy-start | bytes 76
  11.0 3.2 %copy-start.5 = (bf16[2048,128]{1,0:T(8,128)(2,1)S(1)}, bf16[2048,128]{1,0:T(8,128)(2,1)}, u32[]{:S(2)}) copy-start(bf16[2048,128]{1,0:T(8,128)(2,1)} %b_proj.5) | copy-start | bytes 1572868
  11.0 3.3 %copy-start.7 = (f32[4,384]{1,0:T(4,128)S(1)}, f32[4,384]{1,0:T(4,128)}, u32[]{:S(2)}) copy-start(f32[4,384]{1,0:T(4,128)} %taps.5) | copy-start | bytes 18436
  14.2 18.1 %copy-start.2 = (bf16[2048,384]{1,0:T(8,128)(2,1)S(1)}, bf16[2048,384]{1,0:T(8,128)(2,1)}, u32[]{:S(2)}) copy-start(bf16[2048,384]{1,0:T(8,128)(2,1)} %grad.3) | copy-start | bytes 4718596
  14.2 18.1 %copy-start.4 = (bf16[2048,128]{1,0:T(8,128)(2,1)S(1)}, bf16[2048,128]{1,0:T(8,128)(2,1)}, u32[]{:S(2)}) copy-start(bf16[2048,128]{1,0:T(8,128)(2,1)} %c_proj.5) | copy-start | bytes 1572868
  14.3 18.1 %copy-start.9 = (f32[6]{0:T(128)S(1)}, f32[6]{0:T(128)}, u32[]{:S(2)}) copy-start(f32[6]{0:T(128)} %gains.3) | copy-start | bytes 76
  21.0 7.7 %collective-permute-start.1 = (bf16[144,384]{1,0:T(8,128)(2,1)S(1)}, bf16[144,384]{1,0:T(8,128)(2,1)S(1)}, u32[]{:S(2)}, u32[]{:S(2)}) collective-permute-start(bf16[144,384]{1,0:T(8,128)(2,1)S(1)} %get-tuple-element.22), channel_id=1, source_target_pairs={{0,4},{4,8},{8,12},{12,0},{1,5},{5,9},{9,13},{13,1},{2,6},{6,10},{... | collective-permute-start | bytes 331784 | tf_op jit(solution)/shard_map/ppermute | solution.py:344
  22.6 9.7 %collective-permute-start.2 = (bf16[144,384]{1,0:T(8,128)(2,1)S(1)}, bf16[144,384]{1,0:T(8,128)(2,1)S(1)}, u32[]{:S(2)}, u32[]{:S(2)}) collective-permute-start(bf16[144,384]{1,0:T(8,128)(2,1)S(1)} %get-tuple-element.23), channel_id=1, source_target_pairs={{0,8},{4,12},{8,0},{12,4},{1,9},{5,13},{9,1},{13,5},{2,10},{6,14},... | collective-permute-start | bytes 331784 | tf_op jit(solution)/shard_map/ppermute | solution.py:344
  23.6 8.7 %collective-permute-start.3 = (bf16[144,384]{1,0:T(8,128)(2,1)S(1)}, bf16[144,384]{1,0:T(8,128)(2,1)S(1)}, u32[]{:S(2)}, u32[]{:S(2)}) collective-permute-start(bf16[144,384]{1,0:T(8,128)(2,1)S(1)} %get-tuple-element.24), channel_id=1, source_target_pairs={{0,12},{4,0},{8,4},{12,8},{1,13},{5,1},{9,5},{13,9},{2,14},{6,2},{... | collective-permute-start | bytes 331784 | tf_op jit(solution)/shard_map/ppermute | solution.py:344
  43.8 10.8 %collective-permute-start.6 = (f32[8,384]{1,0:T(8,128)S(1)}, f32[8,384]{1,0:T(8,128)S(1)}, u32[]{:S(2)}, u32[]{:S(2)}) collective-permute-start(f32[8,384]{1,0:T(8,128)S(1)} %get-tuple-element.26.tail), channel_id=1, source_target_pairs={{0,12},{4,0},{8,4},{12,8},{1,13},{5,1},{9,5},{13,9},{2,14},{6,2},{... | collective-permute-start | bytes 36872 | tf_op jit(solution)/shard_map/ppermute | solution.py:344
  47.6 7.0 %collective-permute-start.5 = (f32[8,384]{1,0:T(8,128)S(1)}, f32[8,384]{1,0:T(8,128)S(1)}, u32[]{:S(2)}, u32[]{:S(2)}) collective-permute-start(f32[8,384]{1,0:T(8,128)S(1)} %get-tuple-element.26.tail), channel_id=1, source_target_pairs={{0,8},{4,12},{8,0},{12,4},{1,9},{5,13},{9,1},{13,5},{2,10},{6,14},... | collective-permute-start | bytes 36872 | tf_op jit(solution)/shard_map/ppermute | solution.py:344
  48.0 6.6 %collective-permute-start.4 = (f32[8,384]{1,0:T(8,128)S(1)}, f32[8,384]{1,0:T(8,128)S(1)}, u32[]{:S(2)}, u32[]{:S(2)}) collective-permute-start(f32[8,384]{1,0:T(8,128)S(1)} %get-tuple-element.26.tail), channel_id=1, source_target_pairs={{0,4},{4,8},{8,12},{12,0},{1,5},{5,9},{9,13},{13,1},{2,6},{6,10},{... | collective-permute-start | bytes 36872 | tf_op jit(solution)/shard_map/ppermute | solution.py:344

commit v2 on v0

v2 whole, which is shorter than its diff:
```python
import functools

import jax
import jax.numpy as jnp
from jax import lax
from jax.experimental import pallas as pl
from jax.experimental.pallas import tpu as pltpu
from jax.sharding import PartitionSpec as P

CHUNK = 128
STATE = 128
STEP_ROWS = 512
LOG_ONE = -0.2876820724517809
LOG_TWO = -0.6931471805599453
F32 = jnp.float32
BF16 = jnp.bfloat16
HIGHEST = lax.Precision.HIGHEST
VMEM_LIMIT = 20 * 1024 * 1024


def dot(a, b, dims, precision=None):
    return lax.dot_general(a, b, (dims, ((), ())), preferred_element_type=F32, precision=precision)


def per_lane(scalars, count, channels):
    width = channels // count
    lane = lax.broadcasted_iota(jnp.int32, (1, channels), 1)
    row = jnp.zeros((1, channels), F32)
    for head in range(count):
        inside = (lane >= head * width) & (lane < (head + 1) * width)
        row = jnp.where(inside, scalars[head], row)
    return row


def split_two(value):
    high = value.astype(BF16)
    low = (value - high.astype(F32)).astype(BF16)
    return jnp.concatenate([high.astype(F32), low.astype(F32)], axis=0).astype(BF16)


def spread_matrix(count, channels):
    width = channels // count
    row = lax.broadcasted_iota(jnp.int32, (16, channels), 0)
    lane = lax.broadcasted_iota(jnp.int32, (16, channels), 1)
    return jnp.where((row % 8) == lane // width, 1.0, 0.0).astype(BF16)


def spread(pair, onehot):
    return dot(pair, onehot, ((0,), (0,)))


def adjoint_kernel(
    heads, rates_hbm, codes_hbm, gates_hbm, grad_hbm, c_hbm,
    near_out, far_out, front_out, logs_out, scaled_out, low_out, pay_out,
    rates, codes, gates, grad, c_proj, steps, fresh, small_sem, grad_sem, c_sem,
):
    rows, channels = grad.shape
    chunks = rows // CHUNK
    pieces = rows // STEP_ROWS
    small = [
        pltpu.make_async_copy(source, target, small_sem.at[i])
        for i, (source, target) in enumerate(
            ((rates_hbm, rates), (codes_hbm, codes), (gates_hbm, gates))
        )
    ]
    large = []
    for copy in small:
        copy.start()
    for piece in range(pieces):
        at = pl.ds(piece * STEP_ROWS, STEP_ROWS)
        large.append(pltpu.make_async_copy(grad_hbm.at[at], grad.at[at], grad_sem.at[piece]))
        large.append(pltpu.make_async_copy(c_hbm.at[at], c_proj.at[at], c_sem.at[piece]))
    for copy in large:
        copy.start()
    for copy in small:
        copy.wait()

    steps[...] = jnp.zeros_like(steps)
    steps[0:heads, :] = jnp.exp2(-codes[...].astype(F32))
    gate = gates[...]
    steps[6:7, :] = jnp.where(gate == 1, 1.0, 0.0).astype(F32)
    steps[7:8, :] = jnp.where(gate == 2, 1.0, 0.0).astype(F32)
    stacked = jnp.concatenate(
        [steps[:, j * CHUNK : (j + 1) * CHUNK] for j in range(chunks)], axis=0
    ).astype(BF16)
    row = lax.broadcasted_iota(jnp.int32, (CHUNK, CHUNK), 0)
    col = lax.broadcasted_iota(jnp.int32, (CHUNK, CHUNK), 1)
    upper = jnp.where(row <= col, 1.0, 0.0).astype(BF16)
    sums = dot(stacked, upper, ((1,), (0,)))
    sub = lax.broadcasted_iota(jnp.int32, (8, CHUNK), 0)
    rate = jnp.zeros((8, CHUNK), F32)
    for head in range(heads):
        rate = jnp.where(sub == head, rates[head], rate)
    cums, mids, befores = [], [], []
    before = jnp.zeros((8, 1), F32)
    for j in range(chunks):
        part = sums[8 * j : 8 * j + 8, :]
        cum = LOG_ONE * part[6:7, :] + LOG_TWO * part[7:8, :] - rate * part
        cums.append(cum)
        mids.append(cum[:, CHUNK // 2 - 1 : CHUNK // 2])
        befores.append(before)
        before = before + cum[:, CHUNK - 1 : CHUNK]
    for j in range(chunks):
        at = slice(j * CHUNK, (j + 1) * CHUNK)
        size = steps[:, at]
        near_out[0:16, at] = split_two(jnp.exp(cums[j] - mids[j]))
        near_out[16:32, at] = split_two(jnp.exp(mids[j] - cums[j]) * size)
        front_out[:, at] = split_two(jnp.exp(befores[j] + cums[j]))
        far_out[:, at] = split_two(jnp.exp(before - befores[j] - cums[j]) * size)
    pick = lax.broadcasted_iota(jnp.int32, (8, CHUNK), 0)
    place = lax.broadcasted_iota(jnp.int32, (8, CHUNK), 1)
    chosen = jnp.where((pick == 0) | ((pick == 1) & (place < CHUNK // 2)), 1.0, 0.0)
    flat = dot(chosen.astype(BF16), stacked, ((1,), (1,)))
    owner = lax.broadcasted_iota(jnp.int32, (chunks, 8 * chunks), 1) // 8
    chunk_at = lax.broadcasted_iota(jnp.int32, (chunks, 8 * chunks), 0)
    lane_rate = per_lane(rates, heads, channels)
    kind = lax.broadcasted_iota(jnp.int32, (8 * chunks, channels), 0) % 8
    lane_head = lax.broadcasted_iota(jnp.int32, (8 * chunks, channels), 1) // (channels // heads)
    mixer = jnp.where(kind == lane_head, -lane_rate, 0.0)
    mixer = jnp.where(kind == 6, LOG_ONE, jnp.where(kind == 7, LOG_TWO, mixer))
    table = []
    for which in range(2):
        own = jnp.where(owner == chunk_at, flat[which : which + 1, :], 0.0)
        table.append(dot(own, mixer, ((1,), (0,)), HIGHEST))
    whole = jnp.exp(table[0])
    middle = jnp.exp(table[1])
    rest_of = jnp.exp(table[0] - table[1])
    logs_out[0] = whole
    logs_out[1] = middle
    logs_out[2] = rest_of
    decay = jnp.exp(jnp.sum(table[0], axis=0, keepdims=True))
    first = decay.astype(BF16).astype(F32)
    second = (decay - first).astype(BF16).astype(F32)
    third = decay - first - second
    row = lax.broadcasted_iota(jnp.int32, (16, channels), 0)
    tail = jnp.where(
        row == 0, first, jnp.where(row == 1, second, jnp.where(row == 2, third, 0.0))
    )
    pay_out[STATE : STATE + 16, :] = tail.astype(BF16)

    onehot = spread_matrix(heads, channels)
    for piece in range(pieces):
        large[2 * piece].wait()
        large[2 * piece + 1].wait()
        for j in range(piece * STEP_ROWS // CHUNK, (piece + 1) * STEP_ROWS // CHUNK):
            both = slice(j * CHUNK, (j + 1) * CHUNK)
            scale = spread(near_out[0:16, both], onehot)
            scaled = (grad[both, :].astype(F32) * scale).astype(BF16)
            scaled_out[both, :] = scaled
            fresh[both, :] = dot(c_proj[both, :], scaled, ((0,), (0,)))
    for lanes in lane_tiles(channels):
        adjoint = jnp.zeros((STATE, lanes.stop - lanes.start), F32)
        for j in range(chunks - 1, -1, -1):
            both = slice(j * CHUNK, (j + 1) * CHUNK)
            low_out[both, lanes] = (adjoint * rest_of[j : j + 1, lanes]).astype(BF16)
            adjoint = whole[j : j + 1, lanes] * adjoint + (
                middle[j : j + 1, lanes] * fresh[both, lanes]
            )
        pay_out[0:STATE, lanes] = adjoint.astype(BF16)


def lane_tiles(channels):
    return [slice(at, min(at + 128, channels)) for at in range(0, channels, 128)]


def state_kernel(
    heads, parts, taps, near, logs, inputs, halo, b_proj, adjoint_pay,
    window, mixed_out, sigma_out, scaled_out, low_out, *rest
):
    pays, fresh = rest[: parts - 1], rest[parts - 1]
    rows, channels = inputs.shape
    chunks = rows // CHUNK
    window[0:16, :] = halo[...].astype(F32)
    onehot = spread_matrix(heads, channels)
    for j in range(chunks):
        at = j * CHUNK
        both = slice(at, at + CHUNK)
        window[16 + at : 16 + at + CHUNK, :] = inputs[both, :].astype(F32)
        preact = taps[0:1, :] * window[13 + at : 13 + at + CHUNK, :]
        for k in range(1, 4):
            preact = preact + taps[k : k + 1, :] * window[13 + k + at : 13 + k + at + CHUNK, :]
        sigma = 0.5 * jnp.tanh(0.5 * preact) + 0.5
        mixed = preact * sigma
        sigma_out[both, :] = sigma
        mixed_out[both, :] = mixed
        scale = spread(near[16:32, both], onehot)
        scaled = (mixed * scale).astype(BF16)
        scaled_out[both, :] = scaled
        fresh[both, :] = dot(b_proj[both, :], scaled, ((0,), (0,)))
    me = lax.axis_index("seq")
    for lanes in lane_tiles(channels):
        state = jnp.zeros((STATE, lanes.stop - lanes.start), F32)
        for j in range(chunks):
            both = slice(j * CHUNK, (j + 1) * CHUNK)
            low_out[both, lanes] = (state * logs[1, j : j + 1, lanes]).astype(BF16)
            state = logs[0, j : j + 1, lanes] * state + (
                logs[2, j : j + 1, lanes] * fresh[both, lanes]
            )
        state = state.astype(BF16)
        for distance in range(1, parts):
            forward = me + distance < parts
            pays[distance - 1][0:STATE, lanes] = jnp.where(
                forward, state, adjoint_pay[0:STATE, lanes]
            )
    for pay in pays:
        pay[STATE : STATE + 16, :] = adjoint_pay[STATE : STATE + 16, :]


def merged(parts, pays, forward):
    me = lax.axis_index("seq")
    running = jnp.zeros((STATE, pays[0].shape[1]), F32)
    for distance in range(parts - 1, 0, -1):
        held = pays[distance - 1] if forward else pays[parts - distance - 1]
        there = (me >= distance) if forward else (me + distance < parts)
        decay = (
            held[STATE : STATE + 1, :].astype(F32) + held[STATE + 1 : STATE + 2, :].astype(F32)
        ) + held[STATE + 2 : STATE + 3, :].astype(F32)
        running = jnp.where(there, held[0:STATE, :].astype(F32) + decay * running, 0.0)
    return running.astype(BF16)


def inner_kernel(
    heads, gains, near, far, grad, mixed, sigma, b_proj, c_proj,
    mixed_scaled, mixed_low, grad_scaled, grad_low,
    base_out, grad_base, grad_weight, ahead_scores, behind_scores,
):
    rows, channels = grad.shape
    chunks = rows // CHUNK
    row = lax.broadcasted_iota(jnp.int32, (CHUNK, CHUNK), 0)
    col = lax.broadcasted_iota(jnp.int32, (CHUNK, CHUNK), 1)
    for j in range(chunks):
        both = slice(j * CHUNK, (j + 1) * CHUNK)
        b_block = b_proj[both, :]
        c_block = c_proj[both, :]
        ahead = dot(c_block, b_block, ((1,), (1,)))
        ahead_scores[both, :] = jnp.where(row >= col, ahead, 0.0).astype(BF16)
        behind = dot(b_block, c_block, ((1,), (1,)))
        behind_scores[both, :] = jnp.where(row <= col, behind, 0.0).astype(BF16)
    onehot = spread_matrix(heads, channels)
    gain = per_lane(gains, heads, channels)
    for j in range(chunks):
        both = slice(j * CHUNK, (j + 1) * CHUNK)
        inner = dot(
            jnp.concatenate([behind_scores[both, :], b_proj[both, :]], axis=1),
            jnp.concatenate([grad_scaled[both, :], grad_low[both, :]], axis=0),
            ((1,), (0,)),
        )
        slope = sigma[both, :] + mixed[both, :] * (1.0 - sigma[both, :])
        inner = gain * grad[both, :].astype(F32) + spread(near[16:32, both], onehot) * inner
        grad_base[both, :] = slope * inner
        grad_weight[both, :] = slope * spread(far[:, both], onehot)
    for j in range(chunks):
        both = slice(j * CHUNK, (j + 1) * CHUNK)
        inner = dot(
            jnp.concatenate([ahead_scores[both, :], c_proj[both, :]], axis=1),
            jnp.concatenate([mixed_scaled[both, :], mixed_low[both, :]], axis=0),
            ((1,), (0,)),
        )
        base_out[both, :] = gain * mixed[both, :] + spread(near[0:16, both], onehot) * inner


def gradient_kernel(parts, taps, base, weight, inputs, b_proj, *rest):
    pays = rest[: parts - 1]
    grad_hbm, tail_out, edge_out, window, result_rows, sems = rest[parts - 1 :]
    rows, channels = base.shape
    chunks = rows // CHUNK
    adjoint = merged(parts, pays, False)
    window[rows : rows + 8, :] = jnp.zeros((8, channels), F32)
    partial = [jnp.zeros((8, channels), F32) for _ in range(4)]
    copies = []
    for j in range(chunks - 1, -1, -1):
        at = j * CHUNK
        both = slice(at, at + CHUNK)
        grad_pre = base[both, :] + weight[both, :] * dot(b_proj[both, :], adjoint, ((1,), (0,)))
        window[both, :] = grad_pre
        x = inputs[16 + at : 16 + at + CHUNK, :]
        result = taps[3:4, :] * grad_pre
        partial[3] = partial[3] + (grad_pre * x).reshape(CHUNK // 8, 8, channels).sum(axis=0)
        for k in range(3):
            moved = window[at + 3 - k : at + 3 - k + CHUNK, :]
            result = result + taps[k : k + 1, :] * moved
            partial[k] = partial[k] + (moved * x).reshape(CHUNK // 8, 8, channels).sum(axis=0)
        result_rows[both, :] = result.astype(BF16)
        if j == chunks - 1:
            edge_out[...] = result[CHUNK - 16 :, :]
        if at % STEP_ROWS == 0:
            place = pl.ds(at, STEP_ROWS)
            copy = pltpu.make_async_copy(
                result_rows.at[place], grad_hbm.at[place], sems.at[at // STEP_ROWS]
            )
            copy.start()
            copies.append(copy)
    for k in range(4):
        tap = jnp.sum(partial[k], axis=0, keepdims=True)
        for j in range(k, 3):
            tap = tap + window[j - k : j - k + 1, :] * inputs[13 + j : 14 + j, :]
        tail_out[k : k + 1, :] = tap
    tail_out[4:7, :] = window[0:3, :]
    tail_out[7:8, :] = jnp.zeros((1, channels), F32)
    for copy in copies:
        copy.wait()


def output_kernel(heads, parts, front, base, c_proj, *rest):
    pays = rest[: parts - 1]
    out_hbm, result_rows, sems = rest[parts - 1 :]
    rows, channels = base.shape
    chunks = rows // CHUNK
    state = merged(parts, pays, True)
    onehot = spread_matrix(heads, channels)
    copies = []
    for j in range(chunks):
        both = slice(j * CHUNK, (j + 1) * CHUNK)
        carried = dot(c_proj[both, :], state, ((1,), (0,)))
        result = base[both, :] + spread(front[:, both], onehot) * carried
        result_rows[both, :] = result.astype(BF16)
        if (j + 1) * CHUNK % STEP_ROWS == 0:
            at = (j + 1) * CHUNK - STEP_ROWS
            place = pl.ds(at, STEP_ROWS)
            copy = pltpu.make_async_copy(
                result_rows.at[place], out_hbm.at[place], sems.at[at // STEP_ROWS]
            )
            copy.start()
            copies.append(copy)
    for copy in copies:
        copy.wait()


def finish_kernel(parts, scale, taps, tail, edge, *rest):
    others = rest[: parts - 1]
    unused, grad_hbm, conv_out, rows_low, sem = rest[parts - 1 :]
    channels = tail.shape[1]
    me = lax.axis_index("seq")
    after = jnp.where(me + 1 < parts, others[parts - 2][...], 0.0)
    row = lax.broadcasted_iota(jnp.int32, (16, channels), 0)
    result = edge[...]
    for r in range(3):
        extra = jnp.zeros((1, channels), F32)
        for k in range(r + 1):
            extra = extra + taps[k : k + 1, :] * after[4 + r - k : 5 + r - k, :]
        result = jnp.where(row == 13 + r, result + extra, result)
    rows_low[...] = result.astype(BF16)
    rows = grad_hbm.shape[0]
    copy = pltpu.make_async_copy(rows_low, grad_hbm.at[pl.ds(rows - 16, 16)], sem)
    copy.start()
    total = tail[0:4, :]
    for other in others:
        total = total + other[0:4, :]
    conv_out[...] = total * scale
    copy.wait()


def rotated(block, axis, distance):
    size = lax.axis_size(axis)
    return lax.ppermute(block, axis, [(i, (i + distance) % size) for i in range(size)])


def shards(
    inputs,
    b_proj,
    c_proj,
    step_codes,
    gate_codes,
    decay_rates,
    skip_gain,
    conv_weight,
    out_cotangent,
):
    rows, channels = inputs.shape
    heads = decay_rates.shape[0]
    parts = lax.axis_size("seq")
    chunks = rows // CHUNK
    pieces = rows // STEP_ROWS
    hbm = pl.BlockSpec(memory_space=pltpu.HBM)
    vmem = pl.BlockSpec(memory_space=pltpu.VMEM)
    smem = pl.BlockSpec(memory_space=pltpu.SMEM)
    shape = jax.ShapeDtypeStruct
    dma = pltpu.SemaphoreType.DMA
    big = rows * channels

    def call(kernel, in_specs, out_specs, out_shape, scratch, products, aliases=None):
        return pl.pallas_call(
            kernel,
            in_specs=in_specs,
            out_specs=out_specs,
            out_shape=out_shape,
            scratch_shapes=scratch,
            input_output_aliases=aliases or {},
            compiler_params=pltpu.CompilerParams(vmem_limit_bytes=VMEM_LIMIT),
            cost_estimate=pl.CostEstimate(
                flops=products * 2 * big * 128, bytes_accessed=6 * big, transcendentals=big
            ),
        )

    def stay(array):
        return pltpu.with_memory_space_constraint(array, pltpu.HBM)

    halo_from = [(i, i + 1) for i in range(parts - 1)]
    halo = lax.ppermute(inputs[rows - 16 :], "seq", halo_from)
    pay = shape((STATE + 16, channels), BF16)
    narrow = shape((rows, channels), BF16)
    broad = shape((rows, channels), F32)

    near, far, front, logs, grad_scaled, grad_low, adjoint_pay = call(
        functools.partial(adjoint_kernel, heads),
        [hbm] * 5,
        [vmem] * 7,
        [
            shape((32, rows), BF16),
            shape((16, rows), BF16),
            shape((16, rows), BF16),
            shape((3, chunks, channels), F32),
            narrow,
            narrow,
            pay,
        ],
        [
            pltpu.SMEM((heads,), F32),
            pltpu.VMEM((heads, rows), jnp.int32),
            pltpu.VMEM((1, rows), jnp.int32),
            pltpu.VMEM((rows, channels), BF16),
            pltpu.VMEM((rows, 128), BF16),
            pltpu.VMEM((8, rows), F32),
            pltpu.VMEM((rows, channels), F32),
            dma((3,)),
            dma((pieces,)),
            dma((pieces,)),
        ],
        2,
    )(
        stay(decay_rates),
        stay(step_codes),
        stay(gate_codes.reshape(1, rows)),
        stay(out_cotangent),
        stay(c_proj),
    )

    outs = call(
        functools.partial(state_kernel, heads, parts),
        [vmem] * 7,
        [vmem] * (4 + parts),
        [shape((rows + 16, channels), F32), broad, broad, narrow, narrow] + [pay] * (parts - 1),
        [pltpu.VMEM((rows, channels), F32)],
        2,
    )(conv_weight, near, logs, inputs, halo, b_proj, adjoint_pay)
    wide_inputs, mixed, sigma, mixed_scaled, mixed_low = outs[:5]
    pays = [rotated(send, "seq", distance + 1) for distance, send in enumerate(outs[5:])]

    base, grad_base, grad_weight = call(
        functools.partial(inner_kernel, heads),
        [smem] + [vmem] * 11,
        [vmem] * 3,
        [broad] * 3,
        [pltpu.VMEM((rows, CHUNK), BF16), pltpu.VMEM((rows, CHUNK), BF16)],
        6,
    )(
        skip_gain, near, far, out_cotangent, mixed, sigma, b_proj, c_proj,
        mixed_scaled, mixed_low, grad_scaled, grad_low,
    )

    grad_rows, tail, edge = call(
        functools.partial(gradient_kernel, parts),
        [vmem] * (4 + parts),
        [hbm, vmem, vmem],
        [narrow, shape((8, channels), F32), shape((16, channels), F32)],
        [pltpu.VMEM((rows + 8, channels), F32), pltpu.VMEM((rows, channels), BF16), dma((pieces,))],
        2,
    )(conv_weight, grad_base, grad_weight, wide_inputs, b_proj, *pays)
    tails = [rotated(tail, "seq", distance) for distance in range(1, parts)]

    layer_out = call(
        functools.partial(output_kernel, heads, parts),
        [vmem] * (2 + parts),
        hbm,
        narrow,
        [pltpu.VMEM((rows, channels), BF16), dma((pieces,))],
        2,
    )(front, base, c_proj, *pays)

    scale = float((rows * parts) ** -0.5)
    input_grad, conv_grad = call(
        functools.partial(finish_kernel, parts, scale),
        [vmem] * (2 + parts) + [hbm],
        [hbm, vmem],
        [narrow, shape((4, channels), F32)],
        [pltpu.VMEM((16, channels), BF16), dma],
        0,
        {parts + 2: 0},
    )(conv_weight, tail, edge, *tails, grad_rows)
    return layer_out, input_grad, conv_grad


def solution(mesh):
    in_specs = (
        P(("groups", "seq"), ("head", "sub")),
        P(("groups", "seq"), None),
        P(("groups", "seq"), None),
        P(("head", "sub"), ("groups", "seq")),
        P(("groups", "seq")),
        P(("head", "sub")),
        P(("head", "sub")),
        P(None, ("head", "sub")),
        P(("groups", "seq"), ("head", "sub")),
    )
    out_specs = (
        P(("groups", "seq"), ("head", "sub")),
        P(("groups", "seq"), ("head", "sub")),
        P("groups", ("head", "sub")),
    )
    return jax.shard_map(shards, mesh=mesh, in_specs=in_specs, out_specs=out_specs, check_vma=False)
```

time: 188 us -> 46.7 us (0.25)
  matrix products: 60.7 us -> 0 us
  blocking collectives: 56 us -> 0 us
  local copies, waits for them, and re-layouts: 34.3 us -> 0.89 us
  other arithmetic: 27.2 us -> 0 us
  Pallas kernels: 0 us -> 24.8 us
  starting transfers between devices: 6.2 us -> 15 us
  waiting for transfers between devices: 0.01 us -> 4.82 us
    dot_general x24 -> x0, matrix products: 60.7 us -> none  [the longest x4 15.7 us: local_block(): jnp.einsum('hst,shp->thp', weights, grad_b, preferred_element_type=jnp.fl...]
    all_gather x2 -> x0, blocking collectives: 35.9 us -> none  [the longest x1 18.7 us: shards(): end_pieces = lax.all_gather(local_end[None], 'seq', axis=0, tiled=True)]
    pallas_call x0 -> x6, Pallas kernels: none -> 24.8 us  [the longest x1 5.92 us: shards(): call(functools.partial(state_kernel, heads, parts), [vmem] * 7, [vmem] *...]
    unnamed x46 -> x12, local copies, waits for them, and re-layouts: 15.7 us -> 0.03 us
    psum x1 -> x0, blocking collectives: 10.1 us -> none  [shards(): lax.psum(local_grad, 'seq') * (row_count * lax.axis_size('seq')) ** (-0.5)]
    unnamed x1 -> x0, blocking collectives: 9.92 us -> none
    convert_element_type x2 -> x0, other arithmetic: 9.26 us -> none  [the longest x1 5.04 us: shards(): return (layer_out, input_grad.astype(jnp.bfloat16), conv_grad)]
    ppermute x2 -> x7, starting transfers between devices: 6.2 us -> 15 us  [the longest x6 10.1 us: rotated(): lax.ppermute(block, axis, [(i, (i + distance) % size) for i in range(size)])]
  transfers between devices with their start and end apart: 2 -> 7, of which waited for: 0 -> 3; matrix products, arithmetic and copies ran while one was open for 18% -> 0% of each run, Pallas kernels for 0% -> 26%
where the time goes in v2:
time: 46.7 us; the launch traced here: 46.5 us
  Pallas kernels  24.8 us (53%)
  starting transfers between devices  15 us (32%)
  waiting for transfers between devices  4.82 us (10%)
  between operations  0.94 us (2%)
  local copies, waits for them, and re-layouts  0.89 us (2%)
    ppermute x6, starting transfers between devices, rotated(): lax.ppermute(block, axis, [(i, (i + distance) % size) for i in range(size)])  10.1 us
    pallas_call x1, Pallas kernels, shards(): call(functools.partial(state_kernel, heads, parts), [vmem] * 7, [vmem] *...  5.92 us
    pallas_call x1, Pallas kernels, shards(): call(functools.partial(adjoint_kernel, heads), [hbm] * 5, [vmem] * 7, [sh...  5.86 us
    pallas_call x1, Pallas kernels, shards(): call(functools.partial(gradient_kernel, parts), [vmem] * (4 + parts), [hb...  5.73 us
    ppermute x1, starting transfers between devices, shards(): halo = lax.ppermute(inputs[rows - 16:], 'seq', halo_from)  4.92 us
    ppermute x6, waiting for transfers between devices, rotated(): lax.ppermute(block, axis, [(i, (i + distance) % size) for i in range(size)])  4.82 us
    pallas_call x1, Pallas kernels, shards(): call(functools.partial(inner_kernel, heads), [smem] + [vmem] * 11, [vmem]...  4.25 us
    pallas_call x1, Pallas kernels, shards(): call(functools.partial(output_kernel, heads, parts), [vmem] * (2 + parts)...  1.84 us
  transfers between devices with their start and end apart: 7, of which 3 were waited for; matrix products, arithmetic and copies ran while one was open for 0% of the time, Pallas kernels for 26%

profile of v2, /device:TPU:0, one launch (start us, length us, event | category | flops | bytes accessed | tf_op | source)
XLA Modules:
  0.0 46.5 jit_solution(11284690312020774460)
XLA Ops:
  0.6 0.0 copy-start.3
  0.6 0.0 copy-start.4
  0.7 0.0 copy-start.2
  0.7 0.9 %slice.3 = bf16[16,384]{1,0:T(8,128)(2,1)S(1)} slice(bf16[2048,384]{1,0:T(8,128)(2,1)} %inputs.1), slice={[2032:2048], [0:384]} | slice | bytes 24576 | tf_op jit(solution)/shard_map/slice | solution.py:399
  1.5 4.9 %collective-permute-start = (bf16[16,384]{1,0:T(8,128)(2,1)S(1)}, bf16[16,384]{1,0:T(8,128)(2,1)S(1)}, u32[]{:S(2)}, u32[]{:S(2)}) collective-permute-start(bf16[16,384]{1,0:T(8,128)(2,1)S(1)} %slice.3), channel_id=1, source_target_pairs={{0,4},{4,8},{8,12},{1,5},{5,9},{9,13},{2,6},{6,10},{10,14},{3,7},{... | collective-permute-start | bytes 36872 | tf_op jit(solution)/shard_map/ppermute | solution.py:399
  6.4 5.9 %shard_map.112 = (bf16[32,2048]{1,0:T(8,128)(2,1)S(1)}, bf16[16,2048]{1,0:T(8,128)(2,1)S(1)}, bf16[16,2048]{1,0:T(8,128)(2,1)S(1)}, f32[3,16,384]{2,1,0:T(8,128)...) custom-call(f32[6]{0:T(128)} %rates_hbm.1, s32[6,2048]{1,0:T(8,128)} %codes_hbm.1, ...), custom_call_target="tpu_custom_call" | custom-call | flops 402653184 | bytes 4718592 | tf_op jit(solution)/shard_map/pallas_call | solution.py:404
  12.3 0.0 copy-start
  12.3 0.0 copy-start.1
  12.3 0.0 copy-start.5
  12.3 0.0 collective-permute-done.halo
  12.4 0.0 copy-done.3
  12.4 0.0 copy-done.4
  12.4 0.0 copy-done.2
  12.4 5.9 %shard_map.113 = (f32[2064,384]{1,0:T(8,128)S(1)}, f32[2048,384]{1,0:T(8,128)S(1)}, f32[2048,384]{1,0:T(8,128)S(1)}, bf16[2048,384]{1,0:T(8,128)(2,1)S(1)}, bf16...) custom-call(f32[4,384]{1,0:T(4,128)S(1)} %copy-done.4, ...), custom_call_target="tpu_custom_call" | custom-call | flops 402653184 | bytes 4718592 | tf_op jit(solution)/shard_map/pallas_call | solution.py:438
  18.3 1.6 %collective-permute-start.1 = (bf16[144,384]{1,0:T(8,128)(2,1)S(1)}, bf16[144,384]{1,0:T(8,128)(2,1)S(1)}, u32[]{:S(2)}, u32[]{:S(2)}) collective-permute-start(bf16[144,384]{1,0:T(8,128)(2,1)S(1)} %get-tuple-element.38), channel_id=1, source_target_pairs={{0,4},{4,8},{8,12},{12,0},{1,5},{5,9},{9,13},{13,1},{2,6},{6,10},{... | collective-permute-start | bytes 331784 | tf_op jit(solution)/shard_map/ppermute | solution.py:355
  20.0 1.1 %collective-permute-start.2 = (bf16[144,384]{1,0:T(8,128)(2,1)S(1)}, bf16[144,384]{1,0:T(8,128)(2,1)S(1)}, u32[]{:S(2)}, u32[]{:S(2)}) collective-permute-start(bf16[144,384]{1,0:T(8,128)(2,1)S(1)} %get-tuple-element.39), channel_id=1, source_target_pairs={{0,8},{4,12},{8,0},{12,4},{1,9},{5,13},{9,1},{13,5},{2,10},{6,14},... | collective-permute-start | bytes 331784 | tf_op jit(solution)/shard_map/ppermute | solution.py:355
  21.0 2.8 %collective-permute-start.3 = (bf16[144,384]{1,0:T(8,128)(2,1)S(1)}, bf16[144,384]{1,0:T(8,128)(2,1)S(1)}, u32[]{:S(2)}, u32[]{:S(2)}) collective-permute-start(bf16[144,384]{1,0:T(8,128)(2,1)S(1)} %get-tuple-element.40), channel_id=1, source_target_pairs={{0,12},{4,0},{8,4},{12,8},{1,13},{5,1},{9,5},{13,9},{2,14},{6,2},{... | collective-permute-start | bytes 331784 | tf_op jit(solution)/shard_map/ppermute | solution.py:355
  23.9 0.0 copy-done
  23.9 0.0 copy-done.1
  23.9 4.3 %shard_map.114 = (f32[2048,384]{1,0:T(8,128)S(1)}, f32[2048,384]{1,0:T(8,128)S(1)}, f32[2048,384]{1,0:T(8,128)S(1)}) custom-call(f32[6]{0:T(128)S(1)} %copy-done.5, bf16[32,2048]{1,0:T(8,128)(2,1)S(1)} %get-tuple-element.27.near, bf16[16,2048]{1,0:T(8,128)(2,1)S(1)} %get-tuple-element.28.far, bf16[2048,384]{1,0:T(8,128)(2,1)S(1)} %copy-done, ...), custom_call_target="tpu_custom_call" | custom-call | flops 1207959552 | bytes 4718592 | tf_op jit(solution)/shard_map/pallas_call | solution.py:449
  28.2 0.0 collective-permute-done.1.rest_0_
  28.2 1.5 %collective-permute-done.2.rest_1_ = bf16[144,384]{1,0:T(8,128)(2,1)S(1)} collective-permute-done((bf16[144,384]{1,0:T(8,128)(2,1)S(1)}, bf16[144,384]{1,0:T(8,128)(2,1)S(1)}, u32[]{:S(2)}, u32[]{:S(2)}) %collective-permute-start.2) | collective-permute-done | bytes 110624 | tf_op jit(solution)/shard_map/ppermute | solution.py:355
  29.7 0.0 collective-permute-done.3.rest_2_
  29.7 5.7 %shard_map.116 = (bf16[2048,384]{1,0:T(8,128)(2,1)}, f32[8,384]{1,0:T(8,128)S(1)}, f32[16,384]{1,0:T(8,128)S(1)}) custom-call(f32[4,384]{1,0:T(4,128)S(1)} %copy-done.4, f32[2048,384]{1,0:T(8,128)S(1)} %get-tuple-element.41.base, f32[2048,384]{1,0:T(8,128)S(1)} %get-tuple-element.42.weight, f32[2064,384]{1,0:T(8,128)S(1)} %get-tuple-element.43.inputs, ...), custom_call_target="tpu_custom_call" | custom-call | flops 402653184 | bytes 4718592 | tf_op jit(solution)/shard_map/pallas_call | solution.py:461
  35.4 3.9 %collective-permute-start.6 = (f32[8,384]{1,0:T(8,128)S(1)}, f32[8,384]{1,0:T(8,128)S(1)}, u32[]{:S(2)}, u32[]{:S(2)}) collective-permute-start(f32[8,384]{1,0:T(8,128)S(1)} %get-tuple-element.44.tail), channel_id=1, source_target_pairs={{0,12},{4,0},{8,4},{12,8},{1,13},{5,1},{9,5},{13,9},{2,14},{6,2},{... | collective-permute-start | bytes 36872 | tf_op jit(solution)/shard_map/ppermute | solution.py:355
  39.3 0.3 collective-permute-start.5
  39.6 0.3 collective-permute-start.4
  39.9 1.8 %shard_map.115 = bf16[2048,384]{1,0:T(8,128)(2,1)} custom-call(bf16[16,2048]{1,0:T(8,128)(2,1)S(1)} %get-tuple-element.26.front, f32[2048,384]{1,0:T(8,128)S(1)} %get-tuple-element.37.base, bf16[2048,128]{1,0:T(8,128)(2,1)S(1)} %copy-done.1, bf16[144,384]{1,0:T(8,128)(2,1)S(1)} %collective-permute-done.1.rest_0_, ...), custom_call_target="tpu_custom_call" | custom-call | flops 402653184 | bytes 4718592 | tf_op jit(solution)/shard_map/pallas_call | solution.py:471
  41.8 0.0 collective-permute-done.6.rest_2_
  41.8 2.1 %collective-permute-done.5.rest_1_ = f32[8,384]{1,0:T(8,128)S(1)} collective-permute-done((f32[8,384]{1,0:T(8,128)S(1)}, f32[8,384]{1,0:T(8,128)S(1)}, u32[]{:S(2)}, u32[]{:S(2)}) %collective-permute-start.5) | collective-permute-done | bytes 12320 | tf_op jit(solution)/shard_map/ppermute | solution.py:355
  43.9 1.2 %collective-permute-done.4.rest_0_ = f32[8,384]{1,0:T(8,128)S(1)} collective-permute-done((f32[8,384]{1,0:T(8,128)S(1)}, f32[8,384]{1,0:T(8,128)S(1)}, u32[]{:S(2)}, u32[]{:S(2)}) %collective-permute-start.4) | collective-permute-done | bytes 12320 | tf_op jit(solution)/shard_map/ppermute | solution.py:355
  45.1 1.2 %shard_map.117 = (bf16[2048,384]{1,0:T(8,128)(2,1)}, f32[4,384]{1,0:T(4,128)}) custom-call(f32[4,384]{1,0:T(4,128)S(1)} %copy-done.4, f32[8,384]{1,0:T(8,128)S(1)} %get-tuple-element.44.tail, f32[16,384]{1,0:T(8,128)S(1)} %get-tuple-element.45.edge, f32[8,384]{1,0:T(8,128)S(1)} %collective-permute-done.4.rest_0_, ...), custom_call_target="tpu_custom_call", output_to_operand_aliasing={{0}: (6, {})} | custom-call | bytes 4718592 | tf_op jit(solution)/shard_map/pallas_call | solution.py:481
  (1 shorter events, 0.0 us)
Async XLA Ops:
  0.6 11.7 %copy-start.3 = (bf16[2048,384]{1,0:T(8,128)(2,1)S(1)}, bf16[2048,384]{1,0:T(8,128)(2,1)}, u32[]{:S(2)}) copy-start(bf16[2048,384]{1,0:T(8,128)(2,1)} %inputs.1) | copy-start | bytes 4718596
  0.6 11.7 %copy-start.4 = (f32[4,384]{1,0:T(4,128)S(1)}, f32[4,384]{1,0:T(4,128)}, u32[]{:S(2)}) copy-start(f32[4,384]{1,0:T(4,128)} %taps.5) | copy-start | bytes 18436
  0.7 11.7 %copy-start.2 = (bf16[2048,128]{1,0:T(8,128)(2,1)S(1)}, bf16[2048,128]{1,0:T(8,128)(2,1)}, u32[]{:S(2)}) copy-start(bf16[2048,128]{1,0:T(8,128)(2,1)} %b_proj.5) | copy-start | bytes 1572868
  1.5 10.8 %collective-permute-start = (bf16[16,384]{1,0:T(8,128)(2,1)S(1)}, bf16[16,384]{1,0:T(8,128)(2,1)S(1)}, u32[]{:S(2)}, u32[]{:S(2)}) collective-permute-start(bf16[16,384]{1,0:T(8,128)(2,1)S(1)} %slice.3), channel_id=1, source_target_pairs={{0,4},{4,8},{8,12},{1,5},{5,9},{9,13},{2,6},{6,10},{10,14},{3,7},{... | collective-permute-start | bytes 36872 | tf_op jit(solution)/shard_map/ppermute | solution.py:399
  12.3 11.6 %copy-start = (bf16[2048,384]{1,0:T(8,128)(2,1)S(1)}, bf16[2048,384]{1,0:T(8,128)(2,1)}, u32[]{:S(2)}) copy-start(bf16[2048,384]{1,0:T(8,128)(2,1)} %grad.1) | copy-start | bytes 4718596
  12.3 11.6 %copy-start.1 = (bf16[2048,128]{1,0:T(8,128)(2,1)S(1)}, bf16[2048,128]{1,0:T(8,128)(2,1)}, u32[]{:S(2)}) copy-start(bf16[2048,128]{1,0:T(8,128)(2,1)} %c_proj.3) | copy-start | bytes 1572868
  12.3 11.6 %copy-start.5 = (f32[6]{0:T(128)S(1)}, f32[6]{0:T(128)}, u32[]{:S(2)}) copy-start(f32[6]{0:T(128)} %gains.1) | copy-start | bytes 76
  18.3 9.8 %collective-permute-start.1 = (bf16[144,384]{1,0:T(8,128)(2,1)S(1)}, bf16[144,384]{1,0:T(8,128)(2,1)S(1)}, u32[]{:S(2)}, u32[]{:S(2)}) collective-permute-start(bf16[144,384]{1,0:T(8,128)(2,1)S(1)} %get-tuple-element.38), channel_id=1, source_target_pairs={{0,4},{4,8},{8,12},{12,0},{1,5},{5,9},{9,13},{13,1},{2,6},{6,10},{... | collective-permute-start | bytes 331784 | tf_op jit(solution)/shard_map/ppermute | solution.py:355
  20.0 9.7 %collective-permute-start.2 = (bf16[144,384]{1,0:T(8,128)(2,1)S(1)}, bf16[144,384]{1,0:T(8,128)(2,1)S(1)}, u32[]{:S(2)}, u32[]{:S(2)}) collective-permute-start(bf16[144,384]{1,0:T(8,128)(2,1)S(1)} %get-tuple-element.39), channel_id=1, source_target_pairs={{0,8},{4,12},{8,0},{12,4},{1,9},{5,13},{9,1},{13,5},{2,10},{6,14},... | collective-permute-start | bytes 331784 | tf_op jit(solution)/shard_map/ppermute | solution.py:355
  21.0 8.6 %collective-permute-start.3 = (bf16[144,384]{1,0:T(8,128)(2,1)S(1)}, bf16[144,384]{1,0:T(8,128)(2,1)S(1)}, u32[]{:S(2)}, u32[]{:S(2)}) collective-permute-start(bf16[144,384]{1,0:T(8,128)(2,1)S(1)} %get-tuple-element.40), channel_id=1, source_target_pairs={{0,12},{4,0},{8,4},{12,8},{1,13},{5,1},{9,5},{13,9},{2,14},{6,2},{... | collective-permute-start | bytes 331784 | tf_op jit(solution)/shard_map/ppermute | solution.py:355
  35.4 6.4 %collective-permute-start.6 = (f32[8,384]{1,0:T(8,128)S(1)}, f32[8,384]{1,0:T(8,128)S(1)}, u32[]{:S(2)}, u32[]{:S(2)}) collective-permute-start(f32[8,384]{1,0:T(8,128)S(1)} %get-tuple-element.44.tail), channel_id=1, source_target_pairs={{0,12},{4,0},{8,4},{12,8},{1,13},{5,1},{9,5},{13,9},{2,14},{6,2},{... | collective-permute-start | bytes 36872 | tf_op jit(solution)/shard_map/ppermute | solution.py:355
  39.3 4.6 %collective-permute-start.5 = (f32[8,384]{1,0:T(8,128)S(1)}, f32[8,384]{1,0:T(8,128)S(1)}, u32[]{:S(2)}, u32[]{:S(2)}) collective-permute-start(f32[8,384]{1,0:T(8,128)S(1)} %get-tuple-element.44.tail), channel_id=1, source_target_pairs={{0,8},{4,12},{8,0},{12,4},{1,9},{5,13},{9,1},{13,5},{2,10},{6,14},... | collective-permute-start | bytes 36872 | tf_op jit(solution)/shard_map/ppermute | solution.py:355
  39.6 5.5 %collective-permute-start.4 = (f32[8,384]{1,0:T(8,128)S(1)}, f32[8,384]{1,0:T(8,128)S(1)}, u32[]{:S(2)}, u32[]{:S(2)}) collective-permute-start(f32[8,384]{1,0:T(8,128)S(1)} %get-tuple-element.44.tail), channel_id=1, source_target_pairs={{0,4},{4,8},{8,12},{12,0},{1,5},{5,9},{9,13},{13,1},{2,6},{6,10},{... | collective-permute-start | bytes 36872 | tf_op jit(solution)/shard_map/ppermute | solution.py:355

commit v3 on v2

--- a/solution.py
+++ b/solution.py
@@ -51,8 +51,8 @@
 
 def adjoint_kernel(
     heads, rates_hbm, codes_hbm, gates_hbm, grad_hbm, c_hbm,
-    near_out, far_out, front_out, logs_out, scaled_out, low_out, pay_out,
-    rates, codes, gates, grad, c_proj, steps, fresh, small_sem, grad_sem, c_sem,
+    near_out, far_out, front_out, logs_out, pay_out,
+    rates, codes, gates, grad, c_proj, steps, small_sem, grad_sem, c_sem,
 ):
     rows, channels = grad.shape
     chunks = rows // CHUNK
@@ -139,24 +139,15 @@
     pay_out[STATE : STATE + 16, :] = tail.astype(BF16)
 
     onehot = spread_matrix(heads, channels)
+    total = jnp.zeros((STATE, channels), F32)
     for piece in range(pieces):
+        both = slice(piece * STEP_ROWS, (piece + 1) * STEP_ROWS)
+        scale = spread(front_out[:, both], onehot)
         large[2 * piece].wait()
         large[2 * piece + 1].wait()
-        for j in range(piece * STEP_ROWS // CHUNK, (piece + 1) * STEP_ROWS // CHUNK):
-            both = slice(j * CHUNK, (j + 1) * CHUNK)
-            scale = spread(near_out[0:16, both], onehot)
-            scaled = (grad[both, :].astype(F32) * scale).astype(BF16)
-            scaled_out[both, :] = scaled
-            fresh[both, :] = dot(c_proj[both, :], scaled, ((0,), (0,)))
-    for lanes in lane_tiles(channels):
-        adjoint = jnp.zeros((STATE, lanes.stop - lanes.start), F32)
-        for j in range(chunks - 1, -1, -1):
-            both = slice(j * CHUNK, (j + 1) * CHUNK)
-            low_out[both, lanes] = (adjoint * rest_of[j : j + 1, lanes]).astype(BF16)
-            adjoint = whole[j : j + 1, lanes] * adjoint + (
-                middle[j : j + 1, lanes] * fresh[both, lanes]
-            )
-        pay_out[0:STATE, lanes] = adjoint.astype(BF16)
+        scaled = (grad[both, :].astype(F32) * scale).astype(BF16)
+        total = total + dot(c_proj[both, :], scaled, ((0,), (0,)))
+    pay_out[0:STATE, :] = total.astype(BF16)
 
 
 def lane_tiles(channels):
@@ -164,45 +155,40 @@
 
 
 def state_kernel(
-    heads, parts, taps, near, logs, inputs, halo, b_proj, adjoint_pay,
-    window, mixed_out, sigma_out, scaled_out, low_out, *rest
+    heads, parts, taps, far, inputs, halo, b_proj, adjoint_pay, mixed_out, sigma_out, *pays
 ):
-    pays, fresh = rest[: parts - 1], rest[parts - 1]
     rows, channels = inputs.shape
-    chunks = rows // CHUNK
-    window[0:16, :] = halo[...].astype(F32)
+    pieces = rows // STEP_ROWS
+    me = lax.axis_index("seq")
+    before = jnp.where(me > 0, halo[...].astype(F32), 0.0).astype(BF16)
     onehot = spread_matrix(heads, channels)
-    for j in range(chunks):
-        at = j * CHUNK
-        both = slice(at, at + CHUNK)
-        window[16 + at : 16 + at + CHUNK, :] = inputs[both, :].astype(F32)
-        preact = taps[0:1, :] * window[13 + at : 13 + at + CHUNK, :]
-        for k in range(1, 4):
-            preact = preact + taps[k : k + 1, :] * window[13 + k + at : 13 + k + at + CHUNK, :]
-        sigma = 0.5 * jnp.tanh(0.5 * preact) + 0.5
-        mixed = preact * sigma
-        sigma_out[both, :] = sigma
-        mixed_out[both, :] = mixed
-        scale = spread(near[16:32, both], onehot)
-        scaled = (mixed * scale).astype(BF16)
-        scaled_out[both, :] = scaled
-        fresh[both, :] = dot(b_proj[both, :], scaled, ((0,), (0,)))
-    me = lax.axis_index("seq")
-    for lanes in lane_tiles(channels):
-        state = jnp.zeros((STATE, lanes.stop - lanes.start), F32)
-        for j in range(chunks):
-            both = slice(j * CHUNK, (j + 1) * CHUNK)
-            low_out[both, lanes] = (state * logs[1, j : j + 1, lanes]).astype(BF16)
-            state = logs[0, j : j + 1, lanes] * state + (
-                logs[2, j : j + 1, lanes] * fresh[both, lanes]
-            )
-        state = state.astype(BF16)
-        for distance in range(1, parts):
-            forward = me + distance < parts
-            pays[distance - 1][0:STATE, lanes] = jnp.where(
-                forward, state, adjoint_pay[0:STATE, lanes]
-            )
-    for pay in pays:
+    row = lax.broadcasted_iota(jnp.int32, (3 * CHUNK, CHUNK + 16), 0)
+    col = lax.broadcasted_iota(jnp.int32, (3 * CHUNK, CHUNK + 16), 1)
+    shift = jnp.where(col == row % CHUNK + 13 + row // CHUNK, 1.0, 0.0).astype(BF16)
+    total = jnp.zeros((STATE, channels), F32)
+    for piece in range(pieces):
+        scaled = []
+        for at in range(piece * STEP_ROWS, (piece + 1) * STEP_ROWS, CHUNK):
+            both = slice(at, at + CHUNK)
+            if at == 0:
+                block = jnp.concatenate([before, inputs[both, :]], axis=0)
+            else:
+                block = inputs[at - 16 : at + CHUNK, :]
+            moved = dot(shift, block, ((1,), (0,)))
+            preact = taps[3:4, :] * inputs[both, :].astype(F32)
+            for k in range(3):
+                preact = preact + taps[k : k + 1, :] * moved[k * CHUNK : (k + 1) * CHUNK, :]
+            sigma = 0.5 * jnp.tanh(0.5 * preact) + 0.5
+            mixed = preact * sigma
+            sigma_out[both, :] = sigma
+            mixed_out[both, :] = mixed
+            scaled.append((mixed * spread(far[:, both], onehot)).astype(BF16))
+        both = slice(piece * STEP_ROWS, (piece + 1) * STEP_ROWS)
+        total = total + dot(b_proj[both, :], jnp.concatenate(scaled, axis=0), ((0,), (0,)))
+    state = total.astype(BF16)
+    for distance in range(1, parts):
+        pay = pays[distance - 1]
+        pay[0:STATE, :] = jnp.where(me + distance < parts, state, adjoint_pay[0:STATE, :])
         pay[STATE : STATE + 16, :] = adjoint_pay[STATE : STATE + 16, :]
 
 
@@ -220,26 +206,48 @@
 
 
 def inner_kernel(
-    heads, gains, near, far, grad, mixed, sigma, b_proj, c_proj,
-    mixed_scaled, mixed_low, grad_scaled, grad_low,
-    base_out, grad_base, grad_weight, ahead_scores, behind_scores,
+    heads, gains, near, far, logs, grad, mixed, sigma, b_proj, c_proj,
+    base_out, grad_base, grad_weight,
+    ahead_scores, behind_scores, mixed_scaled, mixed_low, grad_scaled, grad_low,
+    mixed_fresh, grad_fresh,
 ):
     rows, channels = grad.shape
     chunks = rows // CHUNK
+    blocks = [slice(j * CHUNK, (j + 1) * CHUNK) for j in range(chunks)]
     row = lax.broadcasted_iota(jnp.int32, (CHUNK, CHUNK), 0)
     col = lax.broadcasted_iota(jnp.int32, (CHUNK, CHUNK), 1)
-    for j in range(chunks):
-        both = slice(j * CHUNK, (j + 1) * CHUNK)
-        b_block = b_proj[both, :]
-        c_block = c_proj[both, :]
-        ahead = dot(c_block, b_block, ((1,), (1,)))
-        ahead_scores[both, :] = jnp.where(row >= col, ahead, 0.0).astype(BF16)
-        behind = dot(b_block, c_block, ((1,), (1,)))
-        behind_scores[both, :] = jnp.where(row <= col, behind, 0.0).astype(BF16)
     onehot = spread_matrix(heads, channels)
     gain = per_lane(gains, heads, channels)
-    for j in range(chunks):
-        both = slice(j * CHUNK, (j + 1) * CHUNK)
+    for both in blocks:
+        scale = spread(near[0:16, both], onehot)
+        grad_scaled[both, :] = (grad[both, :].astype(F32) * scale).astype(BF16)
+    for both in blocks:
+        scale = spread(near[16:32, both], onehot)
+        mixed_scaled[both, :] = (mixed[both, :] * scale).astype(BF16)
+    for both in blocks:
+        grad_fresh[both, :] = dot(c_proj[both, :], grad_scaled[both, :], ((0,), (0,)))
+    for both in blocks:
+        mixed_fresh[both, :] = dot(b_proj[both, :], mixed_scaled[both, :], ((0,), (0,)))
+    for both in blocks:
+        ahead = dot(c_proj[both, :], b_proj[both, :], ((1,), (1,)))
+        ahead_scores[both, :] = jnp.where(row >= col, ahead, 0.0).astype(BF16)
+    for both in blocks:
+        behind = dot(b_proj[both, :], c_proj[both, :], ((1,), (1,)))
+        behind_scores[both, :] = jnp.where(row <= col, behind, 0.0).astype(BF16)
+    for lanes in lane_tiles(channels):
+        adjoint = jnp.zeros((STATE, lanes.stop - lanes.start), F32)
+        for j in range(chunks - 1, -1, -1):
+            grad_low[blocks[j], lanes] = (adjoint * logs[2, j : j + 1, lanes]).astype(BF16)
+            adjoint = logs[0, j : j + 1, lanes] * adjoint + (
+                logs[1, j : j + 1, lanes] * grad_fresh[blocks[j], lanes]
+            )
+        state = jnp.zeros((STATE, lanes.stop - lanes.start), F32)
+        for j in range(chunks):
+            mixed_low[blocks[j], lanes] = (state * logs[1, j : j + 1, lanes]).astype(BF16)
+            state = logs[0, j : j + 1, lanes] * state + (
+                logs[2, j : j + 1, lanes] * mixed_fresh[blocks[j], lanes]
+            )
+    for both in blocks:
         inner = dot(
             jnp.concatenate([behind_scores[both, :], b_proj[both, :]], axis=1),
             jnp.concatenate([grad_scaled[both, :], grad_low[both, :]], axis=0),
@@ -249,8 +257,7 @@
         inner = gain * grad[both, :].astype(F32) + spread(near[16:32, both], onehot) * inner
         grad_base[both, :] = slope * inner
         grad_weight[both, :] = slope * spread(far[:, both], onehot)
-    for j in range(chunks):
-        both = slice(j * CHUNK, (j + 1) * CHUNK)
+    for both in blocks:
         inner = dot(
             jnp.concatenate([ahead_scores[both, :], c_proj[both, :]], axis=1),
             jnp.concatenate([mixed_scaled[both, :], mixed_low[both, :]], axis=0),
@@ -259,71 +266,68 @@
         base_out[both, :] = gain * mixed[both, :] + spread(near[0:16, both], onehot) * inner
 
 
-def gradient_kernel(parts, taps, base, weight, inputs, b_proj, *rest):
+def gradient_kernel(parts, taps, base, weight, inputs, halo, b_proj, *rest):
     pays = rest[: parts - 1]
-    grad_hbm, tail_out, edge_out, window, result_rows, sems = rest[parts - 1 :]
+    grad_out, tail_out, edge_out, window = rest[parts - 1 :]
     rows, channels = base.shape
     chunks = rows // CHUNK
     adjoint = merged(parts, pays, False)
-    window[rows : rows + 8, :] = jnp.zeros((8, channels), F32)
+    me = lax.axis_index("seq")
+    window[rows : rows + 16, :] = jnp.zeros((16, channels), BF16)
+    row = lax.broadcasted_iota(jnp.int32, (3 * CHUNK, CHUNK + 16), 0)
+    col = lax.broadcasted_iota(jnp.int32, (3 * CHUNK, CHUNK + 16), 1)
+    shift = jnp.where(col == row % CHUNK + 3 - row // CHUNK, 1.0, 0.0).astype(BF16)
     partial = [jnp.zeros((8, channels), F32) for _ in range(4)]
-    copies = []
     for j in range(chunks - 1, -1, -1):
         at = j * CHUNK
         both = slice(at, at + CHUNK)
         grad_pre = base[both, :] + weight[both, :] * dot(b_proj[both, :], adjoint, ((1,), (0,)))
-        window[both, :] = grad_pre
-        x = inputs[16 + at : 16 + at + CHUNK, :]
+        window[both, :] = grad_pre.astype(BF16)
+        moved = dot(shift, window[at : at + CHUNK + 16, :], ((1,), (0,)))
+        x = inputs[both, :].astype(F32)
         result = taps[3:4, :] * grad_pre
         partial[3] = partial[3] + (grad_pre * x).reshape(CHUNK // 8, 8, channels).sum(axis=0)
         for k in range(3):
-            moved = window[at + 3 - k : at + 3 - k + CHUNK, :]
-            result = result + taps[k : k + 1, :] * moved
-            partial[k] = partial[k] + (moved * x).reshape(CHUNK // 8, 8, channels).sum(axis=0)
-        result_rows[both, :] = result.astype(BF16)
+            part = moved[k * CHUNK : (k + 1) * CHUNK, :]
+            result = result + taps[k : k + 1, :] * part
+            partial[k] = partial[k] + (part * x).reshape(CHUNK // 8, 8, channels).sum(axis=0)
+        grad_out[both, :] = result.astype(BF16)
         if j == chunks - 1:
             edge_out[...] = result[CHUNK - 16 :, :]
-        if at % STEP_ROWS == 0:
-            place = pl.ds(at, STEP_ROWS)
-            copy = pltpu.make_async_copy(
-                result_rows.at[place], grad_hbm.at[place], sems.at[at // STEP_ROWS]
-            )
-            copy.start()
-            copies.append(copy)
+        if j == 0:
+            first = grad_pre[0:8, :]
+    before = jnp.where(me > 0, halo[...].astype(F32), 0.0)
     for k in range(4):
         tap = jnp.sum(partial[k], axis=0, keepdims=True)
         for j in range(k, 3):
-            tap = tap + window[j - k : j - k + 1, :] * inputs[13 + j : 14 + j, :]
+            tap = tap + first[j - k : j - k + 1, :] * before[13 + j : 14 + j, :]
         tail_out[k : k + 1, :] = tap
-    tail_out[4:7, :] = window[0:3, :]
+    tail_out[4:7, :] = first[0:3, :]
     tail_out[7:8, :] = jnp.zeros((1, channels), F32)
-    for copy in copies:
-        copy.wait()
-
-
-def output_kernel(heads, parts, front, base, c_proj, *rest):
+
+
+def output_kernel(heads, parts, front, base, c_proj, grad_rows, *rest):
     pays = rest[: parts - 1]
-    out_hbm, result_rows, sems = rest[parts - 1 :]
+    out_hbm, grad_hbm, result_rows, sems, grad_sem = rest[parts - 1 :]
     rows, channels = base.shape
-    chunks = rows // CHUNK
+    grad_copy = pltpu.make_async_copy(grad_rows, grad_hbm, grad_sem)
+    grad_copy.start()
     state = merged(parts, pays, True)
     onehot = spread_matrix(heads, channels)
     copies = []
-    for j in range(chunks):
-        both = slice(j * CHUNK, (j + 1) * CHUNK)
-        carried = dot(c_proj[both, :], state, ((1,), (0,)))
-        result = base[both, :] + spread(front[:, both], onehot) * carried
-        result_rows[both, :] = result.astype(BF16)
-        if (j + 1) * CHUNK % STEP_ROWS == 0:
-            at = (j + 1) * CHUNK - STEP_ROWS
-            place = pl.ds(at, STEP_ROWS)
-            copy = pltpu.make_async_copy(
-                result_rows.at[place], out_hbm.at[place], sems.at[at // STEP_ROWS]
-            )
-            copy.start()
-            copies.append(copy)
+    for piece in range(rows // STEP_ROWS):
+        for at in range(piece * STEP_ROWS, (piece + 1) * STEP_ROWS, CHUNK):
+            both = slice(at, at + CHUNK)
+            carried = dot(c_proj[both, :], state, ((1,), (0,)))
+            result = base[both, :] + spread(front[:, both], onehot) * carried
+            result_rows[both, :] = result.astype(BF16)
+        place = pl.ds(piece * STEP_ROWS, STEP_ROWS)
+        copy = pltpu.make_async_copy(result_rows.at[place], out_hbm.at[place], sems.at[piece])
+        copy.start()
+        copies.append(copy)
     for copy in copies:
         copy.wait()
+    grad_copy.wait()
 
 
 def finish_kernel(parts, scale, taps, tail, edge, *rest):
@@ -395,23 +399,20 @@
     def stay(array):
         return pltpu.with_memory_space_constraint(array, pltpu.HBM)
 
-    halo_from = [(i, i + 1) for i in range(parts - 1)]
-    halo = lax.ppermute(inputs[rows - 16 :], "seq", halo_from)
+    halo = rotated(inputs[rows - 16 :], "seq", 1)
     pay = shape((STATE + 16, channels), BF16)
     narrow = shape((rows, channels), BF16)
     broad = shape((rows, channels), F32)
 
-    near, far, front, logs, grad_scaled, grad_low, adjoint_pay = call(
+    near, far, front, logs, adjoint_pay = call(
         functools.partial(adjoint_kernel, heads),
         [hbm] * 5,
-        [vmem] * 7,
+        [vmem] * 5,
         [
             shape((32, rows), BF16),
             shape((16, rows), BF16),
             shape((16, rows), BF16),
             shape((3, chunks, channels), F32),
-            narrow,
-            narrow,
             pay,
         ],
         [
@@ -421,7 +422,6 @@
             pltpu.VMEM((rows, channels), BF16),
             pltpu.VMEM((rows, 128), BF16),
             pltpu.VMEM((8, rows), F32),
-            pltpu.VMEM((rows, channels), F32),
             dma((3,)),
             dma((pieces,)),
             dma((pieces,)),
@@ -437,45 +437,45 @@
 
     outs = call(
         functools.partial(state_kernel, heads, parts),
-        [vmem] * 7,
-        [vmem] * (4 + parts),
-        [shape((rows + 16, channels), F32), broad, broad, narrow, narrow] + [pay] * (parts - 1),
-        [pltpu.VMEM((rows, channels), F32)],
+        [vmem] * 6,
+        [vmem] * (1 + parts),
+        [broad, broad] + [pay] * (parts - 1),
+        [],
         2,
-    )(conv_weight, near, logs, inputs, halo, b_proj, adjoint_pay)
-    wide_inputs, mixed, sigma, mixed_scaled, mixed_low = outs[:5]
-    pays = [rotated(send, "seq", distance + 1) for distance, send in enumerate(outs[5:])]
-
+    )(conv_weight, far, inputs, halo, b_proj, adjoint_pay)
+    mixed, sigma = outs[:2]
+    pays = [rotated(send, "seq", distance + 1) for distance, send in enumerate(outs[2:])]
+
+    tile = pltpu.VMEM((rows, CHUNK), BF16)
+    low = pltpu.VMEM((rows, channels), BF16)
+    high = pltpu.VMEM((rows, channels), F32)
     base, grad_base, grad_weight = call(
         functools.partial(inner_kernel, heads),
-        [smem] + [vmem] * 11,
+        [smem] + [vmem] * 8,
         [vmem] * 3,
         [broad] * 3,
-        [pltpu.VMEM((rows, CHUNK), BF16), pltpu.VMEM((rows, CHUNK), BF16)],
-        6,
-    )(
-        skip_gain, near, far, out_cotangent, mixed, sigma, b_proj, c_proj,
-        mixed_scaled, mixed_low, grad_scaled, grad_low,
-    )
+        [tile, tile, low, low, low, low, high, high],
+        10,
+    )(skip_gain, near, far, logs, out_cotangent, mixed, sigma, b_proj, c_proj)
 
     grad_rows, tail, edge = call(
         functools.partial(gradient_kernel, parts),
-        [vmem] * (4 + parts),
-        [hbm, vmem, vmem],
+        [vmem] * (5 + parts),
+        [vmem] * 3,
         [narrow, shape((8, channels), F32), shape((16, channels), F32)],
-        [pltpu.VMEM((rows + 8, channels), F32), pltpu.VMEM((rows, channels), BF16), dma((pieces,))],
+        [pltpu.VMEM((rows + 16, channels), BF16)],
         2,
-    )(conv_weight, grad_base, grad_weight, wide_inputs, b_proj, *pays)
+    )(conv_weight, grad_base, grad_weight, inputs, halo, b_proj, *pays)
     tails = [rotated(tail, "seq", distance) for distance in range(1, parts)]
 
-    layer_out = call(
+    layer_out, grad_rows = call(
         functools.partial(output_kernel, heads, parts),
-        [vmem] * (2 + parts),
-        hbm,
-        narrow,
-        [pltpu.VMEM((rows, channels), BF16), dma((pieces,))],
+        [vmem] * (3 + parts),
+        [hbm, hbm],
+        [narrow, narrow],
+        [pltpu.VMEM((rows, channels), BF16), dma((pieces,)), dma],
         2,
-    )(front, base, c_proj, *pays)
+    )(front, base, c_proj, grad_rows, *pays)
 
     scale = float((rows * parts) ** -0.5)
     input_grad, conv_grad = call(

time: 46.7 us -> 38.3 us (0.82)
  Pallas kernels: 24.8 us -> 20.6 us
  starting transfers between devices: 15 us -> 12.3 us
  waiting for transfers between devices: 4.82 us -> 3.45 us
    ppermute x1 -> x0, starting transfers between devices: 4.92 us -> none  [shards(): halo = lax.ppermute(inputs[rows - 16:], 'seq', halo_from)]
    pallas_call x5, Pallas kernels: 23.6 us -> 19.3 us  [the longest x1 6.46 us: shards(): call(functools.partial(inner_kernel, heads), [smem] + [vmem] * 8, [vmem]...]
    ppermute x6 -> x7, starting transfers between devices: 10.1 us -> 12.3 us  [rotated(): lax.ppermute(block, axis, [(i, (i + distance) % size) for i in range(size)])]
    ppermute x6 -> x7, waiting for transfers between devices: 4.82 us -> 3.45 us  [rotated(): lax.ppermute(block, axis, [(i, (i + distance) % size) for i in range(size)])]
  transfers between devices with their start and end apart: 7 -> 7, of which waited for: 3 -> 3; matrix products, arithmetic and copies ran while one was open for 0% -> 0% of each run, Pallas kernels for 26% -> 31%
where the time goes in v3:
time: 38.3 us; the launch traced here: 38.1 us
  Pallas kernels  20.6 us (54%)
  starting transfers between devices  12.3 us (32%)
  waiting for transfers between devices  3.45 us (9%)
  between operations  0.92 us (2%)
  local copies, waits for them, and re-layouts  0.89 us (2%)
    ppermute x7, starting transfers between devices, rotated(): lax.ppermute(block, axis, [(i, (i + distance) % size) for i in range(size)])  12.3 us
    pallas_call x1, Pallas kernels, shards(): call(functools.partial(inner_kernel, heads), [smem] + [vmem] * 8, [vmem]...  6.46 us
    pallas_call x1, Pallas kernels, shards(): call(functools.partial(gradient_kernel, parts), [vmem] * (5 + parts), [vm...  4.57 us
    pallas_call x1, Pallas kernels, shards(): call(functools.partial(adjoint_kernel, heads), [hbm] * 5, [vmem] * 5, [sh...  3.54 us
    ppermute x7, waiting for transfers between devices, rotated(): lax.ppermute(block, axis, [(i, (i + distance) % size) for i in range(size)])  3.45 us
    pallas_call x1, Pallas kernels, shards(): call(functools.partial(state_kernel, heads, parts), [vmem] * 6, [vmem] *...  2.93 us
    pallas_call x1, Pallas kernels, shards(): call(functools.partial(output_kernel, heads, parts), [vmem] * (3 + parts)...  1.84 us
    pallas_call x1, Pallas kernels, shards(): call(functools.partial(finish_kernel, parts, scale), [vmem] * (2 + parts)...  1.22 us
  transfers between devices with their start and end apart: 7, of which 3 were waited for; matrix products, arithmetic and copies ran while one was open for 0% of the time, Pallas kernels for 31%

profile of v3, /device:TPU:0, one launch (start us, length us, event | category | flops | bytes accessed | tf_op | source)
XLA Modules:
  0.0 38.1 jit_solution(10678951647528673030)
XLA Ops:
  0.6 0.0 copy-start
  0.6 0.0 copy-start.4
  0.7 0.0 copy-start.3
  0.7 0.9 %slice.3 = bf16[16,384]{1,0:T(8,128)(2,1)S(1)} slice(bf16[2048,384]{1,0:T(8,128)(2,1)} %inputs.3), slice={[2032:2048], [0:384]} | slice | bytes 24576 | tf_op jit(solution)/shard_map/slice | solution.py:402
  1.5 3.0 %collective-permute-start = (bf16[16,384]{1,0:T(8,128)(2,1)S(1)}, bf16[16,384]{1,0:T(8,128)(2,1)S(1)}, u32[]{:S(2)}, u32[]{:S(2)}) collective-permute-start(bf16[16,384]{1,0:T(8,128)(2,1)S(1)} %slice.3), channel_id=1, source_target_pairs={{0,4},{4,8},{8,12},{12,0},{1,5},{5,9},{9,13},{13,1},{2,6},{6,10},{... | collective-permute-start | bytes 36872 | tf_op jit(solution)/shard_map/ppermute | solution.py:359
  4.5 3.5 %shard_map.112 = (bf16[32,2048]{1,0:T(8,128)(2,1)S(1)}, bf16[16,2048]{1,0:T(8,128)(2,1)S(1)}, bf16[16,2048]{1,0:T(8,128)(2,1)S(1)}, f32[3,16,384]{2,1,0:T(8,128)S(1)}, bf16[144,384]{1,0:T(8,128)(2,1)S(1)}) custom-call(f32[6]{0:T(128)} %rates_hbm.1, s32[6,2048]{1,0:T(8,128)} %codes_hbm.1, s32[1,2048]{1,0:T(1,128)} %bitcast.1, bf16[2048,384]{1,0:T(8,128)(2,1)} %grad.1, ...), custom_call_target="tpu_custom_call" | custom-call | flops 402653184 | bytes 4718592 | tf_op jit(solution)/shard_map/pallas_call | solution.py:407
  8.1 0.0 copy-start.1
  8.1 0.0 copy-start.2
  8.1 0.0 copy-start.5
  8.1 0.1 collective-permute-done.halo
  8.2 0.0 copy-done
  8.2 0.0 copy-done.4
  8.2 0.0 copy-done.3
  8.2 2.9 %shard_map.113 = (f32[2048,384]{1,0:T(8,128)S(1)}, f32[2048,384]{1,0:T(8,128)S(1)}, bf16[144,384]{1,0:T(8,128)(2,1)S(1)}, bf16[144,384]{1,0:T(8,128)(2,1)S(1)}, bf16[144,384]{1,0:T(8,128)(2,1)S(1)}) custom-call(f32[4,384]{1,0:T(4,128)S(1)} %copy-done.4, bf16[16,2048]{1,0:T(8,128)(2,1)S(1)} %get-tuple-element.25.far, bf16[2048,384]{1,0:T(8,128)(2,1)S(1)} %copy-done, ...), custom_call_target="tpu_custom_call" | custom-call | flops 402653184 | bytes 4718592 | tf_op jit(solution)/shard_map/pallas_call | solution.py:438
  11.2 1.5 %collective-permute-start.1 = (bf16[144,384]{1,0:T(8,128)(2,1)S(1)}, bf16[144,384]{1,0:T(8,128)(2,1)S(1)}, u32[]{:S(2)}, u32[]{:S(2)}) collective-permute-start(bf16[144,384]{1,0:T(8,128)(2,1)S(1)} %get-tuple-element.33), channel_id=1, source_target_pairs={{0,4},{4,8},{8,12},{12,0},{1,5},{5,9},{9,13},{13,1},{2,6},{6,10},{... | collective-permute-start | bytes 331784 | tf_op jit(solution)/shard_map/ppermute | solution.py:359
  12.7 1.1 %collective-permute-start.2 = (bf16[144,384]{1,0:T(8,128)(2,1)S(1)}, bf16[144,384]{1,0:T(8,128)(2,1)S(1)}, u32[]{:S(2)}, u32[]{:S(2)}) collective-permute-start(bf16[144,384]{1,0:T(8,128)(2,1)S(1)} %get-tuple-element.34), channel_id=1, source_target_pairs={{0,8},{4,12},{8,0},{12,4},{1,9},{5,13},{9,1},{13,5},{2,10},{6,14},... | collective-permute-start | bytes 331784 | tf_op jit(solution)/shard_map/ppermute | solution.py:359
  13.8 2.8 %collective-permute-start.3 = (bf16[144,384]{1,0:T(8,128)(2,1)S(1)}, bf16[144,384]{1,0:T(8,128)(2,1)S(1)}, u32[]{:S(2)}, u32[]{:S(2)}) collective-permute-start(bf16[144,384]{1,0:T(8,128)(2,1)S(1)} %get-tuple-element.35), channel_id=1, source_target_pairs={{0,12},{4,0},{8,4},{12,8},{1,13},{5,1},{9,5},{13,9},{2,14},{6,2},{... | collective-permute-start | bytes 331784 | tf_op jit(solution)/shard_map/ppermute | solution.py:359
  16.7 0.0 copy-done.1
  16.7 0.0 copy-done.2
  16.7 6.5 %shard_map.114 = (f32[2048,384]{1,0:T(8,128)S(1)}, f32[2048,384]{1,0:T(8,128)S(1)}, f32[2048,384]{1,0:T(8,128)S(1)}) custom-call(f32[6]{0:T(128)S(1)} %copy-done.5, bf16[32,2048]{1,0:T(8,128)(2,1)S(1)} %get-tuple-element.24.near, bf16[16,2048]{1,0:T(8,128)(2,1)S(1)} %get-tuple-element.25.far, f32[3,16,384]{2,1,0:T(8,128)S(1)} %get-tuple-element.26.logs, ...), custom_call_target="tpu_custom_call" | custom-call | flops 2013265920 | bytes 4718592 | tf_op jit(solution)/shard_map/pallas_call | solution.py:452
  23.2 0.0 collective-permute-done.1.rest_0_
  23.2 0.0 collective-permute-done.2.rest_1_
  23.2 0.0 collective-permute-done.3.rest_2_
  23.2 4.6 %shard_map.115 = (bf16[2048,384]{1,0:T(8,128)(2,1)S(1)}, f32[8,384]{1,0:T(8,128)S(1)}, f32[16,384]{1,0:T(8,128)S(1)}) custom-call(f32[4,384]{1,0:T(4,128)S(1)} %copy-done.4, f32[2048,384]{1,0:T(8,128)S(1)} %get-tuple-element.31.base, f32[2048,384]{1,0:T(8,128)S(1)} %get-tuple-element.32.weight, bf16[2048,384]{1,0:T(8,128)(2,1)S(1)} %copy-done, ...), custom_call_target="tpu_custom_call" | custom-call | flops 402653184 | bytes 4718592 | tf_op jit(solution)/shard_map/pallas_call | solution.py:461
  27.8 3.1 %collective-permute-start.6 = (f32[8,384]{1,0:T(8,128)S(1)}, f32[8,384]{1,0:T(8,128)S(1)}, u32[]{:S(2)}, u32[]{:S(2)}) collective-permute-start(f32[8,384]{1,0:T(8,128)S(1)} %get-tuple-element.38.tail), channel_id=1, source_target_pairs={{0,12},{4,0},{8,4},{12,8},{1,13},{5,1},{9,5},{13,9},{2,14},{6,2},{... | collective-permute-start | bytes 36872 | tf_op jit(solution)/shard_map/ppermute | solution.py:359
  30.9 0.3 collective-permute-start.5
  31.2 0.3 collective-permute-start.4
  31.6 1.8 %shard_map.116 = (bf16[2048,384]{1,0:T(8,128)(2,1)}, bf16[2048,384]{1,0:T(8,128)(2,1)}) custom-call(bf16[16,2048]{1,0:T(8,128)(2,1)S(1)} %get-tuple-element.23.front, f32[2048,384]{1,0:T(8,128)S(1)} %get-tuple-element.30.base, bf16[2048,128]{1,0:T(8,128)(2,1)S(1)} %copy-done.2, bf16[2048,384]{1,0:T(8,128)(2,1)S(1)} %get-tuple-element.36.grad_rows, ...), custom_call_target="tpu_custom_call" | custom-call | flops 402653184 | bytes 4718592 | tf_op jit(solution)/shard_map/pallas_call | solution.py:471
  33.4 0.0 collective-permute-done.6.rest_2_
  33.4 2.1 %collective-permute-done.5.rest_1_ = f32[8,384]{1,0:T(8,128)S(1)} collective-permute-done((f32[8,384]{1,0:T(8,128)S(1)}, f32[8,384]{1,0:T(8,128)S(1)}, u32[]{:S(2)}, u32[]{:S(2)}) %collective-permute-start.5) | collective-permute-done | bytes 12320 | tf_op jit(solution)/shard_map/ppermute | solution.py:359
  35.5 1.2 %collective-permute-done.4.rest_0_ = f32[8,384]{1,0:T(8,128)S(1)} collective-permute-done((f32[8,384]{1,0:T(8,128)S(1)}, f32[8,384]{1,0:T(8,128)S(1)}, u32[]{:S(2)}, u32[]{:S(2)}) %collective-permute-start.4) | collective-permute-done | bytes 12320 | tf_op jit(solution)/shard_map/ppermute | solution.py:359
  36.7 1.2 %shard_map.117 = (bf16[2048,384]{1,0:T(8,128)(2,1)}, f32[4,384]{1,0:T(4,128)}) custom-call(f32[4,384]{1,0:T(4,128)S(1)} %copy-done.4, f32[8,384]{1,0:T(8,128)S(1)} %get-tuple-element.38.tail, f32[16,384]{1,0:T(8,128)S(1)} %get-tuple-element.39.edge, f32[8,384]{1,0:T(8,128)S(1)} %collective-permute-done.4.rest_0_, ...), custom_call_target="tpu_custom_call", output_to_operand_aliasing={{0}: (6, {})} | custom-call | bytes 4718592 | tf_op jit(solution)/shard_map/pallas_call | solution.py:481
  (1 shorter events, 0.0 us)
Async XLA Ops:
  0.6 7.6 %copy-start = (bf16[2048,384]{1,0:T(8,128)(2,1)S(1)}, bf16[2048,384]{1,0:T(8,128)(2,1)}, u32[]{:S(2)}) copy-start(bf16[2048,384]{1,0:T(8,128)(2,1)} %inputs.3) | copy-start | bytes 4718596
  0.6 7.6 %copy-start.4 = (f32[4,384]{1,0:T(4,128)S(1)}, f32[4,384]{1,0:T(4,128)}, u32[]{:S(2)}) copy-start(f32[4,384]{1,0:T(4,128)} %taps.5) | copy-start | bytes 18436
  0.7 7.6 %copy-start.3 = (bf16[2048,128]{1,0:T(8,128)(2,1)S(1)}, bf16[2048,128]{1,0:T(8,128)(2,1)}, u32[]{:S(2)}) copy-start(bf16[2048,128]{1,0:T(8,128)(2,1)} %b_proj.5) | copy-start | bytes 1572868
  1.5 6.7 %collective-permute-start = (bf16[16,384]{1,0:T(8,128)(2,1)S(1)}, bf16[16,384]{1,0:T(8,128)(2,1)S(1)}, u32[]{:S(2)}, u32[]{:S(2)}) collective-permute-start(bf16[16,384]{1,0:T(8,128)(2,1)S(1)} %slice.3), channel_id=1, source_target_pairs={{0,4},{4,8},{8,12},{12,0},{1,5},{5,9},{9,13},{13,1},{2,6},{6,10},{... | collective-permute-start | bytes 36872 | tf_op jit(solution)/shard_map/ppermute | solution.py:359
  8.1 8.6 %copy-start.1 = (bf16[2048,384]{1,0:T(8,128)(2,1)S(1)}, bf16[2048,384]{1,0:T(8,128)(2,1)}, u32[]{:S(2)}) copy-start(bf16[2048,384]{1,0:T(8,128)(2,1)} %grad.1) | copy-start | bytes 4718596
  8.1 8.6 %copy-start.2 = (bf16[2048,128]{1,0:T(8,128)(2,1)S(1)}, bf16[2048,128]{1,0:T(8,128)(2,1)}, u32[]{:S(2)}) copy-start(bf16[2048,128]{1,0:T(8,128)(2,1)} %c_proj.3) | copy-start | bytes 1572868
  8.1 8.6 %copy-start.5 = (f32[6]{0:T(128)S(1)}, f32[6]{0:T(128)}, u32[]{:S(2)}) copy-start(f32[6]{0:T(128)} %gains.1) | copy-start | bytes 76
  11.2 12.0 %collective-permute-start.1 = (bf16[144,384]{1,0:T(8,128)(2,1)S(1)}, bf16[144,384]{1,0:T(8,128)(2,1)S(1)}, u32[]{:S(2)}, u32[]{:S(2)}) collective-permute-start(bf16[144,384]{1,0:T(8,128)(2,1)S(1)} %get-tuple-element.33), channel_id=1, source_target_pairs={{0,4},{4,8},{8,12},{12,0},{1,5},{5,9},{9,13},{13,1},{2,6},{6,10},{... | collective-permute-start | bytes 331784 | tf_op jit(solution)/shard_map/ppermute | solution.py:359
  12.7 10.4 %collective-permute-start.2 = (bf16[144,384]{1,0:T(8,128)(2,1)S(1)}, bf16[144,384]{1,0:T(8,128)(2,1)S(1)}, u32[]{:S(2)}, u32[]{:S(2)}) collective-permute-start(bf16[144,384]{1,0:T(8,128)(2,1)S(1)} %get-tuple-element.34), channel_id=1, source_target_pairs={{0,8},{4,12},{8,0},{12,4},{1,9},{5,13},{9,1},{13,5},{2,10},{6,14},... | collective-permute-start | bytes 331784 | tf_op jit(solution)/shard_map/ppermute | solution.py:359
  13.8 9.3 %collective-permute-start.3 = (bf16[144,384]{1,0:T(8,128)(2,1)S(1)}, bf16[144,384]{1,0:T(8,128)(2,1)S(1)}, u32[]{:S(2)}, u32[]{:S(2)}) collective-permute-start(bf16[144,384]{1,0:T(8,128)(2,1)S(1)} %get-tuple-element.35), channel_id=1, source_target_pairs={{0,12},{4,0},{8,4},{12,8},{1,13},{5,1},{9,5},{13,9},{2,14},{6,2},{... | collective-permute-start | bytes 331784 | tf_op jit(solution)/shard_map/ppermute | solution.py:359
  27.8 5.6 %collective-permute-start.6 = (f32[8,384]{1,0:T(8,128)S(1)}, f32[8,384]{1,0:T(8,128)S(1)}, u32[]{:S(2)}, u32[]{:S(2)}) collective-permute-start(f32[8,384]{1,0:T(8,128)S(1)} %get-tuple-element.38.tail), channel_id=1, source_target_pairs={{0,12},{4,0},{8,4},{12,8},{1,13},{5,1},{9,5},{13,9},{2,14},{6,2},{... | collective-permute-start | bytes 36872 | tf_op jit(solution)/shard_map/ppermute | solution.py:359
  30.9 4.6 %collective-permute-start.5 = (f32[8,384]{1,0:T(8,128)S(1)}, f32[8,384]{1,0:T(8,128)S(1)}, u32[]{:S(2)}, u32[]{:S(2)}) collective-permute-start(f32[8,384]{1,0:T(8,128)S(1)} %get-tuple-element.38.tail), channel_id=1, source_target_pairs={{0,8},{4,12},{8,0},{12,4},{1,9},{5,13},{9,1},{13,5},{2,10},{6,14},... | collective-permute-start | bytes 36872 | tf_op jit(solution)/shard_map/ppermute | solution.py:359
  31.2 5.5 %collective-permute-start.4 = (f32[8,384]{1,0:T(8,128)S(1)}, f32[8,384]{1,0:T(8,128)S(1)}, u32[]{:S(2)}, u32[]{:S(2)}) collective-permute-start(f32[8,384]{1,0:T(8,128)S(1)} %get-tuple-element.38.tail), channel_id=1, source_target_pairs={{0,4},{4,8},{8,12},{12,0},{1,5},{5,9},{9,13},{13,1},{2,6},{6,10},{... | collective-permute-start | bytes 36872 | tf_op jit(solution)/shard_map/ppermute | solution.py:359

commit v4 on v3

--- a/solution.py
+++ b/solution.py
@@ -139,15 +139,13 @@
     pay_out[STATE : STATE + 16, :] = tail.astype(BF16)
 
     onehot = spread_matrix(heads, channels)
-    total = jnp.zeros((STATE, channels), F32)
+    for copy in large:
+        copy.wait()
     for piece in range(pieces):
         both = slice(piece * STEP_ROWS, (piece + 1) * STEP_ROWS)
         scale = spread(front_out[:, both], onehot)
-        large[2 * piece].wait()
-        large[2 * piece + 1].wait()
-        scaled = (grad[both, :].astype(F32) * scale).astype(BF16)
-        total = total + dot(c_proj[both, :], scaled, ((0,), (0,)))
-    pay_out[0:STATE, :] = total.astype(BF16)
+        grad[both, :] = (grad[both, :].astype(F32) * scale).astype(BF16)
+    pay_out[0:STATE, :] = dot(c_proj[...], grad[...], ((0,), (0,))).astype(BF16)
 
 
 def lane_tiles(channels):
@@ -155,37 +153,32 @@
 
 
 def state_kernel(
-    heads, parts, taps, far, inputs, halo, b_proj, adjoint_pay, mixed_out, sigma_out, *pays
+    heads, parts, taps, far, inputs, halo, b_proj, adjoint_pay, mixed_out, sigma_out, *rest
 ):
+    pays, scaled = rest[: parts - 1], rest[parts - 1]
     rows, channels = inputs.shape
-    pieces = rows // STEP_ROWS
     me = lax.axis_index("seq")
     before = jnp.where(me > 0, halo[...].astype(F32), 0.0).astype(BF16)
     onehot = spread_matrix(heads, channels)
     row = lax.broadcasted_iota(jnp.int32, (3 * CHUNK, CHUNK + 16), 0)
     col = lax.broadcasted_iota(jnp.int32, (3 * CHUNK, CHUNK + 16), 1)
     shift = jnp.where(col == row % CHUNK + 13 + row // CHUNK, 1.0, 0.0).astype(BF16)
-    total = jnp.zeros((STATE, channels), F32)
-    for piece in range(pieces):
-        scaled = []
-        for at in range(piece * STEP_ROWS, (piece + 1) * STEP_ROWS, CHUNK):
-            both = slice(at, at + CHUNK)
-            if at == 0:
-                block = jnp.concatenate([before, inputs[both, :]], axis=0)
-            else:
-                block = inputs[at - 16 : at + CHUNK, :]
-            moved = dot(shift, block, ((1,), (0,)))
-            preact = taps[3:4, :] * inputs[both, :].astype(F32)
-            for k in range(3):
-                preact = preact + taps[k : k + 1, :] * moved[k * CHUNK : (k + 1) * CHUNK, :]
-            sigma = 0.5 * jnp.tanh(0.5 * preact) + 0.5
-            mixed = preact * sigma
-            sigma_out[both, :] = sigma
-            mixed_out[both, :] = mixed
-            scaled.append((mixed * spread(far[:, both], onehot)).astype(BF16))
-        both = slice(piece * STEP_ROWS, (piece + 1) * STEP_ROWS)
-        total = total + dot(b_proj[both, :], jnp.concatenate(scaled, axis=0), ((0,), (0,)))
-    state = total.astype(BF16)
+    for at in range(0, rows, CHUNK):
+        both = slice(at, at + CHUNK)
+        if at == 0:
+            block = jnp.concatenate([before, inputs[both, :]], axis=0)
+        else:
+            block = inputs[at - 16 : at + CHUNK, :]
+        moved = dot(shift, block, ((1,), (0,)))
+        preact = taps[3:4, :] * inputs[both, :].astype(F32)
+        for k in range(3):
+            preact = preact + taps[k : k + 1, :] * moved[k * CHUNK : (k + 1) * CHUNK, :]
+        sigma = 0.5 * jnp.tanh(0.5 * preact) + 0.5
+        mixed = preact * sigma
+        sigma_out[both, :] = sigma
+        mixed_out[both, :] = mixed
+        scaled[both, :] = (mixed * spread(far[:, both], onehot)).astype(BF16)
+    state = dot(b_proj[...], scaled[...], ((0,), (0,))).astype(BF16)
     for distance in range(1, parts):
         pay = pays[distance - 1]
         pay[0:STATE, :] = jnp.where(me + distance < parts, state, adjoint_pay[0:STATE, :])
@@ -268,7 +261,7 @@
 
 def gradient_kernel(parts, taps, base, weight, inputs, halo, b_proj, *rest):
     pays = rest[: parts - 1]
-    grad_out, tail_out, edge_out, window = rest[parts - 1 :]
+    grad_out, tail_out, edge_out, window, exact = rest[parts - 1 :]
     rows, channels = base.shape
     chunks = rows // CHUNK
     adjoint = merged(parts, pays, False)
@@ -278,11 +271,15 @@
     col = lax.broadcasted_iota(jnp.int32, (3 * CHUNK, CHUNK + 16), 1)
     shift = jnp.where(col == row % CHUNK + 3 - row // CHUNK, 1.0, 0.0).astype(BF16)
     partial = [jnp.zeros((8, channels), F32) for _ in range(4)]
-    for j in range(chunks - 1, -1, -1):
+    for j in range(chunks):
+        both = slice(j * CHUNK, (j + 1) * CHUNK)
+        grad_pre = base[both, :] + weight[both, :] * dot(b_proj[both, :], adjoint, ((1,), (0,)))
+        window[both, :] = grad_pre.astype(BF16)
+        exact[both, :] = grad_pre
+    for j in range(chunks):
         at = j * CHUNK
         both = slice(at, at + CHUNK)
-        grad_pre = base[both, :] + weight[both, :] * dot(b_proj[both, :], adjoint, ((1,), (0,)))
-        window[both, :] = grad_pre.astype(BF16)
+        grad_pre = exact[both, :]
         moved = dot(shift, window[at : at + CHUNK + 16, :], ((1,), (0,)))
         x = inputs[both, :].astype(F32)
         result = taps[3:4, :] * grad_pre
@@ -294,8 +291,7 @@
         grad_out[both, :] = result.astype(BF16)
         if j == chunks - 1:
             edge_out[...] = result[CHUNK - 16 :, :]
-        if j == 0:
-            first = grad_pre[0:8, :]
+    first = exact[0:8, :]
     before = jnp.where(me > 0, halo[...].astype(F32), 0.0)
     for k in range(4):
         tap = jnp.sum(partial[k], axis=0, keepdims=True)
@@ -440,7 +436,7 @@
         [vmem] * 6,
         [vmem] * (1 + parts),
         [broad, broad] + [pay] * (parts - 1),
-        [],
+        [pltpu.VMEM((rows, channels), BF16)],
         2,
     )(conv_weight, far, inputs, halo, b_proj, adjoint_pay)
     mixed, sigma = outs[:2]
@@ -463,7 +459,7 @@
         [vmem] * (5 + parts),
         [vmem] * 3,
         [narrow, shape((8, channels), F32), shape((16, channels), F32)],
-        [pltpu.VMEM((rows + 16, channels), BF16)],
+        [pltpu.VMEM((rows + 16, channels), BF16), pltpu.VMEM((rows, channels), F32)],
         2,
     )(conv_weight, grad_base, grad_weight, inputs, halo, b_proj, *pays)
     tails = [rotated(tail, "seq", distance) for distance in range(1, parts)]

time: 38.3 us -> 35.9 us (0.937)
  Pallas kernels: 20.6 us -> 17.8 us
  waiting for transfers between devices: 3.45 us -> 4.61 us
  starting transfers between devices: 12.3 us -> 11.5 us
    pallas_call x1, Pallas kernels: 4.57 us -> 3 us  [shards(): call(functools.partial(gradient_kernel, parts), [vmem] * (5 + parts), [vm...]
    ppermute x7, waiting for transfers between devices: 3.45 us -> 4.61 us  [rotated(): lax.ppermute(block, axis, [(i, (i + distance) % size) for i in range(size)])]
    pallas_call x1, Pallas kernels: 3.54 us -> 2.68 us  [shards(): call(functools.partial(adjoint_kernel, heads), [hbm] * 5, [vmem] * 5, [sh...]
    ppermute x7, starting transfers between devices: 12.3 us -> 11.5 us  [rotated(): lax.ppermute(block, axis, [(i, (i + distance) % size) for i in range(size)])]
where the time goes in v4:
time: 35.9 us; the launch traced here: 35.7 us
  Pallas kernels  17.8 us (50%)
  starting transfers between devices  11.5 us (32%)
  waiting for transfers between devices  4.61 us (13%)
  between operations  0.92 us (3%)
  local copies, waits for them, and re-layouts  0.89 us (2%)
    ppermute x7, starting transfers between devices, rotated(): lax.ppermute(block, axis, [(i, (i + distance) % size) for i in range(size)])  11.5 us
    pallas_call x1, Pallas kernels, shards(): call(functools.partial(inner_kernel, heads), [smem] + [vmem] * 8, [vmem]...  6.46 us
    ppermute x7, waiting for transfers between devices, rotated(): lax.ppermute(block, axis, [(i, (i + distance) % size) for i in range(size)])  4.61 us
    pallas_call x1, Pallas kernels, shards(): call(functools.partial(gradient_kernel, parts), [vmem] * (5 + parts), [vm...  3 us
    pallas_call x1, Pallas kernels, shards(): call(functools.partial(adjoint_kernel, heads), [hbm] * 5, [vmem] * 5, [sh...  2.68 us
    pallas_call x1, Pallas kernels, shards(): call(functools.partial(state_kernel, heads, parts), [vmem] * 6, [vmem] *...  2.59 us
    pallas_call x1, Pallas kernels, shards(): call(functools.partial(output_kernel, heads, parts), [vmem] * (3 + parts)...  1.84 us
    pallas_call x1, Pallas kernels, shards(): call(functools.partial(finish_kernel, parts, scale), [vmem] * (2 + parts)...  1.22 us
  transfers between devices with their start and end apart: 7, of which 3 were waited for; matrix products, arithmetic and copies ran while one was open for 0% of the time, Pallas kernels for 31%

profile of v4, /device:TPU:0, one launch (start us, length us, event | category | flops | bytes accessed | tf_op | source)
XLA Modules:
  0.0 35.7 jit_solution(12115730755976554968)
XLA Ops:
  0.6 0.0 copy-start
  0.6 0.0 copy-start.4
  0.7 0.0 copy-start.3
  0.7 0.9 %slice.3 = bf16[16,384]{1,0:T(8,128)(2,1)S(1)} slice(bf16[2048,384]{1,0:T(8,128)(2,1)} %inputs.3), slice={[2032:2048], [0:384]} | slice | bytes 24576 | tf_op jit(solution)/shard_map/slice | solution.py:398
  1.5 3.0 %collective-permute-start = (bf16[16,384]{1,0:T(8,128)(2,1)S(1)}, bf16[16,384]{1,0:T(8,128)(2,1)S(1)}, u32[]{:S(2)}, u32[]{:S(2)}) collective-permute-start(bf16[16,384]{1,0:T(8,128)(2,1)S(1)} %slice.3), channel_id=1, source_target_pairs={{0,4},{4,8},{8,12},{12,0},{1,5},{5,9},{9,13},{13,1},{2,6},{6,10},{... | collective-permute-start | bytes 36872 | tf_op jit(solution)/shard_map/ppermute | solution.py:355
  4.5 2.7 %shard_map.112 = (bf16[32,2048]{1,0:T(8,128)(2,1)S(1)}, bf16[16,2048]{1,0:T(8,128)(2,1)S(1)}, bf16[16,2048]{1,0:T(8,128)(2,1)S(1)}, f32[3,16,384]{2,1,0:T(8,128)S(1)}, bf16[144,384]{1,0:T(8,128)(2,1)S(1)}) custom-call(f32[6]{0:T(128)} %rates_hbm.1, s32[6,2048]{1,0:T(8,128)} %codes_hbm.1, s32[1,2048]{1,0:T(1,128)} %bitcast.1, bf16[2048,384]{1,0:T(8,128)(2,1)} %grad.1, ...), custom_call_target="tpu_custom_call" | custom-call | flops 402653184 | bytes 4718592 | tf_op jit(solution)/shard_map/pallas_call | solution.py:403
  7.2 0.0 copy-start.1
  7.2 0.0 copy-start.2
  7.3 0.0 copy-start.5
  7.3 1.0 %collective-permute-done.halo = bf16[16,384]{1,0:T(8,128)(2,1)S(1)} collective-permute-done((bf16[16,384]{1,0:T(8,128)(2,1)S(1)}, bf16[16,384]{1,0:T(8,128)(2,1)S(1)}, u32[]{:S(2)}, u32[]{:S(2)}) %collective-permute-start) | collective-permute-done | bytes 12320 | tf_op jit(solution)/shard_map/ppermute | solution.py:355
  8.2 0.0 copy-done
  8.2 0.0 copy-done.4
  8.2 0.0 copy-done.3
  8.2 2.6 %shard_map.113 = (f32[2048,384]{1,0:T(8,128)S(1)}, f32[2048,384]{1,0:T(8,128)S(1)}, bf16[144,384]{1,0:T(8,128)(2,1)S(1)}, bf16[144,384]{1,0:T(8,128)(2,1)S(1)}, bf16[144,384]{1,0:T(8,128)(2,1)S(1)}) custom-call(f32[4,384]{1,0:T(4,128)S(1)} %copy-done.4, bf16[16,2048]{1,0:T(8,128)(2,1)S(1)} %get-tuple-element.25.far, bf16[2048,384]{1,0:T(8,128)(2,1)S(1)} %copy-done, ...), custom_call_target="tpu_custom_call" | custom-call | flops 402653184 | bytes 4718592 | tf_op jit(solution)/shard_map/pallas_call | solution.py:434
  10.8 0.7 %collective-permute-start.1 = (bf16[144,384]{1,0:T(8,128)(2,1)S(1)}, bf16[144,384]{1,0:T(8,128)(2,1)S(1)}, u32[]{:S(2)}, u32[]{:S(2)}) collective-permute-start(bf16[144,384]{1,0:T(8,128)(2,1)S(1)} %get-tuple-element.33), channel_id=1, source_target_pairs={{0,4},{4,8},{8,12},{12,0},{1,5},{5,9},{9,13},{13,1},{2,6},{6,10},{... | collective-permute-start | bytes 331784 | tf_op jit(solution)/shard_map/ppermute | solution.py:355
  11.5 1.9 %collective-permute-start.2 = (bf16[144,384]{1,0:T(8,128)(2,1)S(1)}, bf16[144,384]{1,0:T(8,128)(2,1)S(1)}, u32[]{:S(2)}, u32[]{:S(2)}) collective-permute-start(bf16[144,384]{1,0:T(8,128)(2,1)S(1)} %get-tuple-element.34), channel_id=1, source_target_pairs={{0,8},{4,12},{8,0},{12,4},{1,9},{5,13},{9,1},{13,5},{2,10},{6,14},... | collective-permute-start | bytes 331784 | tf_op jit(solution)/shard_map/ppermute | solution.py:355
  13.5 2.0 %collective-permute-start.3 = (bf16[144,384]{1,0:T(8,128)(2,1)S(1)}, bf16[144,384]{1,0:T(8,128)(2,1)S(1)}, u32[]{:S(2)}, u32[]{:S(2)}) collective-permute-start(bf16[144,384]{1,0:T(8,128)(2,1)S(1)} %get-tuple-element.35), channel_id=1, source_target_pairs={{0,12},{4,0},{8,4},{12,8},{1,13},{5,1},{9,5},{13,9},{2,14},{6,2},{... | collective-permute-start | bytes 331784 | tf_op jit(solution)/shard_map/ppermute | solution.py:355
  15.5 0.0 copy-done.1
  15.5 0.0 copy-done.2
  15.5 6.5 %shard_map.114 = (f32[2048,384]{1,0:T(8,128)S(1)}, f32[2048,384]{1,0:T(8,128)S(1)}, f32[2048,384]{1,0:T(8,128)S(1)}) custom-call(f32[6]{0:T(128)S(1)} %copy-done.5, bf16[32,2048]{1,0:T(8,128)(2,1)S(1)} %get-tuple-element.24.near, bf16[16,2048]{1,0:T(8,128)(2,1)S(1)} %get-tuple-element.25.far, f32[3,16,384]{2,1,0:T(8,128)S(1)} %get-tuple-element.26.logs, ...), custom_call_target="tpu_custom_call" | custom-call | flops 2013265920 | bytes 4718592 | tf_op jit(solution)/shard_map/pallas_call | solution.py:448
  22.0 0.0 collective-permute-done.1.rest_0_
  22.0 0.0 collective-permute-done.2.rest_1_
  22.0 0.0 collective-permute-done.3.rest_2_
  22.0 3.0 %shard_map.115 = (bf16[2048,384]{1,0:T(8,128)(2,1)S(1)}, f32[8,384]{1,0:T(8,128)S(1)}, f32[16,384]{1,0:T(8,128)S(1)}) custom-call(f32[4,384]{1,0:T(4,128)S(1)} %copy-done.4, f32[2048,384]{1,0:T(8,128)S(1)} %get-tuple-element.31.base, f32[2048,384]{1,0:T(8,128)S(1)} %get-tuple-element.32.weight, bf16[2048,384]{1,0:T(8,128)(2,1)S(1)} %copy-done, ...), custom_call_target="tpu_custom_call" | custom-call | flops 402653184 | bytes 4718592 | tf_op jit(solution)/shard_map/pallas_call | solution.py:457
  25.0 3.1 %collective-permute-start.6 = (f32[8,384]{1,0:T(8,128)S(1)}, f32[8,384]{1,0:T(8,128)S(1)}, u32[]{:S(2)}, u32[]{:S(2)}) collective-permute-start(f32[8,384]{1,0:T(8,128)S(1)} %get-tuple-element.38.tail), channel_id=1, source_target_pairs={{0,12},{4,0},{8,4},{12,8},{1,13},{5,1},{9,5},{13,9},{2,14},{6,2},{... | collective-permute-start | bytes 36872 | tf_op jit(solution)/shard_map/ppermute | solution.py:355
  28.1 0.7 %collective-permute-start.5 = (f32[8,384]{1,0:T(8,128)S(1)}, f32[8,384]{1,0:T(8,128)S(1)}, u32[]{:S(2)}, u32[]{:S(2)}) collective-permute-start(f32[8,384]{1,0:T(8,128)S(1)} %get-tuple-element.38.tail), channel_id=1, source_target_pairs={{0,8},{4,12},{8,0},{12,4},{1,9},{5,13},{9,1},{13,5},{2,10},{6,14},... | collective-permute-start | bytes 36872 | tf_op jit(solution)/shard_map/ppermute | solution.py:355
  28.8 0.0 collective-permute-start.4
  28.8 1.8 %shard_map.116 = (bf16[2048,384]{1,0:T(8,128)(2,1)}, bf16[2048,384]{1,0:T(8,128)(2,1)}) custom-call(bf16[16,2048]{1,0:T(8,128)(2,1)S(1)} %get-tuple-element.23.front, f32[2048,384]{1,0:T(8,128)S(1)} %get-tuple-element.30.base, bf16[2048,128]{1,0:T(8,128)(2,1)S(1)} %copy-done.2, bf16[2048,384]{1,0:T(8,128)(2,1)S(1)} %get-tuple-element.36.grad_rows, ...), custom_call_target="tpu_custom_call" | custom-call | flops 402653184 | bytes 4718592 | tf_op jit(solution)/shard_map/pallas_call | solution.py:467
  30.7 0.0 collective-permute-done.6.rest_2_
  30.7 2.0 %collective-permute-done.5.rest_1_ = f32[8,384]{1,0:T(8,128)S(1)} collective-permute-done((f32[8,384]{1,0:T(8,128)S(1)}, f32[8,384]{1,0:T(8,128)S(1)}, u32[]{:S(2)}, u32[]{:S(2)}) %collective-permute-start.5) | collective-permute-done | bytes 12320 | tf_op jit(solution)/shard_map/ppermute | solution.py:355
  32.7 1.6 %collective-permute-done.4.rest_0_ = f32[8,384]{1,0:T(8,128)S(1)} collective-permute-done((f32[8,384]{1,0:T(8,128)S(1)}, f32[8,384]{1,0:T(8,128)S(1)}, u32[]{:S(2)}, u32[]{:S(2)}) %collective-permute-start.4) | collective-permute-done | bytes 12320 | tf_op jit(solution)/shard_map/ppermute | solution.py:355
  34.3 1.2 %shard_map.117 = (bf16[2048,384]{1,0:T(8,128)(2,1)}, f32[4,384]{1,0:T(4,128)}) custom-call(f32[4,384]{1,0:T(4,128)S(1)} %copy-done.4, f32[8,384]{1,0:T(8,128)S(1)} %get-tuple-element.38.tail, f32[16,384]{1,0:T(8,128)S(1)} %get-tuple-element.39.edge, f32[8,384]{1,0:T(8,128)S(1)} %collective-permute-done.4.rest_0_, ...), custom_call_target="tpu_custom_call", output_to_operand_aliasing={{0}: (6, {})} | custom-call | bytes 4718592 | tf_op jit(solution)/shard_map/pallas_call | solution.py:477
  (1 shorter events, 0.0 us)
Async XLA Ops:
  0.6 7.6 %copy-start = (bf16[2048,384]{1,0:T(8,128)(2,1)S(1)}, bf16[2048,384]{1,0:T(8,128)(2,1)}, u32[]{:S(2)}) copy-start(bf16[2048,384]{1,0:T(8,128)(2,1)} %inputs.3) | copy-start | bytes 4718596
  0.6 7.6 %copy-start.4 = (f32[4,384]{1,0:T(4,128)S(1)}, f32[4,384]{1,0:T(4,128)}, u32[]{:S(2)}) copy-start(f32[4,384]{1,0:T(4,128)} %taps.5) | copy-start | bytes 18436
  0.7 7.6 %copy-start.3 = (bf16[2048,128]{1,0:T(8,128)(2,1)S(1)}, bf16[2048,128]{1,0:T(8,128)(2,1)}, u32[]{:S(2)}) copy-start(bf16[2048,128]{1,0:T(8,128)(2,1)} %b_proj.5) | copy-start | bytes 1572868
  1.5 6.7 %collective-permute-start = (bf16[16,384]{1,0:T(8,128)(2,1)S(1)}, bf16[16,384]{1,0:T(8,128)(2,1)S(1)}, u32[]{:S(2)}, u32[]{:S(2)}) collective-permute-start(bf16[16,384]{1,0:T(8,128)(2,1)S(1)} %slice.3), channel_id=1, source_target_pairs={{0,4},{4,8},{8,12},{12,0},{1,5},{5,9},{9,13},{13,1},{2,6},{6,10},{... | collective-permute-start | bytes 36872 | tf_op jit(solution)/shard_map/ppermute | solution.py:355
  7.2 8.2 %copy-start.1 = (bf16[2048,384]{1,0:T(8,128)(2,1)S(1)}, bf16[2048,384]{1,0:T(8,128)(2,1)}, u32[]{:S(2)}) copy-start(bf16[2048,384]{1,0:T(8,128)(2,1)} %grad.1) | copy-start | bytes 4718596
  7.2 8.2 %copy-start.2 = (bf16[2048,128]{1,0:T(8,128)(2,1)S(1)}, bf16[2048,128]{1,0:T(8,128)(2,1)}, u32[]{:S(2)}) copy-start(bf16[2048,128]{1,0:T(8,128)(2,1)} %c_proj.3) | copy-start | bytes 1572868
  7.3 8.2 %copy-start.5 = (f32[6]{0:T(128)S(1)}, f32[6]{0:T(128)}, u32[]{:S(2)}) copy-start(f32[6]{0:T(128)} %gains.1) | copy-start | bytes 76
  10.8 11.1 %collective-permute-start.1 = (bf16[144,384]{1,0:T(8,128)(2,1)S(1)}, bf16[144,384]{1,0:T(8,128)(2,1)S(1)}, u32[]{:S(2)}, u32[]{:S(2)}) collective-permute-start(bf16[144,384]{1,0:T(8,128)(2,1)S(1)} %get-tuple-element.33), channel_id=1, source_target_pairs={{0,4},{4,8},{8,12},{12,0},{1,5},{5,9},{9,13},{13,1},{2,6},{6,10},{... | collective-permute-start | bytes 331784 | tf_op jit(solution)/shard_map/ppermute | solution.py:355
  11.5 10.4 %collective-permute-start.2 = (bf16[144,384]{1,0:T(8,128)(2,1)S(1)}, bf16[144,384]{1,0:T(8,128)(2,1)S(1)}, u32[]{:S(2)}, u32[]{:S(2)}) collective-permute-start(bf16[144,384]{1,0:T(8,128)(2,1)S(1)} %get-tuple-element.34), channel_id=1, source_target_pairs={{0,8},{4,12},{8,0},{12,4},{1,9},{5,13},{9,1},{13,5},{2,10},{6,14},... | collective-permute-start | bytes 331784 | tf_op jit(solution)/shard_map/ppermute | solution.py:355
  13.5 8.5 %collective-permute-start.3 = (bf16[144,384]{1,0:T(8,128)(2,1)S(1)}, bf16[144,384]{1,0:T(8,128)(2,1)S(1)}, u32[]{:S(2)}, u32[]{:S(2)}) collective-permute-start(bf16[144,384]{1,0:T(8,128)(2,1)S(1)} %get-tuple-element.35), channel_id=1, source_target_pairs={{0,12},{4,0},{8,4},{12,8},{1,13},{5,1},{9,5},{13,9},{2,14},{6,2},{... | collective-permute-start | bytes 331784 | tf_op jit(solution)/shard_map/ppermute | solution.py:355
  25.0 5.7 %collective-permute-start.6 = (f32[8,384]{1,0:T(8,128)S(1)}, f32[8,384]{1,0:T(8,128)S(1)}, u32[]{:S(2)}, u32[]{:S(2)}) collective-permute-start(f32[8,384]{1,0:T(8,128)S(1)} %get-tuple-element.38.tail), channel_id=1, source_target_pairs={{0,12},{4,0},{8,4},{12,8},{1,13},{5,1},{9,5},{13,9},{2,14},{6,2},{... | collective-permute-start | bytes 36872 | tf_op jit(solution)/shard_map/ppermute | solution.py:355
  28.1 4.6 %collective-permute-start.5 = (f32[8,384]{1,0:T(8,128)S(1)}, f32[8,384]{1,0:T(8,128)S(1)}, u32[]{:S(2)}, u32[]{:S(2)}) collective-permute-start(f32[8,384]{1,0:T(8,128)S(1)} %get-tuple-element.38.tail), channel_id=1, source_target_pairs={{0,8},{4,12},{8,0},{12,4},{1,9},{5,13},{9,1},{13,5},{2,10},{6,14},... | collective-permute-start | bytes 36872 | tf_op jit(solution)/shard_map/ppermute | solution.py:355
  28.8 5.5 %collective-permute-start.4 = (f32[8,384]{1,0:T(8,128)S(1)}, f32[8,384]{1,0:T(8,128)S(1)}, u32[]{:S(2)}, u32[]{:S(2)}) collective-permute-start(f32[8,384]{1,0:T(8,128)S(1)} %get-tuple-element.38.tail), channel_id=1, source_target_pairs={{0,4},{4,8},{8,12},{12,0},{1,5},{5,9},{9,13},{13,1},{2,6},{6,10},{... | collective-permute-start | bytes 36872 | tf_op jit(solution)/shard_map/ppermute | solution.py:355

commit v5 on v4

--- a/solution.py
+++ b/solution.py
@@ -15,7 +15,7 @@
 F32 = jnp.float32
 BF16 = jnp.bfloat16
 HIGHEST = lax.Precision.HIGHEST
-VMEM_LIMIT = 20 * 1024 * 1024
+VMEM_LIMIT = 28 * 1024 * 1024
 
 
 def dot(a, b, dims, precision=None):
@@ -148,6 +148,20 @@
     pay_out[0:STATE, :] = dot(c_proj[...], grad[...], ((0,), (0,))).astype(BF16)
 
 
+def back_shift():
+    row = lax.broadcasted_iota(jnp.int32, (3 * CHUNK, CHUNK + 16), 0)
+    col = lax.broadcasted_iota(jnp.int32, (3 * CHUNK, CHUNK + 16), 1)
+    return jnp.where(col == row % CHUNK + 13 + row // CHUNK, 1.0, 0.0).astype(BF16)
+
+
+def shifted_inputs(shift, before, inputs, at):
+    if at == 0:
+        block = jnp.concatenate([before, inputs[0:CHUNK, :]], axis=0)
+    else:
+        block = inputs[at - 16 : at + CHUNK, :]
+    return dot(shift, block, ((1,), (0,)))
+
+
 def lane_tiles(channels):
     return [slice(at, min(at + 128, channels)) for at in range(0, channels, 128)]
 
@@ -160,16 +174,10 @@
     me = lax.axis_index("seq")
     before = jnp.where(me > 0, halo[...].astype(F32), 0.0).astype(BF16)
     onehot = spread_matrix(heads, channels)
-    row = lax.broadcasted_iota(jnp.int32, (3 * CHUNK, CHUNK + 16), 0)
-    col = lax.broadcasted_iota(jnp.int32, (3 * CHUNK, CHUNK + 16), 1)
-    shift = jnp.where(col == row % CHUNK + 13 + row // CHUNK, 1.0, 0.0).astype(BF16)
+    shift = back_shift()
     for at in range(0, rows, CHUNK):
         both = slice(at, at + CHUNK)
-        if at == 0:
-            block = jnp.concatenate([before, inputs[both, :]], axis=0)
-        else:
-            block = inputs[at - 16 : at + CHUNK, :]
-        moved = dot(shift, block, ((1,), (0,)))
+        moved = shifted_inputs(shift, before, inputs, at)
         preact = taps[3:4, :] * inputs[both, :].astype(F32)
         for k in range(3):
             preact = preact + taps[k : k + 1, :] * moved[k * CHUNK : (k + 1) * CHUNK, :]
@@ -199,10 +207,10 @@
 
 
 def inner_kernel(
-    heads, gains, near, far, logs, grad, mixed, sigma, b_proj, c_proj,
-    base_out, grad_base, grad_weight,
+    heads, gains, near, far, logs, grad, mixed, sigma, b_proj, c_proj, inputs, halo,
+    base_out, grad_base, grad_weight, tap_base, tap_weight,
     ahead_scores, behind_scores, mixed_scaled, mixed_low, grad_scaled, grad_low,
-    mixed_fresh, grad_fresh,
+    mixed_fresh, grad_fresh, base_products, weight_products,
 ):
     rows, channels = grad.shape
     chunks = rows // CHUNK
@@ -211,6 +219,8 @@
     col = lax.broadcasted_iota(jnp.int32, (CHUNK, CHUNK), 1)
     onehot = spread_matrix(heads, channels)
     gain = per_lane(gains, heads, channels)
+    shift = back_shift()
+    before = jnp.where(lax.axis_index("seq") > 0, halo[...].astype(F32), 0.0).astype(BF16)
     for both in blocks:
         scale = spread(near[0:16, both], onehot)
         grad_scaled[both, :] = (grad[both, :].astype(F32) * scale).astype(BF16)
@@ -248,8 +258,19 @@
         )
         slope = sigma[both, :] + mixed[both, :] * (1.0 - sigma[both, :])
         inner = gain * grad[both, :].astype(F32) + spread(near[16:32, both], onehot) * inner
-        grad_base[both, :] = slope * inner
-        grad_weight[both, :] = slope * spread(far[:, both], onehot)
+        part = slope * inner
+        weight = slope * spread(far[:, both], onehot)
+        grad_base[both, :] = part
+        grad_weight[both, :] = weight
+        part = part.astype(BF16)
+        weight = weight.astype(BF16)
+        moved = shifted_inputs(shift, before, inputs, both.start)
+        for k in range(4):
+            x = inputs[both, :]
+            if k < 3:
+                x = moved[k * CHUNK : (k + 1) * CHUNK, :].astype(BF16)
+            base_products[k, both, :] = part * x
+            weight_products[k, both, :] = weight * x
     for both in blocks:
         inner = dot(
             jnp.concatenate([ahead_scores[both, :], c_proj[both, :]], axis=1),
@@ -257,20 +278,24 @@
             ((1,), (0,)),
         )
         base_out[both, :] = gain * mixed[both, :] + spread(near[0:16, both], onehot) * inner
-
-
-def gradient_kernel(parts, taps, base, weight, inputs, halo, b_proj, *rest):
+    ones = jnp.ones((8, rows), BF16)
+    tap_base[...] = jnp.zeros_like(tap_base)
+    for k in range(4):
+        sums = dot(ones, base_products[k], ((1,), (0,)))
+        tap_base[k : k + 1, :] = sums[0:1, :]
+        tap_weight[k] = dot(b_proj[...], weight_products[k], ((0,), (0,)))
+
+
+def gradient_kernel(parts, taps, base, weight, tap_base, tap_weight, b_proj, *rest):
     pays = rest[: parts - 1]
     grad_out, tail_out, edge_out, window, exact = rest[parts - 1 :]
     rows, channels = base.shape
     chunks = rows // CHUNK
     adjoint = merged(parts, pays, False)
-    me = lax.axis_index("seq")
     window[rows : rows + 16, :] = jnp.zeros((16, channels), BF16)
     row = lax.broadcasted_iota(jnp.int32, (3 * CHUNK, CHUNK + 16), 0)
     col = lax.broadcasted_iota(jnp.int32, (3 * CHUNK, CHUNK + 16), 1)
     shift = jnp.where(col == row % CHUNK + 3 - row // CHUNK, 1.0, 0.0).astype(BF16)
-    partial = [jnp.zeros((8, channels), F32) for _ in range(4)]
     for j in range(chunks):
         both = slice(j * CHUNK, (j + 1) * CHUNK)
         grad_pre = base[both, :] + weight[both, :] * dot(b_proj[both, :], adjoint, ((1,), (0,)))
@@ -281,24 +306,17 @@
         both = slice(at, at + CHUNK)
         grad_pre = exact[both, :]
         moved = dot(shift, window[at : at + CHUNK + 16, :], ((1,), (0,)))
-        x = inputs[both, :].astype(F32)
         result = taps[3:4, :] * grad_pre
-        partial[3] = partial[3] + (grad_pre * x).reshape(CHUNK // 8, 8, channels).sum(axis=0)
         for k in range(3):
-            part = moved[k * CHUNK : (k + 1) * CHUNK, :]
-            result = result + taps[k : k + 1, :] * part
-            partial[k] = partial[k] + (part * x).reshape(CHUNK // 8, 8, channels).sum(axis=0)
+            result = result + taps[k : k + 1, :] * moved[k * CHUNK : (k + 1) * CHUNK, :]
         grad_out[both, :] = result.astype(BF16)
         if j == chunks - 1:
             edge_out[...] = result[CHUNK - 16 :, :]
-    first = exact[0:8, :]
-    before = jnp.where(me > 0, halo[...].astype(F32), 0.0)
+    carried = adjoint.astype(F32)
     for k in range(4):
-        tap = jnp.sum(partial[k], axis=0, keepdims=True)
-        for j in range(k, 3):
-            tap = tap + first[j - k : j - k + 1, :] * before[13 + j : 14 + j, :]
-        tail_out[k : k + 1, :] = tap
-    tail_out[4:7, :] = first[0:3, :]
+        tap = jnp.sum(carried * tap_weight[k], axis=0, keepdims=True)
+        tail_out[k : k + 1, :] = tap_base[k : k + 1, :] + tap
+    tail_out[4:7, :] = exact[0:3, :]
     tail_out[7:8, :] = jnp.zeros((1, channels), F32)
 
 
@@ -445,14 +463,15 @@
     tile = pltpu.VMEM((rows, CHUNK), BF16)
     low = pltpu.VMEM((rows, channels), BF16)
     high = pltpu.VMEM((rows, channels), F32)
-    base, grad_base, grad_weight = call(
+    products = pltpu.VMEM((4, rows, channels), BF16)
+    base, grad_base, grad_weight, tap_base, tap_weight = call(
         functools.partial(inner_kernel, heads),
-        [smem] + [vmem] * 8,
-        [vmem] * 3,
-        [broad] * 3,
-        [tile, tile, low, low, low, low, high, high],
-        10,
-    )(skip_gain, near, far, logs, out_cotangent, mixed, sigma, b_proj, c_proj)
+        [smem] + [vmem] * 10,
+        [vmem] * 5,
+        [broad] * 3 + [shape((8, channels), F32), shape((4, STATE, channels), F32)],
+        [tile, tile, low, low, low, low, high, high, products, products],
+        18,
+    )(skip_gain, near, far, logs, out_cotangent, mixed, sigma, b_proj, c_proj, inputs, halo)
 
     grad_rows, tail, edge = call(
         functools.partial(gradient_kernel, parts),
@@ -461,7 +480,7 @@
         [narrow, shape((8, channels), F32), shape((16, channels), F32)],
         [pltpu.VMEM((rows + 16, channels), BF16), pltpu.VMEM((rows, channels), F32)],
         2,
-    )(conv_weight, grad_base, grad_weight, inputs, halo, b_proj, *pays)
+    )(conv_weight, grad_base, grad_weight, tap_base, tap_weight, b_proj, *pays)
     tails = [rotated(tail, "seq", distance) for distance in range(1, parts)]
 
     layer_out, grad_rows = call(

time: 35.9 us -> 36.7 us (1.022)
  Pallas kernels: 17.8 us -> 20.9 us
  waiting for transfers between devices: 4.61 us -> 2.79 us
  starting transfers between devices: 11.5 us -> 11 us
    pallas_call x1, Pallas kernels: 6.46 us -> 10.1 us  [shards(): call(functools.partial(inner_kernel, heads), [smem] + [vmem] * 10, [vmem]...]
    ppermute x7, waiting for transfers between devices: 4.61 us -> 2.79 us  [rotated(): lax.ppermute(block, axis, [(i, (i + distance) % size) for i in range(size)])]
    pallas_call x1, Pallas kernels: 3 us -> 2.44 us  [shards(): call(functools.partial(gradient_kernel, parts), [vmem] * (5 + parts), [vm...]
    ppermute x7, starting transfers between devices: 11.5 us -> 11 us  [rotated(): lax.ppermute(block, axis, [(i, (i + distance) % size) for i in range(size)])]
  transfers between devices with their start and end apart: 7 -> 7, of which waited for: 3 -> 2; matrix products, arithmetic and copies ran while one was open for 0% -> 0% of each run, Pallas kernels for 31% -> 40%
where the time goes in v5:
time: 36.7 us; the launch traced here: 36.5 us
  Pallas kernels  20.9 us (57%)
  starting transfers between devices  11 us (30%)
  waiting for transfers between devices  2.79 us (8%)
  between operations  0.93 us (3%)
  local copies, waits for them, and re-layouts  0.89 us (2%)
    ppermute x7, starting transfers between devices, rotated(): lax.ppermute(block, axis, [(i, (i + distance) % size) for i in range(size)])  11 us
    pallas_call x1, Pallas kernels, shards(): call(functools.partial(inner_kernel, heads), [smem] + [vmem] * 10, [vmem]...  10.1 us
    ppermute x7, waiting for transfers between devices, rotated(): lax.ppermute(block, axis, [(i, (i + distance) % size) for i in range(size)])  2.79 us
    pallas_call x1, Pallas kernels, shards(): call(functools.partial(adjoint_kernel, heads), [hbm] * 5, [vmem] * 5, [sh...  2.68 us
    pallas_call x1, Pallas kernels, shards(): call(functools.partial(state_kernel, heads, parts), [vmem] * 6, [vmem] *...  2.58 us
    pallas_call x1, Pallas kernels, shards(): call(functools.partial(gradient_kernel, parts), [vmem] * (5 + parts), [vm...  2.44 us
    pallas_call x1, Pallas kernels, shards(): call(functools.partial(output_kernel, heads, parts), [vmem] * (3 + parts)...  1.86 us
    pallas_call x1, Pallas kernels, shards(): call(functools.partial(finish_kernel, parts, scale), [vmem] * (2 + parts)...  1.22 us
  transfers between devices with their start and end apart: 7, of which 2 were waited for; matrix products, arithmetic and copies ran while one was open for 0% of the time, Pallas kernels for 40%

profile of v5, /device:TPU:0, one launch (start us, length us, event | category | flops | bytes accessed | tf_op | source)
XLA Modules:
  0.0 36.5 jit_solution(15485557838300821305)
XLA Ops:
  0.6 0.0 copy-start.2
  0.6 0.0 copy-start.4
  0.7 0.0 copy-start.1
  0.7 0.9 %slice.3 = bf16[16,384]{1,0:T(8,128)(2,1)S(1)} slice(bf16[2048,384]{1,0:T(8,128)(2,1)} %inputs.3), slice={[2032:2048], [0:384]} | slice | bytes 24576 | tf_op jit(solution)/shard_map/slice | solution.py:416
  1.5 3.0 %collective-permute-start = (bf16[16,384]{1,0:T(8,128)(2,1)S(1)}, bf16[16,384]{1,0:T(8,128)(2,1)S(1)}, u32[]{:S(2)}, u32[]{:S(2)}) collective-permute-start(bf16[16,384]{1,0:T(8,128)(2,1)S(1)} %slice.3), channel_id=1, source_target_pairs={{0,4},{4,8},{8,12},{12,0},{1,5},{5,9},{9,13},{13,1},{2,6},{6,10},{... | collective-permute-start | bytes 36872 | tf_op jit(solution)/shard_map/ppermute | solution.py:373
  4.5 2.7 %shard_map.112 = (bf16[32,2048]{1,0:T(8,128)(2,1)S(1)}, bf16[16,2048]{1,0:T(8,128)(2,1)S(1)}, bf16[16,2048]{1,0:T(8,128)(2,1)S(1)}, f32[3,16,384]{2,1,0:T(8,128)S(1)}, bf16[144,384]{1,0:T(8,128)(2,1)S(1)}) custom-call(f32[6]{0:T(128)} %rates_hbm.1, s32[6,2048]{1,0:T(8,128)} %codes_hbm.1, s32[1,2048]{1,0:T(1,128)} %bitcast.1, bf16[2048,384]{1,0:T(8,128)(2,1)} %grad.1, ...), custom_call_target="tpu_custom_call" | custom-call | flops 402653184 | bytes 4718592 | tf_op jit(solution)/shard_map/pallas_call | solution.py:421
  7.2 0.0 copy-start
  7.2 0.0 copy-start.3
  7.3 0.0 copy-start.5
  7.3 1.0 %collective-permute-done.halo = bf16[16,384]{1,0:T(8,128)(2,1)S(1)} collective-permute-done((bf16[16,384]{1,0:T(8,128)(2,1)S(1)}, bf16[16,384]{1,0:T(8,128)(2,1)S(1)}, u32[]{:S(2)}, u32[]{:S(2)}) %collective-permute-start) | collective-permute-done | bytes 12320 | tf_op jit(solution)/shard_map/ppermute | solution.py:373
  8.2 0.0 copy-done.2
  8.2 0.0 copy-done.4
  8.2 0.0 copy-done.1
  8.2 2.6 %shard_map.113 = (f32[2048,384]{1,0:T(8,128)S(1)}, f32[2048,384]{1,0:T(8,128)S(1)}, bf16[144,384]{1,0:T(8,128)(2,1)S(1)}, bf16[144,384]{1,0:T(8,128)(2,1)S(1)}, bf16[144,384]{1,0:T(8,128)(2,1)S(1)}) custom-call(f32[4,384]{1,0:T(4,128)S(1)} %copy-done.4, bf16[16,2048]{1,0:T(8,128)(2,1)S(1)} %get-tuple-element.27.far, bf16[2048,384]{1,0:T(8,128)(2,1)S(1)} %copy-done.2, ...), custom_call_target="tpu_custom_call" | custom-call | flops 402653184 | bytes 4718592 | tf_op jit(solution)/shard_map/pallas_call | solution.py:452
  10.8 0.7 %collective-permute-start.1 = (bf16[144,384]{1,0:T(8,128)(2,1)S(1)}, bf16[144,384]{1,0:T(8,128)(2,1)S(1)}, u32[]{:S(2)}, u32[]{:S(2)}) collective-permute-start(bf16[144,384]{1,0:T(8,128)(2,1)S(1)} %get-tuple-element.37), channel_id=1, source_target_pairs={{0,4},{4,8},{8,12},{12,0},{1,5},{5,9},{9,13},{13,1},{2,6},{6,10},{... | collective-permute-start | bytes 331784 | tf_op jit(solution)/shard_map/ppermute | solution.py:373
  11.5 1.9 %collective-permute-start.2 = (bf16[144,384]{1,0:T(8,128)(2,1)S(1)}, bf16[144,384]{1,0:T(8,128)(2,1)S(1)}, u32[]{:S(2)}, u32[]{:S(2)}) collective-permute-start(bf16[144,384]{1,0:T(8,128)(2,1)S(1)} %get-tuple-element.38), channel_id=1, source_target_pairs={{0,8},{4,12},{8,0},{12,4},{1,9},{5,13},{9,1},{13,5},{2,10},{6,14},... | collective-permute-start | bytes 331784 | tf_op jit(solution)/shard_map/ppermute | solution.py:373
  13.5 2.0 %collective-permute-start.3 = (bf16[144,384]{1,0:T(8,128)(2,1)S(1)}, bf16[144,384]{1,0:T(8,128)(2,1)S(1)}, u32[]{:S(2)}, u32[]{:S(2)}) collective-permute-start(bf16[144,384]{1,0:T(8,128)(2,1)S(1)} %get-tuple-element.39), channel_id=1, source_target_pairs={{0,12},{4,0},{8,4},{12,8},{1,13},{5,1},{9,5},{13,9},{2,14},{6,2},{... | collective-permute-start | bytes 331784 | tf_op jit(solution)/shard_map/ppermute | solution.py:373
  15.5 0.0 copy-done
  15.5 0.0 copy-done.3
  15.5 10.1 %shard_map.114 = (f32[2048,384]{1,0:T(8,128)S(1)}, f32[2048,384]{1,0:T(8,128)S(1)}, f32[2048,384]{1,0:T(8,128)S(1)}, f32[8,384]{1,0:T(8,128)S(1)}, f32[4,128,384]{2,1,0:T(8,128)S(1)}) custom-call(f32[6]{0:T(128)S(1)} %copy-done.5, bf16[32,2048]{1,0:T(8,128)(2,1)S(1)} %get-tuple-element.26.near, bf16[16,2048]{1,0:T(8,128)(2,1)S(1)} %get-tuple-element.27.far, ...), custom_call_target="tpu_custom_call" | custom-call | flops 3623878656 | bytes 4718592 | tf_op jit(solution)/shard_map/pallas_call | solution.py:467
  25.6 0.0 collective-permute-done.1.rest_0_
  25.6 0.0 collective-permute-done.2.rest_1_
  25.6 0.0 collective-permute-done.3.rest_2_
  25.6 2.4 %shard_map.115 = (bf16[2048,384]{1,0:T(8,128)(2,1)S(1)}, f32[8,384]{1,0:T(8,128)S(1)}, f32[16,384]{1,0:T(8,128)S(1)}) custom-call(f32[4,384]{1,0:T(4,128)S(1)} %copy-done.4, f32[2048,384]{1,0:T(8,128)S(1)} %get-tuple-element.33.base, f32[2048,384]{1,0:T(8,128)S(1)} %get-tuple-element.34.weight, f32[8,384]{1,0:T(8,128)S(1)} %get-tuple-element.35.tap_base, ...), custom_call_target="tpu_custom_call" | custom-call | flops 402653184 | bytes 4718592 | tf_op jit(solution)/shard_map/pallas_call | solution.py:476
  28.1 0.5 %collective-permute-start.6 = (f32[8,384]{1,0:T(8,128)S(1)}, f32[8,384]{1,0:T(8,128)S(1)}, u32[]{:S(2)}, u32[]{:S(2)}) collective-permute-start(f32[8,384]{1,0:T(8,128)S(1)} %get-tuple-element.42.tail), channel_id=1, source_target_pairs={{0,12},{4,0},{8,4},{12,8},{1,13},{5,1},{9,5},{13,9},{2,14},{6,2},{... | collective-permute-start | bytes 36872 | tf_op jit(solution)/shard_map/ppermute | solution.py:373
  28.6 1.1 %collective-permute-start.5 = (f32[8,384]{1,0:T(8,128)S(1)}, f32[8,384]{1,0:T(8,128)S(1)}, u32[]{:S(2)}, u32[]{:S(2)}) collective-permute-start(f32[8,384]{1,0:T(8,128)S(1)} %get-tuple-element.42.tail), channel_id=1, source_target_pairs={{0,8},{4,12},{8,0},{12,4},{1,9},{5,13},{9,1},{13,5},{2,10},{6,14},... | collective-permute-start | bytes 36872 | tf_op jit(solution)/shard_map/ppermute | solution.py:373
  29.6 1.8 %collective-permute-start.4 = (f32[8,384]{1,0:T(8,128)S(1)}, f32[8,384]{1,0:T(8,128)S(1)}, u32[]{:S(2)}, u32[]{:S(2)}) collective-permute-start(f32[8,384]{1,0:T(8,128)S(1)} %get-tuple-element.42.tail), channel_id=1, source_target_pairs={{0,4},{4,8},{8,12},{12,0},{1,5},{5,9},{9,13},{13,1},{2,6},{6,10},{... | collective-permute-start | bytes 36872 | tf_op jit(solution)/shard_map/ppermute | solution.py:373
  31.4 1.9 %shard_map.116 = (bf16[2048,384]{1,0:T(8,128)(2,1)}, bf16[2048,384]{1,0:T(8,128)(2,1)}) custom-call(bf16[16,2048]{1,0:T(8,128)(2,1)S(1)} %get-tuple-element.25.front, f32[2048,384]{1,0:T(8,128)S(1)} %get-tuple-element.32.base, bf16[2048,128]{1,0:T(8,128)(2,1)S(1)} %copy-done, bf16[2048,384]{1,0:T(8,128)(2,1)S(1)} %get-tuple-element.40.grad_rows, ...), custom_call_target="tpu_custom_call" | custom-call | flops 402653184 | bytes 4718592 | tf_op jit(solution)/shard_map/pallas_call | solution.py:486
  33.3 0.0 collective-permute-done.6.rest_2_
  33.3 0.0 collective-permute-done.5.rest_1_
  33.3 1.8 %collective-permute-done.4.rest_0_ = f32[8,384]{1,0:T(8,128)S(1)} collective-permute-done((f32[8,384]{1,0:T(8,128)S(1)}, f32[8,384]{1,0:T(8,128)S(1)}, u32[]{:S(2)}, u32[]{:S(2)}) %collective-permute-start.4) | collective-permute-done | bytes 12320 | tf_op jit(solution)/shard_map/ppermute | solution.py:373
  35.1 1.2 %shard_map.117 = (bf16[2048,384]{1,0:T(8,128)(2,1)}, f32[4,384]{1,0:T(4,128)}) custom-call(f32[4,384]{1,0:T(4,128)S(1)} %copy-done.4, f32[8,384]{1,0:T(8,128)S(1)} %get-tuple-element.42.tail, f32[16,384]{1,0:T(8,128)S(1)} %get-tuple-element.43.edge, f32[8,384]{1,0:T(8,128)S(1)} %collective-permute-done.4.rest_0_, ...), custom_call_target="tpu_custom_call", output_to_operand_aliasing={{0}: (6, {})} | custom-call | bytes 4718592 | tf_op jit(solution)/shard_map/pallas_call | solution.py:496
  (1 shorter events, 0.0 us)
Async XLA Ops:
  0.6 7.6 %copy-start.2 = (bf16[2048,384]{1,0:T(8,128)(2,1)S(1)}, bf16[2048,384]{1,0:T(8,128)(2,1)}, u32[]{:S(2)}) copy-start(bf16[2048,384]{1,0:T(8,128)(2,1)} %inputs.3) | copy-start | bytes 4718596
  0.6 7.6 %copy-start.4 = (f32[4,384]{1,0:T(4,128)S(1)}, f32[4,384]{1,0:T(4,128)}, u32[]{:S(2)}) copy-start(f32[4,384]{1,0:T(4,128)} %taps.5) | copy-start | bytes 18436
  0.7 7.6 %copy-start.1 = (bf16[2048,128]{1,0:T(8,128)(2,1)S(1)}, bf16[2048,128]{1,0:T(8,128)(2,1)}, u32[]{:S(2)}) copy-start(bf16[2048,128]{1,0:T(8,128)(2,1)} %b_proj.5) | copy-start | bytes 1572868
  1.5 6.7 %collective-permute-start = (bf16[16,384]{1,0:T(8,128)(2,1)S(1)}, bf16[16,384]{1,0:T(8,128)(2,1)S(1)}, u32[]{:S(2)}, u32[]{:S(2)}) collective-permute-start(bf16[16,384]{1,0:T(8,128)(2,1)S(1)} %slice.3), channel_id=1, source_target_pairs={{0,4},{4,8},{8,12},{12,0},{1,5},{5,9},{9,13},{13,1},{2,6},{6,10},{... | collective-permute-start | bytes 36872 | tf_op jit(solution)/shard_map/ppermute | solution.py:373
  7.2 8.2 %copy-start = (bf16[2048,128]{1,0:T(8,128)(2,1)S(1)}, bf16[2048,128]{1,0:T(8,128)(2,1)}, u32[]{:S(2)}) copy-start(bf16[2048,128]{1,0:T(8,128)(2,1)} %c_proj.3) | copy-start | bytes 1572868
  7.2 8.2 %copy-start.3 = (bf16[2048,384]{1,0:T(8,128)(2,1)S(1)}, bf16[2048,384]{1,0:T(8,128)(2,1)}, u32[]{:S(2)}) copy-start(bf16[2048,384]{1,0:T(8,128)(2,1)} %grad.1) | copy-start | bytes 4718596
  7.3 8.2 %copy-start.5 = (f32[6]{0:T(128)S(1)}, f32[6]{0:T(128)}, u32[]{:S(2)}) copy-start(f32[6]{0:T(128)} %gains.1) | copy-start | bytes 76
  10.8 14.8 %collective-permute-start.1 = (bf16[144,384]{1,0:T(8,128)(2,1)S(1)}, bf16[144,384]{1,0:T(8,128)(2,1)S(1)}, u32[]{:S(2)}, u32[]{:S(2)}) collective-permute-start(bf16[144,384]{1,0:T(8,128)(2,1)S(1)} %get-tuple-element.37), channel_id=1, source_target_pairs={{0,4},{4,8},{8,12},{12,0},{1,5},{5,9},{9,13},{13,1},{2,6},{6,10},{... | collective-permute-start | bytes 331784 | tf_op jit(solution)/shard_map/ppermute | solution.py:373
  11.5 14.1 %collective-permute-start.2 = (bf16[144,384]{1,0:T(8,128)(2,1)S(1)}, bf16[144,384]{1,0:T(8,128)(2,1)S(1)}, u32[]{:S(2)}, u32[]{:S(2)}) collective-permute-start(bf16[144,384]{1,0:T(8,128)(2,1)S(1)} %get-tuple-element.38), channel_id=1, source_target_pairs={{0,8},{4,12},{8,0},{12,4},{1,9},{5,13},{9,1},{13,5},{2,10},{6,14},... | collective-permute-start | bytes 331784 | tf_op jit(solution)/shard_map/ppermute | solution.py:373
  13.5 12.1 %collective-permute-start.3 = (bf16[144,384]{1,0:T(8,128)(2,1)S(1)}, bf16[144,384]{1,0:T(8,128)(2,1)S(1)}, u32[]{:S(2)}, u32[]{:S(2)}) collective-permute-start(bf16[144,384]{1,0:T(8,128)(2,1)S(1)} %get-tuple-element.39), channel_id=1, source_target_pairs={{0,12},{4,0},{8,4},{12,8},{1,13},{5,1},{9,5},{13,9},{2,14},{6,2},{... | collective-permute-start | bytes 331784 | tf_op jit(solution)/shard_map/ppermute | solution.py:373
  28.1 5.2 %collective-permute-start.6 = (f32[8,384]{1,0:T(8,128)S(1)}, f32[8,384]{1,0:T(8,128)S(1)}, u32[]{:S(2)}, u32[]{:S(2)}) collective-permute-start(f32[8,384]{1,0:T(8,128)S(1)} %get-tuple-element.42.tail), channel_id=1, source_target_pairs={{0,12},{4,0},{8,4},{12,8},{1,13},{5,1},{9,5},{13,9},{2,14},{6,2},{... | collective-permute-start | bytes 36872 | tf_op jit(solution)/shard_map/ppermute | solution.py:373
  28.6 4.7 %collective-permute-start.5 = (f32[8,384]{1,0:T(8,128)S(1)}, f32[8,384]{1,0:T(8,128)S(1)}, u32[]{:S(2)}, u32[]{:S(2)}) collective-permute-start(f32[8,384]{1,0:T(8,128)S(1)} %get-tuple-element.42.tail), channel_id=1, source_target_pairs={{0,8},{4,12},{8,0},{12,4},{1,9},{5,13},{9,1},{13,5},{2,10},{6,14},... | collective-permute-start | bytes 36872 | tf_op jit(solution)/shard_map/ppermute | solution.py:373
  29.6 5.5 %collective-permute-start.4 = (f32[8,384]{1,0:T(8,128)S(1)}, f32[8,384]{1,0:T(8,128)S(1)}, u32[]{:S(2)}, u32[]{:S(2)}) collective-permute-start(f32[8,384]{1,0:T(8,128)S(1)} %get-tuple-element.42.tail), channel_id=1, source_target_pairs={{0,4},{4,8},{8,12},{12,0},{1,5},{5,9},{9,13},{13,1},{2,6},{6,10},{... | collective-permute-start | bytes 36872 | tf_op jit(solution)/shard_map/ppermute | solution.py:373

commit v6 on v4

--- a/solution.py
+++ b/solution.py
@@ -49,30 +49,24 @@
     return dot(pair, onehot, ((0,), (0,)))
 
 
-def adjoint_kernel(
-    heads, rates_hbm, codes_hbm, gates_hbm, grad_hbm, c_hbm,
-    near_out, far_out, front_out, logs_out, pay_out,
-    rates, codes, gates, grad, c_proj, steps, small_sem, grad_sem, c_sem,
+def reduce_kernel(
+    heads, parts, rates_hbm, codes_hbm, gates_hbm, taps_hbm, inputs_hbm, b_hbm, grad_hbm, c_hbm,
+    near_out, far_out, front_out, logs_out, lead_out, mixed_out, sigma_out,
+    inputs, b_proj, grad, c_proj, *rest
 ):
+    pays = rest[: parts - 1]
+    rates, codes, gates, taps, steps, scaled, lead_pair, extra, sems = rest[parts - 1 :]
     rows, channels = grad.shape
     chunks = rows // CHUNK
-    pieces = rows // STEP_ROWS
-    small = [
-        pltpu.make_async_copy(source, target, small_sem.at[i])
-        for i, (source, target) in enumerate(
-            ((rates_hbm, rates), (codes_hbm, codes), (gates_hbm, gates))
-        )
+    sources = (rates_hbm, codes_hbm, gates_hbm, taps_hbm, inputs_hbm, b_hbm, grad_hbm, c_hbm)
+    targets = (rates, codes, gates, taps, inputs, b_proj, grad, c_proj)
+    copies = [
+        pltpu.make_async_copy(source, target, sems.at[i])
+        for i, (source, target) in enumerate(zip(sources, targets))
     ]
-    large = []
-    for copy in small:
+    for copy in copies:
         copy.start()
-    for piece in range(pieces):
-        at = pl.ds(piece * STEP_ROWS, STEP_ROWS)
-        large.append(pltpu.make_async_copy(grad_hbm.at[at], grad.at[at], grad_sem.at[piece]))
-        large.append(pltpu.make_async_copy(c_hbm.at[at], c_proj.at[at], c_sem.at[piece]))
-    for copy in large:
-        copy.start()
-    for copy in small:
+    for copy in copies[:3]:
         copy.wait()
 
     steps[...] = jnp.zeros_like(steps)
@@ -107,6 +101,7 @@
         near_out[16:32, at] = split_two(jnp.exp(mids[j] - cums[j]) * size)
         front_out[:, at] = split_two(jnp.exp(befores[j] + cums[j]))
         far_out[:, at] = split_two(jnp.exp(before - befores[j] - cums[j]) * size)
+    lead_pair[...] = split_two(jnp.exp(-jnp.maximum(cums[0], -8.0)) * steps[:, 0:CHUNK])
     pick = lax.broadcasted_iota(jnp.int32, (8, CHUNK), 0)
     place = lax.broadcasted_iota(jnp.int32, (8, CHUNK), 1)
     chosen = jnp.where((pick == 0) | ((pick == 1) & (place < CHUNK // 2)), 1.0, 0.0)
@@ -130,43 +125,20 @@
     logs_out[2] = rest_of
     decay = jnp.exp(jnp.sum(table[0], axis=0, keepdims=True))
     first = decay.astype(BF16).astype(F32)
-    second = (decay - first).astype(BF16).astype(F32)
-    third = decay - first - second
-    row = lax.broadcasted_iota(jnp.int32, (16, channels), 0)
-    tail = jnp.where(
-        row == 0, first, jnp.where(row == 1, second, jnp.where(row == 2, third, 0.0))
-    )
-    pay_out[STATE : STATE + 16, :] = tail.astype(BF16)
+    extra[...] = jnp.zeros_like(extra)
+    extra[0:1, :] = first
+    extra[1:2, :] = decay - first
 
     onehot = spread_matrix(heads, channels)
-    for copy in large:
+    lead_out[...] = spread(lead_pair[:, 0:16], onehot)
+    for copy in copies[3:6]:
         copy.wait()
-    for piece in range(pieces):
-        both = slice(piece * STEP_ROWS, (piece + 1) * STEP_ROWS)
-        scale = spread(front_out[:, both], onehot)
-        grad[both, :] = (grad[both, :].astype(F32) * scale).astype(BF16)
-    pay_out[0:STATE, :] = dot(c_proj[...], grad[...], ((0,), (0,))).astype(BF16)
-
-
-def lane_tiles(channels):
-    return [slice(at, min(at + 128, channels)) for at in range(0, channels, 128)]
-
-
-def state_kernel(
-    heads, parts, taps, far, inputs, halo, b_proj, adjoint_pay, mixed_out, sigma_out, *rest
-):
-    pays, scaled = rest[: parts - 1], rest[parts - 1]
-    rows, channels = inputs.shape
-    me = lax.axis_index("seq")
-    before = jnp.where(me > 0, halo[...].astype(F32), 0.0).astype(BF16)
-    onehot = spread_matrix(heads, channels)
-    row = lax.broadcasted_iota(jnp.int32, (3 * CHUNK, CHUNK + 16), 0)
-    col = lax.broadcasted_iota(jnp.int32, (3 * CHUNK, CHUNK + 16), 1)
-    shift = jnp.where(col == row % CHUNK + 13 + row // CHUNK, 1.0, 0.0).astype(BF16)
+    shift = back_shift()
+    nothing = jnp.zeros((16, channels), BF16)
     for at in range(0, rows, CHUNK):
         both = slice(at, at + CHUNK)
         if at == 0:
-            block = jnp.concatenate([before, inputs[both, :]], axis=0)
+            block = jnp.concatenate([nothing, inputs[both, :]], axis=0)
         else:
             block = inputs[at - 16 : at + CHUNK, :]
         moved = dot(shift, block, ((1,), (0,)))
@@ -175,32 +147,105 @@
             preact = preact + taps[k : k + 1, :] * moved[k * CHUNK : (k + 1) * CHUNK, :]
         sigma = 0.5 * jnp.tanh(0.5 * preact) + 0.5
         mixed = preact * sigma
+        scale = spread(far_out[:, both], onehot)
         sigma_out[both, :] = sigma
         mixed_out[both, :] = mixed
-        scaled[both, :] = (mixed * spread(far[:, both], onehot)).astype(BF16)
+        scaled[both, :] = (mixed * scale).astype(BF16)
+        if at == 0:
+            extra[11:14, :] = scale[0:3, :]
     state = dot(b_proj[...], scaled[...], ((0,), (0,))).astype(BF16)
+    extra[2:5, :] = inputs[0:16, :].astype(F32)[0:3, :]
+    extra[5:8, :] = inputs[rows - 16 : rows, :].astype(F32)[13:16, :]
+    extra[8:11, 0:STATE] = b_proj[0:16, :].astype(F32)[0:3, :]
+    for copy in copies[6:]:
+        copy.wait()
+    for at in range(0, rows, STEP_ROWS):
+        both = slice(at, at + STEP_ROWS)
+        scale = spread(front_out[:, both], onehot)
+        scaled[both, :] = (grad[both, :].astype(F32) * scale).astype(BF16)
+    adjoint = dot(c_proj[...], scaled[...], ((0,), (0,))).astype(BF16)
+    me = lax.axis_index("seq")
     for distance in range(1, parts):
         pay = pays[distance - 1]
-        pay[0:STATE, :] = jnp.where(me + distance < parts, state, adjoint_pay[0:STATE, :])
-        pay[STATE : STATE + 16, :] = adjoint_pay[STATE : STATE + 16, :]
-
-
-def merged(parts, pays, forward):
+        pay[0:STATE, :] = jnp.where(me + distance < parts, state, adjoint)
+        pay[STATE : STATE + 16, :] = extra[...].astype(BF16)
+
+
+def back_shift():
+    row = lax.broadcasted_iota(jnp.int32, (3 * CHUNK, CHUNK + 16), 0)
+    col = lax.broadcasted_iota(jnp.int32, (3 * CHUNK, CHUNK + 16), 1)
+    return jnp.where(col == row % CHUNK + 13 + row // CHUNK, 1.0, 0.0).astype(BF16)
+
+
+def tail_rows(pay):
+    return pay[STATE : STATE + 16, :].astype(F32)
+
+
+def first_preact(taps, halo, first):
+    joined = jnp.concatenate([halo[0:3, :], first[0:8, :]], axis=0)
+    preact = taps[0:1, :] * joined[0:8, :]
+    for k in range(1, 4):
+        preact = preact + taps[k : k + 1, :] * joined[k : k + 8, :]
+    return preact
+
+
+def first_change(taps, halo, first):
+    true = first_preact(taps, halo, first)
+    bare = first_preact(taps, jnp.zeros_like(halo), first)
+    change = true * (0.5 * jnp.tanh(0.5 * true) + 0.5) - bare * (0.5 * jnp.tanh(0.5 * bare) + 0.5)
+    row = lax.broadcasted_iota(jnp.int32, change.shape, 0)
+    change = jnp.where(row < 3, change, 0.0)
+    return jnp.concatenate([change, jnp.zeros_like(change)], axis=0)
+
+
+def lane_tiles(channels):
+    return [slice(at, min(at + 128, channels)) for at in range(0, channels, 128)]
+
+
+def merged_adjoint(parts, pays):
     me = lax.axis_index("seq")
     running = jnp.zeros((STATE, pays[0].shape[1]), F32)
     for distance in range(parts - 1, 0, -1):
-        held = pays[distance - 1] if forward else pays[parts - distance - 1]
-        there = (me >= distance) if forward else (me + distance < parts)
-        decay = (
-            held[STATE : STATE + 1, :].astype(F32) + held[STATE + 1 : STATE + 2, :].astype(F32)
-        ) + held[STATE + 2 : STATE + 3, :].astype(F32)
+        held = pays[parts - distance - 1]
+        tail = tail_rows(held)
+        decay = tail[0:1, :] + tail[1:2, :]
+        there = me + distance < parts
         running = jnp.where(there, held[0:STATE, :].astype(F32) + decay * running, 0.0)
     return running.astype(BF16)
 
 
+def own_halo(pays):
+    return jnp.where(lax.axis_index("seq") > 0, tail_rows(pays[0])[5:8, :], 0.0)
+
+
+def merged_state(parts, taps, pays):
+    me = lax.axis_index("seq")
+    channels = pays[0].shape[1]
+    running = jnp.zeros((STATE, channels), F32)
+    tails = [tail_rows(pay) for pay in pays]
+    blank = jnp.zeros((5, channels), F32)
+    for distance in range(parts - 1, 0, -1):
+        held = pays[distance - 1]
+        tail = tails[distance - 1]
+        state = held[0:STATE, :].astype(F32)
+        if distance < parts - 1:
+            halo = jnp.where(me > distance, tails[distance][5:8, :], 0.0)
+            first = jnp.concatenate([tail[2:5, :], blank], axis=0)
+            scale = jnp.concatenate([tail[11:14, :], blank, blank, blank[0:3, :]], axis=0)
+            change = (first_change(taps, halo, first) * scale).astype(BF16)
+            row = lax.broadcasted_iota(jnp.int32, (16, STATE), 0)
+            lines = jnp.concatenate([tail[8:11, 0:STATE], blank[:, 0:STATE]], axis=0)
+            lines = jnp.concatenate([lines, jnp.zeros_like(lines)], axis=0)
+            lines = jnp.where(row < 3, lines, 0.0).astype(BF16)
+            state = state + dot(lines, change, ((0,), (0,)))
+        decay = tail[0:1, :] + tail[1:2, :]
+        running = jnp.where(me >= distance, state + decay * running, 0.0)
+    return running
+
+
 def inner_kernel(
     heads, gains, near, far, logs, grad, mixed, sigma, b_proj, c_proj,
-    base_out, grad_base, grad_weight,
+    base_out, grad_base, grad_weight, first_out,
     ahead_scores, behind_scores, mixed_scaled, mixed_low, grad_scaled, grad_low,
     mixed_fresh, grad_fresh,
 ):
@@ -248,8 +293,12 @@
         )
         slope = sigma[both, :] + mixed[both, :] * (1.0 - sigma[both, :])
         inner = gain * grad[both, :].astype(F32) + spread(near[16:32, both], onehot) * inner
+        weight = spread(far[:, both], onehot)
         grad_base[both, :] = slope * inner
-        grad_weight[both, :] = slope * spread(far[:, both], onehot)
+        grad_weight[both, :] = slope * weight
+        if both.start == 0:
+            first_out[0:8, :] = inner[0:8, :]
+            first_out[8:16, :] = weight[0:8, :]
     for both in blocks:
         inner = dot(
             jnp.concatenate([ahead_scores[both, :], c_proj[both, :]], axis=1),
@@ -259,13 +308,16 @@
         base_out[both, :] = gain * mixed[both, :] + spread(near[0:16, both], onehot) * inner
 
 
-def gradient_kernel(parts, taps, base, weight, inputs, halo, b_proj, *rest):
+def gradient_kernel(parts, taps, base, weight, unscaled, inputs, b_proj, *rest):
     pays = rest[: parts - 1]
     grad_out, tail_out, edge_out, window, exact = rest[parts - 1 :]
     rows, channels = base.shape
     chunks = rows // CHUNK
-    adjoint = merged(parts, pays, False)
-    me = lax.axis_index("seq")
+    adjoint = merged_adjoint(parts, pays)
+    halo = own_halo(pays)
+    preact = first_preact(taps, halo, inputs[0:16, :].astype(F32))
+    sigma = 0.5 * jnp.tanh(0.5 * preact) + 0.5
+    slope = sigma + preact * sigma * (1.0 - sigma)
     window[rows : rows + 16, :] = jnp.zeros((16, channels), BF16)
     row = lax.broadcasted_iota(jnp.int32, (3 * CHUNK, CHUNK + 16), 0)
     col = lax.broadcasted_iota(jnp.int32, (3 * CHUNK, CHUNK + 16), 1)
@@ -273,7 +325,11 @@
     partial = [jnp.zeros((8, channels), F32) for _ in range(4)]
     for j in range(chunks):
         both = slice(j * CHUNK, (j + 1) * CHUNK)
-        grad_pre = base[both, :] + weight[both, :] * dot(b_proj[both, :], adjoint, ((1,), (0,)))
+        carried = dot(b_proj[both, :], adjoint, ((1,), (0,)))
+        grad_pre = base[both, :] + weight[both, :] * carried
+        if j == 0:
+            first = slope * (unscaled[0:8, :] + unscaled[8:16, :] * carried[0:8, :])
+            grad_pre = jnp.concatenate([first, grad_pre[8:, :]], axis=0)
         window[both, :] = grad_pre.astype(BF16)
         exact[both, :] = grad_pre
     for j in range(chunks):
@@ -291,25 +347,37 @@
         grad_out[both, :] = result.astype(BF16)
         if j == chunks - 1:
             edge_out[...] = result[CHUNK - 16 :, :]
-    first = exact[0:8, :]
-    before = jnp.where(me > 0, halo[...].astype(F32), 0.0)
     for k in range(4):
         tap = jnp.sum(partial[k], axis=0, keepdims=True)
         for j in range(k, 3):
-            tap = tap + first[j - k : j - k + 1, :] * before[13 + j : 14 + j, :]
+            tap = tap + first[j - k : j - k + 1, :] * halo[j : j + 1, :]
         tail_out[k : k + 1, :] = tap
     tail_out[4:7, :] = first[0:3, :]
     tail_out[7:8, :] = jnp.zeros((1, channels), F32)
 
 
-def output_kernel(heads, parts, front, base, c_proj, grad_rows, *rest):
+def output_kernel(
+    heads, parts, gains, taps, front, lead, base, inputs, b_proj, c_proj, grad_rows, *rest
+):
     pays = rest[: parts - 1]
     out_hbm, grad_hbm, result_rows, sems, grad_sem = rest[parts - 1 :]
     rows, channels = base.shape
     grad_copy = pltpu.make_async_copy(grad_rows, grad_hbm, grad_sem)
     grad_copy.start()
-    state = merged(parts, pays, True)
+    incoming = merged_state(parts, taps, pays)
     onehot = spread_matrix(heads, channels)
+    change = first_change(taps, own_halo(pays), inputs[0:16, :].astype(F32))
+    change_scaled = (change * lead[...]).astype(BF16)
+    state = incoming + dot(b_proj[0:16, :], change_scaled, ((0,), (0,)))
+    state = state.astype(BF16)
+    row = lax.broadcasted_iota(jnp.int32, (16, 16), 0)
+    col = lax.broadcasted_iota(jnp.int32, (16, 16), 1)
+    scores = dot(c_proj[0:16, :], b_proj[0:16, :], ((1,), (1,)))
+    scores = jnp.where(row >= col, scores, 0.0).astype(BF16)
+    top = dot(c_proj[0:16, :], incoming.astype(BF16), ((1,), (0,)))
+    top = top + dot(scores, change_scaled, ((1,), (0,)))
+    top = top * spread(front[:, 0:16], onehot) + base[0:16, :]
+    top = top + per_lane(gains, heads, channels) * change
     copies = []
     for piece in range(rows // STEP_ROWS):
         for at in range(piece * STEP_ROWS, (piece + 1) * STEP_ROWS, CHUNK):
@@ -317,6 +385,8 @@
             carried = dot(c_proj[both, :], state, ((1,), (0,)))
             result = base[both, :] + spread(front[:, both], onehot) * carried
             result_rows[both, :] = result.astype(BF16)
+            if at == 0:
+                result_rows[0:16, :] = top.astype(BF16)
         place = pl.ds(piece * STEP_ROWS, STEP_ROWS)
         copy = pltpu.make_async_copy(result_rows.at[place], out_hbm.at[place], sems.at[piece])
         copy.start()
@@ -395,61 +465,63 @@
     def stay(array):
         return pltpu.with_memory_space_constraint(array, pltpu.HBM)
 
-    halo = rotated(inputs[rows - 16 :], "seq", 1)
     pay = shape((STATE + 16, channels), BF16)
     narrow = shape((rows, channels), BF16)
     broad = shape((rows, channels), F32)
-
-    near, far, front, logs, adjoint_pay = call(
-        functools.partial(adjoint_kernel, heads),
-        [hbm] * 5,
-        [vmem] * 5,
+    slim = shape((rows, STATE), BF16)
+
+    outs = call(
+        functools.partial(reduce_kernel, heads, parts),
+        [hbm] * 8,
+        [vmem] * (10 + parts),
         [
             shape((32, rows), BF16),
             shape((16, rows), BF16),
             shape((16, rows), BF16),
             shape((3, chunks, channels), F32),
-            pay,
-        ],
+            shape((16, channels), F32),
+            broad,
+            broad,
+            narrow,
+            slim,
+            narrow,
+            slim,
+        ]
+        + [pay] * (parts - 1),
         [
             pltpu.SMEM((heads,), F32),
             pltpu.VMEM((heads, rows), jnp.int32),
             pltpu.VMEM((1, rows), jnp.int32),
+            pltpu.VMEM((4, channels), F32),
+            pltpu.VMEM((8, rows), F32),
             pltpu.VMEM((rows, channels), BF16),
-            pltpu.VMEM((rows, 128), BF16),
-            pltpu.VMEM((8, rows), F32),
-            dma((3,)),
-            dma((pieces,)),
-            dma((pieces,)),
+            pltpu.VMEM((16, CHUNK), BF16),
+            pltpu.VMEM((16, channels), F32),
+            dma((8,)),
         ],
-        2,
+        4,
     )(
         stay(decay_rates),
         stay(step_codes),
         stay(gate_codes.reshape(1, rows)),
+        stay(conv_weight),
+        stay(inputs),
+        stay(b_proj),
         stay(out_cotangent),
         stay(c_proj),
     )
-
-    outs = call(
-        functools.partial(state_kernel, heads, parts),
-        [vmem] * 6,
-        [vmem] * (1 + parts),
-        [broad, broad] + [pay] * (parts - 1),
-        [pltpu.VMEM((rows, channels), BF16)],
-        2,
-    )(conv_weight, far, inputs, halo, b_proj, adjoint_pay)
-    mixed, sigma = outs[:2]
-    pays = [rotated(send, "seq", distance + 1) for distance, send in enumerate(outs[2:])]
+    near, far, front, logs, lead, mixed, sigma = outs[:7]
+    inputs, b_proj, out_cotangent, c_proj = outs[7:11]
+    pays = [rotated(send, "seq", distance + 1) for distance, send in enumerate(outs[11:])]
 
     tile = pltpu.VMEM((rows, CHUNK), BF16)
     low = pltpu.VMEM((rows, channels), BF16)
     high = pltpu.VMEM((rows, channels), F32)
-    base, grad_base, grad_weight = call(
+    base, grad_base, grad_weight, unscaled = call(
         functools.partial(inner_kernel, heads),
         [smem] + [vmem] * 8,
-        [vmem] * 3,
-        [broad] * 3,
+        [vmem] * 4,
+        [broad] * 3 + [shape((16, channels), F32)],
         [tile, tile, low, low, low, low, high, high],
         10,
     )(skip_gain, near, far, logs, out_cotangent, mixed, sigma, b_proj, c_proj)
@@ -461,17 +533,17 @@
         [narrow, shape((8, channels), F32), shape((16, channels), F32)],
         [pltpu.VMEM((rows + 16, channels), BF16), pltpu.VMEM((rows, channels), F32)],
         2,
-    )(conv_weight, grad_base, grad_weight, inputs, halo, b_proj, *pays)
+    )(conv_weight, grad_base, grad_weight, unscaled, inputs, b_proj, *pays)
     tails = [rotated(tail, "seq", distance) for distance in range(1, parts)]
 
     layer_out, grad_rows = call(
         functools.partial(output_kernel, heads, parts),
-        [vmem] * (3 + parts),
+        [smem] + [vmem] * (7 + parts),
         [hbm, hbm],
         [narrow, narrow],
         [pltpu.VMEM((rows, channels), BF16), dma((pieces,)), dma],
         2,
-    )(front, base, c_proj, grad_rows, *pays)
+    )(skip_gain, conv_weight, front, lead, base, inputs, b_proj, c_proj, grad_rows, *pays)
 
     scale = float((rows * parts) ** -0.5)
     input_grad, conv_grad = call(

time: 35.9 us -> 33.3 us (0.928)
  waiting for transfers between devices: 4.61 us -> 2.2 us
  Pallas kernels: 17.8 us -> 18.9 us
  local copies, waits for them, and re-layouts: 0.89 us -> 0.01 us
  starting transfers between devices: 11.5 us -> 11.1 us
    ppermute x7 -> x6, waiting for transfers between devices: 4.61 us -> 2.2 us  [rotated(): lax.ppermute(block, axis, [(i, (i + distance) % size) for i in range(size)])]
    pallas_call x3 -> x2, Pallas kernels: 7.11 us -> 8.27 us  [the longest x1 5.22 us: shards(): call(functools.partial(reduce_kernel, heads, parts), [hbm] * 8, [vmem] *...]
    slice x1 -> x0, local copies, waits for them, and re-layouts: 0.85 us -> none  [shards(): halo = rotated(inputs[rows - 16:], 'seq', 1)]
    ppermute x7 -> x6, starting transfers between devices: 11.5 us -> 11.1 us  [rotated(): lax.ppermute(block, axis, [(i, (i + distance) % size) for i in range(size)])]
  transfers between devices with their start and end apart: 7 -> 6, of which waited for: 3 -> 2; matrix products, arithmetic and copies ran while one was open for 0% -> 0% of each run, Pallas kernels for 31% -> 29%
where the time goes in v6:
time: 33.3 us; the launch traced here: 33.1 us
  Pallas kernels  18.9 us (57%)
  starting transfers between devices  11.1 us (33%)
  waiting for transfers between devices  2.2 us (7%)
  between operations  0.88 us (3%)
    ppermute x6, starting transfers between devices, rotated(): lax.ppermute(block, axis, [(i, (i + distance) % size) for i in range(size)])  11.1 us
    pallas_call x1, Pallas kernels, shards(): call(functools.partial(inner_kernel, heads), [smem] + [vmem] * 8, [vmem]...  6.42 us
    pallas_call x1, Pallas kernels, shards(): call(functools.partial(reduce_kernel, heads, parts), [hbm] * 8, [vmem] *...  5.22 us
    pallas_call x1, Pallas kernels, shards(): call(functools.partial(output_kernel, heads, parts), [smem] + [vmem] * (7...  3.05 us
    pallas_call x1, Pallas kernels, shards(): call(functools.partial(gradient_kernel, parts), [vmem] * (5 + parts), [vm...  3.01 us
    ppermute x6, waiting for transfers between devices, rotated(): lax.ppermute(block, axis, [(i, (i + distance) % size) for i in range(size)])  2.2 us
    pallas_call x1, Pallas kernels, shards(): call(functools.partial(finish_kernel, parts, scale), [vmem] * (2 + parts)...  1.22 us
  transfers between devices with their start and end apart: 6, of which 2 were waited for; matrix products, arithmetic and copies ran while one was open for 0% of the time, Pallas kernels for 29%

profile of v6, /device:TPU:0, one launch (start us, length us, event | category | flops | bytes accessed | tf_op | source)
XLA Modules:
  0.0 33.1 jit_solution(4917573968997242193)
XLA Ops:
  0.6 0.0 copy-start.1
  0.6 5.2 %shard_map.112 = (bf16[32,2048]{1,0:T(8,128)(2,1)S(1)}, bf16[16,2048]{1,0:T(8,128)(2,1)S(1)}, bf16[16,2048]{1,0:T(8,128)(2,1)S(1)}, f32[3,16,384]{2,1,0:T(8,128)...) custom-call(f32[6]{0:T(128)} %rates_hbm.1, ...), custom_call_target="tpu_custom_call" | custom-call | flops 805306368 | bytes 4718592 | tf_op jit(solution)/shard_map/pallas_call | solution.py:473
  5.9 3.1 %collective-permute-start = (bf16[144,384]{1,0:T(8,128)(2,1)S(1)}, bf16[144,384]{1,0:T(8,128)(2,1)S(1)}, u32[]{:S(2)}, u32[]{:S(2)}) collective-permute-start(bf16[144,384]{1,0:T(8,128)(2,1)S(1)} %get-tuple-element.43), channel_id=1, source_target_pairs={{0,4},{4,8},{8,12},{12,0},{1,5},{5,9},{9,13},{13,1},{2,6},{6,10},{... | collective-permute-start | bytes 331784 | tf_op jit(solution)/shard_map/ppermute | solution.py:425
  8.9 2.6 %collective-permute-start.1 = (bf16[144,384]{1,0:T(8,128)(2,1)S(1)}, bf16[144,384]{1,0:T(8,128)(2,1)S(1)}, u32[]{:S(2)}, u32[]{:S(2)}) collective-permute-start(bf16[144,384]{1,0:T(8,128)(2,1)S(1)} %get-tuple-element.44), channel_id=1, source_target_pairs={{0,8},{4,12},{8,0},{12,4},{1,9},{5,13},{9,1},{13,5},{2,10},{6,14},... | collective-permute-start | bytes 331784 | tf_op jit(solution)/shard_map/ppermute | solution.py:425
  11.5 1.3 %collective-permute-start.2 = (bf16[144,384]{1,0:T(8,128)(2,1)S(1)}, bf16[144,384]{1,0:T(8,128)(2,1)S(1)}, u32[]{:S(2)}, u32[]{:S(2)}) collective-permute-start(bf16[144,384]{1,0:T(8,128)(2,1)S(1)} %get-tuple-element.45), channel_id=1, source_target_pairs={{0,12},{4,0},{8,4},{12,8},{1,13},{5,1},{9,5},{13,9},{2,14},{6,2},{... | collective-permute-start | bytes 331784 | tf_op jit(solution)/shard_map/ppermute | solution.py:425
  12.9 0.0 copy-done.1
  12.9 0.0 copy-start
  12.9 6.4 %shard_map.113 = (f32[2048,384]{1,0:T(8,128)S(1)}, f32[2048,384]{1,0:T(8,128)S(1)}, f32[2048,384]{1,0:T(8,128)S(1)}, f32[16,384]{1,0:T(8,128)S(1)}) custom-call(f32[6]{0:T(128)S(1)} %copy-done.1, bf16[32,2048]{1,0:T(8,128)(2,1)S(1)} %get-tuple-element.30.near, bf16[16,2048]{1,0:T(8,128)(2,1)S(1)} %get-tuple-element.31.far, ...), custom_call_target="tpu_custom_call" | custom-call | flops 2013265920 | bytes 4718592 | tf_op jit(solution)/shard_map/pallas_call | solution.py:520
  19.3 0.0 collective-permute-done.rest_0_
  19.3 0.0 collective-permute-done.1.rest_1_
  19.3 0.0 collective-permute-done.2.rest_2_
  19.3 0.0 copy-done
  19.4 3.0 %shard_map.114 = (bf16[2048,384]{1,0:T(8,128)(2,1)S(1)}, f32[8,384]{1,0:T(8,128)S(1)}, f32[16,384]{1,0:T(8,128)S(1)}) custom-call(f32[4,384]{1,0:T(4,128)S(1)} %copy-done, f32[2048,384]{1,0:T(8,128)S(1)} %get-tuple-element.40.base, f32[2048,384]{1,0:T(8,128)S(1)} %get-tuple-element.41.weight, f32[16,384]{1,0:T(8,128)S(1)} %get-tuple-element.42.unscaled, ...), custom_call_target="tpu_custom_call" | custom-call | flops 402653184 | bytes 4718592 | tf_op jit(solution)/shard_map/pallas_call | solution.py:529
  22.4 3.5 %collective-permute-start.5 = (f32[8,384]{1,0:T(8,128)S(1)}, f32[8,384]{1,0:T(8,128)S(1)}, u32[]{:S(2)}, u32[]{:S(2)}) collective-permute-start(f32[8,384]{1,0:T(8,128)S(1)} %get-tuple-element.48.tail), channel_id=1, source_target_pairs={{0,12},{4,0},{8,4},{12,8},{1,13},{5,1},{9,5},{13,9},{2,14},{6,2},{... | collective-permute-start | bytes 36872 | tf_op jit(solution)/shard_map/ppermute | solution.py:425
  25.8 0.4 %collective-permute-start.4 = (f32[8,384]{1,0:T(8,128)S(1)}, f32[8,384]{1,0:T(8,128)S(1)}, u32[]{:S(2)}, u32[]{:S(2)}) collective-permute-start(f32[8,384]{1,0:T(8,128)S(1)} %get-tuple-element.48.tail), channel_id=1, source_target_pairs={{0,8},{4,12},{8,0},{12,4},{1,9},{5,13},{9,1},{13,5},{2,10},{6,14},... | collective-permute-start | bytes 36872 | tf_op jit(solution)/shard_map/ppermute | solution.py:425
  26.2 0.2 collective-permute-start.3
  26.5 3.0 %shard_map.115 = (bf16[2048,384]{1,0:T(8,128)(2,1)}, bf16[2048,384]{1,0:T(8,128)(2,1)}) custom-call(f32[6]{0:T(128)S(1)} %copy-done.1, f32[4,384]{1,0:T(4,128)S(1)} %copy-done, bf16[16,2048]{1,0:T(8,128)(2,1)S(1)} %get-tuple-element.28.front, f32[16,384]{1,0:T(8,128)S(1)} %get-tuple-element.29.lead, f32[2048,384]{1,0:T(8,128)S(1)} %get-tuple-element.38.base, ...), custom_call_target="tpu_custom_call" | custom-call | flops 402653184 | bytes 4718592 | tf_op jit(solution)/shard_map/pallas_call | solution.py:539
  29.5 0.0 collective-permute-done.5.rest_2_
  29.5 0.9 %collective-permute-done.4.rest_1_ = f32[8,384]{1,0:T(8,128)S(1)} collective-permute-done((f32[8,384]{1,0:T(8,128)S(1)}, f32[8,384]{1,0:T(8,128)S(1)}, u32[]{:S(2)}, u32[]{:S(2)}) %collective-permute-start.4) | collective-permute-done | bytes 12320 | tf_op jit(solution)/shard_map/ppermute | solution.py:425
  30.4 1.3 %collective-permute-done.3.rest_0_ = f32[8,384]{1,0:T(8,128)S(1)} collective-permute-done((f32[8,384]{1,0:T(8,128)S(1)}, f32[8,384]{1,0:T(8,128)S(1)}, u32[]{:S(2)}, u32[]{:S(2)}) %collective-permute-start.3) | collective-permute-done | bytes 12320 | tf_op jit(solution)/shard_map/ppermute | solution.py:425
  31.7 1.2 %shard_map.116 = (bf16[2048,384]{1,0:T(8,128)(2,1)}, f32[4,384]{1,0:T(4,128)}) custom-call(f32[4,384]{1,0:T(4,128)S(1)} %copy-done, f32[8,384]{1,0:T(8,128)S(1)} %get-tuple-element.48.tail, f32[16,384]{1,0:T(8,128)S(1)} %get-tuple-element.49.edge, f32[8,384]{1,0:T(8,128)S(1)} %collective-permute-done.3.rest_0_, ...), custom_call_target="tpu_custom_call", output_to_operand_aliasing={{0}: (6, {})} | custom-call | bytes 4718592 | tf_op jit(solution)/shard_map/pallas_call | solution.py:549
Async XLA Ops:
  0.6 12.2 %copy-start.1 = (f32[6]{0:T(128)S(1)}, f32[6]{0:T(128)}, u32[]{:S(2)}) copy-start(f32[6]{0:T(128)} %gains.3) | copy-start | bytes 76
  5.9 13.4 %collective-permute-start = (bf16[144,384]{1,0:T(8,128)(2,1)S(1)}, bf16[144,384]{1,0:T(8,128)(2,1)S(1)}, u32[]{:S(2)}, u32[]{:S(2)}) collective-permute-start(bf16[144,384]{1,0:T(8,128)(2,1)S(1)} %get-tuple-element.43), channel_id=1, source_target_pairs={{0,4},{4,8},{8,12},{12,0},{1,5},{5,9},{9,13},{13,1},{2,6},{6,10},{... | collective-permute-start | bytes 331784 | tf_op jit(solution)/shard_map/ppermute | solution.py:425
  8.9 10.4 %collective-permute-start.1 = (bf16[144,384]{1,0:T(8,128)(2,1)S(1)}, bf16[144,384]{1,0:T(8,128)(2,1)S(1)}, u32[]{:S(2)}, u32[]{:S(2)}) collective-permute-start(bf16[144,384]{1,0:T(8,128)(2,1)S(1)} %get-tuple-element.44), channel_id=1, source_target_pairs={{0,8},{4,12},{8,0},{12,4},{1,9},{5,13},{9,1},{13,5},{2,10},{6,14},... | collective-permute-start | bytes 331784 | tf_op jit(solution)/shard_map/ppermute | solution.py:425
  11.5 7.8 %collective-permute-start.2 = (bf16[144,384]{1,0:T(8,128)(2,1)S(1)}, bf16[144,384]{1,0:T(8,128)(2,1)S(1)}, u32[]{:S(2)}, u32[]{:S(2)}) collective-permute-start(bf16[144,384]{1,0:T(8,128)(2,1)S(1)} %get-tuple-element.45), channel_id=1, source_target_pairs={{0,12},{4,0},{8,4},{12,8},{1,13},{5,1},{9,5},{13,9},{2,14},{6,2},{... | collective-permute-start | bytes 331784 | tf_op jit(solution)/shard_map/ppermute | solution.py:425
  12.9 6.5 %copy-start = (f32[4,384]{1,0:T(4,128)S(1)}, f32[4,384]{1,0:T(4,128)}, u32[]{:S(2)}) copy-start(f32[4,384]{1,0:T(4,128)} %taps.5) | copy-start | bytes 18436
  22.4 7.2 %collective-permute-start.5 = (f32[8,384]{1,0:T(8,128)S(1)}, f32[8,384]{1,0:T(8,128)S(1)}, u32[]{:S(2)}, u32[]{:S(2)}) collective-permute-start(f32[8,384]{1,0:T(8,128)S(1)} %get-tuple-element.48.tail), channel_id=1, source_target_pairs={{0,12},{4,0},{8,4},{12,8},{1,13},{5,1},{9,5},{13,9},{2,14},{6,2},{... | collective-permute-start | bytes 36872 | tf_op jit(solution)/shard_map/ppermute | solution.py:425
  25.8 4.6 %collective-permute-start.4 = (f32[8,384]{1,0:T(8,128)S(1)}, f32[8,384]{1,0:T(8,128)S(1)}, u32[]{:S(2)}, u32[]{:S(2)}) collective-permute-start(f32[8,384]{1,0:T(8,128)S(1)} %get-tuple-element.48.tail), channel_id=1, source_target_pairs={{0,8},{4,12},{8,0},{12,4},{1,9},{5,13},{9,1},{13,5},{2,10},{6,14},... | collective-permute-start | bytes 36872 | tf_op jit(solution)/shard_map/ppermute | solution.py:425
  26.2 5.5 %collective-permute-start.3 = (f32[8,384]{1,0:T(8,128)S(1)}, f32[8,384]{1,0:T(8,128)S(1)}, u32[]{:S(2)}, u32[]{:S(2)}) collective-permute-start(f32[8,384]{1,0:T(8,128)S(1)} %get-tuple-element.48.tail), channel_id=1, source_target_pairs={{0,4},{4,8},{8,12},{12,0},{1,5},{5,9},{9,13},{13,1},{2,6},{6,10},{... | collective-permute-start | bytes 36872 | tf_op jit(solution)/shard_map/ppermute | solution.py:425

commit v7 on v6

--- a/solution.py
+++ b/solution.py
@@ -50,23 +50,26 @@
 
 
 def reduce_kernel(
-    heads, parts, rates_hbm, codes_hbm, gates_hbm, taps_hbm, inputs_hbm, b_hbm, grad_hbm, c_hbm,
-    near_out, far_out, front_out, logs_out, lead_out, mixed_out, sigma_out,
+    heads, parts,
+    rates_hbm, gains_hbm, codes_hbm, gates_hbm, taps_hbm, inputs_hbm, b_hbm, grad_hbm, c_hbm,
+    near_out, far_out, front_out, logs_out, lead_out, gain_out, mixed_out, sigma_out,
     inputs, b_proj, grad, c_proj, *rest
 ):
     pays = rest[: parts - 1]
-    rates, codes, gates, taps, steps, scaled, lead_pair, extra, sems = rest[parts - 1 :]
+    rates, gains, codes, gates, taps, steps, scaled, lead_pair, extra, sems = rest[parts - 1 :]
     rows, channels = grad.shape
     chunks = rows // CHUNK
-    sources = (rates_hbm, codes_hbm, gates_hbm, taps_hbm, inputs_hbm, b_hbm, grad_hbm, c_hbm)
-    targets = (rates, codes, gates, taps, inputs, b_proj, grad, c_proj)
+    sources = (
+        rates_hbm, gains_hbm, codes_hbm, gates_hbm, taps_hbm, inputs_hbm, b_hbm, grad_hbm, c_hbm
+    )
+    targets = (rates, gains, codes, gates, taps, inputs, b_proj, grad, c_proj)
     copies = [
         pltpu.make_async_copy(source, target, sems.at[i])
         for i, (source, target) in enumerate(zip(sources, targets))
     ]
     for copy in copies:
         copy.start()
-    for copy in copies[:3]:
+    for copy in copies[:4]:
         copy.wait()
 
     steps[...] = jnp.zeros_like(steps)
@@ -131,7 +134,8 @@
 
     onehot = spread_matrix(heads, channels)
     lead_out[...] = spread(lead_pair[:, 0:16], onehot)
-    for copy in copies[3:6]:
+    gain_out[...] = jnp.broadcast_to(per_lane(gains, heads, channels), (8, channels))
+    for copy in copies[4:7]:
         copy.wait()
     shift = back_shift()
     nothing = jnp.zeros((16, channels), BF16)
@@ -157,7 +161,7 @@
     extra[2:5, :] = inputs[0:16, :].astype(F32)[0:3, :]
     extra[5:8, :] = inputs[rows - 16 : rows, :].astype(F32)[13:16, :]
     extra[8:11, 0:STATE] = b_proj[0:16, :].astype(F32)[0:3, :]
-    for copy in copies[6:]:
+    for copy in copies[7:]:
         copy.wait()
     for at in range(0, rows, STEP_ROWS):
         both = slice(at, at + STEP_ROWS)
@@ -255,7 +259,7 @@
     row = lax.broadcasted_iota(jnp.int32, (CHUNK, CHUNK), 0)
     col = lax.broadcasted_iota(jnp.int32, (CHUNK, CHUNK), 1)
     onehot = spread_matrix(heads, channels)
-    gain = per_lane(gains, heads, channels)
+    gain = gains[0:1, :]
     for both in blocks:
         scale = spread(near[0:16, both], onehot)
         grad_scaled[both, :] = (grad[both, :].astype(F32) * scale).astype(BF16)
@@ -377,7 +381,7 @@
     top = dot(c_proj[0:16, :], incoming.astype(BF16), ((1,), (0,)))
     top = top + dot(scores, change_scaled, ((1,), (0,)))
     top = top * spread(front[:, 0:16], onehot) + base[0:16, :]
-    top = top + per_lane(gains, heads, channels) * change
+    top = top + gains[0:1, :] * change
     copies = []
     for piece in range(rows // STEP_ROWS):
         for at in range(piece * STEP_ROWS, (piece + 1) * STEP_ROWS, CHUNK):
@@ -443,7 +447,6 @@
     pieces = rows // STEP_ROWS
     hbm = pl.BlockSpec(memory_space=pltpu.HBM)
     vmem = pl.BlockSpec(memory_space=pltpu.VMEM)
-    smem = pl.BlockSpec(memory_space=pltpu.SMEM)
     shape = jax.ShapeDtypeStruct
     dma = pltpu.SemaphoreType.DMA
     big = rows * channels
@@ -472,14 +475,15 @@
 
     outs = call(
         functools.partial(reduce_kernel, heads, parts),
-        [hbm] * 8,
-        [vmem] * (10 + parts),
+        [hbm] * 9,
+        [vmem] * (11 + parts),
         [
             shape((32, rows), BF16),
             shape((16, rows), BF16),
             shape((16, rows), BF16),
             shape((3, chunks, channels), F32),
             shape((16, channels), F32),
+            shape((8, channels), F32),
             broad,
             broad,
             narrow,
@@ -490,6 +494,7 @@
         + [pay] * (parts - 1),
         [
             pltpu.SMEM((heads,), F32),
+            pltpu.SMEM((heads,), F32),
             pltpu.VMEM((heads, rows), jnp.int32),
             pltpu.VMEM((1, rows), jnp.int32),
             pltpu.VMEM((4, channels), F32),
@@ -497,11 +502,12 @@
             pltpu.VMEM((rows, channels), BF16),
             pltpu.VMEM((16, CHUNK), BF16),
             pltpu.VMEM((16, channels), F32),
-            dma((8,)),
+            dma((9,)),
         ],
         4,
     )(
         stay(decay_rates),
+        stay(skip_gain),
         stay(step_codes),
         stay(gate_codes.reshape(1, rows)),
         stay(conv_weight),
@@ -510,21 +516,21 @@
         stay(out_cotangent),
         stay(c_proj),
     )
-    near, far, front, logs, lead, mixed, sigma = outs[:7]
-    inputs, b_proj, out_cotangent, c_proj = outs[7:11]
-    pays = [rotated(send, "seq", distance + 1) for distance, send in enumerate(outs[11:])]
+    near, far, front, logs, lead, gain, mixed, sigma = outs[:8]
+    inputs, b_proj, out_cotangent, c_proj = outs[8:12]
+    pays = [rotated(send, "seq", distance + 1) for distance, send in enumerate(outs[12:])]
 
     tile = pltpu.VMEM((rows, CHUNK), BF16)
     low = pltpu.VMEM((rows, channels), BF16)
     high = pltpu.VMEM((rows, channels), F32)
     base, grad_base, grad_weight, unscaled = call(
         functools.partial(inner_kernel, heads),
-        [smem] + [vmem] * 8,
+        [vmem] * 9,
         [vmem] * 4,
         [broad] * 3 + [shape((16, channels), F32)],
         [tile, tile, low, low, low, low, high, high],
         10,
-    )(skip_gain, near, far, logs, out_cotangent, mixed, sigma, b_proj, c_proj)
+    )(gain, near, far, logs, out_cotangent, mixed, sigma, b_proj, c_proj)
 
     grad_rows, tail, edge = call(
         functools.partial(gradient_kernel, parts),
@@ -538,12 +544,12 @@
 
     layer_out, grad_rows = call(
         functools.partial(output_kernel, heads, parts),
-        [smem] + [vmem] * (7 + parts),
+        [vmem] * (8 + parts),
         [hbm, hbm],
         [narrow, narrow],
         [pltpu.VMEM((rows, channels), BF16), dma((pieces,)), dma],
         2,
-    )(skip_gain, conv_weight, front, lead, base, inputs, b_proj, c_proj, grad_rows, *pays)
+    )(gain, conv_weight, front, lead, base, inputs, b_proj, c_proj, grad_rows, *pays)
 
     scale = float((rows * parts) ** -0.5)
     input_grad, conv_grad = call(

time: 33.3 us -> 33.3 us (level)
  Pallas kernels: 18.9 us -> 17.8 us
  waiting for transfers between devices: 2.2 us -> 2.85 us
  starting transfers between devices: 11.1 us -> 11.6 us
    pallas_call x3, Pallas kernels: 14.7 us -> 13.6 us  [the longest x1 5.84 us: shards(): call(functools.partial(inner_kernel, heads), [vmem] * 9, [vmem] * 4, [bro...]
    ppermute x6, waiting for transfers between devices: 2.2 us -> 2.85 us  [rotated(): lax.ppermute(block, axis, [(i, (i + distance) % size) for i in range(size)])]
    ppermute x6, starting transfers between devices: 11.1 us -> 11.6 us  [rotated(): lax.ppermute(block, axis, [(i, (i + distance) % size) for i in range(size)])]
  transfers between devices with their start and end apart: 6 -> 6, of which waited for: 2 -> 3; matrix products, arithmetic and copies ran while one was open for 0% -> 0% of each run, Pallas kernels for 29% -> 25%
where the time goes in v7:
time: 33.3 us; the launch traced here: 33.1 us
  Pallas kernels  17.8 us (53%)
  starting transfers between devices  11.6 us (35%)
  waiting for transfers between devices  2.85 us (9%)
  between operations  0.85 us (3%)
    ppermute x6, starting transfers between devices, rotated(): lax.ppermute(block, axis, [(i, (i + distance) % size) for i in range(size)])  11.6 us
    pallas_call x1, Pallas kernels, shards(): call(functools.partial(inner_kernel, heads), [vmem] * 9, [vmem] * 4, [bro...  5.84 us
    pallas_call x1, Pallas kernels, shards(): call(functools.partial(reduce_kernel, heads, parts), [hbm] * 9, [vmem] *...  5.22 us
    pallas_call x1, Pallas kernels, shards(): call(functools.partial(gradient_kernel, parts), [vmem] * (5 + parts), [vm...  3.02 us
    ppermute x6, waiting for transfers between devices, rotated(): lax.ppermute(block, axis, [(i, (i + distance) % size) for i in range(size)])  2.85 us
    pallas_call x1, Pallas kernels, shards(): call(functools.partial(output_kernel, heads, parts), [vmem] * (8 + parts)...  2.51 us
    pallas_call x1, Pallas kernels, shards(): call(functools.partial(finish_kernel, parts, scale), [vmem] * (2 + parts)...  1.22 us
  transfers between devices with their start and end apart: 6, of which 3 were waited for; matrix products, arithmetic and copies ran while one was open for 0% of the time, Pallas kernels for 25%

profile of v7, /device:TPU:0, one launch (start us, length us, event | category | flops | bytes accessed | tf_op | source)
XLA Modules:
  0.0 33.1 jit_solution(16734391318240594985)
XLA Ops:
  0.6 5.2 %shard_map.112 = (bf16[32,2048]{1,0:T(8,128)(2,1)S(1)}, bf16[16,2048]{1,0:T(8,128)(2,1)S(1)}, bf16[16,2048]{1,0:T(8,128)(2,1)S(1)}, f32[3,16,384]{2,1,0:T(8,128)...) custom-call(f32[6]{0:T(128)} %rates_hbm.1, ...), custom_call_target="tpu_custom_call" | custom-call | flops 805306368 | bytes 4718592 | tf_op jit(solution)/shard_map/pallas_call | solution.py:476
  5.9 3.1 %collective-permute-start = (bf16[144,384]{1,0:T(8,128)(2,1)S(1)}, bf16[144,384]{1,0:T(8,128)(2,1)S(1)}, u32[]{:S(2)}, u32[]{:S(2)}) collective-permute-start(bf16[144,384]{1,0:T(8,128)(2,1)S(1)} %get-tuple-element.45), channel_id=1, source_target_pairs={{0,4},{4,8},{8,12},{12,0},{1,5},{5,9},{9,13},{13,1},{2,6},{6,10},{... | collective-permute-start | bytes 331784 | tf_op jit(solution)/shard_map/ppermute | solution.py:429
  8.9 2.6 %collective-permute-start.1 = (bf16[144,384]{1,0:T(8,128)(2,1)S(1)}, bf16[144,384]{1,0:T(8,128)(2,1)S(1)}, u32[]{:S(2)}, u32[]{:S(2)}) collective-permute-start(bf16[144,384]{1,0:T(8,128)(2,1)S(1)} %get-tuple-element.46), channel_id=1, source_target_pairs={{0,8},{4,12},{8,0},{12,4},{1,9},{5,13},{9,1},{13,5},{2,10},{6,14},... | collective-permute-start | bytes 331784 | tf_op jit(solution)/shard_map/ppermute | solution.py:429
  11.5 1.3 %collective-permute-start.2 = (bf16[144,384]{1,0:T(8,128)(2,1)S(1)}, bf16[144,384]{1,0:T(8,128)(2,1)S(1)}, u32[]{:S(2)}, u32[]{:S(2)}) collective-permute-start(bf16[144,384]{1,0:T(8,128)(2,1)S(1)} %get-tuple-element.47), channel_id=1, source_target_pairs={{0,12},{4,0},{8,4},{12,8},{1,13},{5,1},{9,5},{13,9},{2,14},{6,2},{... | collective-permute-start | bytes 331784 | tf_op jit(solution)/shard_map/ppermute | solution.py:429
  12.9 0.0 copy-start
  12.9 5.8 %shard_map.113 = (f32[2048,384]{1,0:T(8,128)S(1)}, f32[2048,384]{1,0:T(8,128)S(1)}, f32[2048,384]{1,0:T(8,128)S(1)}, f32[16,384]{1,0:T(8,128)S(1)}) custom-call(f32[8,384]{1,0:T(8,128)S(1)} %get-tuple-element.29.gains, bf16[32,2048]{1,0:T(8,128)(2,1)S(1)} %get-tuple-element.32.near, bf16[16,2048]{1,0:T(8,128)(2,1)S(1)} %get-tuple-element.33.far, ...), custom_call_target="tpu_custom_call" | custom-call | flops 2013265920 | bytes 4718592 | tf_op jit(solution)/shard_map/pallas_call | solution.py:526
  18.7 0.0 collective-permute-done.rest_0_
  18.7 0.1 collective-permute-done.1.rest_1_
  18.9 0.0 collective-permute-done.2.rest_2_
  18.9 0.0 copy-done
  18.9 3.0 %shard_map.114 = (bf16[2048,384]{1,0:T(8,128)(2,1)S(1)}, f32[8,384]{1,0:T(8,128)S(1)}, f32[16,384]{1,0:T(8,128)S(1)}) custom-call(f32[4,384]{1,0:T(4,128)S(1)} %copy-done, f32[2048,384]{1,0:T(8,128)S(1)} %get-tuple-element.42.base, f32[2048,384]{1,0:T(8,128)S(1)} %get-tuple-element.43.weight, f32[16,384]{1,0:T(8,128)S(1)} %get-tuple-element.44.unscaled, ...), custom_call_target="tpu_custom_call" | custom-call | flops 402653184 | bytes 4718592 | tf_op jit(solution)/shard_map/pallas_call | solution.py:535
  21.9 3.9 %collective-permute-start.5 = (f32[8,384]{1,0:T(8,128)S(1)}, f32[8,384]{1,0:T(8,128)S(1)}, u32[]{:S(2)}, u32[]{:S(2)}) collective-permute-start(f32[8,384]{1,0:T(8,128)S(1)} %get-tuple-element.50.tail), channel_id=1, source_target_pairs={{0,12},{4,0},{8,4},{12,8},{1,13},{5,1},{9,5},{13,9},{2,14},{6,2},{... | collective-permute-start | bytes 36872 | tf_op jit(solution)/shard_map/ppermute | solution.py:429
  25.8 0.4 %collective-permute-start.4 = (f32[8,384]{1,0:T(8,128)S(1)}, f32[8,384]{1,0:T(8,128)S(1)}, u32[]{:S(2)}, u32[]{:S(2)}) collective-permute-start(f32[8,384]{1,0:T(8,128)S(1)} %get-tuple-element.50.tail), channel_id=1, source_target_pairs={{0,8},{4,12},{8,0},{12,4},{1,9},{5,13},{9,1},{13,5},{2,10},{6,14},... | collective-permute-start | bytes 36872 | tf_op jit(solution)/shard_map/ppermute | solution.py:429
  26.2 0.2 collective-permute-start.3
  26.5 2.5 %shard_map.115 = (bf16[2048,384]{1,0:T(8,128)(2,1)}, bf16[2048,384]{1,0:T(8,128)(2,1)}) custom-call(f32[8,384]{1,0:T(8,128)S(1)} %get-tuple-element.29.gains, f32[4,384]{1,0:T(4,128)S(1)} %copy-done, bf16[16,2048]{1,0:T(8,128)(2,1)S(1)} %get-tuple-element.30.front, f32[16,384]{1,0:T(8,128)S(1)} %get-tuple-element.31.lead, ...), custom_call_target="tpu_custom_call" | custom-call | flops 402653184 | bytes 4718592 | tf_op jit(solution)/shard_map/pallas_call | solution.py:545
  29.0 0.0 collective-permute-done.5.rest_2_
  29.0 1.4 %collective-permute-done.4.rest_1_ = f32[8,384]{1,0:T(8,128)S(1)} collective-permute-done((f32[8,384]{1,0:T(8,128)S(1)}, f32[8,384]{1,0:T(8,128)S(1)}, u32[]{:S(2)}, u32[]{:S(2)}) %collective-permute-start.4) | collective-permute-done | bytes 12320 | tf_op jit(solution)/shard_map/ppermute | solution.py:429
  30.4 1.3 %collective-permute-done.3.rest_0_ = f32[8,384]{1,0:T(8,128)S(1)} collective-permute-done((f32[8,384]{1,0:T(8,128)S(1)}, f32[8,384]{1,0:T(8,128)S(1)}, u32[]{:S(2)}, u32[]{:S(2)}) %collective-permute-start.3) | collective-permute-done | bytes 12320 | tf_op jit(solution)/shard_map/ppermute | solution.py:429
  31.7 1.2 %shard_map.116 = (bf16[2048,384]{1,0:T(8,128)(2,1)}, f32[4,384]{1,0:T(4,128)}) custom-call(f32[4,384]{1,0:T(4,128)S(1)} %copy-done, f32[8,384]{1,0:T(8,128)S(1)} %get-tuple-element.50.tail, f32[16,384]{1,0:T(8,128)S(1)} %get-tuple-element.51.edge, f32[8,384]{1,0:T(8,128)S(1)} %collective-permute-done.3.rest_0_, ...), custom_call_target="tpu_custom_call", output_to_operand_aliasing={{0}: (6, {})} | custom-call | bytes 4718592 | tf_op jit(solution)/shard_map/pallas_call | solution.py:555
Async XLA Ops:
  5.9 12.9 %collective-permute-start = (bf16[144,384]{1,0:T(8,128)(2,1)S(1)}, bf16[144,384]{1,0:T(8,128)(2,1)S(1)}, u32[]{:S(2)}, u32[]{:S(2)}) collective-permute-start(bf16[144,384]{1,0:T(8,128)(2,1)S(1)} %get-tuple-element.45), channel_id=1, source_target_pairs={{0,4},{4,8},{8,12},{12,0},{1,5},{5,9},{9,13},{13,1},{2,6},{6,10},{... | collective-permute-start | bytes 331784 | tf_op jit(solution)/shard_map/ppermute | solution.py:429
  8.9 9.9 %collective-permute-start.1 = (bf16[144,384]{1,0:T(8,128)(2,1)S(1)}, bf16[144,384]{1,0:T(8,128)(2,1)S(1)}, u32[]{:S(2)}, u32[]{:S(2)}) collective-permute-start(bf16[144,384]{1,0:T(8,128)(2,1)S(1)} %get-tuple-element.46), channel_id=1, source_target_pairs={{0,8},{4,12},{8,0},{12,4},{1,9},{5,13},{9,1},{13,5},{2,10},{6,14},... | collective-permute-start | bytes 331784 | tf_op jit(solution)/shard_map/ppermute | solution.py:429
  11.5 7.3 %collective-permute-start.2 = (bf16[144,384]{1,0:T(8,128)(2,1)S(1)}, bf16[144,384]{1,0:T(8,128)(2,1)S(1)}, u32[]{:S(2)}, u32[]{:S(2)}) collective-permute-start(bf16[144,384]{1,0:T(8,128)(2,1)S(1)} %get-tuple-element.47), channel_id=1, source_target_pairs={{0,12},{4,0},{8,4},{12,8},{1,13},{5,1},{9,5},{13,9},{2,14},{6,2},{... | collective-permute-start | bytes 331784 | tf_op jit(solution)/shard_map/ppermute | solution.py:429
  12.9 6.0 %copy-start = (f32[4,384]{1,0:T(4,128)S(1)}, f32[4,384]{1,0:T(4,128)}, u32[]{:S(2)}) copy-start(f32[4,384]{1,0:T(4,128)} %taps.5) | copy-start | bytes 18436
  21.9 7.1 %collective-permute-start.5 = (f32[8,384]{1,0:T(8,128)S(1)}, f32[8,384]{1,0:T(8,128)S(1)}, u32[]{:S(2)}, u32[]{:S(2)}) collective-permute-start(f32[8,384]{1,0:T(8,128)S(1)} %get-tuple-element.50.tail), channel_id=1, source_target_pairs={{0,12},{4,0},{8,4},{12,8},{1,13},{5,1},{9,5},{13,9},{2,14},{6,2},{... | collective-permute-start | bytes 36872 | tf_op jit(solution)/shard_map/ppermute | solution.py:429
  25.8 4.6 %collective-permute-start.4 = (f32[8,384]{1,0:T(8,128)S(1)}, f32[8,384]{1,0:T(8,128)S(1)}, u32[]{:S(2)}, u32[]{:S(2)}) collective-permute-start(f32[8,384]{1,0:T(8,128)S(1)} %get-tuple-element.50.tail), channel_id=1, source_target_pairs={{0,8},{4,12},{8,0},{12,4},{1,9},{5,13},{9,1},{13,5},{2,10},{6,14},... | collective-permute-start | bytes 36872 | tf_op jit(solution)/shard_map/ppermute | solution.py:429
  26.2 5.5 %collective-permute-start.3 = (f32[8,384]{1,0:T(8,128)S(1)}, f32[8,384]{1,0:T(8,128)S(1)}, u32[]{:S(2)}, u32[]{:S(2)}) collective-permute-start(f32[8,384]{1,0:T(8,128)S(1)} %get-tuple-element.50.tail), channel_id=1, source_target_pairs={{0,4},{4,8},{8,12},{12,0},{1,5},{5,9},{9,13},{13,1},{2,6},{6,10},{... | collective-permute-start | bytes 36872 | tf_op jit(solution)/shard_map/ppermute | solution.py:429

commit v8 on v7

--- a/solution.py
+++ b/solution.py
@@ -9,6 +9,7 @@
 
 CHUNK = 128
 STATE = 128
+PIECES = 4
 STEP_ROWS = 512
 LOG_ONE = -0.2876820724517809
 LOG_TWO = -0.6931471805599453
@@ -63,13 +64,18 @@
         rates_hbm, gains_hbm, codes_hbm, gates_hbm, taps_hbm, inputs_hbm, b_hbm, grad_hbm, c_hbm
     )
     targets = (rates, gains, codes, gates, taps, inputs, b_proj, grad, c_proj)
-    copies = [
-        pltpu.make_async_copy(source, target, sems.at[i])
-        for i, (source, target) in enumerate(zip(sources, targets))
-    ]
-    for copy in copies:
-        copy.start()
-    for copy in copies[:4]:
+    copies = []
+    for i, (source, target) in enumerate(zip(sources, targets)):
+        cuts = PIECES if i in (5, 7) else 1
+        high = source.shape[0] // cuts if cuts > 1 else None
+        parts_of = []
+        for cut in range(cuts):
+            place = pl.ds(cut * high, high) if cuts > 1 else slice(None)
+            copy = pltpu.make_async_copy(source.at[place], target.at[place], sems.at[i, cut])
+            copy.start()
+            parts_of.append(copy)
+        copies.append(parts_of)
+    for copy in sum(copies[:4], []):
         copy.wait()
 
     steps[...] = jnp.zeros_like(steps)
@@ -135,7 +141,7 @@
     onehot = spread_matrix(heads, channels)
     lead_out[...] = spread(lead_pair[:, 0:16], onehot)
     gain_out[...] = jnp.broadcast_to(per_lane(gains, heads, channels), (8, channels))
-    for copy in copies[4:7]:
+    for copy in sum(copies[4:7], []):
         copy.wait()
     shift = back_shift()
     nothing = jnp.zeros((16, channels), BF16)
@@ -161,7 +167,7 @@
     extra[2:5, :] = inputs[0:16, :].astype(F32)[0:3, :]
     extra[5:8, :] = inputs[rows - 16 : rows, :].astype(F32)[13:16, :]
     extra[8:11, 0:STATE] = b_proj[0:16, :].astype(F32)[0:3, :]
-    for copy in copies[7:]:
+    for copy in sum(copies[7:], []):
         copy.wait()
     for at in range(0, rows, STEP_ROWS):
         both = slice(at, at + STEP_ROWS)
@@ -171,7 +177,7 @@
     me = lax.axis_index("seq")
     for distance in range(1, parts):
         pay = pays[distance - 1]
-        pay[0:STATE, :] = jnp.where(me + distance < parts, state, adjoint)
+        pay[0:STATE, :] = jnp.where(partner(me, distance, parts) > me, state, adjoint)
         pay[STATE : STATE + 16, :] = extra[...].astype(BF16)
 
 
@@ -181,8 +187,8 @@
     return jnp.where(col == row % CHUNK + 13 + row // CHUNK, 1.0, 0.0).astype(BF16)
 
 
-def tail_rows(pay):
-    return pay[STATE : STATE + 16, :].astype(F32)
+def tail_rows(held, source):
+    return held[source, STATE : STATE + 16, :].astype(F32)
 
 
 def first_preact(taps, halo, first):
@@ -206,50 +212,64 @@
     return [slice(at, min(at + 128, channels)) for at in range(0, channels, 128)]
 
 
-def merged_adjoint(parts, pays):
+def partner(me, distance, parts):
+    return (me ^ distance) if parts & (parts - 1) == 0 else (me + distance) % parts
+
+
+def sender(me, distance, parts):
+    return (me ^ distance) if parts & (parts - 1) == 0 else (me + parts - distance) % parts
+
+
+def sort_blocks(parts, pays, held):
     me = lax.axis_index("seq")
-    running = jnp.zeros((STATE, pays[0].shape[1]), F32)
-    for distance in range(parts - 1, 0, -1):
-        held = pays[parts - distance - 1]
-        tail = tail_rows(held)
+    held[me] = jnp.zeros(held.shape[1:], BF16)
+    for distance in range(1, parts):
+        held[sender(me, distance, parts)] = pays[distance - 1][...]
+
+
+def merged_adjoint(parts, held):
+    me = lax.axis_index("seq")
+    running = jnp.zeros((STATE, held.shape[2]), F32)
+    for source in range(parts - 1, 0, -1):
+        tail = tail_rows(held, source)
         decay = tail[0:1, :] + tail[1:2, :]
-        there = me + distance < parts
-        running = jnp.where(there, held[0:STATE, :].astype(F32) + decay * running, 0.0)
+        block = held[source, 0:STATE, :].astype(F32)
+        running = jnp.where(source > me, block + decay * running, running)
     return running.astype(BF16)
 
 
-def own_halo(pays):
-    return jnp.where(lax.axis_index("seq") > 0, tail_rows(pays[0])[5:8, :], 0.0)
-
-
-def merged_state(parts, taps, pays):
+def own_halo(held):
     me = lax.axis_index("seq")
-    channels = pays[0].shape[1]
+    return jnp.where(me > 0, tail_rows(held, jnp.maximum(me - 1, 0))[5:8, :], 0.0)
+
+
+def merged_state(parts, taps, held):
+    me = lax.axis_index("seq")
+    channels = held.shape[2]
     running = jnp.zeros((STATE, channels), F32)
-    tails = [tail_rows(pay) for pay in pays]
     blank = jnp.zeros((5, channels), F32)
-    for distance in range(parts - 1, 0, -1):
-        held = pays[distance - 1]
-        tail = tails[distance - 1]
-        state = held[0:STATE, :].astype(F32)
-        if distance < parts - 1:
-            halo = jnp.where(me > distance, tails[distance][5:8, :], 0.0)
+    tails = [tail_rows(held, source) for source in range(parts - 1)]
+    for source in range(parts - 1):
+        tail = tails[source]
+        state = held[source, 0:STATE, :].astype(F32)
+        if source > 0:
             first = jnp.concatenate([tail[2:5, :], blank], axis=0)
             scale = jnp.concatenate([tail[11:14, :], blank, blank, blank[0:3, :]], axis=0)
-            change = (first_change(taps, halo, first) * scale).astype(BF16)
+            change = first_change(taps, tails[source - 1][5:8, :], first)
+            change = (change * scale).astype(BF16)
             row = lax.broadcasted_iota(jnp.int32, (16, STATE), 0)
             lines = jnp.concatenate([tail[8:11, 0:STATE], blank[:, 0:STATE]], axis=0)
             lines = jnp.concatenate([lines, jnp.zeros_like(lines)], axis=0)
             lines = jnp.where(row < 3, lines, 0.0).astype(BF16)
             state = state + dot(lines, change, ((0,), (0,)))
         decay = tail[0:1, :] + tail[1:2, :]
-        running = jnp.where(me >= distance, state + decay * running, 0.0)
+        running = jnp.where(source < me, state + decay * running, running)
     return running
 
 
 def inner_kernel(
     heads, gains, near, far, logs, grad, mixed, sigma, b_proj, c_proj,
-    base_out, grad_base, grad_weight, first_out,
+    inputs, base_out, grad_base, grad_weight, first_out, moved_out,
     ahead_scores, behind_scores, mixed_scaled, mixed_low, grad_scaled, grad_low,
     mixed_fresh, grad_fresh,
 ):
@@ -310,23 +330,30 @@
             ((1,), (0,)),
         )
         base_out[both, :] = gain * mixed[both, :] + spread(near[0:16, both], onehot) * inner
-
-
-def gradient_kernel(parts, taps, base, weight, unscaled, inputs, b_proj, *rest):
+    shift = back_shift()
+    for both in blocks:
+        if both.start == 0:
+            nothing = jnp.zeros((16, channels), BF16)
+            block = jnp.concatenate([nothing, inputs[both, :]], axis=0)
+        else:
+            block = inputs[both.start - 16 : both.stop, :]
+        moved = dot(shift, block, ((1,), (0,)))
+        for k in range(3):
+            moved_out[k, both, :] = moved[k * CHUNK : (k + 1) * CHUNK, :].astype(BF16)
+
+
+def gradient_kernel(parts, taps, base, weight, unscaled, inputs, moved, b_proj, *rest):
     pays = rest[: parts - 1]
-    grad_out, tail_out, edge_out, window, exact = rest[parts - 1 :]
+    exact, window, tail_out, held, products = rest[parts - 1 :]
     rows, channels = base.shape
     chunks = rows // CHUNK
-    adjoint = merged_adjoint(parts, pays)
-    halo = own_halo(pays)
+    sort_blocks(parts, pays, held)
+    adjoint = merged_adjoint(parts, held)
+    halo = own_halo(held)
     preact = first_preact(taps, halo, inputs[0:16, :].astype(F32))
     sigma = 0.5 * jnp.tanh(0.5 * preact) + 0.5
     slope = sigma + preact * sigma * (1.0 - sigma)
     window[rows : rows + 16, :] = jnp.zeros((16, channels), BF16)
-    row = lax.broadcasted_iota(jnp.int32, (3 * CHUNK, CHUNK + 16), 0)
-    col = lax.broadcasted_iota(jnp.int32, (3 * CHUNK, CHUNK + 16), 1)
-    shift = jnp.where(col == row % CHUNK + 3 - row // CHUNK, 1.0, 0.0).astype(BF16)
-    partial = [jnp.zeros((8, channels), F32) for _ in range(4)]
     for j in range(chunks):
         both = slice(j * CHUNK, (j + 1) * CHUNK)
         carried = dot(b_proj[both, :], adjoint, ((1,), (0,)))
@@ -334,25 +361,15 @@
         if j == 0:
             first = slope * (unscaled[0:8, :] + unscaled[8:16, :] * carried[0:8, :])
             grad_pre = jnp.concatenate([first, grad_pre[8:, :]], axis=0)
-        window[both, :] = grad_pre.astype(BF16)
         exact[both, :] = grad_pre
-    for j in range(chunks):
-        at = j * CHUNK
-        both = slice(at, at + CHUNK)
-        grad_pre = exact[both, :]
-        moved = dot(shift, window[at : at + CHUNK + 16, :], ((1,), (0,)))
-        x = inputs[both, :].astype(F32)
-        result = taps[3:4, :] * grad_pre
-        partial[3] = partial[3] + (grad_pre * x).reshape(CHUNK // 8, 8, channels).sum(axis=0)
+        low = grad_pre.astype(BF16)
+        window[both, :] = low
         for k in range(3):
-            part = moved[k * CHUNK : (k + 1) * CHUNK, :]
-            result = result + taps[k : k + 1, :] * part
-            partial[k] = partial[k] + (part * x).reshape(CHUNK // 8, 8, channels).sum(axis=0)
-        grad_out[both, :] = result.astype(BF16)
-        if j == chunks - 1:
-            edge_out[...] = result[CHUNK - 16 :, :]
+            products[k, both, :] = low * moved[k, both, :]
+        products[3, both, :] = low * inputs[both, :]
+    ones = jnp.ones((8, rows), BF16)
     for k in range(4):
-        tap = jnp.sum(partial[k], axis=0, keepdims=True)
+        tap = dot(ones, products[k], ((1,), (0,)))[0:1, :]
         for j in range(k, 3):
             tap = tap + first[j - k : j - k + 1, :] * halo[j : j + 1, :]
         tail_out[k : k + 1, :] = tap
@@ -361,16 +378,15 @@
 
 
 def output_kernel(
-    heads, parts, gains, taps, front, lead, base, inputs, b_proj, c_proj, grad_rows, *rest
+    heads, parts, gains, taps, front, lead, base, inputs, b_proj, c_proj, exact, window, *rest
 ):
     pays = rest[: parts - 1]
-    out_hbm, grad_hbm, result_rows, sems, grad_sem = rest[parts - 1 :]
+    out_hbm, grad_hbm, edge_out, held, result_rows, grad_rows, sems, grad_sems = rest[parts - 1 :]
     rows, channels = base.shape
-    grad_copy = pltpu.make_async_copy(grad_rows, grad_hbm, grad_sem)
-    grad_copy.start()
-    incoming = merged_state(parts, taps, pays)
+    sort_blocks(parts, pays, held)
+    incoming = merged_state(parts, taps, held)
     onehot = spread_matrix(heads, channels)
-    change = first_change(taps, own_halo(pays), inputs[0:16, :].astype(F32))
+    change = first_change(taps, own_halo(held), inputs[0:16, :].astype(F32))
     change_scaled = (change * lead[...]).astype(BF16)
     state = incoming + dot(b_proj[0:16, :], change_scaled, ((0,), (0,)))
     state = state.astype(BF16)
@@ -382,10 +398,20 @@
     top = top + dot(scores, change_scaled, ((1,), (0,)))
     top = top * spread(front[:, 0:16], onehot) + base[0:16, :]
     top = top + gains[0:1, :] * change
+    row = lax.broadcasted_iota(jnp.int32, (3 * CHUNK, CHUNK + 16), 0)
+    col = lax.broadcasted_iota(jnp.int32, (3 * CHUNK, CHUNK + 16), 1)
+    shift = jnp.where(col == row % CHUNK + 3 - row // CHUNK, 1.0, 0.0).astype(BF16)
     copies = []
     for piece in range(rows // STEP_ROWS):
         for at in range(piece * STEP_ROWS, (piece + 1) * STEP_ROWS, CHUNK):
             both = slice(at, at + CHUNK)
+            moved = dot(shift, window[at : at + CHUNK + 16, :], ((1,), (0,)))
+            result = taps[3:4, :] * exact[both, :]
+            for k in range(3):
+                result = result + taps[k : k + 1, :] * moved[k * CHUNK : (k + 1) * CHUNK, :]
+            grad_rows[both, :] = result.astype(BF16)
+            if at + CHUNK == rows:
+                edge_out[...] = result[CHUNK - 16 :, :]
             carried = dot(c_proj[both, :], state, ((1,), (0,)))
             result = base[both, :] + spread(front[:, both], onehot) * carried
             result_rows[both, :] = result.astype(BF16)
@@ -395,9 +421,13 @@
         copy = pltpu.make_async_copy(result_rows.at[place], out_hbm.at[place], sems.at[piece])
         copy.start()
         copies.append(copy)
+        copy = pltpu.make_async_copy(
+            grad_rows.at[place], grad_hbm.at[place], grad_sems.at[piece]
+        )
+        copy.start()
+        copies.append(copy)
     for copy in copies:
         copy.wait()
-    grad_copy.wait()
 
 
 def finish_kernel(parts, scale, taps, tail, edge, *rest):
@@ -405,7 +435,10 @@
     unused, grad_hbm, conv_out, rows_low, sem = rest[parts - 1 :]
     channels = tail.shape[1]
     me = lax.axis_index("seq")
-    after = jnp.where(me + 1 < parts, others[parts - 2][...], 0.0)
+    after = jnp.zeros(tail.shape, F32)
+    for distance in range(1, parts):
+        here = sender(me, distance, parts) == me + 1
+        after = jnp.where(here, others[distance - 1][...], after)
     row = lax.broadcasted_iota(jnp.int32, (16, channels), 0)
     result = edge[...]
     for r in range(3):
@@ -426,7 +459,7 @@
 
 def rotated(block, axis, distance):
     size = lax.axis_size(axis)
-    return lax.ppermute(block, axis, [(i, (i + distance) % size) for i in range(size)])
+    return lax.ppermute(block, axis, [(i, partner(i, distance, size)) for i in range(size)])
 
 
 def shards(
@@ -502,7 +535,7 @@
             pltpu.VMEM((rows, channels), BF16),
             pltpu.VMEM((16, CHUNK), BF16),
             pltpu.VMEM((16, channels), F32),
-            dma((9,)),
+            dma((9, PIECES)),
         ],
         4,
     )(
@@ -523,33 +556,34 @@
     tile = pltpu.VMEM((rows, CHUNK), BF16)
     low = pltpu.VMEM((rows, channels), BF16)
     high = pltpu.VMEM((rows, channels), F32)
-    base, grad_base, grad_weight, unscaled = call(
+    base, grad_base, grad_weight, unscaled, moved = call(
         functools.partial(inner_kernel, heads),
-        [vmem] * 9,
-        [vmem] * 4,
-        [broad] * 3 + [shape((16, channels), F32)],
+        [vmem] * 10,
+        [vmem] * 5,
+        [broad] * 3 + [shape((16, channels), F32), shape((3, rows, channels), BF16)],
         [tile, tile, low, low, low, low, high, high],
         10,
-    )(gain, near, far, logs, out_cotangent, mixed, sigma, b_proj, c_proj)
-
-    grad_rows, tail, edge = call(
+    )(gain, near, far, logs, out_cotangent, mixed, sigma, b_proj, c_proj, inputs)
+
+    held = pltpu.VMEM((parts, STATE + 16, channels), BF16)
+    exact, window, tail = call(
         functools.partial(gradient_kernel, parts),
-        [vmem] * (5 + parts),
+        [vmem] * (6 + parts),
         [vmem] * 3,
-        [narrow, shape((8, channels), F32), shape((16, channels), F32)],
-        [pltpu.VMEM((rows + 16, channels), BF16), pltpu.VMEM((rows, channels), F32)],
+        [broad, shape((rows + 16, channels), BF16), shape((8, channels), F32)],
+        [held, pltpu.VMEM((4, rows, channels), BF16)],
         2,
-    )(conv_weight, grad_base, grad_weight, unscaled, inputs, b_proj, *pays)
+    )(conv_weight, grad_base, grad_weight, unscaled, inputs, moved, b_proj, *pays)
     tails = [rotated(tail, "seq", distance) for distance in range(1, parts)]
 
-    layer_out, grad_rows = call(
+    layer_out, grad_rows, edge = call(
         functools.partial(output_kernel, heads, parts),
-        [vmem] * (8 + parts),
-        [hbm, hbm],
-        [narrow, narrow],
-        [pltpu.VMEM((rows, channels), BF16), dma((pieces,)), dma],
-        2,
-    )(gain, conv_weight, front, lead, base, inputs, b_proj, c_proj, grad_rows, *pays)
+        [vmem] * (9 + parts),
+        [hbm, hbm, vmem],
+        [narrow, narrow, shape((16, channels), F32)],
+        [held, low, low, dma((pieces,)), dma((pieces,))],
+        4,
+    )(gain, conv_weight, front, lead, base, inputs, b_proj, c_proj, exact, window, *pays)
 
     scale = float((rows * parts) ** -0.5)
     input_grad, conv_grad = call(

time: 33.3 us -> 33.1 us (level)
  Pallas kernels: 17.8 us -> 20.7 us
  waiting for transfers between devices: 2.85 us -> 1.29 us
  starting transfers between devices: 11.6 us -> 10.1 us
    pallas_call x3, Pallas kernels: 11.4 us -> 14 us  [the longest x1 7.45 us: shards(): call(functools.partial(inner_kernel, heads), [vmem] * 10, [vmem] * 5, [br...]
    ppermute x6, waiting for transfers between devices: 2.85 us -> 1.29 us  [rotated(): lax.ppermute(block, axis, [(i, partner(i, distance, size)) for i in range...]
    ppermute x6, starting transfers between devices: 11.6 us -> 10.1 us  [rotated(): lax.ppermute(block, axis, [(i, partner(i, distance, size)) for i in range...]
  transfers between devices with their start and end apart: 6 -> 6, of which waited for: 3 -> 1; matrix products, arithmetic and copies ran while one was open for 0% -> 0% of each run, Pallas kernels for 25% -> 35%
where the time goes in v8:
time: 33.1 us; the launch traced here: 33 us
  Pallas kernels  20.7 us (63%)
  starting transfers between devices  10.1 us (31%)
  waiting for transfers between devices  1.29 us (4%)
  between operations  0.85 us (3%)
    ppermute x6, starting transfers between devices, rotated(): lax.ppermute(block, axis, [(i, partner(i, distance, size)) for i in range...  10.1 us
    pallas_call x1, Pallas kernels, shards(): call(functools.partial(inner_kernel, heads), [vmem] * 10, [vmem] * 5, [br...  7.45 us
    pallas_call x1, Pallas kernels, shards(): call(functools.partial(reduce_kernel, heads, parts), [hbm] * 9, [vmem] *...  5.48 us
    pallas_call x1, Pallas kernels, shards(): call(functools.partial(output_kernel, heads, parts), [vmem] * (9 + parts)...  4.01 us
    pallas_call x1, Pallas kernels, shards(): call(functools.partial(gradient_kernel, parts), [vmem] * (6 + parts), [vm...  2.54 us
    ppermute x6, waiting for transfers between devices, rotated(): lax.ppermute(block, axis, [(i, partner(i, distance, size)) for i in range...  1.29 us
    pallas_call x1, Pallas kernels, shards(): call(functools.partial(finish_kernel, parts, scale), [vmem] * (2 + parts)...  1.23 us
  transfers between devices with their start and end apart: 6, of which 1 were waited for; matrix products, arithmetic and copies ran while one was open for 0% of the time, Pallas kernels for 35%

profile of v8, /device:TPU:0, one launch (start us, length us, event | category | flops | bytes accessed | tf_op | source)
XLA Modules:
  0.0 33.0 jit_solution(16225062707650960338)
XLA Ops:
  0.6 5.5 %shard_map.112 = (bf16[32,2048]{1,0:T(8,128)(2,1)S(1)}, bf16[16,2048]{1,0:T(8,128)(2,1)S(1)}, bf16[16,2048]{1,0:T(8,128)(2,1)S(1)}, f32[3,16,384]{2,1,0:T(8,128)...) custom-call(f32[6]{0:T(128)} %rates_hbm.1, ...), custom_call_target="tpu_custom_call" | custom-call | flops 805306368 | bytes 4718592 | tf_op jit(solution)/shard_map/pallas_call | solution.py:509
  6.1 3.1 %collective-permute-start = (bf16[144,384]{1,0:T(8,128)(2,1)S(1)}, bf16[144,384]{1,0:T(8,128)(2,1)S(1)}, u32[]{:S(2)}, u32[]{:S(2)}) collective-permute-start(bf16[144,384]{1,0:T(8,128)(2,1)S(1)} %get-tuple-element.48), channel_id=1, source_target_pairs={{0,4},{4,0},{8,12},{12,8},{1,5},{5,1},{9,13},{13,9},{2,6},{6,2},{1... | collective-permute-start | bytes 331784 | tf_op jit(solution)/shard_map/ppermute | solution.py:462
  9.2 2.6 %collective-permute-start.1 = (bf16[144,384]{1,0:T(8,128)(2,1)S(1)}, bf16[144,384]{1,0:T(8,128)(2,1)S(1)}, u32[]{:S(2)}, u32[]{:S(2)}) collective-permute-start(bf16[144,384]{1,0:T(8,128)(2,1)S(1)} %get-tuple-element.49), channel_id=1, source_target_pairs={{0,8},{4,12},{8,0},{12,4},{1,9},{5,13},{9,1},{13,5},{2,10},{6,14},... | collective-permute-start | bytes 331784 | tf_op jit(solution)/shard_map/ppermute | solution.py:462
  11.8 0.0 collective-permute-start.2
  11.8 0.0 copy-start
  11.8 7.4 %shard_map.113 = (f32[2048,384]{1,0:T(8,128)S(1)}, f32[2048,384]{1,0:T(8,128)S(1)}, f32[2048,384]{1,0:T(8,128)S(1)}, f32[16,384]{1,0:T(8,128)S(1)}, bf16[3,2048,384]{2,1,0:T(8,128)(2,1)S(1)}) custom-call(f32[8,384]{1,0:T(8,128)S(1)} %get-tuple-element.31.gains, bf16[32,2048]{1,0:T(8,128)(2,1)S(1)} %get-tuple-element.34.near, ...), custom_call_target="tpu_custom_call" | custom-call | flops 2013265920 | bytes 4718592 | tf_op jit(solution)/shard_map/pallas_call | solution.py:559
  19.3 0.0 collective-permute-done.rest_0_
  19.3 1.3 %collective-permute-done.1.rest_1_ = bf16[144,384]{1,0:T(8,128)(2,1)S(1)} collective-permute-done((bf16[144,384]{1,0:T(8,128)(2,1)S(1)}, bf16[144,384]{1,0:T(8,128)(2,1)S(1)}, u32[]{:S(2)}, u32[]{:S(2)}) %collective-permute-start.1) | collective-permute-done | bytes 110624 | tf_op jit(solution)/shard_map/ppermute | solution.py:462
  20.6 0.0 collective-permute-done.2.rest_2_
  20.6 0.0 copy-done
  20.6 2.5 %shard_map.114 = (f32[2048,384]{1,0:T(8,128)S(1)}, bf16[2064,384]{1,0:T(8,128)(2,1)S(1)}, f32[8,384]{1,0:T(8,128)S(1)}) custom-call(f32[4,384]{1,0:T(4,128)S(1)} %copy-done, f32[2048,384]{1,0:T(8,128)S(1)} %get-tuple-element.44.base, f32[2048,384]{1,0:T(8,128)S(1)} %get-tuple-element.45.weight, f32[16,384]{1,0:T(8,128)S(1)} %get-tuple-element.46.unscaled, ...), custom_call_target="tpu_custom_call" | custom-call | flops 402653184 | bytes 4718592 | tf_op jit(solution)/shard_map/pallas_call | solution.py:569
  23.1 2.6 %collective-permute-start.5 = (f32[8,384]{1,0:T(8,128)S(1)}, f32[8,384]{1,0:T(8,128)S(1)}, u32[]{:S(2)}, u32[]{:S(2)}) collective-permute-start(f32[8,384]{1,0:T(8,128)S(1)} %get-tuple-element.54.tail), channel_id=1, source_target_pairs={{0,12},{4,8},{8,4},{12,0},{1,13},{5,9},{9,5},{13,1},{2,14},{6,10},... | collective-permute-start | bytes 36872 | tf_op jit(solution)/shard_map/ppermute | solution.py:462
  25.7 0.6 %collective-permute-start.4 = (f32[8,384]{1,0:T(8,128)S(1)}, f32[8,384]{1,0:T(8,128)S(1)}, u32[]{:S(2)}, u32[]{:S(2)}) collective-permute-start(f32[8,384]{1,0:T(8,128)S(1)} %get-tuple-element.54.tail), channel_id=1, source_target_pairs={{0,8},{4,12},{8,0},{12,4},{1,9},{5,13},{9,1},{13,5},{2,10},{6,14},... | collective-permute-start | bytes 36872 | tf_op jit(solution)/shard_map/ppermute | solution.py:462
  26.3 1.2 %collective-permute-start.3 = (f32[8,384]{1,0:T(8,128)S(1)}, f32[8,384]{1,0:T(8,128)S(1)}, u32[]{:S(2)}, u32[]{:S(2)}) collective-permute-start(f32[8,384]{1,0:T(8,128)S(1)} %get-tuple-element.54.tail), channel_id=1, source_target_pairs={{0,4},{4,0},{8,12},{12,8},{1,5},{5,1},{9,13},{13,9},{2,6},{6,2},{1... | collective-permute-start | bytes 36872 | tf_op jit(solution)/shard_map/ppermute | solution.py:462
  27.5 4.0 %shard_map.115 = (bf16[2048,384]{1,0:T(8,128)(2,1)}, bf16[2048,384]{1,0:T(8,128)(2,1)}, f32[16,384]{1,0:T(8,128)S(1)}) custom-call(f32[8,384]{1,0:T(8,128)S(1)} %get-tuple-element.31.gains, f32[4,384]{1,0:T(4,128)S(1)} %copy-done, bf16[16,2048]{1,0:T(8,128)(2,1)S(1)} %get-tuple-element.32.front, f32[16,384]{1,0:T(8,128)S(1)} %get-tuple-element.33.lead, ...), custom_call_target="tpu_custom_call" | custom-call | flops 805306368 | bytes 4718592 | tf_op jit(solution)/shard_map/pallas_call | solution.py:579
  31.5 0.0 collective-permute-done.5.rest_2_
  31.5 0.0 collective-permute-done.4.rest_1_
  31.5 0.0 collective-permute-done.3.rest_0_
  31.6 1.2 %shard_map.116 = (bf16[2048,384]{1,0:T(8,128)(2,1)}, f32[4,384]{1,0:T(4,128)}) custom-call(f32[4,384]{1,0:T(4,128)S(1)} %copy-done, f32[8,384]{1,0:T(8,128)S(1)} %get-tuple-element.54.tail, f32[16,384]{1,0:T(8,128)S(1)} %get-tuple-element.55.edge, f32[8,384]{1,0:T(8,128)S(1)} %collective-permute-done.3.rest_0_, ...), custom_call_target="tpu_custom_call", output_to_operand_aliasing={{0}: (6, {})} | custom-call | bytes 4718592 | tf_op jit(solution)/shard_map/pallas_call | solution.py:589
Async XLA Ops:
  6.1 13.1 %collective-permute-start = (bf16[144,384]{1,0:T(8,128)(2,1)S(1)}, bf16[144,384]{1,0:T(8,128)(2,1)S(1)}, u32[]{:S(2)}, u32[]{:S(2)}) collective-permute-start(bf16[144,384]{1,0:T(8,128)(2,1)S(1)} %get-tuple-element.48), channel_id=1, source_target_pairs={{0,4},{4,0},{8,12},{12,8},{1,5},{5,1},{9,13},{13,9},{2,6},{6,2},{1... | collective-permute-start | bytes 331784 | tf_op jit(solution)/shard_map/ppermute | solution.py:462
  9.2 11.3 %collective-permute-start.1 = (bf16[144,384]{1,0:T(8,128)(2,1)S(1)}, bf16[144,384]{1,0:T(8,128)(2,1)S(1)}, u32[]{:S(2)}, u32[]{:S(2)}) collective-permute-start(bf16[144,384]{1,0:T(8,128)(2,1)S(1)} %get-tuple-element.49), channel_id=1, source_target_pairs={{0,8},{4,12},{8,0},{12,4},{1,9},{5,13},{9,1},{13,5},{2,10},{6,14},... | collective-permute-start | bytes 331784 | tf_op jit(solution)/shard_map/ppermute | solution.py:462
  11.8 8.8 %collective-permute-start.2 = (bf16[144,384]{1,0:T(8,128)(2,1)S(1)}, bf16[144,384]{1,0:T(8,128)(2,1)S(1)}, u32[]{:S(2)}, u32[]{:S(2)}) collective-permute-start(bf16[144,384]{1,0:T(8,128)(2,1)S(1)} %get-tuple-element.50), channel_id=1, source_target_pairs={{0,12},{4,8},{8,4},{12,0},{1,13},{5,9},{9,5},{13,1},{2,14},{6,10},... | collective-permute-start | bytes 331784 | tf_op jit(solution)/shard_map/ppermute | solution.py:462
  11.8 8.8 %copy-start = (f32[4,384]{1,0:T(4,128)S(1)}, f32[4,384]{1,0:T(4,128)}, u32[]{:S(2)}) copy-start(f32[4,384]{1,0:T(4,128)} %taps.5) | copy-start | bytes 18436
  23.1 8.4 %collective-permute-start.5 = (f32[8,384]{1,0:T(8,128)S(1)}, f32[8,384]{1,0:T(8,128)S(1)}, u32[]{:S(2)}, u32[]{:S(2)}) collective-permute-start(f32[8,384]{1,0:T(8,128)S(1)} %get-tuple-element.54.tail), channel_id=1, source_target_pairs={{0,12},{4,8},{8,4},{12,0},{1,13},{5,9},{9,5},{13,1},{2,14},{6,10},... | collective-permute-start | bytes 36872 | tf_op jit(solution)/shard_map/ppermute | solution.py:462
  25.7 5.9 %collective-permute-start.4 = (f32[8,384]{1,0:T(8,128)S(1)}, f32[8,384]{1,0:T(8,128)S(1)}, u32[]{:S(2)}, u32[]{:S(2)}) collective-permute-start(f32[8,384]{1,0:T(8,128)S(1)} %get-tuple-element.54.tail), channel_id=1, source_target_pairs={{0,8},{4,12},{8,0},{12,4},{1,9},{5,13},{9,1},{13,5},{2,10},{6,14},... | collective-permute-start | bytes 36872 | tf_op jit(solution)/shard_map/ppermute | solution.py:462
  26.3 5.2 %collective-permute-start.3 = (f32[8,384]{1,0:T(8,128)S(1)}, f32[8,384]{1,0:T(8,128)S(1)}, u32[]{:S(2)}, u32[]{:S(2)}) collective-permute-start(f32[8,384]{1,0:T(8,128)S(1)} %get-tuple-element.54.tail), channel_id=1, source_target_pairs={{0,4},{4,0},{8,12},{12,8},{1,5},{5,1},{9,13},{13,9},{2,6},{6,2},{1... | collective-permute-start | bytes 36872 | tf_op jit(solution)/shard_map/ppermute | solution.py:462

commit v9 on v8

--- a/solution.py
+++ b/solution.py
@@ -9,7 +9,6 @@
 
 CHUNK = 128
 STATE = 128
-PIECES = 4
 STEP_ROWS = 512
 LOG_ONE = -0.2876820724517809
 LOG_TWO = -0.6931471805599453
@@ -39,11 +38,17 @@
     return jnp.concatenate([high.astype(F32), low.astype(F32)], axis=0).astype(BF16)
 
 
+def head_of(lane, width):
+    if width & (width - 1) == 0:
+        return lane >> (width.bit_length() - 1)
+    return lane // width
+
+
 def spread_matrix(count, channels):
     width = channels // count
     row = lax.broadcasted_iota(jnp.int32, (16, channels), 0)
     lane = lax.broadcasted_iota(jnp.int32, (16, channels), 1)
-    return jnp.where((row % 8) == lane // width, 1.0, 0.0).astype(BF16)
+    return jnp.where((row & 7) == head_of(lane, width), 1.0, 0.0).astype(BF16)
 
 
 def spread(pair, onehot):
@@ -64,18 +69,13 @@
         rates_hbm, gains_hbm, codes_hbm, gates_hbm, taps_hbm, inputs_hbm, b_hbm, grad_hbm, c_hbm
     )
     targets = (rates, gains, codes, gates, taps, inputs, b_proj, grad, c_proj)
-    copies = []
-    for i, (source, target) in enumerate(zip(sources, targets)):
-        cuts = PIECES if i in (5, 7) else 1
-        high = source.shape[0] // cuts if cuts > 1 else None
-        parts_of = []
-        for cut in range(cuts):
-            place = pl.ds(cut * high, high) if cuts > 1 else slice(None)
-            copy = pltpu.make_async_copy(source.at[place], target.at[place], sems.at[i, cut])
-            copy.start()
-            parts_of.append(copy)
-        copies.append(parts_of)
-    for copy in sum(copies[:4], []):
+    copies = [
+        pltpu.make_async_copy(source, target, sems.at[i])
+        for i, (source, target) in enumerate(zip(sources, targets))
+    ]
+    for copy in copies:
+        copy.start()
+    for copy in copies[:4]:
         copy.wait()
 
     steps[...] = jnp.zeros_like(steps)
@@ -115,11 +115,12 @@
     place = lax.broadcasted_iota(jnp.int32, (8, CHUNK), 1)
     chosen = jnp.where((pick == 0) | ((pick == 1) & (place < CHUNK // 2)), 1.0, 0.0)
     flat = dot(chosen.astype(BF16), stacked, ((1,), (1,)))
-    owner = lax.broadcasted_iota(jnp.int32, (chunks, 8 * chunks), 1) // 8
+    owner = lax.broadcasted_iota(jnp.int32, (chunks, 8 * chunks), 1) >> 3
     chunk_at = lax.broadcasted_iota(jnp.int32, (chunks, 8 * chunks), 0)
     lane_rate = per_lane(rates, heads, channels)
-    kind = lax.broadcasted_iota(jnp.int32, (8 * chunks, channels), 0) % 8
-    lane_head = lax.broadcasted_iota(jnp.int32, (8 * chunks, channels), 1) // (channels // heads)
+    kind = lax.broadcasted_iota(jnp.int32, (8 * chunks, channels), 0) & 7
+    lane = lax.broadcasted_iota(jnp.int32, (8 * chunks, channels), 1)
+    lane_head = head_of(lane, channels // heads)
     mixer = jnp.where(kind == lane_head, -lane_rate, 0.0)
     mixer = jnp.where(kind == 6, LOG_ONE, jnp.where(kind == 7, LOG_TWO, mixer))
     table = []
@@ -141,7 +142,7 @@
     onehot = spread_matrix(heads, channels)
     lead_out[...] = spread(lead_pair[:, 0:16], onehot)
     gain_out[...] = jnp.broadcast_to(per_lane(gains, heads, channels), (8, channels))
-    for copy in sum(copies[4:7], []):
+    for copy in copies[4:7]:
         copy.wait()
     shift = back_shift()
     nothing = jnp.zeros((16, channels), BF16)
@@ -167,7 +168,7 @@
     extra[2:5, :] = inputs[0:16, :].astype(F32)[0:3, :]
     extra[5:8, :] = inputs[rows - 16 : rows, :].astype(F32)[13:16, :]
     extra[8:11, 0:STATE] = b_proj[0:16, :].astype(F32)[0:3, :]
-    for copy in sum(copies[7:], []):
+    for copy in copies[7:]:
         copy.wait()
     for at in range(0, rows, STEP_ROWS):
         both = slice(at, at + STEP_ROWS)
@@ -184,7 +185,8 @@
 def back_shift():
     row = lax.broadcasted_iota(jnp.int32, (3 * CHUNK, CHUNK + 16), 0)
     col = lax.broadcasted_iota(jnp.int32, (3 * CHUNK, CHUNK + 16), 1)
-    return jnp.where(col == row % CHUNK + 13 + row // CHUNK, 1.0, 0.0).astype(BF16)
+    at = (row & (CHUNK - 1)) + 13 + (row >> 7)
+    return jnp.where(col == at, 1.0, 0.0).astype(BF16)
 
 
 def tail_rows(held, source):
@@ -400,7 +402,7 @@
     top = top + gains[0:1, :] * change
     row = lax.broadcasted_iota(jnp.int32, (3 * CHUNK, CHUNK + 16), 0)
     col = lax.broadcasted_iota(jnp.int32, (3 * CHUNK, CHUNK + 16), 1)
-    shift = jnp.where(col == row % CHUNK + 3 - row // CHUNK, 1.0, 0.0).astype(BF16)
+    shift = jnp.where(col == (row & (CHUNK - 1)) + 3 - (row >> 7), 1.0, 0.0).astype(BF16)
     copies = []
     for piece in range(rows // STEP_ROWS):
         for at in range(piece * STEP_ROWS, (piece + 1) * STEP_ROWS, CHUNK):
@@ -535,7 +537,7 @@
             pltpu.VMEM((rows, channels), BF16),
             pltpu.VMEM((16, CHUNK), BF16),
             pltpu.VMEM((16, channels), F32),
-            dma((9, PIECES)),
+            dma((9,)),
         ],
         4,
     )(

time: 33.1 us -> 32.9 us (level)
  no operation moved by 1% of the time
where the time goes in v9:
time: 32.9 us; the launch traced here: 32.7 us
  Pallas kernels  20.5 us (62%)
  starting transfers between devices  10.1 us (31%)
  waiting for transfers between devices  1.29 us (4%)
  between operations  0.85 us (3%)
    ppermute x6, starting transfers between devices, rotated(): lax.ppermute(block, axis, [(i, partner(i, distance, size)) for i in range...  10.1 us
    pallas_call x1, Pallas kernels, shards(): call(functools.partial(inner_kernel, heads), [vmem] * 10, [vmem] * 5, [br...  7.45 us
    pallas_call x1, Pallas kernels, shards(): call(functools.partial(reduce_kernel, heads, parts), [hbm] * 9, [vmem] *...  5.24 us
    pallas_call x1, Pallas kernels, shards(): call(functools.partial(output_kernel, heads, parts), [vmem] * (9 + parts)...  4.01 us
    pallas_call x1, Pallas kernels, shards(): call(functools.partial(gradient_kernel, parts), [vmem] * (6 + parts), [vm...  2.54 us
    ppermute x6, waiting for transfers between devices, rotated(): lax.ppermute(block, axis, [(i, partner(i, distance, size)) for i in range...  1.29 us
    pallas_call x1, Pallas kernels, shards(): call(functools.partial(finish_kernel, parts, scale), [vmem] * (2 + parts)...  1.23 us
  transfers between devices with their start and end apart: 6, of which 1 were waited for; matrix products, arithmetic and copies ran while one was open for 0% of the time, Pallas kernels for 35%

profile of v9, /device:TPU:0, one launch (start us, length us, event | category | flops | bytes accessed | tf_op | source)
XLA Modules:
  0.0 32.7 jit_solution(15153858692128509365)
XLA Ops:
  0.6 5.2 %shard_map.112 = (bf16[32,2048]{1,0:T(8,128)(2,1)S(1)}, bf16[16,2048]{1,0:T(8,128)(2,1)S(1)}, bf16[16,2048]{1,0:T(8,128)(2,1)S(1)}, f32[3,16,384]{2,1,0:T(8,128)...) custom-call(f32[6]{0:T(128)} %rates_hbm.1, ...), custom_call_target="tpu_custom_call" | custom-call | flops 805306368 | bytes 4718592 | tf_op jit(solution)/shard_map/pallas_call | solution.py:511
  5.9 3.1 %collective-permute-start = (bf16[144,384]{1,0:T(8,128)(2,1)S(1)}, bf16[144,384]{1,0:T(8,128)(2,1)S(1)}, u32[]{:S(2)}, u32[]{:S(2)}) collective-permute-start(bf16[144,384]{1,0:T(8,128)(2,1)S(1)} %get-tuple-element.48), channel_id=1, source_target_pairs={{0,4},{4,0},{8,12},{12,8},{1,5},{5,1},{9,13},{13,9},{2,6},{6,2},{1... | collective-permute-start | bytes 331784 | tf_op jit(solution)/shard_map/ppermute | solution.py:464
  9.0 2.6 %collective-permute-start.1 = (bf16[144,384]{1,0:T(8,128)(2,1)S(1)}, bf16[144,384]{1,0:T(8,128)(2,1)S(1)}, u32[]{:S(2)}, u32[]{:S(2)}) collective-permute-start(bf16[144,384]{1,0:T(8,128)(2,1)S(1)} %get-tuple-element.49), channel_id=1, source_target_pairs={{0,8},{4,12},{8,0},{12,4},{1,9},{5,13},{9,1},{13,5},{2,10},{6,14},... | collective-permute-start | bytes 331784 | tf_op jit(solution)/shard_map/ppermute | solution.py:464
  11.6 0.0 collective-permute-start.2
  11.6 0.0 copy-start
  11.6 7.5 %shard_map.113 = (f32[2048,384]{1,0:T(8,128)S(1)}, f32[2048,384]{1,0:T(8,128)S(1)}, f32[2048,384]{1,0:T(8,128)S(1)}, f32[16,384]{1,0:T(8,128)S(1)}, bf16[3,2048,384]{2,1,0:T(8,128)(2,1)S(1)}) custom-call(f32[8,384]{1,0:T(8,128)S(1)} %get-tuple-element.31.gains, bf16[32,2048]{1,0:T(8,128)(2,1)S(1)} %get-tuple-element.34.near, ...), custom_call_target="tpu_custom_call" | custom-call | flops 2013265920 | bytes 4718592 | tf_op jit(solution)/shard_map/pallas_call | solution.py:561
  19.0 0.0 collective-permute-done.rest_0_
  19.0 1.3 %collective-permute-done.1.rest_1_ = bf16[144,384]{1,0:T(8,128)(2,1)S(1)} collective-permute-done((bf16[144,384]{1,0:T(8,128)(2,1)S(1)}, bf16[144,384]{1,0:T(8,128)(2,1)S(1)}, u32[]{:S(2)}, u32[]{:S(2)}) %collective-permute-start.1) | collective-permute-done | bytes 110624 | tf_op jit(solution)/shard_map/ppermute | solution.py:464
  20.3 0.0 collective-permute-done.2.rest_2_
  20.3 0.0 copy-done
  20.3 2.5 %shard_map.114 = (f32[2048,384]{1,0:T(8,128)S(1)}, bf16[2064,384]{1,0:T(8,128)(2,1)S(1)}, f32[8,384]{1,0:T(8,128)S(1)}) custom-call(f32[4,384]{1,0:T(4,128)S(1)} %copy-done, f32[2048,384]{1,0:T(8,128)S(1)} %get-tuple-element.44.base, f32[2048,384]{1,0:T(8,128)S(1)} %get-tuple-element.45.weight, f32[16,384]{1,0:T(8,128)S(1)} %get-tuple-element.46.unscaled, ...), custom_call_target="tpu_custom_call" | custom-call | flops 402653184 | bytes 4718592 | tf_op jit(solution)/shard_map/pallas_call | solution.py:571
  22.9 2.6 %collective-permute-start.5 = (f32[8,384]{1,0:T(8,128)S(1)}, f32[8,384]{1,0:T(8,128)S(1)}, u32[]{:S(2)}, u32[]{:S(2)}) collective-permute-start(f32[8,384]{1,0:T(8,128)S(1)} %get-tuple-element.54.tail), channel_id=1, source_target_pairs={{0,12},{4,8},{8,4},{12,0},{1,13},{5,9},{9,5},{13,1},{2,14},{6,10},... | collective-permute-start | bytes 36872 | tf_op jit(solution)/shard_map/ppermute | solution.py:464
  25.5 0.6 %collective-permute-start.4 = (f32[8,384]{1,0:T(8,128)S(1)}, f32[8,384]{1,0:T(8,128)S(1)}, u32[]{:S(2)}, u32[]{:S(2)}) collective-permute-start(f32[8,384]{1,0:T(8,128)S(1)} %get-tuple-element.54.tail), channel_id=1, source_target_pairs={{0,8},{4,12},{8,0},{12,4},{1,9},{5,13},{9,1},{13,5},{2,10},{6,14},... | collective-permute-start | bytes 36872 | tf_op jit(solution)/shard_map/ppermute | solution.py:464
  26.1 1.2 %collective-permute-start.3 = (f32[8,384]{1,0:T(8,128)S(1)}, f32[8,384]{1,0:T(8,128)S(1)}, u32[]{:S(2)}, u32[]{:S(2)}) collective-permute-start(f32[8,384]{1,0:T(8,128)S(1)} %get-tuple-element.54.tail), channel_id=1, source_target_pairs={{0,4},{4,0},{8,12},{12,8},{1,5},{5,1},{9,13},{13,9},{2,6},{6,2},{1... | collective-permute-start | bytes 36872 | tf_op jit(solution)/shard_map/ppermute | solution.py:464
  27.3 4.0 %shard_map.115 = (bf16[2048,384]{1,0:T(8,128)(2,1)}, bf16[2048,384]{1,0:T(8,128)(2,1)}, f32[16,384]{1,0:T(8,128)S(1)}) custom-call(f32[8,384]{1,0:T(8,128)S(1)} %get-tuple-element.31.gains, f32[4,384]{1,0:T(4,128)S(1)} %copy-done, bf16[16,2048]{1,0:T(8,128)(2,1)S(1)} %get-tuple-element.32.front, f32[16,384]{1,0:T(8,128)S(1)} %get-tuple-element.33.lead, ...), custom_call_target="tpu_custom_call" | custom-call | flops 805306368 | bytes 4718592 | tf_op jit(solution)/shard_map/pallas_call | solution.py:581
  31.3 0.0 collective-permute-done.5.rest_2_
  31.3 0.0 collective-permute-done.4.rest_1_
  31.3 0.0 collective-permute-done.3.rest_0_
  31.3 1.2 %shard_map.116 = (bf16[2048,384]{1,0:T(8,128)(2,1)}, f32[4,384]{1,0:T(4,128)}) custom-call(f32[4,384]{1,0:T(4,128)S(1)} %copy-done, f32[8,384]{1,0:T(8,128)S(1)} %get-tuple-element.54.tail, f32[16,384]{1,0:T(8,128)S(1)} %get-tuple-element.55.edge, f32[8,384]{1,0:T(8,128)S(1)} %collective-permute-done.3.rest_0_, ...), custom_call_target="tpu_custom_call", output_to_operand_aliasing={{0}: (6, {})} | custom-call | bytes 4718592 | tf_op jit(solution)/shard_map/pallas_call | solution.py:591
Async XLA Ops:
  5.9 13.2 %collective-permute-start = (bf16[144,384]{1,0:T(8,128)(2,1)S(1)}, bf16[144,384]{1,0:T(8,128)(2,1)S(1)}, u32[]{:S(2)}, u32[]{:S(2)}) collective-permute-start(bf16[144,384]{1,0:T(8,128)(2,1)S(1)} %get-tuple-element.48), channel_id=1, source_target_pairs={{0,4},{4,0},{8,12},{12,8},{1,5},{5,1},{9,13},{13,9},{2,6},{6,2},{1... | collective-permute-start | bytes 331784 | tf_op jit(solution)/shard_map/ppermute | solution.py:464
  9.0 11.3 %collective-permute-start.1 = (bf16[144,384]{1,0:T(8,128)(2,1)S(1)}, bf16[144,384]{1,0:T(8,128)(2,1)S(1)}, u32[]{:S(2)}, u32[]{:S(2)}) collective-permute-start(bf16[144,384]{1,0:T(8,128)(2,1)S(1)} %get-tuple-element.49), channel_id=1, source_target_pairs={{0,8},{4,12},{8,0},{12,4},{1,9},{5,13},{9,1},{13,5},{2,10},{6,14},... | collective-permute-start | bytes 331784 | tf_op jit(solution)/shard_map/ppermute | solution.py:464
  11.6 8.8 %collective-permute-start.2 = (bf16[144,384]{1,0:T(8,128)(2,1)S(1)}, bf16[144,384]{1,0:T(8,128)(2,1)S(1)}, u32[]{:S(2)}, u32[]{:S(2)}) collective-permute-start(bf16[144,384]{1,0:T(8,128)(2,1)S(1)} %get-tuple-element.50), channel_id=1, source_target_pairs={{0,12},{4,8},{8,4},{12,0},{1,13},{5,9},{9,5},{13,1},{2,14},{6,10},... | collective-permute-start | bytes 331784 | tf_op jit(solution)/shard_map/ppermute | solution.py:464
  11.6 8.8 %copy-start = (f32[4,384]{1,0:T(4,128)S(1)}, f32[4,384]{1,0:T(4,128)}, u32[]{:S(2)}) copy-start(f32[4,384]{1,0:T(4,128)} %taps.5) | copy-start | bytes 18436
  22.9 8.4 %collective-permute-start.5 = (f32[8,384]{1,0:T(8,128)S(1)}, f32[8,384]{1,0:T(8,128)S(1)}, u32[]{:S(2)}, u32[]{:S(2)}) collective-permute-start(f32[8,384]{1,0:T(8,128)S(1)} %get-tuple-element.54.tail), channel_id=1, source_target_pairs={{0,12},{4,8},{8,4},{12,0},{1,13},{5,9},{9,5},{13,1},{2,14},{6,10},... | collective-permute-start | bytes 36872 | tf_op jit(solution)/shard_map/ppermute | solution.py:464
  25.5 5.9 %collective-permute-start.4 = (f32[8,384]{1,0:T(8,128)S(1)}, f32[8,384]{1,0:T(8,128)S(1)}, u32[]{:S(2)}, u32[]{:S(2)}) collective-permute-start(f32[8,384]{1,0:T(8,128)S(1)} %get-tuple-element.54.tail), channel_id=1, source_target_pairs={{0,8},{4,12},{8,0},{12,4},{1,9},{5,13},{9,1},{13,5},{2,10},{6,14},... | collective-permute-start | bytes 36872 | tf_op jit(solution)/shard_map/ppermute | solution.py:464
  26.1 5.2 %collective-permute-start.3 = (f32[8,384]{1,0:T(8,128)S(1)}, f32[8,384]{1,0:T(8,128)S(1)}, u32[]{:S(2)}, u32[]{:S(2)}) collective-permute-start(f32[8,384]{1,0:T(8,128)S(1)} %get-tuple-element.54.tail), channel_id=1, source_target_pairs={{0,4},{4,0},{8,12},{12,8},{1,5},{5,1},{9,13},{13,9},{2,6},{6,2},{1... | collective-permute-start | bytes 36872 | tf_op jit(solution)/shard_map/ppermute | solution.py:464

commit v10 on v9

--- a/solution.py
+++ b/solution.py
@@ -271,7 +271,7 @@
 
 def inner_kernel(
     heads, gains, near, far, logs, grad, mixed, sigma, b_proj, c_proj,
-    inputs, base_out, grad_base, grad_weight, first_out, moved_out,
+    base_out, grad_base, grad_weight, first_out,
     ahead_scores, behind_scores, mixed_scaled, mixed_low, grad_scaled, grad_low,
     mixed_fresh, grad_fresh,
 ):
@@ -332,21 +332,11 @@
             ((1,), (0,)),
         )
         base_out[both, :] = gain * mixed[both, :] + spread(near[0:16, both], onehot) * inner
-    shift = back_shift()
-    for both in blocks:
-        if both.start == 0:
-            nothing = jnp.zeros((16, channels), BF16)
-            block = jnp.concatenate([nothing, inputs[both, :]], axis=0)
-        else:
-            block = inputs[both.start - 16 : both.stop, :]
-        moved = dot(shift, block, ((1,), (0,)))
-        for k in range(3):
-            moved_out[k, both, :] = moved[k * CHUNK : (k + 1) * CHUNK, :].astype(BF16)
-
-
-def gradient_kernel(parts, taps, base, weight, unscaled, inputs, moved, b_proj, *rest):
+
+
+def gradient_kernel(parts, taps, base, weight, unscaled, inputs, b_proj, *rest):
     pays = rest[: parts - 1]
-    exact, window, tail_out, held, products = rest[parts - 1 :]
+    grad_out, tail_out, edge_out, window, exact, held = rest[parts - 1 :]
     rows, channels = base.shape
     chunks = rows // CHUNK
     sort_blocks(parts, pays, held)
@@ -356,6 +346,10 @@
     sigma = 0.5 * jnp.tanh(0.5 * preact) + 0.5
     slope = sigma + preact * sigma * (1.0 - sigma)
     window[rows : rows + 16, :] = jnp.zeros((16, channels), BF16)
+    row = lax.broadcasted_iota(jnp.int32, (3 * CHUNK, CHUNK + 16), 0)
+    col = lax.broadcasted_iota(jnp.int32, (3 * CHUNK, CHUNK + 16), 1)
+    shift = jnp.where(col == (row & (CHUNK - 1)) + 3 - (row >> 7), 1.0, 0.0).astype(BF16)
+    partial = [jnp.zeros((8, channels), F32) for _ in range(4)]
     for j in range(chunks):
         both = slice(j * CHUNK, (j + 1) * CHUNK)
         carried = dot(b_proj[both, :], adjoint, ((1,), (0,)))
@@ -363,15 +357,25 @@
         if j == 0:
             first = slope * (unscaled[0:8, :] + unscaled[8:16, :] * carried[0:8, :])
             grad_pre = jnp.concatenate([first, grad_pre[8:, :]], axis=0)
+        window[both, :] = grad_pre.astype(BF16)
         exact[both, :] = grad_pre
-        low = grad_pre.astype(BF16)
-        window[both, :] = low
+    for j in range(chunks):
+        at = j * CHUNK
+        both = slice(at, at + CHUNK)
+        grad_pre = exact[both, :]
+        moved = dot(shift, window[at : at + CHUNK + 16, :], ((1,), (0,)))
+        x = inputs[both, :].astype(F32)
+        result = taps[3:4, :] * grad_pre
+        partial[3] = partial[3] + (grad_pre * x).reshape(CHUNK // 8, 8, channels).sum(axis=0)
         for k in range(3):
-            products[k, both, :] = low * moved[k, both, :]
-        products[3, both, :] = low * inputs[both, :]
-    ones = jnp.ones((8, rows), BF16)
+            part = moved[k * CHUNK : (k + 1) * CHUNK, :]
+            result = result + taps[k : k + 1, :] * part
+            partial[k] = partial[k] + (part * x).reshape(CHUNK // 8, 8, channels).sum(axis=0)
+        grad_out[both, :] = result.astype(BF16)
+        if j == chunks - 1:
+            edge_out[...] = result[CHUNK - 16 :, :]
     for k in range(4):
-        tap = dot(ones, products[k], ((1,), (0,)))[0:1, :]
+        tap = jnp.sum(partial[k], axis=0, keepdims=True)
         for j in range(k, 3):
             tap = tap + first[j - k : j - k + 1, :] * halo[j : j + 1, :]
         tail_out[k : k + 1, :] = tap
@@ -380,11 +384,13 @@
 
 
 def output_kernel(
-    heads, parts, gains, taps, front, lead, base, inputs, b_proj, c_proj, exact, window, *rest
+    heads, parts, gains, taps, front, lead, base, inputs, b_proj, c_proj, grad_rows, *rest
 ):
     pays = rest[: parts - 1]
-    out_hbm, grad_hbm, edge_out, held, result_rows, grad_rows, sems, grad_sems = rest[parts - 1 :]
+    out_hbm, grad_hbm, held, result_rows, sems, grad_sem = rest[parts - 1 :]
     rows, channels = base.shape
+    grad_copy = pltpu.make_async_copy(grad_rows, grad_hbm, grad_sem)
+    grad_copy.start()
     sort_blocks(parts, pays, held)
     incoming = merged_state(parts, taps, held)
     onehot = spread_matrix(heads, channels)
@@ -400,20 +406,10 @@
     top = top + dot(scores, change_scaled, ((1,), (0,)))
     top = top * spread(front[:, 0:16], onehot) + base[0:16, :]
     top = top + gains[0:1, :] * change
-    row = lax.broadcasted_iota(jnp.int32, (3 * CHUNK, CHUNK + 16), 0)
-    col = lax.broadcasted_iota(jnp.int32, (3 * CHUNK, CHUNK + 16), 1)
-    shift = jnp.where(col == (row & (CHUNK - 1)) + 3 - (row >> 7), 1.0, 0.0).astype(BF16)
     copies = []
     for piece in range(rows // STEP_ROWS):
         for at in range(piece * STEP_ROWS, (piece + 1) * STEP_ROWS, CHUNK):
             both = slice(at, at + CHUNK)
-            moved = dot(shift, window[at : at + CHUNK + 16, :], ((1,), (0,)))
-            result = taps[3:4, :] * exact[both, :]
-            for k in range(3):
-                result = result + taps[k : k + 1, :] * moved[k * CHUNK : (k + 1) * CHUNK, :]
-            grad_rows[both, :] = result.astype(BF16)
-            if at + CHUNK == rows:
-                edge_out[...] = result[CHUNK - 16 :, :]
             carried = dot(c_proj[both, :], state, ((1,), (0,)))
             result = base[both, :] + spread(front[:, both], onehot) * carried
             result_rows[both, :] = result.astype(BF16)
@@ -423,13 +419,9 @@
         copy = pltpu.make_async_copy(result_rows.at[place], out_hbm.at[place], sems.at[piece])
         copy.start()
         copies.append(copy)
-        copy = pltpu.make_async_copy(
-            grad_rows.at[place], grad_hbm.at[place], grad_sems.at[piece]
-        )
-        copy.start()
-        copies.append(copy)
     for copy in copies:
         copy.wait()
+    grad_copy.wait()
 
 
 def finish_kernel(parts, scale, taps, tail, edge, *rest):
@@ -558,34 +550,34 @@
     tile = pltpu.VMEM((rows, CHUNK), BF16)
     low = pltpu.VMEM((rows, channels), BF16)
     high = pltpu.VMEM((rows, channels), F32)
-    base, grad_base, grad_weight, unscaled, moved = call(
+    base, grad_base, grad_weight, unscaled = call(
         functools.partial(inner_kernel, heads),
-        [vmem] * 10,
-        [vmem] * 5,
-        [broad] * 3 + [shape((16, channels), F32), shape((3, rows, channels), BF16)],
+        [vmem] * 9,
+        [vmem] * 4,
+        [broad] * 3 + [shape((16, channels), F32)],
         [tile, tile, low, low, low, low, high, high],
         10,
-    )(gain, near, far, logs, out_cotangent, mixed, sigma, b_proj, c_proj, inputs)
+    )(gain, near, far, logs, out_cotangent, mixed, sigma, b_proj, c_proj)
 
     held = pltpu.VMEM((parts, STATE + 16, channels), BF16)
-    exact, window, tail = call(
+    grad_rows, tail, edge = call(
         functools.partial(gradient_kernel, parts),
-        [vmem] * (6 + parts),
+        [vmem] * (5 + parts),
         [vmem] * 3,
-        [broad, shape((rows + 16, channels), BF16), shape((8, channels), F32)],
-        [held, pltpu.VMEM((4, rows, channels), BF16)],
+        [narrow, shape((8, channels), F32), shape((16, channels), F32)],
+        [pltpu.VMEM((rows + 16, channels), BF16), high, held],
         2,
-    )(conv_weight, grad_base, grad_weight, unscaled, inputs, moved, b_proj, *pays)
+    )(conv_weight, grad_base, grad_weight, unscaled, inputs, b_proj, *pays)
     tails = [rotated(tail, "seq", distance) for distance in range(1, parts)]
 
-    layer_out, grad_rows, edge = call(
+    layer_out, grad_rows = call(
         functools.partial(output_kernel, heads, parts),
-        [vmem] * (9 + parts),
-        [hbm, hbm, vmem],
-        [narrow, narrow, shape((16, channels), F32)],
-        [held, low, low, dma((pieces,)), dma((pieces,))],
-        4,
-    )(gain, conv_weight, front, lead, base, inputs, b_proj, c_proj, exact, window, *pays)
+        [vmem] * (8 + parts),
+        [hbm, hbm],
+        [narrow, narrow],
+        [held, low, dma((pieces,)), dma],
+        2,
+    )(gain, conv_weight, front, lead, base, inputs, b_proj, c_proj, grad_rows, *pays)
 
     scale = float((rows * parts) ** -0.5)
     input_grad, conv_grad = call(

time: 32.9 us -> 31.9 us (0.970)
  Pallas kernels: 20.5 us -> 17.9 us
  waiting for transfers between devices: 1.29 us -> 3.05 us
    pallas_call x3, Pallas kernels: 14 us -> 11.4 us  [the longest x1 5.83 us: shards(): call(functools.partial(inner_kernel, heads), [vmem] * 9, [vmem] * 4, [bro...]
    ppermute x6, waiting for transfers between devices: 1.29 us -> 3.05 us  [rotated(): lax.ppermute(block, axis, [(i, partner(i, distance, size)) for i in range...]
  transfers between devices with their start and end apart: 6 -> 6, of which waited for: 1 -> 2; matrix products, arithmetic and copies ran while one was open for 0% -> 0% of each run, Pallas kernels for 35% -> 26%
where the time goes in v10:
time: 31.9 us; the launch traced here: 31.8 us
  Pallas kernels  17.9 us (56%)
  starting transfers between devices  10.1 us (32%)
  waiting for transfers between devices  3.05 us (10%)
  between operations  0.68 us (2%)
    ppermute x6, starting transfers between devices, rotated(): lax.ppermute(block, axis, [(i, partner(i, distance, size)) for i in range...  10.1 us
    pallas_call x1, Pallas kernels, shards(): call(functools.partial(inner_kernel, heads), [vmem] * 9, [vmem] * 4, [bro...  5.83 us
    pallas_call x1, Pallas kernels, shards(): call(functools.partial(reduce_kernel, heads, parts), [hbm] * 9, [vmem] *...  5.25 us
    ppermute x6, waiting for transfers between devices, rotated(): lax.ppermute(block, axis, [(i, partner(i, distance, size)) for i in range...  3.05 us
    pallas_call x1, Pallas kernels, shards(): call(functools.partial(gradient_kernel, parts), [vmem] * (5 + parts), [vm...  3.05 us
    pallas_call x1, Pallas kernels, shards(): call(functools.partial(output_kernel, heads, parts), [vmem] * (8 + parts)...  2.56 us
    pallas_call x1, Pallas kernels, shards(): call(functools.partial(finish_kernel, parts, scale), [vmem] * (2 + parts)...  1.22 us
  transfers between devices with their start and end apart: 6, of which 2 were waited for; matrix products, arithmetic and copies ran while one was open for 0% of the time, Pallas kernels for 26%

profile of v10, /device:TPU:0, one launch (start us, length us, event | category | flops | bytes accessed | tf_op | source)
XLA Modules:
  0.0 31.8 jit_solution(9688688292544668816)
XLA Ops:
  0.6 5.2 %shard_map.112 = (bf16[32,2048]{1,0:T(8,128)(2,1)S(1)}, bf16[16,2048]{1,0:T(8,128)(2,1)S(1)}, bf16[16,2048]{1,0:T(8,128)(2,1)S(1)}, f32[3,16,384]{2,1,0:T(8,128)...) custom-call(f32[6]{0:T(128)} %rates_hbm.1, ...), custom_call_target="tpu_custom_call" | custom-call | flops 805306368 | bytes 4718592 | tf_op jit(solution)/shard_map/pallas_call | solution.py:503
  5.9 3.1 %collective-permute-start = (bf16[144,384]{1,0:T(8,128)(2,1)S(1)}, bf16[144,384]{1,0:T(8,128)(2,1)S(1)}, u32[]{:S(2)}, u32[]{:S(2)}) collective-permute-start(bf16[144,384]{1,0:T(8,128)(2,1)S(1)} %get-tuple-element.45), channel_id=1, source_target_pairs={{0,4},{4,0},{8,12},{12,8},{1,5},{5,1},{9,13},{13,9},{2,6},{6,2},{1... | collective-permute-start | bytes 331784 | tf_op jit(solution)/shard_map/ppermute | solution.py:456
  9.0 2.6 %collective-permute-start.1 = (bf16[144,384]{1,0:T(8,128)(2,1)S(1)}, bf16[144,384]{1,0:T(8,128)(2,1)S(1)}, u32[]{:S(2)}, u32[]{:S(2)}) collective-permute-start(bf16[144,384]{1,0:T(8,128)(2,1)S(1)} %get-tuple-element.46), channel_id=1, source_target_pairs={{0,8},{4,12},{8,0},{12,4},{1,9},{5,13},{9,1},{13,5},{2,10},{6,14},... | collective-permute-start | bytes 331784 | tf_op jit(solution)/shard_map/ppermute | solution.py:456
  11.6 0.0 collective-permute-start.2
  11.6 0.0 copy-start
  11.6 5.8 %shard_map.113 = (f32[2048,384]{1,0:T(8,128)S(1)}, f32[2048,384]{1,0:T(8,128)S(1)}, f32[2048,384]{1,0:T(8,128)S(1)}, f32[16,384]{1,0:T(8,128)S(1)}) custom-call(f32[8,384]{1,0:T(8,128)S(1)} %get-tuple-element.29.gains, bf16[32,2048]{1,0:T(8,128)(2,1)S(1)} %get-tuple-element.32.near, bf16[16,2048]{1,0:T(8,128)(2,1)S(1)} %get-tuple-element.33.far, ...), custom_call_target="tpu_custom_call" | custom-call | flops 2013265920 | bytes 4718592 | tf_op jit(solution)/shard_map/pallas_call | solution.py:553
  17.4 0.0 collective-permute-done.rest_0_
  17.4 2.9 %collective-permute-done.1.rest_1_ = bf16[144,384]{1,0:T(8,128)(2,1)S(1)} collective-permute-done((bf16[144,384]{1,0:T(8,128)(2,1)S(1)}, bf16[144,384]{1,0:T(8,128)(2,1)S(1)}, u32[]{:S(2)}, u32[]{:S(2)}) %collective-permute-start.1) | collective-permute-done | bytes 110624 | tf_op jit(solution)/shard_map/ppermute | solution.py:456
  20.3 0.0 collective-permute-done.2.rest_2_
  20.3 0.0 copy-done
  20.3 3.0 %shard_map.114 = (bf16[2048,384]{1,0:T(8,128)(2,1)S(1)}, f32[8,384]{1,0:T(8,128)S(1)}, f32[16,384]{1,0:T(8,128)S(1)}) custom-call(f32[4,384]{1,0:T(4,128)S(1)} %copy-done, f32[2048,384]{1,0:T(8,128)S(1)} %get-tuple-element.42.base, f32[2048,384]{1,0:T(8,128)S(1)} %get-tuple-element.43.weight, f32[16,384]{1,0:T(8,128)S(1)} %get-tuple-element.44.unscaled, ...), custom_call_target="tpu_custom_call" | custom-call | flops 402653184 | bytes 4718592 | tf_op jit(solution)/shard_map/pallas_call | solution.py:563
  23.4 2.6 %collective-permute-start.5 = (f32[8,384]{1,0:T(8,128)S(1)}, f32[8,384]{1,0:T(8,128)S(1)}, u32[]{:S(2)}, u32[]{:S(2)}) collective-permute-start(f32[8,384]{1,0:T(8,128)S(1)} %get-tuple-element.50.tail), channel_id=1, source_target_pairs={{0,12},{4,8},{8,4},{12,0},{1,13},{5,9},{9,5},{13,1},{2,14},{6,10},... | collective-permute-start | bytes 36872 | tf_op jit(solution)/shard_map/ppermute | solution.py:456
  25.9 0.7 %collective-permute-start.4 = (f32[8,384]{1,0:T(8,128)S(1)}, f32[8,384]{1,0:T(8,128)S(1)}, u32[]{:S(2)}, u32[]{:S(2)}) collective-permute-start(f32[8,384]{1,0:T(8,128)S(1)} %get-tuple-element.50.tail), channel_id=1, source_target_pairs={{0,8},{4,12},{8,0},{12,4},{1,9},{5,13},{9,1},{13,5},{2,10},{6,14},... | collective-permute-start | bytes 36872 | tf_op jit(solution)/shard_map/ppermute | solution.py:456
  26.6 1.2 %collective-permute-start.3 = (f32[8,384]{1,0:T(8,128)S(1)}, f32[8,384]{1,0:T(8,128)S(1)}, u32[]{:S(2)}, u32[]{:S(2)}) collective-permute-start(f32[8,384]{1,0:T(8,128)S(1)} %get-tuple-element.50.tail), channel_id=1, source_target_pairs={{0,4},{4,0},{8,12},{12,8},{1,5},{5,1},{9,13},{13,9},{2,6},{6,2},{1... | collective-permute-start | bytes 36872 | tf_op jit(solution)/shard_map/ppermute | solution.py:456
  27.8 2.6 %shard_map.115 = (bf16[2048,384]{1,0:T(8,128)(2,1)}, bf16[2048,384]{1,0:T(8,128)(2,1)}) custom-call(f32[8,384]{1,0:T(8,128)S(1)} %get-tuple-element.29.gains, f32[4,384]{1,0:T(4,128)S(1)} %copy-done, bf16[16,2048]{1,0:T(8,128)(2,1)S(1)} %get-tuple-element.30.front, f32[16,384]{1,0:T(8,128)S(1)} %get-tuple-element.31.lead, ...), custom_call_target="tpu_custom_call" | custom-call | flops 402653184 | bytes 4718592 | tf_op jit(solution)/shard_map/pallas_call | solution.py:573
  30.4 0.0 collective-permute-done.5.rest_2_
  30.4 0.1 collective-permute-done.4.rest_1_
  30.5 0.0 collective-permute-done.3.rest_0_
  30.5 1.2 %shard_map.116 = (bf16[2048,384]{1,0:T(8,128)(2,1)}, f32[4,384]{1,0:T(4,128)}) custom-call(f32[4,384]{1,0:T(4,128)S(1)} %copy-done, f32[8,384]{1,0:T(8,128)S(1)} %get-tuple-element.50.tail, f32[16,384]{1,0:T(8,128)S(1)} %get-tuple-element.51.edge, f32[8,384]{1,0:T(8,128)S(1)} %collective-permute-done.3.rest_0_, ...), custom_call_target="tpu_custom_call", output_to_operand_aliasing={{0}: (6, {})} | custom-call | bytes 4718592 | tf_op jit(solution)/shard_map/pallas_call | solution.py:583
Async XLA Ops:
  5.9 11.5 %collective-permute-start = (bf16[144,384]{1,0:T(8,128)(2,1)S(1)}, bf16[144,384]{1,0:T(8,128)(2,1)S(1)}, u32[]{:S(2)}, u32[]{:S(2)}) collective-permute-start(bf16[144,384]{1,0:T(8,128)(2,1)S(1)} %get-tuple-element.45), channel_id=1, source_target_pairs={{0,4},{4,0},{8,12},{12,8},{1,5},{5,1},{9,13},{13,9},{2,6},{6,2},{1... | collective-permute-start | bytes 331784 | tf_op jit(solution)/shard_map/ppermute | solution.py:456
  9.0 11.3 %collective-permute-start.1 = (bf16[144,384]{1,0:T(8,128)(2,1)S(1)}, bf16[144,384]{1,0:T(8,128)(2,1)S(1)}, u32[]{:S(2)}, u32[]{:S(2)}) collective-permute-start(bf16[144,384]{1,0:T(8,128)(2,1)S(1)} %get-tuple-element.46), channel_id=1, source_target_pairs={{0,8},{4,12},{8,0},{12,4},{1,9},{5,13},{9,1},{13,5},{2,10},{6,14},... | collective-permute-start | bytes 331784 | tf_op jit(solution)/shard_map/ppermute | solution.py:456
  11.6 8.8 %collective-permute-start.2 = (bf16[144,384]{1,0:T(8,128)(2,1)S(1)}, bf16[144,384]{1,0:T(8,128)(2,1)S(1)}, u32[]{:S(2)}, u32[]{:S(2)}) collective-permute-start(bf16[144,384]{1,0:T(8,128)(2,1)S(1)} %get-tuple-element.47), channel_id=1, source_target_pairs={{0,12},{4,8},{8,4},{12,0},{1,13},{5,9},{9,5},{13,1},{2,14},{6,10},... | collective-permute-start | bytes 331784 | tf_op jit(solution)/shard_map/ppermute | solution.py:456
  11.6 8.8 %copy-start = (f32[4,384]{1,0:T(4,128)S(1)}, f32[4,384]{1,0:T(4,128)}, u32[]{:S(2)}) copy-start(f32[4,384]{1,0:T(4,128)} %taps.5) | copy-start | bytes 18436
  23.4 7.0 %collective-permute-start.5 = (f32[8,384]{1,0:T(8,128)S(1)}, f32[8,384]{1,0:T(8,128)S(1)}, u32[]{:S(2)}, u32[]{:S(2)}) collective-permute-start(f32[8,384]{1,0:T(8,128)S(1)} %get-tuple-element.50.tail), channel_id=1, source_target_pairs={{0,12},{4,8},{8,4},{12,0},{1,13},{5,9},{9,5},{13,1},{2,14},{6,10},... | collective-permute-start | bytes 36872 | tf_op jit(solution)/shard_map/ppermute | solution.py:456
  25.9 4.6 %collective-permute-start.4 = (f32[8,384]{1,0:T(8,128)S(1)}, f32[8,384]{1,0:T(8,128)S(1)}, u32[]{:S(2)}, u32[]{:S(2)}) collective-permute-start(f32[8,384]{1,0:T(8,128)S(1)} %get-tuple-element.50.tail), channel_id=1, source_target_pairs={{0,8},{4,12},{8,0},{12,4},{1,9},{5,13},{9,1},{13,5},{2,10},{6,14},... | collective-permute-start | bytes 36872 | tf_op jit(solution)/shard_map/ppermute | solution.py:456
  26.6 3.9 %collective-permute-start.3 = (f32[8,384]{1,0:T(8,128)S(1)}, f32[8,384]{1,0:T(8,128)S(1)}, u32[]{:S(2)}, u32[]{:S(2)}) collective-permute-start(f32[8,384]{1,0:T(8,128)S(1)} %get-tuple-element.50.tail), channel_id=1, source_target_pairs={{0,4},{4,0},{8,12},{12,8},{1,5},{5,1},{9,13},{13,9},{2,6},{6,2},{1... | collective-permute-start | bytes 36872 | tf_op jit(solution)/shard_map/ppermute | solution.py:456

commit v11 on v9

--- a/solution.py
+++ b/solution.py
@@ -383,7 +383,7 @@
     heads, parts, gains, taps, front, lead, base, inputs, b_proj, c_proj, exact, window, *rest
 ):
     pays = rest[: parts - 1]
-    out_hbm, grad_hbm, edge_out, held, result_rows, grad_rows, sems, grad_sems = rest[parts - 1 :]
+    out_hbm, grad_hbm, edge_out, held, result_rows, grad_rows, sems = rest[parts - 1 :]
     rows, channels = base.shape
     sort_blocks(parts, pays, held)
     incoming = merged_state(parts, taps, held)
@@ -403,33 +403,28 @@
     row = lax.broadcasted_iota(jnp.int32, (3 * CHUNK, CHUNK + 16), 0)
     col = lax.broadcasted_iota(jnp.int32, (3 * CHUNK, CHUNK + 16), 1)
     shift = jnp.where(col == (row & (CHUNK - 1)) + 3 - (row >> 7), 1.0, 0.0).astype(BF16)
-    copies = []
-    for piece in range(rows // STEP_ROWS):
-        for at in range(piece * STEP_ROWS, (piece + 1) * STEP_ROWS, CHUNK):
-            both = slice(at, at + CHUNK)
-            moved = dot(shift, window[at : at + CHUNK + 16, :], ((1,), (0,)))
-            result = taps[3:4, :] * exact[both, :]
-            for k in range(3):
-                result = result + taps[k : k + 1, :] * moved[k * CHUNK : (k + 1) * CHUNK, :]
-            grad_rows[both, :] = result.astype(BF16)
-            if at + CHUNK == rows:
-                edge_out[...] = result[CHUNK - 16 :, :]
-            carried = dot(c_proj[both, :], state, ((1,), (0,)))
-            result = base[both, :] + spread(front[:, both], onehot) * carried
-            result_rows[both, :] = result.astype(BF16)
-            if at == 0:
-                result_rows[0:16, :] = top.astype(BF16)
-        place = pl.ds(piece * STEP_ROWS, STEP_ROWS)
-        copy = pltpu.make_async_copy(result_rows.at[place], out_hbm.at[place], sems.at[piece])
-        copy.start()
-        copies.append(copy)
-        copy = pltpu.make_async_copy(
-            grad_rows.at[place], grad_hbm.at[place], grad_sems.at[piece]
-        )
-        copy.start()
-        copies.append(copy)
-    for copy in copies:
-        copy.wait()
+    for at in range(0, rows, CHUNK):
+        both = slice(at, at + CHUNK)
+        moved = dot(shift, window[at : at + CHUNK + 16, :], ((1,), (0,)))
+        result = taps[3:4, :] * exact[both, :]
+        for k in range(3):
+            result = result + taps[k : k + 1, :] * moved[k * CHUNK : (k + 1) * CHUNK, :]
+        grad_rows[both, :] = result.astype(BF16)
+        if at + CHUNK == rows:
+            edge_out[...] = result[CHUNK - 16 :, :]
+    grad_copy = pltpu.make_async_copy(grad_rows, grad_hbm, sems.at[0])
+    grad_copy.start()
+    for at in range(0, rows, CHUNK):
+        both = slice(at, at + CHUNK)
+        carried = dot(c_proj[both, :], state, ((1,), (0,)))
+        result = base[both, :] + spread(front[:, both], onehot) * carried
+        result_rows[both, :] = result.astype(BF16)
+        if at == 0:
+            result_rows[0:16, :] = top.astype(BF16)
+    out_copy = pltpu.make_async_copy(result_rows, out_hbm, sems.at[1])
+    out_copy.start()
+    grad_copy.wait()
+    out_copy.wait()
 
 
 def finish_kernel(parts, scale, taps, tail, edge, *rest):
@@ -479,7 +474,6 @@
     heads = decay_rates.shape[0]
     parts = lax.axis_size("seq")
     chunks = rows // CHUNK
-    pieces = rows // STEP_ROWS
     hbm = pl.BlockSpec(memory_space=pltpu.HBM)
     vmem = pl.BlockSpec(memory_space=pltpu.VMEM)
     shape = jax.ShapeDtypeStruct
@@ -583,7 +577,7 @@
         [vmem] * (9 + parts),
         [hbm, hbm, vmem],
         [narrow, narrow, shape((16, channels), F32)],
-        [held, low, low, dma((pieces,)), dma((pieces,))],
+        [held, low, low, dma((2,))],
         4,
     )(gain, conv_weight, front, lead, base, inputs, b_proj, c_proj, exact, window, *pays)
 

time: 32.9 us -> 33.1 us (level)
  no operation moved by 1% of the time
where the time goes in v11:
time: 33.1 us; the launch traced here: 32.9 us
  Pallas kernels  20.7 us (63%)
  starting transfers between devices  10.1 us (31%)
  waiting for transfers between devices  1.29 us (4%)
  between operations  0.85 us (3%)
    ppermute x6, starting transfers between devices, rotated(): lax.ppermute(block, axis, [(i, partner(i, distance, size)) for i in range...  10.1 us
    pallas_call x1, Pallas kernels, shards(): call(functools.partial(inner_kernel, heads), [vmem] * 10, [vmem] * 5, [br...  7.45 us
    pallas_call x1, Pallas kernels, shards(): call(functools.partial(reduce_kernel, heads, parts), [hbm] * 9, [vmem] *...  5.24 us
    pallas_call x1, Pallas kernels, shards(): call(functools.partial(output_kernel, heads, parts), [vmem] * (9 + parts)...  4.22 us
    pallas_call x1, Pallas kernels, shards(): call(functools.partial(gradient_kernel, parts), [vmem] * (6 + parts), [vm...  2.54 us
    ppermute x6, waiting for transfers between devices, rotated(): lax.ppermute(block, axis, [(i, partner(i, distance, size)) for i in range...  1.29 us
    pallas_call x1, Pallas kernels, shards(): call(functools.partial(finish_kernel, parts, scale), [vmem] * (2 + parts)...  1.23 us
  transfers between devices with their start and end apart: 6, of which 1 were waited for; matrix products, arithmetic and copies ran while one was open for 0% of the time, Pallas kernels for 35%

profile of v11, /device:TPU:0, one launch (start us, length us, event | category | flops | bytes accessed | tf_op | source)
XLA Modules:
  0.0 32.9 jit_solution(10236930011194208021)
XLA Ops:
  0.6 5.2 %shard_map.112 = (bf16[32,2048]{1,0:T(8,128)(2,1)S(1)}, bf16[16,2048]{1,0:T(8,128)(2,1)S(1)}, bf16[16,2048]{1,0:T(8,128)(2,1)S(1)}, f32[3,16,384]{2,1,0:T(8,128)...) custom-call(f32[6]{0:T(128)} %rates_hbm.1, ...), custom_call_target="tpu_custom_call" | custom-call | flops 805306368 | bytes 4718592 | tf_op jit(solution)/shard_map/pallas_call | solution.py:505
  5.9 3.1 %collective-permute-start = (bf16[144,384]{1,0:T(8,128)(2,1)S(1)}, bf16[144,384]{1,0:T(8,128)(2,1)S(1)}, u32[]{:S(2)}, u32[]{:S(2)}) collective-permute-start(bf16[144,384]{1,0:T(8,128)(2,1)S(1)} %get-tuple-element.48), channel_id=1, source_target_pairs={{0,4},{4,0},{8,12},{12,8},{1,5},{5,1},{9,13},{13,9},{2,6},{6,2},{1... | collective-permute-start | bytes 331784 | tf_op jit(solution)/shard_map/ppermute | solution.py:459
  9.0 2.6 %collective-permute-start.1 = (bf16[144,384]{1,0:T(8,128)(2,1)S(1)}, bf16[144,384]{1,0:T(8,128)(2,1)S(1)}, u32[]{:S(2)}, u32[]{:S(2)}) collective-permute-start(bf16[144,384]{1,0:T(8,128)(2,1)S(1)} %get-tuple-element.49), channel_id=1, source_target_pairs={{0,8},{4,12},{8,0},{12,4},{1,9},{5,13},{9,1},{13,5},{2,10},{6,14},... | collective-permute-start | bytes 331784 | tf_op jit(solution)/shard_map/ppermute | solution.py:459
  11.6 0.0 collective-permute-start.2
  11.6 0.0 copy-start
  11.6 7.5 %shard_map.113 = (f32[2048,384]{1,0:T(8,128)S(1)}, f32[2048,384]{1,0:T(8,128)S(1)}, f32[2048,384]{1,0:T(8,128)S(1)}, f32[16,384]{1,0:T(8,128)S(1)}, bf16[3,2048,384]{2,1,0:T(8,128)(2,1)S(1)}) custom-call(f32[8,384]{1,0:T(8,128)S(1)} %get-tuple-element.31.gains, bf16[32,2048]{1,0:T(8,128)(2,1)S(1)} %get-tuple-element.34.near, ...), custom_call_target="tpu_custom_call" | custom-call | flops 2013265920 | bytes 4718592 | tf_op jit(solution)/shard_map/pallas_call | solution.py:555
  19.0 0.0 collective-permute-done.rest_0_
  19.0 1.3 %collective-permute-done.1.rest_1_ = bf16[144,384]{1,0:T(8,128)(2,1)S(1)} collective-permute-done((bf16[144,384]{1,0:T(8,128)(2,1)S(1)}, bf16[144,384]{1,0:T(8,128)(2,1)S(1)}, u32[]{:S(2)}, u32[]{:S(2)}) %collective-permute-start.1) | collective-permute-done | bytes 110624 | tf_op jit(solution)/shard_map/ppermute | solution.py:459
  20.3 0.0 collective-permute-done.2.rest_2_
  20.3 0.0 copy-done
  20.3 2.5 %shard_map.114 = (f32[2048,384]{1,0:T(8,128)S(1)}, bf16[2064,384]{1,0:T(8,128)(2,1)S(1)}, f32[8,384]{1,0:T(8,128)S(1)}) custom-call(f32[4,384]{1,0:T(4,128)S(1)} %copy-done, f32[2048,384]{1,0:T(8,128)S(1)} %get-tuple-element.44.base, f32[2048,384]{1,0:T(8,128)S(1)} %get-tuple-element.45.weight, f32[16,384]{1,0:T(8,128)S(1)} %get-tuple-element.46.unscaled, ...), custom_call_target="tpu_custom_call" | custom-call | flops 402653184 | bytes 4718592 | tf_op jit(solution)/shard_map/pallas_call | solution.py:565
  22.9 2.6 %collective-permute-start.5 = (f32[8,384]{1,0:T(8,128)S(1)}, f32[8,384]{1,0:T(8,128)S(1)}, u32[]{:S(2)}, u32[]{:S(2)}) collective-permute-start(f32[8,384]{1,0:T(8,128)S(1)} %get-tuple-element.54.tail), channel_id=1, source_target_pairs={{0,12},{4,8},{8,4},{12,0},{1,13},{5,9},{9,5},{13,1},{2,14},{6,10},... | collective-permute-start | bytes 36872 | tf_op jit(solution)/shard_map/ppermute | solution.py:459
  25.5 0.6 %collective-permute-start.4 = (f32[8,384]{1,0:T(8,128)S(1)}, f32[8,384]{1,0:T(8,128)S(1)}, u32[]{:S(2)}, u32[]{:S(2)}) collective-permute-start(f32[8,384]{1,0:T(8,128)S(1)} %get-tuple-element.54.tail), channel_id=1, source_target_pairs={{0,8},{4,12},{8,0},{12,4},{1,9},{5,13},{9,1},{13,5},{2,10},{6,14},... | collective-permute-start | bytes 36872 | tf_op jit(solution)/shard_map/ppermute | solution.py:459
  26.1 1.2 %collective-permute-start.3 = (f32[8,384]{1,0:T(8,128)S(1)}, f32[8,384]{1,0:T(8,128)S(1)}, u32[]{:S(2)}, u32[]{:S(2)}) collective-permute-start(f32[8,384]{1,0:T(8,128)S(1)} %get-tuple-element.54.tail), channel_id=1, source_target_pairs={{0,4},{4,0},{8,12},{12,8},{1,5},{5,1},{9,13},{13,9},{2,6},{6,2},{1... | collective-permute-start | bytes 36872 | tf_op jit(solution)/shard_map/ppermute | solution.py:459
  27.3 4.2 %shard_map.115 = (bf16[2048,384]{1,0:T(8,128)(2,1)}, bf16[2048,384]{1,0:T(8,128)(2,1)}, f32[16,384]{1,0:T(8,128)S(1)}) custom-call(f32[8,384]{1,0:T(8,128)S(1)} %get-tuple-element.31.gains, f32[4,384]{1,0:T(4,128)S(1)} %copy-done, bf16[16,2048]{1,0:T(8,128)(2,1)S(1)} %get-tuple-element.32.front, f32[16,384]{1,0:T(8,128)S(1)} %get-tuple-element.33.lead, ...), custom_call_target="tpu_custom_call" | custom-call | flops 805306368 | bytes 4718592 | tf_op jit(solution)/shard_map/pallas_call | solution.py:575
  31.5 0.0 collective-permute-done.5.rest_2_
  31.5 0.0 collective-permute-done.4.rest_1_
  31.5 0.0 collective-permute-done.3.rest_0_
  31.5 1.2 %shard_map.116 = (bf16[2048,384]{1,0:T(8,128)(2,1)}, f32[4,384]{1,0:T(4,128)}) custom-call(f32[4,384]{1,0:T(4,128)S(1)} %copy-done, f32[8,384]{1,0:T(8,128)S(1)} %get-tuple-element.54.tail, f32[16,384]{1,0:T(8,128)S(1)} %get-tuple-element.55.edge, f32[8,384]{1,0:T(8,128)S(1)} %collective-permute-done.3.rest_0_, ...), custom_call_target="tpu_custom_call", output_to_operand_aliasing={{0}: (6, {})} | custom-call | bytes 4718592 | tf_op jit(solution)/shard_map/pallas_call | solution.py:585
Async XLA Ops:
  5.9 13.2 %collective-permute-start = (bf16[144,384]{1,0:T(8,128)(2,1)S(1)}, bf16[144,384]{1,0:T(8,128)(2,1)S(1)}, u32[]{:S(2)}, u32[]{:S(2)}) collective-permute-start(bf16[144,384]{1,0:T(8,128)(2,1)S(1)} %get-tuple-element.48), channel_id=1, source_target_pairs={{0,4},{4,0},{8,12},{12,8},{1,5},{5,1},{9,13},{13,9},{2,6},{6,2},{1... | collective-permute-start | bytes 331784 | tf_op jit(solution)/shard_map/ppermute | solution.py:459
  9.0 11.3 %collective-permute-start.1 = (bf16[144,384]{1,0:T(8,128)(2,1)S(1)}, bf16[144,384]{1,0:T(8,128)(2,1)S(1)}, u32[]{:S(2)}, u32[]{:S(2)}) collective-permute-start(bf16[144,384]{1,0:T(8,128)(2,1)S(1)} %get-tuple-element.49), channel_id=1, source_target_pairs={{0,8},{4,12},{8,0},{12,4},{1,9},{5,13},{9,1},{13,5},{2,10},{6,14},... | collective-permute-start | bytes 331784 | tf_op jit(solution)/shard_map/ppermute | solution.py:459
  11.6 8.8 %collective-permute-start.2 = (bf16[144,384]{1,0:T(8,128)(2,1)S(1)}, bf16[144,384]{1,0:T(8,128)(2,1)S(1)}, u32[]{:S(2)}, u32[]{:S(2)}) collective-permute-start(bf16[144,384]{1,0:T(8,128)(2,1)S(1)} %get-tuple-element.50), channel_id=1, source_target_pairs={{0,12},{4,8},{8,4},{12,0},{1,13},{5,9},{9,5},{13,1},{2,14},{6,10},... | collective-permute-start | bytes 331784 | tf_op jit(solution)/shard_map/ppermute | solution.py:459
  11.6 8.8 %copy-start = (f32[4,384]{1,0:T(4,128)S(1)}, f32[4,384]{1,0:T(4,128)}, u32[]{:S(2)}) copy-start(f32[4,384]{1,0:T(4,128)} %taps.5) | copy-start | bytes 18436
  22.9 8.6 %collective-permute-start.5 = (f32[8,384]{1,0:T(8,128)S(1)}, f32[8,384]{1,0:T(8,128)S(1)}, u32[]{:S(2)}, u32[]{:S(2)}) collective-permute-start(f32[8,384]{1,0:T(8,128)S(1)} %get-tuple-element.54.tail), channel_id=1, source_target_pairs={{0,12},{4,8},{8,4},{12,0},{1,13},{5,9},{9,5},{13,1},{2,14},{6,10},... | collective-permute-start | bytes 36872 | tf_op jit(solution)/shard_map/ppermute | solution.py:459
  25.5 6.1 %collective-permute-start.4 = (f32[8,384]{1,0:T(8,128)S(1)}, f32[8,384]{1,0:T(8,128)S(1)}, u32[]{:S(2)}, u32[]{:S(2)}) collective-permute-start(f32[8,384]{1,0:T(8,128)S(1)} %get-tuple-element.54.tail), channel_id=1, source_target_pairs={{0,8},{4,12},{8,0},{12,4},{1,9},{5,13},{9,1},{13,5},{2,10},{6,14},... | collective-permute-start | bytes 36872 | tf_op jit(solution)/shard_map/ppermute | solution.py:459
  26.1 5.4 %collective-permute-start.3 = (f32[8,384]{1,0:T(8,128)S(1)}, f32[8,384]{1,0:T(8,128)S(1)}, u32[]{:S(2)}, u32[]{:S(2)}) collective-permute-start(f32[8,384]{1,0:T(8,128)S(1)} %get-tuple-element.54.tail), channel_id=1, source_target_pairs={{0,4},{4,0},{8,12},{12,8},{1,5},{5,1},{9,13},{13,9},{2,6},{6,2},{1... | collective-permute-start | bytes 36872 | tf_op jit(solution)/shard_map/ppermute | solution.py:459

commit v12 on v10

--- a/solution.py
+++ b/solution.py
@@ -387,9 +387,9 @@
     heads, parts, gains, taps, front, lead, base, inputs, b_proj, c_proj, grad_rows, *rest
 ):
     pays = rest[: parts - 1]
-    out_hbm, grad_hbm, held, result_rows, sems, grad_sem = rest[parts - 1 :]
+    out_hbm, grad_hbm, held, result_rows, sems = rest[parts - 1 :]
     rows, channels = base.shape
-    grad_copy = pltpu.make_async_copy(grad_rows, grad_hbm, grad_sem)
+    grad_copy = pltpu.make_async_copy(grad_rows, grad_hbm, sems.at[0])
     grad_copy.start()
     sort_blocks(parts, pays, held)
     incoming = merged_state(parts, taps, held)
@@ -406,22 +406,17 @@
     top = top + dot(scores, change_scaled, ((1,), (0,)))
     top = top * spread(front[:, 0:16], onehot) + base[0:16, :]
     top = top + gains[0:1, :] * change
-    copies = []
-    for piece in range(rows // STEP_ROWS):
-        for at in range(piece * STEP_ROWS, (piece + 1) * STEP_ROWS, CHUNK):
-            both = slice(at, at + CHUNK)
-            carried = dot(c_proj[both, :], state, ((1,), (0,)))
-            result = base[both, :] + spread(front[:, both], onehot) * carried
-            result_rows[both, :] = result.astype(BF16)
-            if at == 0:
-                result_rows[0:16, :] = top.astype(BF16)
-        place = pl.ds(piece * STEP_ROWS, STEP_ROWS)
-        copy = pltpu.make_async_copy(result_rows.at[place], out_hbm.at[place], sems.at[piece])
-        copy.start()
-        copies.append(copy)
-    for copy in copies:
-        copy.wait()
+    for at in range(0, rows, CHUNK):
+        both = slice(at, at + CHUNK)
+        carried = dot(c_proj[both, :], state, ((1,), (0,)))
+        result = base[both, :] + spread(front[:, both], onehot) * carried
+        result_rows[both, :] = result.astype(BF16)
+        if at == 0:
+            result_rows[0:16, :] = top.astype(BF16)
+    out_copy = pltpu.make_async_copy(result_rows, out_hbm, sems.at[1])
+    out_copy.start()
     grad_copy.wait()
+    out_copy.wait()
 
 
 def finish_kernel(parts, scale, taps, tail, edge, *rest):
@@ -471,7 +466,6 @@
     heads = decay_rates.shape[0]
     parts = lax.axis_size("seq")
     chunks = rows // CHUNK
-    pieces = rows // STEP_ROWS
     hbm = pl.BlockSpec(memory_space=pltpu.HBM)
     vmem = pl.BlockSpec(memory_space=pltpu.VMEM)
     shape = jax.ShapeDtypeStruct
@@ -575,7 +569,7 @@
         [vmem] * (8 + parts),
         [hbm, hbm],
         [narrow, narrow],
-        [held, low, dma((pieces,)), dma],
+        [held, low, dma((2,))],
         2,
     )(gain, conv_weight, front, lead, base, inputs, b_proj, c_proj, grad_rows, *pays)
 

time: 31.9 us -> 31.9 us (level)
  no operation moved by 1% of the time
where the time goes in v12:
time: 31.9 us; the launch traced here: 31.8 us
  Pallas kernels  17.8 us (56%)
  starting transfers between devices  10.1 us (32%)
  waiting for transfers between devices  3.12 us (10%)
  between operations  0.68 us (2%)
    ppermute x6, starting transfers between devices, rotated(): lax.ppermute(block, axis, [(i, partner(i, distance, size)) for i in range...  10.1 us
    pallas_call x1, Pallas kernels, shards(): call(functools.partial(inner_kernel, heads), [vmem] * 9, [vmem] * 4, [bro...  5.83 us
    pallas_call x1, Pallas kernels, shards(): call(functools.partial(reduce_kernel, heads, parts), [hbm] * 9, [vmem] *...  5.25 us
    ppermute x6, waiting for transfers between devices, rotated(): lax.ppermute(block, axis, [(i, partner(i, distance, size)) for i in range...  3.12 us
    pallas_call x1, Pallas kernels, shards(): call(functools.partial(gradient_kernel, parts), [vmem] * (5 + parts), [vm...  3.05 us
    pallas_call x1, Pallas kernels, shards(): call(functools.partial(output_kernel, heads, parts), [vmem] * (8 + parts)...  2.48 us
    pallas_call x1, Pallas kernels, shards(): call(functools.partial(finish_kernel, parts, scale), [vmem] * (2 + parts)...  1.22 us
  transfers between devices with their start and end apart: 6, of which 2 were waited for; matrix products, arithmetic and copies ran while one was open for 0% of the time, Pallas kernels for 26%

profile of v12, /device:TPU:0, one launch (start us, length us, event | category | flops | bytes accessed | tf_op | source)
XLA Modules:
  0.0 31.8 jit_solution(18383178354872484961)
XLA Ops:
  0.6 5.2 %shard_map.112 = (bf16[32,2048]{1,0:T(8,128)(2,1)S(1)}, bf16[16,2048]{1,0:T(8,128)(2,1)S(1)}, bf16[16,2048]{1,0:T(8,128)(2,1)S(1)}, f32[3,16,384]{2,1,0:T(8,128)...) custom-call(f32[6]{0:T(128)} %rates_hbm.1, ...), custom_call_target="tpu_custom_call" | custom-call | flops 805306368 | bytes 4718592 | tf_op jit(solution)/shard_map/pallas_call | solution.py:497
  5.9 3.1 %collective-permute-start = (bf16[144,384]{1,0:T(8,128)(2,1)S(1)}, bf16[144,384]{1,0:T(8,128)(2,1)S(1)}, u32[]{:S(2)}, u32[]{:S(2)}) collective-permute-start(bf16[144,384]{1,0:T(8,128)(2,1)S(1)} %get-tuple-element.45), channel_id=1, source_target_pairs={{0,4},{4,0},{8,12},{12,8},{1,5},{5,1},{9,13},{13,9},{2,6},{6,2},{1... | collective-permute-start | bytes 331784 | tf_op jit(solution)/shard_map/ppermute | solution.py:451
  9.0 2.6 %collective-permute-start.1 = (bf16[144,384]{1,0:T(8,128)(2,1)S(1)}, bf16[144,384]{1,0:T(8,128)(2,1)S(1)}, u32[]{:S(2)}, u32[]{:S(2)}) collective-permute-start(bf16[144,384]{1,0:T(8,128)(2,1)S(1)} %get-tuple-element.46), channel_id=1, source_target_pairs={{0,8},{4,12},{8,0},{12,4},{1,9},{5,13},{9,1},{13,5},{2,10},{6,14},... | collective-permute-start | bytes 331784 | tf_op jit(solution)/shard_map/ppermute | solution.py:451
  11.6 0.0 collective-permute-start.2
  11.6 0.0 copy-start
  11.6 5.8 %shard_map.113 = (f32[2048,384]{1,0:T(8,128)S(1)}, f32[2048,384]{1,0:T(8,128)S(1)}, f32[2048,384]{1,0:T(8,128)S(1)}, f32[16,384]{1,0:T(8,128)S(1)}) custom-call(f32[8,384]{1,0:T(8,128)S(1)} %get-tuple-element.29.gains, bf16[32,2048]{1,0:T(8,128)(2,1)S(1)} %get-tuple-element.32.near, bf16[16,2048]{1,0:T(8,128)(2,1)S(1)} %get-tuple-element.33.far, ...), custom_call_target="tpu_custom_call" | custom-call | flops 2013265920 | bytes 4718592 | tf_op jit(solution)/shard_map/pallas_call | solution.py:547
  17.4 0.0 collective-permute-done.rest_0_
  17.4 2.9 %collective-permute-done.1.rest_1_ = bf16[144,384]{1,0:T(8,128)(2,1)S(1)} collective-permute-done((bf16[144,384]{1,0:T(8,128)(2,1)S(1)}, bf16[144,384]{1,0:T(8,128)(2,1)S(1)}, u32[]{:S(2)}, u32[]{:S(2)}) %collective-permute-start.1) | collective-permute-done | bytes 110624 | tf_op jit(solution)/shard_map/ppermute | solution.py:451
  20.3 0.0 collective-permute-done.2.rest_2_
  20.3 0.0 copy-done
  20.3 3.0 %shard_map.114 = (bf16[2048,384]{1,0:T(8,128)(2,1)S(1)}, f32[8,384]{1,0:T(8,128)S(1)}, f32[16,384]{1,0:T(8,128)S(1)}) custom-call(f32[4,384]{1,0:T(4,128)S(1)} %copy-done, f32[2048,384]{1,0:T(8,128)S(1)} %get-tuple-element.42.base, f32[2048,384]{1,0:T(8,128)S(1)} %get-tuple-element.43.weight, f32[16,384]{1,0:T(8,128)S(1)} %get-tuple-element.44.unscaled, ...), custom_call_target="tpu_custom_call" | custom-call | flops 402653184 | bytes 4718592 | tf_op jit(solution)/shard_map/pallas_call | solution.py:557
  23.4 2.6 %collective-permute-start.5 = (f32[8,384]{1,0:T(8,128)S(1)}, f32[8,384]{1,0:T(8,128)S(1)}, u32[]{:S(2)}, u32[]{:S(2)}) collective-permute-start(f32[8,384]{1,0:T(8,128)S(1)} %get-tuple-element.50.tail), channel_id=1, source_target_pairs={{0,12},{4,8},{8,4},{12,0},{1,13},{5,9},{9,5},{13,1},{2,14},{6,10},... | collective-permute-start | bytes 36872 | tf_op jit(solution)/shard_map/ppermute | solution.py:451
  25.9 0.7 %collective-permute-start.4 = (f32[8,384]{1,0:T(8,128)S(1)}, f32[8,384]{1,0:T(8,128)S(1)}, u32[]{:S(2)}, u32[]{:S(2)}) collective-permute-start(f32[8,384]{1,0:T(8,128)S(1)} %get-tuple-element.50.tail), channel_id=1, source_target_pairs={{0,8},{4,12},{8,0},{12,4},{1,9},{5,13},{9,1},{13,5},{2,10},{6,14},... | collective-permute-start | bytes 36872 | tf_op jit(solution)/shard_map/ppermute | solution.py:451
  26.6 1.2 %collective-permute-start.3 = (f32[8,384]{1,0:T(8,128)S(1)}, f32[8,384]{1,0:T(8,128)S(1)}, u32[]{:S(2)}, u32[]{:S(2)}) collective-permute-start(f32[8,384]{1,0:T(8,128)S(1)} %get-tuple-element.50.tail), channel_id=1, source_target_pairs={{0,4},{4,0},{8,12},{12,8},{1,5},{5,1},{9,13},{13,9},{2,6},{6,2},{1... | collective-permute-start | bytes 36872 | tf_op jit(solution)/shard_map/ppermute | solution.py:451
  27.8 2.5 %shard_map.115 = (bf16[2048,384]{1,0:T(8,128)(2,1)}, bf16[2048,384]{1,0:T(8,128)(2,1)}) custom-call(f32[8,384]{1,0:T(8,128)S(1)} %get-tuple-element.29.gains, f32[4,384]{1,0:T(4,128)S(1)} %copy-done, bf16[16,2048]{1,0:T(8,128)(2,1)S(1)} %get-tuple-element.30.front, f32[16,384]{1,0:T(8,128)S(1)} %get-tuple-element.31.lead, ...), custom_call_target="tpu_custom_call" | custom-call | flops 402653184 | bytes 4718592 | tf_op jit(solution)/shard_map/pallas_call | solution.py:567
  30.3 0.0 collective-permute-done.5.rest_2_
  30.3 0.2 collective-permute-done.4.rest_1_
  30.5 0.0 collective-permute-done.3.rest_0_
  30.5 1.2 %shard_map.116 = (bf16[2048,384]{1,0:T(8,128)(2,1)}, f32[4,384]{1,0:T(4,128)}) custom-call(f32[4,384]{1,0:T(4,128)S(1)} %copy-done, f32[8,384]{1,0:T(8,128)S(1)} %get-tuple-element.50.tail, f32[16,384]{1,0:T(8,128)S(1)} %get-tuple-element.51.edge, f32[8,384]{1,0:T(8,128)S(1)} %collective-permute-done.3.rest_0_, ...), custom_call_target="tpu_custom_call", output_to_operand_aliasing={{0}: (6, {})} | custom-call | bytes 4718592 | tf_op jit(solution)/shard_map/pallas_call | solution.py:577
Async XLA Ops:
  5.9 11.5 %collective-permute-start = (bf16[144,384]{1,0:T(8,128)(2,1)S(1)}, bf16[144,384]{1,0:T(8,128)(2,1)S(1)}, u32[]{:S(2)}, u32[]{:S(2)}) collective-permute-start(bf16[144,384]{1,0:T(8,128)(2,1)S(1)} %get-tuple-element.45), channel_id=1, source_target_pairs={{0,4},{4,0},{8,12},{12,8},{1,5},{5,1},{9,13},{13,9},{2,6},{6,2},{1... | collective-permute-start | bytes 331784 | tf_op jit(solution)/shard_map/ppermute | solution.py:451
  9.0 11.3 %collective-permute-start.1 = (bf16[144,384]{1,0:T(8,128)(2,1)S(1)}, bf16[144,384]{1,0:T(8,128)(2,1)S(1)}, u32[]{:S(2)}, u32[]{:S(2)}) collective-permute-start(bf16[144,384]{1,0:T(8,128)(2,1)S(1)} %get-tuple-element.46), channel_id=1, source_target_pairs={{0,8},{4,12},{8,0},{12,4},{1,9},{5,13},{9,1},{13,5},{2,10},{6,14},... | collective-permute-start | bytes 331784 | tf_op jit(solution)/shard_map/ppermute | solution.py:451
  11.6 8.8 %collective-permute-start.2 = (bf16[144,384]{1,0:T(8,128)(2,1)S(1)}, bf16[144,384]{1,0:T(8,128)(2,1)S(1)}, u32[]{:S(2)}, u32[]{:S(2)}) collective-permute-start(bf16[144,384]{1,0:T(8,128)(2,1)S(1)} %get-tuple-element.47), channel_id=1, source_target_pairs={{0,12},{4,8},{8,4},{12,0},{1,13},{5,9},{9,5},{13,1},{2,14},{6,10},... | collective-permute-start | bytes 331784 | tf_op jit(solution)/shard_map/ppermute | solution.py:451
  11.6 8.8 %copy-start = (f32[4,384]{1,0:T(4,128)S(1)}, f32[4,384]{1,0:T(4,128)}, u32[]{:S(2)}) copy-start(f32[4,384]{1,0:T(4,128)} %taps.5) | copy-start | bytes 18436
  23.4 6.9 %collective-permute-start.5 = (f32[8,384]{1,0:T(8,128)S(1)}, f32[8,384]{1,0:T(8,128)S(1)}, u32[]{:S(2)}, u32[]{:S(2)}) collective-permute-start(f32[8,384]{1,0:T(8,128)S(1)} %get-tuple-element.50.tail), channel_id=1, source_target_pairs={{0,12},{4,8},{8,4},{12,0},{1,13},{5,9},{9,5},{13,1},{2,14},{6,10},... | collective-permute-start | bytes 36872 | tf_op jit(solution)/shard_map/ppermute | solution.py:451
  25.9 4.6 %collective-permute-start.4 = (f32[8,384]{1,0:T(8,128)S(1)}, f32[8,384]{1,0:T(8,128)S(1)}, u32[]{:S(2)}, u32[]{:S(2)}) collective-permute-start(f32[8,384]{1,0:T(8,128)S(1)} %get-tuple-element.50.tail), channel_id=1, source_target_pairs={{0,8},{4,12},{8,0},{12,4},{1,9},{5,13},{9,1},{13,5},{2,10},{6,14},... | collective-permute-start | bytes 36872 | tf_op jit(solution)/shard_map/ppermute | solution.py:451
  26.6 3.9 %collective-permute-start.3 = (f32[8,384]{1,0:T(8,128)S(1)}, f32[8,384]{1,0:T(8,128)S(1)}, u32[]{:S(2)}, u32[]{:S(2)}) collective-permute-start(f32[8,384]{1,0:T(8,128)S(1)} %get-tuple-element.50.tail), channel_id=1, source_target_pairs={{0,4},{4,0},{8,12},{12,8},{1,5},{5,1},{9,13},{13,9},{2,6},{6,2},{1... | collective-permute-start | bytes 36872 | tf_op jit(solution)/shard_map/ppermute | solution.py:451

commit v13 on v12

--- a/solution.py
+++ b/solution.py
@@ -62,7 +62,9 @@
     inputs, b_proj, grad, c_proj, *rest
 ):
     pays = rest[: parts - 1]
-    rates, gains, codes, gates, taps, steps, scaled, lead_pair, extra, sems = rest[parts - 1 :]
+    rates, gains, codes, gates, taps, steps, scaled, grad_scaled, lead_pair, extra, sems = rest[
+        parts - 1 :
+    ]
     rows, channels = grad.shape
     chunks = rows // CHUNK
     sources = (
@@ -164,17 +166,17 @@
         scaled[both, :] = (mixed * scale).astype(BF16)
         if at == 0:
             extra[11:14, :] = scale[0:3, :]
+    for copy in copies[7:]:
+        copy.wait()
     state = dot(b_proj[...], scaled[...], ((0,), (0,))).astype(BF16)
     extra[2:5, :] = inputs[0:16, :].astype(F32)[0:3, :]
     extra[5:8, :] = inputs[rows - 16 : rows, :].astype(F32)[13:16, :]
     extra[8:11, 0:STATE] = b_proj[0:16, :].astype(F32)[0:3, :]
-    for copy in copies[7:]:
-        copy.wait()
     for at in range(0, rows, STEP_ROWS):
         both = slice(at, at + STEP_ROWS)
         scale = spread(front_out[:, both], onehot)
-        scaled[both, :] = (grad[both, :].astype(F32) * scale).astype(BF16)
-    adjoint = dot(c_proj[...], scaled[...], ((0,), (0,))).astype(BF16)
+        grad_scaled[both, :] = (grad[both, :].astype(F32) * scale).astype(BF16)
+    adjoint = dot(c_proj[...], grad_scaled[...], ((0,), (0,))).astype(BF16)
     me = lax.axis_index("seq")
     for distance in range(1, parts):
         pay = pays[distance - 1]
@@ -521,6 +523,7 @@
             pltpu.VMEM((4, channels), F32),
             pltpu.VMEM((8, rows), F32),
             pltpu.VMEM((rows, channels), BF16),
+            pltpu.VMEM((rows, channels), BF16),
             pltpu.VMEM((16, CHUNK), BF16),
             pltpu.VMEM((16, channels), F32),
             dma((9,)),

time: 31.9 us -> 31.9 us (level)
  no operation moved by 1% of the time
where the time goes in v13:
time: 31.9 us; the launch traced here: 31.7 us
  Pallas kernels  17.7 us (55%)
  starting transfers between devices  10.1 us (32%)
  waiting for transfers between devices  3.13 us (10%)
  between operations  0.68 us (2%)
    ppermute x6, starting transfers between devices, rotated(): lax.ppermute(block, axis, [(i, partner(i, distance, size)) for i in range...  10.1 us
    pallas_call x1, Pallas kernels, shards(): call(functools.partial(inner_kernel, heads), [vmem] * 9, [vmem] * 4, [bro...  5.82 us
    pallas_call x1, Pallas kernels, shards(): call(functools.partial(reduce_kernel, heads, parts), [hbm] * 9, [vmem] *...  5.17 us
    ppermute x6, waiting for transfers between devices, rotated(): lax.ppermute(block, axis, [(i, partner(i, distance, size)) for i in range...  3.13 us
    pallas_call x1, Pallas kernels, shards(): call(functools.partial(gradient_kernel, parts), [vmem] * (5 + parts), [vm...  3.05 us
    pallas_call x1, Pallas kernels, shards(): call(functools.partial(output_kernel, heads, parts), [vmem] * (8 + parts)...  2.48 us
    pallas_call x1, Pallas kernels, shards(): call(functools.partial(finish_kernel, parts, scale), [vmem] * (2 + parts)...  1.22 us
  transfers between devices with their start and end apart: 6, of which 2 were waited for; matrix products, arithmetic and copies ran while one was open for 0% of the time, Pallas kernels for 26%

profile of v13, /device:TPU:0, one launch (start us, length us, event | category | flops | bytes accessed | tf_op | source)
XLA Modules:
  0.0 31.7 jit_solution(10772934408109795937)
XLA Ops:
  0.6 5.2 %shard_map.112 = (bf16[32,2048]{1,0:T(8,128)(2,1)S(1)}, bf16[16,2048]{1,0:T(8,128)(2,1)S(1)}, bf16[16,2048]{1,0:T(8,128)(2,1)S(1)}, f32[3,16,384]{2,1,0:T(8,128)...) custom-call(f32[6]{0:T(128)} %rates_hbm.1, ...), custom_call_target="tpu_custom_call" | custom-call | flops 805306368 | bytes 4718592 | tf_op jit(solution)/shard_map/pallas_call | solution.py:499
  5.8 3.1 %collective-permute-start = (bf16[144,384]{1,0:T(8,128)(2,1)S(1)}, bf16[144,384]{1,0:T(8,128)(2,1)S(1)}, u32[]{:S(2)}, u32[]{:S(2)}) collective-permute-start(bf16[144,384]{1,0:T(8,128)(2,1)S(1)} %get-tuple-element.45), channel_id=1, source_target_pairs={{0,4},{4,0},{8,12},{12,8},{1,5},{5,1},{9,13},{13,9},{2,6},{6,2},{1... | collective-permute-start | bytes 331784 | tf_op jit(solution)/shard_map/ppermute | solution.py:453
  8.9 2.6 %collective-permute-start.1 = (bf16[144,384]{1,0:T(8,128)(2,1)S(1)}, bf16[144,384]{1,0:T(8,128)(2,1)S(1)}, u32[]{:S(2)}, u32[]{:S(2)}) collective-permute-start(bf16[144,384]{1,0:T(8,128)(2,1)S(1)} %get-tuple-element.46), channel_id=1, source_target_pairs={{0,8},{4,12},{8,0},{12,4},{1,9},{5,13},{9,1},{13,5},{2,10},{6,14},... | collective-permute-start | bytes 331784 | tf_op jit(solution)/shard_map/ppermute | solution.py:453
  11.5 0.0 collective-permute-start.2
  11.5 0.0 copy-start
  11.5 5.8 %shard_map.113 = (f32[2048,384]{1,0:T(8,128)S(1)}, f32[2048,384]{1,0:T(8,128)S(1)}, f32[2048,384]{1,0:T(8,128)S(1)}, f32[16,384]{1,0:T(8,128)S(1)}) custom-call(f32[8,384]{1,0:T(8,128)S(1)} %get-tuple-element.29.gains, bf16[32,2048]{1,0:T(8,128)(2,1)S(1)} %get-tuple-element.32.near, bf16[16,2048]{1,0:T(8,128)(2,1)S(1)} %get-tuple-element.33.far, ...), custom_call_target="tpu_custom_call" | custom-call | flops 2013265920 | bytes 4718592 | tf_op jit(solution)/shard_map/pallas_call | solution.py:550
  17.3 0.0 collective-permute-done.rest_0_
  17.3 2.9 %collective-permute-done.1.rest_1_ = bf16[144,384]{1,0:T(8,128)(2,1)S(1)} collective-permute-done((bf16[144,384]{1,0:T(8,128)(2,1)S(1)}, bf16[144,384]{1,0:T(8,128)(2,1)S(1)}, u32[]{:S(2)}, u32[]{:S(2)}) %collective-permute-start.1) | collective-permute-done | bytes 110624 | tf_op jit(solution)/shard_map/ppermute | solution.py:453
  20.3 0.0 collective-permute-done.2.rest_2_
  20.3 0.0 copy-done
  20.3 3.0 %shard_map.114 = (bf16[2048,384]{1,0:T(8,128)(2,1)S(1)}, f32[8,384]{1,0:T(8,128)S(1)}, f32[16,384]{1,0:T(8,128)S(1)}) custom-call(f32[4,384]{1,0:T(4,128)S(1)} %copy-done, f32[2048,384]{1,0:T(8,128)S(1)} %get-tuple-element.42.base, f32[2048,384]{1,0:T(8,128)S(1)} %get-tuple-element.43.weight, f32[16,384]{1,0:T(8,128)S(1)} %get-tuple-element.44.unscaled, ...), custom_call_target="tpu_custom_call" | custom-call | flops 402653184 | bytes 4718592 | tf_op jit(solution)/shard_map/pallas_call | solution.py:560
  23.3 2.6 %collective-permute-start.5 = (f32[8,384]{1,0:T(8,128)S(1)}, f32[8,384]{1,0:T(8,128)S(1)}, u32[]{:S(2)}, u32[]{:S(2)}) collective-permute-start(f32[8,384]{1,0:T(8,128)S(1)} %get-tuple-element.50.tail), channel_id=1, source_target_pairs={{0,12},{4,8},{8,4},{12,0},{1,13},{5,9},{9,5},{13,1},{2,14},{6,10},... | collective-permute-start | bytes 36872 | tf_op jit(solution)/shard_map/ppermute | solution.py:453
  25.9 0.7 %collective-permute-start.4 = (f32[8,384]{1,0:T(8,128)S(1)}, f32[8,384]{1,0:T(8,128)S(1)}, u32[]{:S(2)}, u32[]{:S(2)}) collective-permute-start(f32[8,384]{1,0:T(8,128)S(1)} %get-tuple-element.50.tail), channel_id=1, source_target_pairs={{0,8},{4,12},{8,0},{12,4},{1,9},{5,13},{9,1},{13,5},{2,10},{6,14},... | collective-permute-start | bytes 36872 | tf_op jit(solution)/shard_map/ppermute | solution.py:453
  26.6 1.2 %collective-permute-start.3 = (f32[8,384]{1,0:T(8,128)S(1)}, f32[8,384]{1,0:T(8,128)S(1)}, u32[]{:S(2)}, u32[]{:S(2)}) collective-permute-start(f32[8,384]{1,0:T(8,128)S(1)} %get-tuple-element.50.tail), channel_id=1, source_target_pairs={{0,4},{4,0},{8,12},{12,8},{1,5},{5,1},{9,13},{13,9},{2,6},{6,2},{1... | collective-permute-start | bytes 36872 | tf_op jit(solution)/shard_map/ppermute | solution.py:453
  27.8 2.5 %shard_map.115 = (bf16[2048,384]{1,0:T(8,128)(2,1)}, bf16[2048,384]{1,0:T(8,128)(2,1)}) custom-call(f32[8,384]{1,0:T(8,128)S(1)} %get-tuple-element.29.gains, f32[4,384]{1,0:T(4,128)S(1)} %copy-done, bf16[16,2048]{1,0:T(8,128)(2,1)S(1)} %get-tuple-element.30.front, f32[16,384]{1,0:T(8,128)S(1)} %get-tuple-element.31.lead, ...), custom_call_target="tpu_custom_call" | custom-call | flops 402653184 | bytes 4718592 | tf_op jit(solution)/shard_map/pallas_call | solution.py:570
  30.3 0.0 collective-permute-done.5.rest_2_
  30.3 0.2 collective-permute-done.4.rest_1_
  30.5 0.0 collective-permute-done.3.rest_0_
  30.5 1.2 %shard_map.116 = (bf16[2048,384]{1,0:T(8,128)(2,1)}, f32[4,384]{1,0:T(4,128)}) custom-call(f32[4,384]{1,0:T(4,128)S(1)} %copy-done, f32[8,384]{1,0:T(8,128)S(1)} %get-tuple-element.50.tail, f32[16,384]{1,0:T(8,128)S(1)} %get-tuple-element.51.edge, f32[8,384]{1,0:T(8,128)S(1)} %collective-permute-done.3.rest_0_, ...), custom_call_target="tpu_custom_call", output_to_operand_aliasing={{0}: (6, {})} | custom-call | bytes 4718592 | tf_op jit(solution)/shard_map/pallas_call | solution.py:580
Async XLA Ops:
  5.8 11.5 %collective-permute-start = (bf16[144,384]{1,0:T(8,128)(2,1)S(1)}, bf16[144,384]{1,0:T(8,128)(2,1)S(1)}, u32[]{:S(2)}, u32[]{:S(2)}) collective-permute-start(bf16[144,384]{1,0:T(8,128)(2,1)S(1)} %get-tuple-element.45), channel_id=1, source_target_pairs={{0,4},{4,0},{8,12},{12,8},{1,5},{5,1},{9,13},{13,9},{2,6},{6,2},{1... | collective-permute-start | bytes 331784 | tf_op jit(solution)/shard_map/ppermute | solution.py:453
  8.9 11.3 %collective-permute-start.1 = (bf16[144,384]{1,0:T(8,128)(2,1)S(1)}, bf16[144,384]{1,0:T(8,128)(2,1)S(1)}, u32[]{:S(2)}, u32[]{:S(2)}) collective-permute-start(bf16[144,384]{1,0:T(8,128)(2,1)S(1)} %get-tuple-element.46), channel_id=1, source_target_pairs={{0,8},{4,12},{8,0},{12,4},{1,9},{5,13},{9,1},{13,5},{2,10},{6,14},... | collective-permute-start | bytes 331784 | tf_op jit(solution)/shard_map/ppermute | solution.py:453
  11.5 8.8 %collective-permute-start.2 = (bf16[144,384]{1,0:T(8,128)(2,1)S(1)}, bf16[144,384]{1,0:T(8,128)(2,1)S(1)}, u32[]{:S(2)}, u32[]{:S(2)}) collective-permute-start(bf16[144,384]{1,0:T(8,128)(2,1)S(1)} %get-tuple-element.47), channel_id=1, source_target_pairs={{0,12},{4,8},{8,4},{12,0},{1,13},{5,9},{9,5},{13,1},{2,14},{6,10},... | collective-permute-start | bytes 331784 | tf_op jit(solution)/shard_map/ppermute | solution.py:453
  11.5 8.8 %copy-start = (f32[4,384]{1,0:T(4,128)S(1)}, f32[4,384]{1,0:T(4,128)}, u32[]{:S(2)}) copy-start(f32[4,384]{1,0:T(4,128)} %taps.5) | copy-start | bytes 18436
  23.3 6.9 %collective-permute-start.5 = (f32[8,384]{1,0:T(8,128)S(1)}, f32[8,384]{1,0:T(8,128)S(1)}, u32[]{:S(2)}, u32[]{:S(2)}) collective-permute-start(f32[8,384]{1,0:T(8,128)S(1)} %get-tuple-element.50.tail), channel_id=1, source_target_pairs={{0,12},{4,8},{8,4},{12,0},{1,13},{5,9},{9,5},{13,1},{2,14},{6,10},... | collective-permute-start | bytes 36872 | tf_op jit(solution)/shard_map/ppermute | solution.py:453
  25.9 4.6 %collective-permute-start.4 = (f32[8,384]{1,0:T(8,128)S(1)}, f32[8,384]{1,0:T(8,128)S(1)}, u32[]{:S(2)}, u32[]{:S(2)}) collective-permute-start(f32[8,384]{1,0:T(8,128)S(1)} %get-tuple-element.50.tail), channel_id=1, source_target_pairs={{0,8},{4,12},{8,0},{12,4},{1,9},{5,13},{9,1},{13,5},{2,10},{6,14},... | collective-permute-start | bytes 36872 | tf_op jit(solution)/shard_map/ppermute | solution.py:453
  26.6 3.9 %collective-permute-start.3 = (f32[8,384]{1,0:T(8,128)S(1)}, f32[8,384]{1,0:T(8,128)S(1)}, u32[]{:S(2)}, u32[]{:S(2)}) collective-permute-start(f32[8,384]{1,0:T(8,128)S(1)} %get-tuple-element.50.tail), channel_id=1, source_target_pairs={{0,4},{4,0},{8,12},{12,8},{1,5},{5,1},{9,13},{13,9},{2,6},{6,2},{1... | collective-permute-start | bytes 36872 | tf_op jit(solution)/shard_map/ppermute | solution.py:453
